TPU v7x, 32 devices: a whole 2x2x4 slice. The times are simulated.
32 devices in a mesh: tm: 8 (over z, y), row: 4 (over x, core).
Axes of the slice: x: 2, y: 2, z: 4, core: 2. Of those that a mesh axis runs over, the one named last changes fastest.
Arguments:
- inv_diag: float32 [32, 512, 512], P('tm', 'row'), may hold values from -0.04 to 1.1, as said below
- coupling: float32 [32, 512, 512], P('tm', 'row'), may hold values from -0.99 to 0.04, as said below
- noise: float32 [32, 512, 1024], P('tm', None, 'row'), may hold values from -2 to 2
- obs_day: int32 [131072], P(('tm', 'row')), may hold values from 0 to 31
- obs_node: int32 [131072], P(('tm', 'row')), may hold values from 0 to 511
- obs_value: float32 [131072], P(('tm', 'row')), may hold values from -0.6 to 0.6
Outputs:
- samples: float32 [32, 512, 1024], P('tm', None, 'row')
Inputs may be any that keep to these rules, and one draw needn't show every extreme that they name: `inv_diag`: one 512 x 512 block a day. `coupling`: one 512 x 512 block a day.
All inputs are finite; a program needn't handle non-finite values.
Results may differ from a plain program's by a relative error of at most 0.0003.
Values sent between devices are 32-bit elements; how exact they have to be, the bound alone decides.
No kernel may reach another device: no remote copies, remote signals or barrier semaphores. Data moves between devices by JAX's collectives and lax.ppermute only.
A program may use at most 256 MiB of HBM per device.

v0:
```python
import jax
import jax.numpy as jnp
from jax import lax
from jax.sharding import PartitionSpec as P

highest = lax.Precision.HIGHEST


def shifted(value, axis, steps):
    count = lax.axis_size(axis)
    leading, last = (max(0, -steps), min(count, count - steps))
    return lax.ppermute(value, axis, [(source, source + steps) for source in range(leading, last)])


def matmul(left_side, right_side):
    return jnp.dot(left_side, right_side, precision=highest, preferred_element_type=jnp.float32)


def transposed_product(left_side, right_side):
    return lax.dot_general(
        left_side,
        right_side,
        (((0,), (0,)), ((), ())),
        precision=highest,
        preferred_element_type=jnp.float32,
    )


def local(inv_diag, coupling, noise, obs_day, obs_node, obs_value):
    part_count = lax.axis_size("tm")
    row_count = lax.axis_size("row")
    my_part = lax.axis_index("tm")
    my_column = lax.axis_index("row")
    day_count, row_share, node_count = inv_diag.shape
    sample_cols = noise.shape[2]
    owner_row = obs_day // day_count * row_count + obs_node // row_share
    within = obs_day % day_count * row_share + obs_node % row_share
    dense_sources = (
        jnp.zeros((part_count * row_count, day_count * row_share), jnp.float32)
        .at[owner_row, within]
        .add(obs_value)
    )
    own_sources = lax.psum_scatter(
        dense_sources, ("tm", "row"), scatter_dimension=0, tiled=True
    ).reshape(day_count, row_share)
    stacked = jnp.concatenate([inv_diag, coupling], axis=0)
    blocks, source_rows = (
        lax.all_gather(stacked, "row", axis=1, tiled=True),
        lax.all_gather(own_sources, "row", axis=1, tiled=True),
    )
    inverse = blocks[:day_count]
    links = blocks[day_count:]
    eye_cols = (
        lax.broadcasted_iota(jnp.int32, (node_count, row_share), 0)
        == lax.broadcasted_iota(jnp.int32, (node_count, row_share), 1) + my_column * row_share
    ).astype(jnp.float32)
    forward_cols = eye_cols
    local_applied = jnp.zeros((node_count,), jnp.float32)
    for day_index in range(day_count):
        local_applied = matmul(
            links[day_index], matmul(inverse[day_index], source_rows[day_index] - local_applied)
        )
        forward_cols = -matmul(links[day_index], matmul(inverse[day_index], forward_cols))
    backward_cols = eye_cols
    for day_index in reversed(range(day_count)):
        backward_cols = -transposed_product(
            inverse[day_index], transposed_product(links[day_index], backward_cols)
        )
    forward_map, backward_map = (
        lax.all_gather(forward_cols, "row", axis=1, tiled=True),
        lax.all_gather(backward_cols, "row", axis=1, tiled=True),
    )

    def forward_section(section_index, incoming):
        departing_flux = matmul(forward_map, incoming) + local_applied
        received = shifted(departing_flux, "tm", 1)
        return jnp.where(my_part == section_index + 1, received, incoming)

    entering = lax.fori_loop(
        0, part_count - 1, forward_section, jnp.zeros((node_count,), jnp.float32)
    )
    applied = entering
    sources = []
    for day_index in range(day_count):
        current = matmul(inverse[day_index], source_rows[day_index] - applied)
        sources.append(current[:, None] + noise[day_index])
        if day_index + 1 < day_count:
            applied = matmul(links[day_index], current)
    local_state = transposed_product(inverse[day_count - 1], sources[day_count - 1])
    for day_index in reversed(range(day_count - 1)):
        local_state = transposed_product(
            inverse[day_index],
            sources[day_index] - transposed_product(links[day_index], local_state),
        )

    def backward_section(section_index, incoming):
        departing_flux = matmul(backward_map, incoming) + local_state
        received = shifted(departing_flux, "tm", -1)
        return jnp.where(my_part == part_count - 2 - section_index, received, incoming)

    leaving = lax.fori_loop(
        0, part_count - 1, backward_section, jnp.zeros((node_count, sample_cols), jnp.float32)
    )
    following = leaving
    results = [None] * day_count
    for day_index in reversed(range(day_count)):
        following = transposed_product(
            inverse[day_index], sources[day_index] - transposed_product(links[day_index], following)
        )
        results[day_index] = following
    return jnp.stack(results)


def solution(mesh):
    return jax.shard_map(
        local,
        mesh=mesh,
        in_specs=(
            P("tm", "row", None),
            P("tm", "row", None),
            P("tm", None, "row"),
            P(("tm", "row")),
            P(("tm", "row")),
            P(("tm", "row")),
        ),
        out_specs=P("tm", None, "row"),
        check_vma=False,
    )
```

profile of v0, /device:TPU:0, one launch (start us, length us, event | category | flops | bytes accessed | tf_op | source)
XLA Modules:
  0.0 511.0 jit_solution(6063060063385912097)
XLA Ops:
  9.7 22.1 %scatter_custom_fusion = f32[16384]{0:T(1024)S(1)} fusion(s32[4096]{0:T(1024)S(1)} %broadcast_select_fusion.2, f32[4096]{0:T(1024)} %param.15, f32[]{:T(128)} %constant.80.clone.1), kind=kCustom, calls=%fused_computation.80 | custom fusion | flops 4096 | bytes 66048
  32.5 3.0 pad_maximum_fusion
  35.7 156.9 %all-reduce.3.cloned.1.call-done = f32[32,512]{1,0:T(8,128)} async-done(((f32[32,512]{1,0:T(8,128)}), f32[32,512]{1,0:T(8,128)}) %all-reduce.3.cloned.1.call-update) | async-done | bytes 65552
  193.3 6.1 %all_gather.13 = f32[4,512]{1,0:T(4,128)S(1)} all-gather(f32[4,128]{1,0:T(4,128)S(1)} %bitcast.232), channel_id=1, replica_groups=mesh['tm'=8,'row'=4] {'row'}, dimensions={1}, use_global_device_ids=true | all-gather | bytes 10240 | tf_op jit(solution)/shard_map/all_gather | solution.py:49
  214.7 2.9 convolution_negate_fusion.4
  217.9 2.2 convolution_bitcast_fusion.4
  222.3 2.3 convolution_bitcast_fusion.3
  224.5 2.2 fusion.22
  226.8 2.2 convolution_bitcast_fusion.2
  229.0 2.2 fusion.15
  231.2 2.2 fusion.4
  233.5 3.0 convolution_negate_fusion.3
  236.5 3.0 fusion.13
  239.5 3.0 convolution_negate_fusion.2
  242.6 3.0 fusion.20
  245.6 3.4 convolution_negate_fusion.1
  249.0 3.0 fusion.27
  252.1 3.9 convolution_negate_fusion
  258.2 2.2 fusion.5
  260.4 57.3 %while.28 = (s32[]{:T(128)}, f32[512]{0:T(512)S(1)}, s32[]{:T(128)}, f32[512,512]{1,0:T(8,128)}, f32[512]{0:T(512)S(1)}, /*index=5*/s32[]{:T(128)}, s32[]{:T(128)}) while((s32[]{:T(128)}, f32[512]{0:T(512)S(1)}, s32[]{:T(128)}, f32[512,512]{1,0:T(8,128)}, f32[512]{0:T(512)S(1)}, /*index=5*/s32[]{:T(128)}, s32[]{:T(128)}) %tuple.77), condition=%wide.region_3.4_spmd.clone, body=%wide.region_2.3_spmd.clone.sunk | while | flops 3147780 | bytes 1077386 | solution.py:79
  260.4 2.2 fusion.102
  262.7 2.7 collective-permute-start
  268.9 4.3 collective-permute-start
  276.8 5.1 collective-permute-start
  285.4 5.1 collective-permute-start
  294.0 5.1 collective-permute-start
  302.6 5.1 collective-permute-start
  311.2 5.1 collective-permute-start
  319.9 2.2 fusion.28
  322.2 2.2 fusion.25
  324.4 2.2 fusion.21
  326.6 2.2 fusion.18
  328.8 2.2 fusion.14
  331.0 2.2 fusion.11
  333.2 3.1 fusion.10
  336.4 3.0 convolution_subtract_fusion.6
  339.4 3.0 fusion.17
  342.5 3.0 convolution_subtract_fusion.5
  345.5 3.2 fusion.24
  348.8 3.0 convolution_subtract_fusion.4
  351.8 3.0 fusion.6
  354.9 121.9 %while.29 = (s32[]{:T(128)}, f32[512,256]{1,0:T(8,128)S(1)}, s32[]{:T(128)}, f32[512,512]{1,0:T(8,128)}, f32[512,256]{1,0:T(8,128)S(1)}, /*index=5*/s32[]{:T(128)}, s32[]{:T(128)}, s32[]{:T(128)}) while((s32[]{:T(128)}, f32[512,256]{1,0:T(8,128)S(1)}, s32[]{:T(128)}, f32[512,512]{1,0:T(8,128)}, f32[512,256]{1,0:T(8,128)S(1)}, ...), condition=%wide.region_5.6_spmd.clone, body=%wide.region_4.5_spmd.clone.sunk | while | flops 805830656 | bytes 6291614 | solution.py:101
  354.9 2.2 convolution_add_fusion.2
  358.4 11.1 %collective-permute-done.1 = f32[512,256]{1,0:T(8,128)S(1)} collective-permute-done((f32[512,256]{1,0:T(8,128)S(1)}, f32[512,256]{1,0:T(8,128)S(1)}, u32[]{:S(2)}, u32[]{:S(2)}) %collective-permute-start.1) | collective-permute-done | bytes 524320 | tf_op jit(solution)/shard_map/while/body/eval_jaxpr/ppermute | solution.py:12
  369.7 2.2 convolution_add_fusion.2
  373.2 13.0 %collective-permute-done.1 = f32[512,256]{1,0:T(8,128)S(1)} collective-permute-done((f32[512,256]{1,0:T(8,128)S(1)}, f32[512,256]{1,0:T(8,128)S(1)}, u32[]{:S(2)}, u32[]{:S(2)}) %collective-permute-start.1) | collective-permute-done | bytes 524320 | tf_op jit(solution)/shard_map/while/body/eval_jaxpr/ppermute | solution.py:12
  386.4 2.2 convolution_add_fusion.2
  389.9 14.4 %collective-permute-done.1 = f32[512,256]{1,0:T(8,128)S(1)} collective-permute-done((f32[512,256]{1,0:T(8,128)S(1)}, f32[512,256]{1,0:T(8,128)S(1)}, u32[]{:S(2)}, u32[]{:S(2)}) %collective-permute-start.1) | collective-permute-done | bytes 524320 | tf_op jit(solution)/shard_map/while/body/eval_jaxpr/ppermute | solution.py:12
  404.5 2.2 convolution_add_fusion.2
  408.0 14.9 %collective-permute-done.1 = f32[512,256]{1,0:T(8,128)S(1)} collective-permute-done((f32[512,256]{1,0:T(8,128)S(1)}, f32[512,256]{1,0:T(8,128)S(1)}, u32[]{:S(2)}, u32[]{:S(2)}) %collective-permute-start.1) | collective-permute-done | bytes 524320 | tf_op jit(solution)/shard_map/while/body/eval_jaxpr/ppermute | solution.py:12
  423.1 2.2 convolution_add_fusion.2
  426.6 16.2 %collective-permute-done.1 = f32[512,256]{1,0:T(8,128)S(1)} collective-permute-done((f32[512,256]{1,0:T(8,128)S(1)}, f32[512,256]{1,0:T(8,128)S(1)}, u32[]{:S(2)}, u32[]{:S(2)}) %collective-permute-start.1) | collective-permute-done | bytes 524320 | tf_op jit(solution)/shard_map/while/body/eval_jaxpr/ppermute | solution.py:12
  442.9 2.2 convolution_add_fusion.2
  446.5 16.1 %collective-permute-done.1 = f32[512,256]{1,0:T(8,128)S(1)} collective-permute-done((f32[512,256]{1,0:T(8,128)S(1)}, f32[512,256]{1,0:T(8,128)S(1)}, u32[]{:S(2)}, u32[]{:S(2)}) %collective-permute-start.1) | collective-permute-done | bytes 524320 | tf_op jit(solution)/shard_map/while/body/eval_jaxpr/ppermute | solution.py:12
  462.8 2.2 convolution_add_fusion.2
  466.3 10.4 %collective-permute-done.1 = f32[512,256]{1,0:T(8,128)S(1)} collective-permute-done((f32[512,256]{1,0:T(8,128)S(1)}, f32[512,256]{1,0:T(8,128)S(1)}, u32[]{:S(2)}, u32[]{:S(2)}) %collective-permute-start.1) | collective-permute-done | bytes 524320 | tf_op jit(solution)/shard_map/while/body/eval_jaxpr/ppermute | solution.py:12
  476.8 3.3 convolution_subtract_fusion.3
  480.1 3.0 fusion.9
  483.2 3.2 convolution_subtract_fusion.2
  486.4 3.0 fusion.16
  489.4 3.0 convolution_subtract_fusion.1
  492.5 3.0 fusion.23
  495.5 3.0 convolution_subtract_fusion
  498.5 3.0 convolution_bitcast_fusion
  (91 shorter events, 59.7 us)
Async XLA Ops:
  7.4 185.2 %all-reduce.3.cloned.1.call-start = ((), (), s32[]{:S(2)}) async-start(), calls=%async_computation.3 | async-start | bytes 131072
  32.5 167.0 %all-gather.4.cloned.1.call-start = ((), (), s32[]{:S(2)}) async-start(), calls=%async_computation | async-start | bytes 10485760 | tf_op jit(solution)/shard_map/all_gather | solution.py:48
  35.6 224.8 %all-gather.6.cloned.1.call-start = ((), (), s32[]{:S(2)}) async-start(), calls=%async_computation.1 | async-start | bytes 1310720 | tf_op jit(solution)/shard_map/all_gather | solution.py:70
  217.6 137.3 %all-gather.8.cloned.1.call-start = ((), (), s32[]{:S(2)}) async-start(), calls=%async_computation.2 | async-start | bytes 1310720 | tf_op jit(solution)/shard_map/all_gather | solution.py:71
  252.1 81.2 %copy-start = (f32[4,512,256]{2,1,0:T(8,128)S(1)}, f32[4,512,256]{2,1,0:T(8,128)}, u32[]{:S(2)}) copy-start(f32[4,512,256]{2,1,0:T(8,128)} %param.12) | copy-start | bytes 6291460
  262.7 4.0 collective-permute-start
  268.9 5.6 %collective-permute-start = (f32[512]{0:T(512)S(1)}, f32[512]{0:T(512)S(1)}, u32[]{:S(2)}, u32[]{:S(2)}) collective-permute-start(f32[512]{0:T(512)S(1)} %add.224), channel_id=1, source_target_pairs={{0,4},{4,8},{8,12},{12,16},{16,20},{20,24},{24,28},{1,5},{5,9},{9,... | collective-permute-start | bytes 6152 | tf_op jit(solution)/shard_map/while/body/eval_jaxpr/ppermute | solution.py:12
  276.8 6.4 %collective-permute-start = (f32[512]{0:T(512)S(1)}, f32[512]{0:T(512)S(1)}, u32[]{:S(2)}, u32[]{:S(2)}) collective-permute-start(f32[512]{0:T(512)S(1)} %add.224), channel_id=1, source_target_pairs={{0,4},{4,8},{8,12},{12,16},{16,20},{20,24},{24,28},{1,5},{5,9},{9,... | collective-permute-start | bytes 6152 | tf_op jit(solution)/shard_map/while/body/eval_jaxpr/ppermute | solution.py:12
  285.4 6.4 %collective-permute-start = (f32[512]{0:T(512)S(1)}, f32[512]{0:T(512)S(1)}, u32[]{:S(2)}, u32[]{:S(2)}) collective-permute-start(f32[512]{0:T(512)S(1)} %add.224), channel_id=1, source_target_pairs={{0,4},{4,8},{8,12},{12,16},{16,20},{20,24},{24,28},{1,5},{5,9},{9,... | collective-permute-start | bytes 6152 | tf_op jit(solution)/shard_map/while/body/eval_jaxpr/ppermute | solution.py:12
  294.0 6.4 %collective-permute-start = (f32[512]{0:T(512)S(1)}, f32[512]{0:T(512)S(1)}, u32[]{:S(2)}, u32[]{:S(2)}) collective-permute-start(f32[512]{0:T(512)S(1)} %add.224), channel_id=1, source_target_pairs={{0,4},{4,8},{8,12},{12,16},{16,20},{20,24},{24,28},{1,5},{5,9},{9,... | collective-permute-start | bytes 6152 | tf_op jit(solution)/shard_map/while/body/eval_jaxpr/ppermute | solution.py:12
  302.6 6.4 %collective-permute-start = (f32[512]{0:T(512)S(1)}, f32[512]{0:T(512)S(1)}, u32[]{:S(2)}, u32[]{:S(2)}) collective-permute-start(f32[512]{0:T(512)S(1)} %add.224), channel_id=1, source_target_pairs={{0,4},{4,8},{8,12},{12,16},{16,20},{20,24},{24,28},{1,5},{5,9},{9,... | collective-permute-start | bytes 6152 | tf_op jit(solution)/shard_map/while/body/eval_jaxpr/ppermute | solution.py:12
  311.2 6.4 %collective-permute-start = (f32[512]{0:T(512)S(1)}, f32[512]{0:T(512)S(1)}, u32[]{:S(2)}, u32[]{:S(2)}) collective-permute-start(f32[512]{0:T(512)S(1)} %add.224), channel_id=1, source_target_pairs={{0,4},{4,8},{8,12},{12,16},{16,20},{20,24},{24,28},{1,5},{5,9},{9,... | collective-permute-start | bytes 6152 | tf_op jit(solution)/shard_map/while/body/eval_jaxpr/ppermute | solution.py:12
  357.1 12.4 %collective-permute-start.1 = (f32[512,256]{1,0:T(8,128)S(1)}, f32[512,256]{1,0:T(8,128)S(1)}, u32[]{:S(2)}, u32[]{:S(2)}) collective-permute-start(f32[512,256]{1,0:T(8,128)S(1)} %convolution_add_fusion.2), channel_id=1, source_target_pairs={{4,0},{8,4},{12,8},{16,12},{20,16},{24,20},{28,24},{5,1},{9,5},{13... | collective-permute-start | bytes 1572872 | tf_op jit(solution)/shard_map/while/body/eval_jaxpr/ppermute | solution.py:12
  371.9 14.3 %collective-permute-start.1 = (f32[512,256]{1,0:T(8,128)S(1)}, f32[512,256]{1,0:T(8,128)S(1)}, u32[]{:S(2)}, u32[]{:S(2)}) collective-permute-start(f32[512,256]{1,0:T(8,128)S(1)} %convolution_add_fusion.2), channel_id=1, source_target_pairs={{4,0},{8,4},{12,8},{16,12},{20,16},{24,20},{28,24},{5,1},{9,5},{13... | collective-permute-start | bytes 1572872 | tf_op jit(solution)/shard_map/while/body/eval_jaxpr/ppermute | solution.py:12
  388.6 15.7 %collective-permute-start.1 = (f32[512,256]{1,0:T(8,128)S(1)}, f32[512,256]{1,0:T(8,128)S(1)}, u32[]{:S(2)}, u32[]{:S(2)}) collective-permute-start(f32[512,256]{1,0:T(8,128)S(1)} %convolution_add_fusion.2), channel_id=1, source_target_pairs={{4,0},{8,4},{12,8},{16,12},{20,16},{24,20},{28,24},{5,1},{9,5},{13... | collective-permute-start | bytes 1572872 | tf_op jit(solution)/shard_map/while/body/eval_jaxpr/ppermute | solution.py:12
  406.7 16.2 %collective-permute-start.1 = (f32[512,256]{1,0:T(8,128)S(1)}, f32[512,256]{1,0:T(8,128)S(1)}, u32[]{:S(2)}, u32[]{:S(2)}) collective-permute-start(f32[512,256]{1,0:T(8,128)S(1)} %convolution_add_fusion.2), channel_id=1, source_target_pairs={{4,0},{8,4},{12,8},{16,12},{20,16},{24,20},{28,24},{5,1},{9,5},{13... | collective-permute-start | bytes 1572872 | tf_op jit(solution)/shard_map/while/body/eval_jaxpr/ppermute | solution.py:12
  425.3 17.5 %collective-permute-start.1 = (f32[512,256]{1,0:T(8,128)S(1)}, f32[512,256]{1,0:T(8,128)S(1)}, u32[]{:S(2)}, u32[]{:S(2)}) collective-permute-start(f32[512,256]{1,0:T(8,128)S(1)} %convolution_add_fusion.2), channel_id=1, source_target_pairs={{4,0},{8,4},{12,8},{16,12},{20,16},{24,20},{28,24},{5,1},{9,5},{13... | collective-permute-start | bytes 1572872 | tf_op jit(solution)/shard_map/while/body/eval_jaxpr/ppermute | solution.py:12
  445.2 17.4 %collective-permute-start.1 = (f32[512,256]{1,0:T(8,128)S(1)}, f32[512,256]{1,0:T(8,128)S(1)}, u32[]{:S(2)}, u32[]{:S(2)}) collective-permute-start(f32[512,256]{1,0:T(8,128)S(1)} %convolution_add_fusion.2), channel_id=1, source_target_pairs={{4,0},{8,4},{12,8},{16,12},{20,16},{24,20},{28,24},{5,1},{9,5},{13... | collective-permute-start | bytes 1572872 | tf_op jit(solution)/shard_map/while/body/eval_jaxpr/ppermute | solution.py:12
  465.0 11.7 %collective-permute-start.1 = (f32[512,256]{1,0:T(8,128)S(1)}, f32[512,256]{1,0:T(8,128)S(1)}, u32[]{:S(2)}, u32[]{:S(2)}) collective-permute-start(f32[512,256]{1,0:T(8,128)S(1)} %convolution_add_fusion.2), channel_id=1, source_target_pairs={{4,0},{8,4},{12,8},{16,12},{20,16},{24,20},{28,24},{5,1},{9,5},{13... | collective-permute-start | bytes 1572872 | tf_op jit(solution)/shard_map/while/body/eval_jaxpr/ppermute | solution.py:12
  476.8 12.6 %copy-start.1 = (f32[4,512,256]{2,1,0:T(8,128)S(1)}, f32[4,512,256]{2,1,0:T(8,128)}, u32[]{:S(2)}) copy-start(f32[4,512,256]{2,1,0:T(8,128)} %param.12) | copy-start | bytes 6291460
Sparse Core Ops, SparseCore 0:
  32.6 159.9 all-reduce.2
Sparse Core Ops, SparseCore 1:
  35.7 60.9 all-gather.3
  217.7 16.3 all-gather.5
  256.1 16.2 all-gather.7
where the time goes:
time: 521 us; the launch traced here: 511 us
  waiting for transfers between devices  262 us (50%)
  matrix products  153 us (29%)
  starting transfers between devices  41.8 us (8%)
  other arithmetic  30.1 us (6%)
  between operations  15.7 us (3%)
  blocking collectives  6.15 us (1%)
    unnamed x5, waiting for transfers between devices  157 us
    ppermute x14, waiting for transfers between devices, shifted(): lax.ppermute(value, axis, [(source, source + steps) for source in range(l...  105 us
    dot_general x37, matrix products, matmul(): jnp.dot(left_side, right_side, precision=highest, preferred_element_type=...  82.2 us
    dot_general x23, matrix products, transposed_product(): lax.dot_general(left_side, right_side, (((0,), (0,)), ((), ())), precisio...  71 us
    ppermute x14, starting transfers between devices, shifted(): lax.ppermute(value, axis, [(source, source + steps) for source in range(l...  41.5 us
    unnamed x6, other arithmetic  23.7 us
  transfers between devices with their start and end apart: 18, of which 15 were waited for; matrix products, arithmetic and copies ran while one was open for 19% of the time, Pallas kernels for 0%

commit v1 on v0

v1 whole, which is shorter than its diff:
```python
import functools

import jax
import jax.numpy as jnp
from jax import lax
from jax.experimental import pallas as pl
from jax.experimental.pallas import tpu as pltpu
from jax.sharding import PartitionSpec as P

F32 = jnp.float32
BF16 = jnp.bfloat16
CORES = 2
PAIR = 2
LINES = 8


def split(value):
    high = value.astype(BF16)
    return high, (value - high.astype(F32)).astype(BF16)


def dot_parts(left, right, dims):
    product = functools.partial(
        lax.dot_general, dimension_numbers=(dims, ((), ())), preferred_element_type=F32
    )
    return product(left[0], right[0]) + (product(left[0], right[1]) + product(left[1], right[0]))


NN = ((1,), (0,))
TN = ((0,), (0,))
NT = ((1,), (1,))


def call(body, out_shape, name, scratch=(), scalars=1, inputs=0, specs=None):
    return pl.pallas_call(
        body,
        out_shape=out_shape,
        grid=(1,),
        in_specs=[pl.BlockSpec(memory_space=pltpu.SMEM)] * scalars
        + (specs or [pl.BlockSpec(memory_space=pltpu.VMEM)] * inputs),
        out_specs=jax.tree.map(lambda _: pl.BlockSpec(memory_space=pltpu.VMEM), out_shape),
        scratch_shapes=list(scratch),
        compiler_params=pltpu.CompilerParams(vmem_limit_bytes=56 * 1024 * 1024),
        name=name,
    )


def shape(*dims, dtype=F32):
    return jax.ShapeDtypeStruct(dims, dtype)


def bin_observations(obs_day, obs_node, obs_value, days, nodes):
    chunk = min(512, obs_day.shape[0])
    chunks = obs_day.shape[0] // chunk

    def body(day_ref, node_ref, value_ref, out_ref):
        total = jnp.zeros((3 * days, nodes), F32)
        for index in range(chunks):
            row = pl.ds(index, 1)
            value = value_ref[row, :]
            high = value.astype(BF16).astype(F32)
            middle = (value - high).astype(BF16).astype(F32)
            low = value - high - middle
            is_day = lax.broadcasted_iota(jnp.int32, (days, chunk), 0) == day_ref[row, :]
            marked = jnp.concatenate(
                [jnp.where(is_day, part, 0.0).astype(BF16) for part in (high, middle, low)], axis=0
            )
            is_node = lax.broadcasted_iota(jnp.int32, (nodes, chunk), 0) == node_ref[row, :]
            total += lax.dot_general(
                marked, is_node.astype(F32).astype(BF16), (NT, ((), ())), preferred_element_type=F32
            )
        out_ref[...] = total[:days] + (total[days : 2 * days] + total[2 * days :])

    return call(body, shape(days, nodes), "bin_observations", scalars=0, inputs=3)(
        *(value.reshape(chunks, chunk) for value in (obs_day, obs_node, obs_value))
    )


def day_step(day, position, row_count, own, pieces, noise, right_side, state):
    nodes, columns = noise.shape[1:]
    share = nodes // row_count
    square = shape(nodes, nodes)
    first = state is None

    def body(position_ref, *refs):
        refs = list(refs)
        inverse_rows = [refs.pop(0) for _ in range(row_count)]
        link_rows = [refs.pop(0) for _ in range(row_count)]
        noise_ref, source_ref = refs.pop(0), refs.pop(0)
        if not first:
            path_ref, gram_ref, sum_ref, applied_ref, back_ref = [refs.pop(0) for _ in range(5)]
        (path_out, gram_out, sum_out, applied_out, back_out) = [refs.pop(0) for _ in range(5)]
        (moved_out, own_out, map_out, local_out, current_out) = [refs.pop(0) for _ in range(5)]
        full_inverse, full_link = refs
        me = position_ref[0]
        for offset in range(row_count):
            at = pl.ds(pl.multiple_of((me ^ offset) * share, share), share)
            full_inverse[at, :] = inverse_rows[offset][0]
            full_link[at, :] = link_rows[offset][0]
        inverse, link = split(full_inverse[...]), split(full_link[...])
        noise_parts = split(noise_ref[0])
        if first:
            moved, moved_parts = full_inverse[...], inverse
            wanted = source_ref[0]
        else:
            moved = dot_parts(inverse, split(path_ref[...]), NN)
            moved_parts = split(moved)
            wanted = source_ref[0] - applied_ref[...]
        current = dot_parts(split(wanted), inverse, NT)
        current_parts = split(current)
        applied_out[...] = dot_parts(current_parts, link, NT)
        back = dot_parts(current_parts, moved_parts, NN)
        gram = dot_parts(moved_parts, moved_parts, TN)
        total = dot_parts(moved_parts, noise_parts, TN)
        if not first:
            back, gram, total = back + back_ref[...], gram + gram_ref[...], total + sum_ref[...]
        path_out[...] = -dot_parts(link, moved_parts, NN)
        gram_out[...] = gram
        sum_out[...] = total
        back_out[...] = back
        moved_out[...] = moved
        own_out[0], own_out[1] = inverse
        step = split(-dot_parts(link, inverse, NN))
        map_out[0], map_out[1] = step
        local_out[...] = dot_parts(inverse, noise_parts, TN)
        current_out[...] = current

    one_day = pl.BlockSpec((1, share, nodes), lambda _: (day, 0, 0))
    specs = []
    operands = []
    for which in range(2):
        for offset in range(row_count):
            if offset < CORES:
                operands.append(own[which][offset])
                specs.append(one_day)
            else:
                operands.append(pieces[which][offset])
                specs.append(pl.BlockSpec(memory_space=pltpu.VMEM))
    operands += [noise, right_side]
    specs += [
        pl.BlockSpec((1, nodes, columns), lambda _: (day, 0, 0)),
        pl.BlockSpec((1, LINES, nodes), lambda _: (day, 0, 0)),
    ]
    if not first:
        operands += list(state)
        specs += [pl.BlockSpec(memory_space=pltpu.VMEM)] * 5
    line = shape(LINES, nodes)
    halves = shape(2, nodes, nodes, dtype=BF16)
    outs = (
        square, square, shape(nodes, columns), line, line,
        square, halves, halves, shape(nodes, columns), line,
    )
    results = call(
        body,
        outs,
        f"day_{day}",
        scratch=[pltpu.VMEM((nodes, nodes), F32)] * 2,
        specs=specs,
    )(position, *operands)
    return results[:5], results[5:]


def local(inv_diag, coupling, noise, obs_day, obs_node, obs_value):
    part_count = lax.axis_size("tm")
    row_count = lax.axis_size("row")
    my_part = lax.axis_index("tm")
    my_row = lax.axis_index("row")
    day_count, share, nodes = inv_diag.shape
    columns = noise.shape[2]
    half = columns // PAIR
    half_nodes = nodes // CORES
    groups = part_count // PAIR
    chips = row_count // CORES

    def to_row(value, distance):
        return lax.ppermute(value, "row", [(i, i ^ distance) for i in range(row_count)])

    def to_pair(value):
        return lax.ppermute(value, "tm", [(i, i ^ 1) for i in range(part_count)])

    def to_group(value, source, target):
        return lax.ppermute(
            value, "tm", [(PAIR * source + i, PAIR * target + i) for i in range(PAIR)]
        )

    position = jnp.reshape(my_row, (1,)).astype(jnp.int32)
    side = jnp.reshape(my_part % PAIR, (1,)).astype(jnp.int32)
    core = jnp.reshape(my_row % CORES, (1,)).astype(jnp.int32)

    pieces = []
    for day in range(day_count):
        rows = [None] * CORES
        links = [None] * CORES
        for chip in range(1, chips):
            got_rows = to_row(inv_diag[day : day + 1], CORES * chip)
            got_links = to_row(coupling[day : day + 1], CORES * chip)
            rows += [got_rows, to_row(got_rows, 1)]
            links += [got_links, to_row(got_links, 1)]
        pieces.append((rows, links))
    own = [[inv_diag, to_row(inv_diag, 1)], [coupling, to_row(coupling, 1)]]

    dense = bin_observations(obs_day, obs_node, obs_value, part_count * day_count, nodes)
    sent = lax.all_to_all(
        dense.reshape(part_count, day_count, nodes), "tm", split_axis=0, concat_axis=0, tiled=True
    )
    right_side = jnp.sum(sent, axis=0)
    distance = 1
    while distance < row_count:
        right_side = right_side + to_row(right_side, distance)
        distance *= 2
    right_side = jnp.broadcast_to(right_side[:, None, :], (day_count, LINES, nodes))

    state = None
    kept = []
    for day in range(day_count):
        state, saved = day_step(
            day, position, row_count, own, pieces[day], noise, right_side, state
        )
        kept.append(saved)
    path, gram, summed, applied, back = state

    def halves_body(side_ref, core_ref, path_ref, sum_ref, path_half, keep, send):
        path_half[...] = path_ref[
            pl.ds(pl.multiple_of(core_ref[0] * half_nodes, half_nodes), half_nodes), :
        ]
        low, high = sum_ref[:, :half], sum_ref[:, half:]
        first = side_ref[0] == 0
        keep[...] = jnp.where(first, low, high)
        send[...] = jnp.where(first, high, low)

    columns_half = shape(nodes, half)
    path_half, keep, send = call(
        halves_body,
        (shape(half_nodes, nodes), columns_half, columns_half),
        "halves",
        scalars=2,
        inputs=2,
    )(side, core, path, summed)
    other_half = to_pair(path_half)
    other_sum = to_pair(send)
    other_applied = to_pair(applied)
    other_rest = to_row(other_half, 1)

    def pair_body(
        side_ref, core_ref, path_ref, half_ref, rest_ref, sum_ref, other_ref, applied_ref,
        other_applied_ref, low_out, high_out, both_out, sum_out, high_sum_out, flux_out,
        low_flux_out, scratch, lines,
    ):
        me, mate = side_ref[0], 1 - side_ref[0]
        mine = core_ref[0]
        scratch[me] = path_ref[...]
        scratch[mate, pl.ds(pl.multiple_of(mine * half_nodes, half_nodes), half_nodes), :] = (
            half_ref[...]
        )
        scratch[
            mate, pl.ds(pl.multiple_of((1 - mine) * half_nodes, half_nodes), half_nodes), :
        ] = rest_ref[...]
        lines[me] = applied_ref[...]
        lines[mate] = other_applied_ref[...]
        low, high = split(scratch[0]), split(scratch[1])
        low_out[0], low_out[1] = low
        high_out[0], high_out[1] = high
        both_out[0], both_out[1] = split(dot_parts(high, low, NN))
        first = me == 0
        low_sum = jnp.where(first, sum_ref[...], other_ref[...])
        high_sum = jnp.where(first, other_ref[...], sum_ref[...])
        sum_out[...] = dot_parts(low, split(high_sum), TN) + low_sum
        high_sum_out[...] = high_sum
        flux_out[...] = dot_parts(split(lines[0]), high, NT) + lines[1]
        low_flux_out[...] = lines[0]

    line = shape(LINES, nodes)
    map_shape = shape(2, nodes, nodes, dtype=BF16)
    low_map, high_map, both_map, pair_sum, high_sum, pair_flux, low_flux = call(
        pair_body,
        (map_shape, map_shape, map_shape, columns_half, columns_half, line, line),
        "pair_maps",
        scratch=[pltpu.VMEM((PAIR, nodes, nodes), F32), pltpu.VMEM((PAIR, LINES, nodes), F32)],
        scalars=2,
        inputs=7,
    )(side, core, path, other_half, other_rest, keep, other_sum, applied, other_applied)

    def link_body(map_ref, local_ref, got_ref, out_ref):
        out_ref[...] = (
            dot_parts((map_ref[0], map_ref[1]), split(got_ref[...]), TN) + local_ref[...]
        )

    def line_body(dims, map_ref, local_ref, got_ref, out_ref):
        out_ref[...] = (
            dot_parts(split(got_ref[...]), (map_ref[0], map_ref[1]), dims) + local_ref[...]
        )

    advance = call(link_body, columns_half, "noise_link", scalars=0, inputs=3)
    forward = call(
        functools.partial(line_body, NT), line, "forward_link", scalars=0, inputs=3
    )
    backward = call(
        functools.partial(line_body, NN), line, "backward_link", scalars=0, inputs=3
    )

    leaving = jnp.zeros((nodes, half), F32)
    current = pair_sum
    for group in range(groups - 1, 0, -1):
        leaving = leaving + to_group(current, group, group - 1)
        if group > 1:
            current = advance(both_map, pair_sum, leaving)

    entering = jnp.zeros((LINES, nodes), F32)
    flux = pair_flux
    for group in range(groups - 1):
        entering = entering + to_group(flux, group, group + 1)
        if group < groups - 2:
            flux = forward(both_map, pair_flux, entering)

    def mean_body(side_ref, low_ref, flux_ref, entering_ref, gram_ref, back_ref, own_out, back_out):
        given = entering_ref[...]
        after = dot_parts(split(given), (low_ref[0], low_ref[1]), NT) + flux_ref[...]
        given = jnp.where(side_ref[0] == 0, given, after)
        own_out[...] = given
        back_out[...] = back_ref[...] - dot_parts(split(given), split(gram_ref[...]), NN)

    own_entering, own_back = call(mean_body, (line, line), "mean_turn", inputs=5)(
        side, low_map, low_flux, entering, gram, back
    )
    other_back = to_pair(own_back)
    low_back = jnp.where(side[0] == 0, own_back, other_back)
    high_back = jnp.where(side[0] == 0, other_back, own_back)
    pair_back = backward(low_map, low_back, high_back)
    mean_leaving = jnp.zeros((LINES, nodes), F32)
    mean = pair_back
    for group in range(groups - 1, 0, -1):
        mean_leaving = mean_leaving + to_group(mean, group, group - 1)
        if group > 1:
            mean = backward(both_map, pair_back, mean_leaving)

    def divide_body(side_ref, high_ref, sum_ref, leaving_ref, mean_ref, back_ref, keep, send, line_out):
        high = (high_ref[0], high_ref[1])
        between = dot_parts(high, split(leaving_ref[...]), TN) + sum_ref[...]
        first = side_ref[0] == 0
        keep[...] = jnp.where(first, between, leaving_ref[...])
        send[...] = jnp.where(first, leaving_ref[...], between)
        mean_between = dot_parts(split(mean_ref[...]), high, NN) + back_ref[...]
        line_out[...] = jnp.where(first, mean_between, mean_ref[...])

    kept_half, sent_half, mean_line = call(
        divide_body, (columns_half, columns_half, line), "divide", inputs=5
    )(side, high_map, high_sum, leaving, mean_leaving, high_back)
    got_half = to_pair(sent_half)

    def mean_days_body(entering_ref, *refs):
        given = split(entering_ref[...])
        out_ref = refs[-1]
        for day in range(day_count):
            moved_ref, own_ref, current_ref = refs[3 * day : 3 * day + 3]
            current = current_ref[...] - dot_parts(given, split(moved_ref[...]), NT)
            out_ref[day] = dot_parts(split(current), (own_ref[0], own_ref[1]), NN)

    mean_days = call(
        mean_days_body, shape(day_count, LINES, nodes), "mean_days", scalars=0,
        inputs=1 + 3 * day_count,
    )(own_entering, *(saved[i] for saved in kept for i in (0, 1, 4)))

    def last_body(side_ref, keep_ref, got_ref, line_ref, days_ref, *refs):
        maps, locals_, out_ref = refs[:day_count], refs[day_count : 2 * day_count], refs[-1]
        first = side_ref[0] == 0
        spread = jnp.full((LINES, columns), 1.0 / LINES, BF16)

        def as_columns(lines):
            return sum(
                lax.dot_general(part, spread, (TN, ((), ())), preferred_element_type=F32)
                for part in split(lines)
            )

        low = jnp.where(first, keep_ref[...], got_ref[...])
        high = jnp.where(first, got_ref[...], keep_ref[...])
        following = jnp.concatenate([low, high], axis=1) + as_columns(line_ref[...])
        for day in reversed(range(day_count)):
            following = (
                dot_parts((maps[day][0], maps[day][1]), split(following), TN)
                + locals_[day][...]
                + as_columns(days_ref[day])
            )
            out_ref[day] = following

    return call(
        last_body, shape(day_count, nodes, columns), "last_days", inputs=4 + 2 * day_count
    )(
        side, kept_half, got_half, mean_line, mean_days,
        *(saved[2] for saved in kept), *(saved[3] for saved in kept),
    )


def solution(mesh):
    return jax.shard_map(
        local,
        mesh=mesh,
        in_specs=(
            P("tm", "row", None),
            P("tm", "row", None),
            P("tm", None, "row"),
            P(("tm", "row")),
            P(("tm", "row")),
            P(("tm", "row")),
        ),
        out_specs=P("tm", None, "row"),
        check_vma=False,
    )
```

time: 521 us -> 221 us (0.42); the launches traced: 511 us -> 220 us
  waiting for transfers between devices: 262 us -> 77.4 us
  matrix products: 153 us -> 0 us
  Pallas kernels: 0 us -> 82.3 us
  other arithmetic: 30.1 us -> 7.41 us
  between operations: 15.7 us -> 0.31 us
  starting transfers between devices: 41.8 us -> 29 us
  local copies, waits for them, and re-layouts: 1.39 us -> 10.8 us
  blocking collectives: 6.15 us -> 13.1 us
    unnamed x5 -> x0, waiting for transfers between devices: 157 us -> none
    dot_general x60 -> x0, matrix products: 153 us -> none  [the longest x37 82.2 us: matmul(): jnp.dot(left_side, right_side, precision=highest, preferred_element_type=...]
    pallas_call x0 -> x18, Pallas kernels: none -> 82.3 us  [the longest x4 34.5 us: day_step(): call(body, outs, f'day_{day}', scratch=[pltpu.VMEM((nodes, nodes), F32)]...]
    ppermute x14 -> x35, waiting for transfers between devices: 105 us -> 77.4 us  [the longest x21 31.7 us: to_row(): lax.ppermute(value, 'row', [(i, i ^ distance) for i in range(row_count)])]
    unnamed x6 -> x0, other arithmetic: 23.7 us -> none
    all_to_all x0 -> x1, blocking collectives: none -> 13.1 us  [local(): lax.all_to_all(dense.reshape(part_count, day_count, nodes), 'tm', split_a...]
    ppermute x14 -> x35, starting transfers between devices: 41.5 us -> 29 us  [the longest x21 14.3 us: to_row(): lax.ppermute(value, 'row', [(i, i ^ distance) for i in range(row_count)])]
    add x8, other arithmetic: 0.05 us -> 6.76 us  [the longest x2 2.65 us: local(): mean_leaving = mean_leaving + to_group(mean, group, group - 1)]
  transfers between devices with their start and end apart: 18 -> 35, of which waited for: 15 -> 13; matrix products, arithmetic and copies ran while one was open for 19% -> 5% of each run, Pallas kernels for 0% -> 24%
where the time goes in v1:
time: 221 us; the launch traced here: 220 us
  Pallas kernels  82.3 us (37%)
  waiting for transfers between devices  77.4 us (35%)
  starting transfers between devices  29 us (13%)
  blocking collectives  13.1 us (6%)
  local copies, waits for them, and re-layouts  10.8 us (5%)
  other arithmetic  7.41 us (3%)
    pallas_call x4, Pallas kernels, day_step(): call(body, outs, f'day_{day}', scratch=[pltpu.VMEM((nodes, nodes), F32)]...  34.5 us
    ppermute x21, waiting for transfers between devices, to_row(): lax.ppermute(value, 'row', [(i, i ^ distance) for i in range(row_count)])  31.7 us
    ppermute x9, waiting for transfers between devices, to_group(): lax.ppermute(value, 'tm', [(PAIR * source + i, PAIR * target + i) for i i...  24.5 us
    ppermute x5, waiting for transfers between devices, to_pair(): return lax.ppermute(value, 'tm', [(i, i ^ 1) for i in range(part_count)])  21.3 us
    ppermute x21, starting transfers between devices, to_row(): lax.ppermute(value, 'row', [(i, i ^ distance) for i in range(row_count)])  14.3 us
    all_to_all x1, blocking collectives, local(): lax.all_to_all(dense.reshape(part_count, day_count, nodes), 'tm', split_a...  13.1 us
    ppermute x9, starting transfers between devices, to_group(): lax.ppermute(value, 'tm', [(PAIR * source + i, PAIR * target + i) for i i...  9.71 us
    pallas_call x1, Pallas kernels, local(): call(last_body, shape(day_count, nodes, columns), 'last_days', inputs=4 +...  9.18 us
  transfers between devices with their start and end apart: 35, of which 13 were waited for; matrix products, arithmetic and copies ran while one was open for 5% of the time, Pallas kernels for 24%

profile of v1, /device:TPU:0, one launch (start us, length us, event | category | flops | bytes accessed | tf_op | source)
XLA Modules:
  0.0 220.4 jit_solution(4557940143199428227)
XLA Ops:
  0.0 2.2 %fusion.1 = (f32[1,128,512]{2,1,0:T(8,128)}, f32[1,128,512]{2,1,0:T(8,128)S(1)}, f32[1,128,512]{2,1,0:T(8,128)}, f32[1,128,512]{2,1,0:T(8,128)}) fusion(f32[4,128,512]{2,1,0:T(8,128)} %refs_0_.7), kind=kLoop, calls=%fused_computation.3 | loop fusion | bytes 2097152 | tf_op jit(solution)/shard_map/slice | solution.py:195
  2.2 3.0 %collective-permute-start.16 = (f32[1,128,512]{2,1,0:T(8,128)}, f32[1,128,512]{2,1,0:T(8,128)}, u32[]{:S(2)}, u32[]{:S(2)}) collective-permute-start(f32[1,128,512]{2,1,0:T(8,128)} %get-tuple-element.119), channel_id=1, source_target_pairs={{0,2},{1,3},{2,0},{3,1},{4,6},{5,7},{6,4},{7,5},{8,10},{9,11},{10,... | collective-permute-start | bytes 786440 | tf_op jit(solution)/shard_map/ppermute | solution.py:176
  5.2 1.0 fusion
  8.5 2.8 %bin_observations.1 = f32[32,512]{1,0:T(8,128)} custom-call(s32[8,512]{1,0:T(8,128)} %reshape.25.day_ref, s32[8,512]{1,0:T(8,128)} %reshape.26.node_ref, f32[8,512]{1,0:T(8,128)} %reshape.27.value_ref), custom_call_target="tpu_custom_call" | custom-call | tf_op jit(solution)/shard_map/bin_observations/pallas_call | solution.py:74
  11.3 0.9 reshape.28
  12.2 13.1 %all_to_all.5 = f32[8,4,512]{2,1,0:T(4,128)S(1)} all-to-all(f32[8,4,512]{2,1,0:T(4,128)S(1)} %reshape.28), channel_id=1, replica_groups=mesh['tm'=8,'row'=4] {'tm'}, dimensions={0} | all-to-all | bytes 131072 | tf_op jit(solution)/shard_map/all_to_all | solution.py:203
  25.4 1.2 collective-permute-done.6
  26.5 1.5 collective-permute-start.7
  28.0 2.2 collective-permute-done.7
  30.2 1.5 collective-permute-start.12
  32.2 1.5 collective-permute-start.10
  33.7 5.7 %collective-permute-done.12.refs_2_ = f32[1,128,512]{2,1,0:T(8,128)S(1)} collective-permute-done((f32[1,128,512]{2,1,0:T(8,128)S(1)}, f32[1,128,512]{2,1,0:T(8,128)S(1)}, u32[]{:S(2)}, u32[]{:S(2)}) %collective-permute-start.12) | collective-permute-done | bytes 262176 | tf_op jit(solution)/shard_map/ppermute | solution.py:176
  39.4 1.5 collective-permute-start.8
  40.9 4.2 %collective-permute-done.14.refs_6_ = f32[1,128,512]{2,1,0:T(8,128)} collective-permute-done((f32[1,128,512]{2,1,0:T(8,128)}, f32[1,128,512]{2,1,0:T(8,128)}, u32[]{:S(2)}, u32[]{:S(2)}) %collective-permute-start.14) | collective-permute-done | bytes 262176 | tf_op jit(solution)/shard_map/ppermute | solution.py:176
  45.1 1.5 collective-permute-start.1
  46.6 4.1 %collective-permute-done.10.refs_6_ = f32[1,128,512]{2,1,0:T(8,128)} collective-permute-done((f32[1,128,512]{2,1,0:T(8,128)}, f32[1,128,512]{2,1,0:T(8,128)}, u32[]{:S(2)}, u32[]{:S(2)}) %collective-permute-start.10) | collective-permute-done | bytes 262176 | tf_op jit(solution)/shard_map/ppermute | solution.py:176
  50.8 1.5 collective-permute-start.4
  52.3 4.1 %collective-permute-done.8.refs_2_ = f32[1,128,512]{2,1,0:T(8,128)} collective-permute-done((f32[1,128,512]{2,1,0:T(8,128)}, f32[1,128,512]{2,1,0:T(8,128)}, u32[]{:S(2)}, u32[]{:S(2)}) %collective-permute-start.8) | collective-permute-done | bytes 262176 | tf_op jit(solution)/shard_map/ppermute | solution.py:176
  56.4 5.5 %collective-permute-done.1.refs_2_ = f32[1,128,512]{2,1,0:T(8,128)S(1)} collective-permute-done((f32[1,128,512]{2,1,0:T(8,128)}, f32[1,128,512]{2,1,0:T(8,128)S(1)}, u32[]{:S(2)}, u32[]{:S(2)}) %collective-permute-start.1) | collective-permute-done | bytes 262176 | tf_op jit(solution)/shard_map/ppermute | solution.py:176
  61.9 3.7 %collective-permute-done.4.refs_6_ = f32[1,128,512]{2,1,0:T(8,128)} collective-permute-done((f32[1,128,512]{2,1,0:T(8,128)}, f32[1,128,512]{2,1,0:T(8,128)}, u32[]{:S(2)}, u32[]{:S(2)}) %collective-permute-start.4) | collective-permute-done | bytes 262176 | tf_op jit(solution)/shard_map/ppermute | solution.py:176
  66.2 0.9 collective-permute-done.13.refs_3_
  68.5 7.0 %day_0.1 = (f32[512,512]{1,0:T(8,128)}, f32[512,512]{1,0:T(8,128)}, f32[512,256]{1,0:T(8,128)}, f32[8,512]{1,0:T(8,128)}, f32[8,512]{1,0:T(8,128)}, /*index=5*/f...) custom-call(s32[1]{0:T(128)} %bitcast.2.position_ref, ...), custom_call_target="tpu_custom_call" | custom-call | tf_op jit(solution)/shard_map/day_0/pallas_call | solution.py:153
  75.5 9.1 %day_1.1 = (f32[512,512]{1,0:T(8,128)}, f32[512,512]{1,0:T(8,128)}, f32[512,256]{1,0:T(8,128)}, f32[8,512]{1,0:T(8,128)}, f32[8,512]{1,0:T(8,128)}, /*index=5*/f...) custom-call(s32[1]{0:T(128)} %bitcast.2.position_ref, ...), custom_call_target="tpu_custom_call" | custom-call | tf_op jit(solution)/shard_map/day_1/pallas_call | solution.py:153
  84.6 9.3 %day_2.1 = (f32[512,512]{1,0:T(8,128)}, f32[512,512]{1,0:T(8,128)}, f32[512,256]{1,0:T(8,128)}, f32[8,512]{1,0:T(8,128)}, f32[8,512]{1,0:T(8,128)}, /*index=5*/f...) custom-call(s32[1]{0:T(128)} %bitcast.2.position_ref, ...), custom_call_target="tpu_custom_call" | custom-call | tf_op jit(solution)/shard_map/day_2/pallas_call | solution.py:153
  93.9 0.7 copy-done.10
  94.7 9.1 %day_3.1 = (f32[512,512]{1,0:T(8,128)}, f32[512,512]{1,0:T(8,128)}, f32[512,256]{1,0:T(8,128)}, f32[8,512]{1,0:T(8,128)}, f32[8,512]{1,0:T(8,128)}, /*index=5*/f...) custom-call(s32[1]{0:T(128)} %bitcast.2.position_ref, ...), custom_call_target="tpu_custom_call" | custom-call | tf_op jit(solution)/shard_map/day_3/pallas_call | solution.py:153
  103.8 2.4 %halves.1 = (f32[256,512]{1,0:T(8,128)}, f32[512,128]{1,0:T(8,128)}, f32[512,128]{1,0:T(8,128)}) custom-call(s32[1]{0:T(128)} %bitcast.side_ref, s32[1]{0:T(128)} %bitcast.1.core_ref, f32[512,512]{1,0:T(8,128)} %get-tuple-element.75.path_ref, f32[512,256]{1,0:T(8,128)} %get-tuple-element.76.sum_ref), custom_call_target="tpu_custom_call" | custom-call | tf_op jit(solution)/shard_map/halves/pallas_call | solution.py:232
  106.5 14.0 %collective-permute-done.20.half_ref = f32[256,512]{1,0:T(8,128)S(1)} collective-permute-done((f32[256,512]{1,0:T(8,128)}, f32[256,512]{1,0:T(8,128)S(1)}, u32[]{:S(2)}, u32[]{:S(2)}) %collective-permute-start.20) | collective-permute-done | bytes 524320 | tf_op jit(solution)/shard_map/ppermute | solution.py:179
  120.9 1.6 collective-permute-start.23
  122.6 7.3 %collective-permute-done.23.other_applied_ref = f32[8,512]{1,0:T(8,128)S(1)} collective-permute-done((f32[8,512]{1,0:T(8,128)}, f32[8,512]{1,0:T(8,128)S(1)}, u32[]{:S(2)}, u32[]{:S(2)}) %collective-permute-start.23) | collective-permute-done | bytes 16416 | tf_op jit(solution)/shard_map/ppermute | solution.py:179
  130.7 4.2 %pair_maps.1 = (bf16[2,512,512]{2,1,0:T(8,128)(2,1)}, bf16[2,512,512]{2,1,0:T(8,128)(2,1)}, bf16[2,512,512]{2,1,0:T(8,128)(2,1)}, f32[512,128]{1,0:T(8,128)}, f3...) custom-call(s32[1]{0:T(128)} %bitcast.side_ref, s32[1]{0:T(128)} %bitcast.1.core_ref, ...), custom_call_target="tpu_custom_call" | custom-call | tf_op jit(solution)/shard_map/pair_maps/pallas_call | solution.py:274
  134.9 0.7 collective-permute-start.24
  135.6 0.7 copy-done.4
  136.3 2.7 %noise_link.2 = f32[512,128]{1,0:T(8,128)} custom-call(bf16[2,512,512]{2,1,0:T(8,128)(2,1)} %get-tuple-element.84.map_ref, f32[512,128]{1,0:T(8,128)} %get-tuple-element.83.local_ref, f32[512,128]{1,0:T(8,128)} %copy-done.4), custom_call_target="tpu_custom_call" | custom-call | tf_op jit(solution)/shard_map/noise_link/pallas_call | solution.py:306
  138.9 0.7 collective-permute-start.25
  139.6 2.9 %collective-permute-start.27 = (f32[8,512]{1,0:T(8,128)}, f32[8,512]{1,0:T(8,128)S(1)}, u32[]{:S(2)}, u32[]{:S(2)}) collective-permute-start(f32[8,512]{1,0:T(8,128)} %get-tuple-element.87.local_ref), channel_id=1, source_target_pairs={{0,8},{4,12},{1,9},{5,13},{2,10},{6,14},{3,11},{7,15}} | collective-permute-start | bytes 49160 | tf_op jit(solution)/shard_map/ppermute | solution.py:182
  142.5 1.6 collective-permute-done.27.got_ref
  144.7 2.4 %forward_link.2 = f32[8,512]{1,0:T(8,128)} custom-call(bf16[2,512,512]{2,1,0:T(8,128)(2,1)} %get-tuple-element.84.map_ref, f32[8,512]{1,0:T(8,128)} %get-tuple-element.87.local_ref, f32[8,512]{1,0:T(8,128)} %copy-done.17), custom_call_target="tpu_custom_call" | custom-call | tf_op jit(solution)/shard_map/forward_link/pallas_call | solution.py:313
  147.1 0.7 collective-permute-start.28
  147.8 1.3 add.37.got_ref
  149.1 2.4 %forward_link.3 = f32[8,512]{1,0:T(8,128)} custom-call(bf16[2,512,512]{2,1,0:T(8,128)(2,1)} %get-tuple-element.84.map_ref, f32[8,512]{1,0:T(8,128)} %get-tuple-element.87.local_ref, f32[8,512]{1,0:T(8,128)} %add.37.got_ref), custom_call_target="tpu_custom_call" | custom-call | tf_op jit(solution)/shard_map/forward_link/pallas_call | solution.py:313
  151.5 0.7 collective-permute-start.29
  152.1 1.3 add.38.entering_ref
  153.5 2.9 %mean_turn.1 = (f32[8,512]{1,0:T(8,128)}, f32[8,512]{1,0:T(8,128)}) custom-call(s32[1]{0:T(128)} %bitcast.side_ref, bf16[2,512,512]{2,1,0:T(8,128)(2,1)} %get-tuple-element.85.low_ref.map_ref, f32[8,512]{1,0:T(8,128)} %get-tuple-element.86.flux_ref, f32[8,512]{1,0:T(8,128)} %add.38.entering_ref, f32[512,512]{1,0:T(8,128)} %get-tuple-element.88.gram_ref, ...), custom_call_target="tpu_custom_call" | custom-call | tf_op jit(solution)/shard_map/mean_turn/pallas_call | solution.py:322
  156.4 1.0 collective-permute-start.30
  157.4 0.7 add.35.got_ref
  158.1 2.7 %noise_link.3 = f32[512,128]{1,0:T(8,128)} custom-call(bf16[2,512,512]{2,1,0:T(8,128)(2,1)} %get-tuple-element.84.map_ref, f32[512,128]{1,0:T(8,128)} %get-tuple-element.83.local_ref, f32[512,128]{1,0:T(8,128)} %add.35.got_ref), custom_call_target="tpu_custom_call" | custom-call | tf_op jit(solution)/shard_map/noise_link/pallas_call | solution.py:306
  160.8 1.4 collective-permute-start.26
  162.3 0.6 broadcast_select_fusion
  162.9 2.2 backward_link.3.local_ref
  165.0 0.7 collective-permute-start.31
  166.3 2.2 backward_link.4
  168.5 0.7 collective-permute-start.32
  169.1 1.3 add.39.got_ref
  170.5 2.2 backward_link.5
  172.6 1.5 collective-permute-start.33
  174.2 22.9 %collective-permute-done.33 = f32[8,512]{1,0:T(8,128)S(1)} collective-permute-done((f32[8,512]{1,0:T(8,128)}, f32[8,512]{1,0:T(8,128)S(1)}, u32[]{:S(2)}, u32[]{:S(2)}) %collective-permute-start.33) | collective-permute-done | bytes 16416 | tf_op jit(solution)/shard_map/ppermute | solution.py:182
  197.0 1.3 add.40.mean_ref
  198.3 0.7 add.36.leaving_ref
  199.1 2.8 %divide.1 = (f32[512,128]{1,0:T(8,128)}, f32[512,128]{1,0:T(8,128)}, f32[8,512]{1,0:T(8,128)}) custom-call(s32[1]{0:T(128)} %bitcast.side_ref, bf16[2,512,512]{2,1,0:T(8,128)(2,1)} %get-tuple-element.81.high_ref, f32[512,128]{1,0:T(8,128)} %get-tuple-element.82.sum_ref, f32[512,128]{1,0:T(8,128)} %add.36.leaving_ref, f32[8,512]{1,0:T(8,128)} %add.40.mean_ref, ...), custom_call_target="tpu_custom_call" | custom-call | tf_op jit(solution)/shard_map/divide/pallas_call | solution.py:345
  201.9 1.6 collective-permute-start.34
  203.5 7.0 %mean_days.1.days_ref = f32[4,8,512]{2,1,0:T(8,128)} custom-call(f32[8,512]{1,0:T(8,128)} %get-tuple-element.94.entering_ref, f32[512,512]{1,0:T(8,128)} %get-tuple-element.95.refs_0_, bf16[2,512,512]{2,1,0:T(8,128)(2,1)} %get-tuple-element.96.refs_1_, f32[8,512]{1,0:T(8,128)} %get-tuple-element.97.refs_2_, f32[512,512]{1,0:T(8,128)} %get-tuple-element.98.refs_3_, ...), custom_call_target="tpu_custom_call" | custom-call | tf_op jit(solution)/shard_map/mean_days/pallas_call | solution.py:358
  210.5 0.7 copy-done.13
  211.2 9.2 %last_days.1 = f32[4,512,256]{2,1,0:T(8,128)} custom-call(s32[1]{0:T(128)} %bitcast.side_ref, f32[512,128]{1,0:T(8,128)} %get-tuple-element.91.keep_ref, f32[512,128]{1,0:T(8,128)} %copy-done.13, f32[8,512]{1,0:T(8,128)} %get-tuple-element.93.line_ref, f32[4,8,512]{2,1,0:T(8,128)} %mean_days.1.days_ref, bf16[2,512,512]{2,1,0:T(8,128)(2,1)} %get-tuple-element.107.refs_0_, ...), custom_call_target="tpu_custom_call" | custom-call | tf_op jit(solution)/shard_map/last_days/pallas_call | solution.py:385
  (90 shorter events, 7.9 us)
Async XLA Ops:
  0.0 6.2 %copy-start = (f32[4,128,512]{2,1,0:T(8,128)S(1)}, f32[4,128,512]{2,1,0:T(8,128)}, u32[]{:S(2)}) copy-start(f32[4,128,512]{2,1,0:T(8,128)} %refs_0_.7) | copy-start | bytes 3145732
  0.0 5.2 %copy-start.1 = (f32[4,128,512]{2,1,0:T(8,128)S(1)}, f32[4,128,512]{2,1,0:T(8,128)}, u32[]{:S(2)}) copy-start(f32[4,128,512]{2,1,0:T(8,128)} %refs_4_.7) | copy-start | bytes 3145732
  0.0 6.7 %copy-start.20 = (s32[4096]{0:T(1024)S(1)}, s32[4096]{0:T(1024)}, u32[]{:S(2)}) copy-start(s32[4096]{0:T(1024)} %param.9) | copy-start | bytes 49156
  0.0 7.3 %copy-start.21 = (s32[4096]{0:T(1024)S(1)}, s32[4096]{0:T(1024)}, u32[]{:S(2)}) copy-start(s32[4096]{0:T(1024)} %param.10) | copy-start | bytes 49156
  0.0 7.9 %copy-start.22 = (f32[4096]{0:T(1024)S(1)}, f32[4096]{0:T(1024)}, u32[]{:S(2)}) copy-start(f32[4096]{0:T(1024)} %param.11) | copy-start | bytes 49156
  2.2 29.4 %collective-permute-start.16 = (f32[1,128,512]{2,1,0:T(8,128)}, f32[1,128,512]{2,1,0:T(8,128)}, u32[]{:S(2)}, u32[]{:S(2)}) collective-permute-start(f32[1,128,512]{2,1,0:T(8,128)} %get-tuple-element.119), channel_id=1, source_target_pairs={{0,2},{1,3},{2,0},{3,1},{4,6},{5,7},{6,4},{7,5},{8,10},{9,11},{10,... | collective-permute-start | bytes 786440 | tf_op jit(solution)/shard_map/ppermute | solution.py:176
  6.2 26.0 %collective-permute-start.18 = (f32[1,128,512]{2,1,0:T(8,128)}, f32[1,128,512]{2,1,0:T(8,128)}, u32[]{:S(2)}, u32[]{:S(2)}) collective-permute-start(f32[1,128,512]{2,1,0:T(8,128)} %get-tuple-element.115), channel_id=1, source_target_pairs={{0,2},{1,3},{2,0},{3,1},{4,6},{5,7},{6,4},{7,5},{8,10},{9,11},{10,... | collective-permute-start | bytes 786440 | tf_op jit(solution)/shard_map/ppermute | solution.py:176
  6.2 61.1 %collective-permute-start = (f32[4,128,512]{2,1,0:T(8,128)S(1)}, f32[4,128,512]{2,1,0:T(8,128)S(1)}, u32[]{:S(2)}, u32[]{:S(2)}) collective-permute-start(f32[4,128,512]{2,1,0:T(8,128)S(1)} %copy-done), channel_id=1, source_target_pairs={{0,1},{1,0},{2,3},{3,2},{4,5},{5,4},{6,7},{7,6},{8,9},{9,8},{10,11... | collective-permute-start | bytes 3145736 | tf_op jit(solution)/shard_map/ppermute | solution.py:176
  6.2 61.4 %collective-permute-start.3 = (f32[4,128,512]{2,1,0:T(8,128)S(1)}, f32[4,128,512]{2,1,0:T(8,128)}, u32[]{:S(2)}, u32[]{:S(2)}) collective-permute-start(f32[4,128,512]{2,1,0:T(8,128)S(1)} %copy-done.1), channel_id=1, source_target_pairs={{0,1},{1,0},{2,3},{3,2},{4,5},{5,4},{6,7},{7,6},{8,9},{9,8},{10,11... | collective-permute-start | bytes 3145736 | tf_op jit(solution)/shard_map/ppermute | solution.py:176
  25.3 1.2 collective-permute-start.6
  26.5 3.7 %collective-permute-start.7 = (f32[4,512]{1,0:T(4,128)S(1)}, f32[4,512]{1,0:T(4,128)S(1)}, u32[]{:S(2)}, u32[]{:S(2)}) collective-permute-start(f32[4,512]{1,0:T(4,128)S(1)} %add.33), channel_id=1, source_target_pairs={{0,2},{1,3},{2,0},{3,1},{4,6},{5,7},{6,4},{7,5},{8,10},{9,11},{10,... | collective-permute-start | bytes 24584 | tf_op jit(solution)/shard_map/ppermute | solution.py:176
  30.2 9.2 %collective-permute-start.12 = (f32[1,128,512]{2,1,0:T(8,128)S(1)}, f32[1,128,512]{2,1,0:T(8,128)S(1)}, u32[]{:S(2)}, u32[]{:S(2)}) collective-permute-start(f32[1,128,512]{2,1,0:T(8,128)S(1)} %get-tuple-element.120), channel_id=1, source_target_pairs={{0,2},{1,3},{2,0},{3,1},{4,6},{5,7},{6,4},{7,5},{8,10},{9,11},{10,... | collective-permute-start | bytes 786440 | tf_op jit(solution)/shard_map/ppermute | solution.py:176
  31.7 13.5 %collective-permute-start.14 = (f32[1,128,512]{2,1,0:T(8,128)}, f32[1,128,512]{2,1,0:T(8,128)}, u32[]{:S(2)}, u32[]{:S(2)}) collective-permute-start(f32[1,128,512]{2,1,0:T(8,128)} %get-tuple-element.116), channel_id=1, source_target_pairs={{0,2},{1,3},{2,0},{3,1},{4,6},{5,7},{6,4},{7,5},{8,10},{9,11},{10,... | collective-permute-start | bytes 786440 | tf_op jit(solution)/shard_map/ppermute | solution.py:176
  32.2 18.6 %collective-permute-start.10 = (f32[1,128,512]{2,1,0:T(8,128)}, f32[1,128,512]{2,1,0:T(8,128)}, u32[]{:S(2)}, u32[]{:S(2)}) collective-permute-start(f32[1,128,512]{2,1,0:T(8,128)} %get-tuple-element.117), channel_id=1, source_target_pairs={{0,2},{1,3},{2,0},{3,1},{4,6},{5,7},{6,4},{7,5},{8,10},{9,11},{10,... | collective-permute-start | bytes 786440 | tf_op jit(solution)/shard_map/ppermute | solution.py:176
  39.4 28.2 %copy-start.9 = (f32[1,128,512]{2,1,0:T(8,128)}, f32[1,128,512]{2,1,0:T(8,128)S(1)}, u32[]{:S(2)}) copy-start(f32[1,128,512]{2,1,0:T(8,128)S(1)} %collective-permute-done.12.refs_2_) | copy-start | bytes 786436
  39.4 17.0 %collective-permute-start.8 = (f32[1,128,512]{2,1,0:T(8,128)}, f32[1,128,512]{2,1,0:T(8,128)}, u32[]{:S(2)}, u32[]{:S(2)}) collective-permute-start(f32[1,128,512]{2,1,0:T(8,128)} %get-tuple-element.121), channel_id=1, source_target_pairs={{0,2},{1,3},{2,0},{3,1},{4,6},{5,7},{6,4},{7,5},{8,10},{9,11},{10,... | collective-permute-start | bytes 786440 | tf_op jit(solution)/shard_map/ppermute | solution.py:176
  45.1 16.7 %collective-permute-start.1 = (f32[1,128,512]{2,1,0:T(8,128)}, f32[1,128,512]{2,1,0:T(8,128)S(1)}, u32[]{:S(2)}, u32[]{:S(2)}) collective-permute-start(f32[1,128,512]{2,1,0:T(8,128)} %get-tuple-element.122), channel_id=1, source_target_pairs={{0,2},{1,3},{2,0},{3,1},{4,6},{5,7},{6,4},{7,5},{8,10},{9,11},{10,... | collective-permute-start | bytes 786440 | tf_op jit(solution)/shard_map/ppermute | solution.py:176
  50.8 14.8 %collective-permute-start.4 = (f32[1,128,512]{2,1,0:T(8,128)}, f32[1,128,512]{2,1,0:T(8,128)}, u32[]{:S(2)}, u32[]{:S(2)}) collective-permute-start(f32[1,128,512]{2,1,0:T(8,128)} %get-tuple-element.118), channel_id=1, source_target_pairs={{0,2},{1,3},{2,0},{3,1},{4,6},{5,7},{6,4},{7,5},{8,10},{9,11},{10,... | collective-permute-start | bytes 786440 | tf_op jit(solution)/shard_map/ppermute | solution.py:176
  56.4 9.2 %collective-permute-start.17 = (f32[1,128,512]{2,1,0:T(8,128)}, f32[1,128,512]{2,1,0:T(8,128)S(1)}, u32[]{:S(2)}, u32[]{:S(2)}) collective-permute-start(f32[1,128,512]{2,1,0:T(8,128)} %collective-permute-done.16.refs_2_), channel_id=1, source_target_pairs={{0,1},{1,0},{2,3},{3,2},{4,5},{5,4},{6,7},{7,6},{8,9},{9,8},{10,11... | collective-permute-start | bytes 786440 | tf_op jit(solution)/shard_map/ppermute | solution.py:176
  61.9 22.7 %copy-start.8 = (f32[1,128,512]{2,1,0:T(8,128)}, f32[1,128,512]{2,1,0:T(8,128)S(1)}, u32[]{:S(2)}) copy-start(f32[1,128,512]{2,1,0:T(8,128)S(1)} %collective-permute-done.1.refs_2_) | copy-start | bytes 786436
  61.9 4.2 %collective-permute-start.19 = (f32[1,128,512]{2,1,0:T(8,128)}, f32[1,128,512]{2,1,0:T(8,128)S(1)}, u32[]{:S(2)}, u32[]{:S(2)}) collective-permute-start(f32[1,128,512]{2,1,0:T(8,128)} %collective-permute-done.18.refs_6_), channel_id=1, source_target_pairs={{0,1},{1,0},{2,3},{3,2},{4,5},{5,4},{6,7},{7,6},{8,9},{9,8},{10,11... | collective-permute-start | bytes 786440 | tf_op jit(solution)/shard_map/ppermute | solution.py:176
  65.6 1.5 collective-permute-start.13
  65.6 2.2 copy-start.15
  65.6 9.9 %collective-permute-start.15 = (f32[1,128,512]{2,1,0:T(8,128)}, f32[1,128,512]{2,1,0:T(8,128)}, u32[]{:S(2)}, u32[]{:S(2)}) collective-permute-start(f32[1,128,512]{2,1,0:T(8,128)} %collective-permute-done.14.refs_6_), channel_id=1, source_target_pairs={{0,1},{1,0},{2,3},{3,2},{4,5},{5,4},{6,7},{7,6},{8,9},{9,8},{10,11... | collective-permute-start | bytes 786440 | tf_op jit(solution)/shard_map/ppermute | solution.py:176
  66.1 1.7 copy-start.16
  66.1 18.5 %collective-permute-start.11 = (f32[1,128,512]{2,1,0:T(8,128)}, f32[1,128,512]{2,1,0:T(8,128)}, u32[]{:S(2)}, u32[]{:S(2)}) collective-permute-start(f32[1,128,512]{2,1,0:T(8,128)} %collective-permute-done.10.refs_6_), channel_id=1, source_target_pairs={{0,1},{1,0},{2,3},{3,2},{4,5},{5,4},{6,7},{7,6},{8,9},{9,8},{10,11... | collective-permute-start | bytes 786440 | tf_op jit(solution)/shard_map/ppermute | solution.py:176
  67.1 0.7 copy-start.12
  67.1 17.5 %collective-permute-start.9 = (f32[1,128,512]{2,1,0:T(8,128)}, f32[1,128,512]{2,1,0:T(8,128)}, u32[]{:S(2)}, u32[]{:S(2)}) collective-permute-start(f32[1,128,512]{2,1,0:T(8,128)} %collective-permute-done.8.refs_2_), channel_id=1, source_target_pairs={{0,1},{1,0},{2,3},{3,2},{4,5},{5,4},{6,7},{7,6},{8,9},{9,8},{10,11... | collective-permute-start | bytes 786440 | tf_op jit(solution)/shard_map/ppermute | solution.py:176
  67.3 1.2 copy-start.2
  67.3 26.6 %collective-permute-start.2 = (f32[1,128,512]{2,1,0:T(8,128)S(1)}, f32[1,128,512]{2,1,0:T(8,128)S(1)}, u32[]{:S(2)}, u32[]{:S(2)}) collective-permute-start(f32[1,128,512]{2,1,0:T(8,128)S(1)} %collective-permute-done.1.refs_2_), channel_id=1, source_target_pairs={{0,1},{1,0},{2,3},{3,2},{4,5},{5,4},{6,7},{7,6},{8,9},{9,8},{10,11... | collective-permute-start | bytes 786440 | tf_op jit(solution)/shard_map/ppermute | solution.py:176
  67.7 26.3 %collective-permute-start.5 = (f32[1,128,512]{2,1,0:T(8,128)}, f32[1,128,512]{2,1,0:T(8,128)S(1)}, u32[]{:S(2)}, u32[]{:S(2)}) collective-permute-start(f32[1,128,512]{2,1,0:T(8,128)} %collective-permute-done.4.refs_6_), channel_id=1, source_target_pairs={{0,1},{1,0},{2,3},{3,2},{4,5},{5,4},{6,7},{7,6},{8,9},{9,8},{10,11... | collective-permute-start | bytes 786440 | tf_op jit(solution)/shard_map/ppermute | solution.py:176
  93.9 0.7 copy-start.10
  93.9 0.8 copy-start.11
  106.2 14.4 %collective-permute-start.20 = (f32[256,512]{1,0:T(8,128)}, f32[256,512]{1,0:T(8,128)S(1)}, u32[]{:S(2)}, u32[]{:S(2)}) collective-permute-start(f32[256,512]{1,0:T(8,128)} %get-tuple-element.77), channel_id=1, source_target_pairs={{0,4},{4,0},{8,12},{12,8},{16,20},{20,16},{24,28},{28,24},{1,5},{5... | collective-permute-start | bytes 1572872 | tf_op jit(solution)/shard_map/ppermute | solution.py:179
  120.5 9.3 %copy-start.6 = (f32[256,512]{1,0:T(8,128)}, f32[256,512]{1,0:T(8,128)S(1)}, u32[]{:S(2)}) copy-start(f32[256,512]{1,0:T(8,128)S(1)} %collective-permute-done.20.half_ref) | copy-start | bytes 1572868
  120.5 9.3 %collective-permute-start.21 = (f32[256,512]{1,0:T(8,128)S(1)}, f32[256,512]{1,0:T(8,128)S(1)}, u32[]{:S(2)}, u32[]{:S(2)}) collective-permute-start(f32[256,512]{1,0:T(8,128)S(1)} %collective-permute-done.20.half_ref), channel_id=1, source_target_pairs={{0,1},{1,0},{2,3},{3,2},{4,5},{5,4},{6,7},{7,6},{8,9},{9,8},{10,11... | collective-permute-start | bytes 1572872 | tf_op jit(solution)/shard_map/ppermute | solution.py:176
  120.5 9.3 %collective-permute-start.22 = (f32[512,128]{1,0:T(8,128)}, f32[512,128]{1,0:T(8,128)S(1)}, u32[]{:S(2)}, u32[]{:S(2)}) collective-permute-start(f32[512,128]{1,0:T(8,128)} %get-tuple-element.79), channel_id=1, source_target_pairs={{0,4},{4,0},{8,12},{12,8},{16,20},{20,16},{24,28},{28,24},{1,5},{5... | collective-permute-start | bytes 786440 | tf_op jit(solution)/shard_map/ppermute | solution.py:179
  120.9 8.9 %collective-permute-start.23 = (f32[8,512]{1,0:T(8,128)}, f32[8,512]{1,0:T(8,128)S(1)}, u32[]{:S(2)}, u32[]{:S(2)}) collective-permute-start(f32[8,512]{1,0:T(8,128)} %get-tuple-element.80.applied_ref), channel_id=1, source_target_pairs={{0,4},{4,0},{8,12},{12,8},{16,20},{20,16},{24,28},{28,24},{1,5},{5... | collective-permute-start | bytes 49160 | tf_op jit(solution)/shard_map/ppermute | solution.py:179
  129.8 0.6 copy-start.19
  129.8 0.7 copy-start.14
  129.8 0.9 copy-start.7
  134.9 0.7 collective-permute-start.24
  135.6 0.7 copy-start.4
  138.9 18.5 %collective-permute-start.25 = (f32[512,128]{1,0:T(8,128)}, f32[512,128]{1,0:T(8,128)S(1)}, u32[]{:S(2)}, u32[]{:S(2)}) collective-permute-start(f32[512,128]{1,0:T(8,128)} %noise_link.2), channel_id=1, source_target_pairs={{16,8},{20,12},{17,9},{21,13},{18,10},{22,14},{19,11},{23,15}} | collective-permute-start | bytes 786440 | tf_op jit(solution)/shard_map/ppermute | solution.py:182
  139.6 17.8 %copy-start.5 = (f32[512,128]{1,0:T(8,128)S(1)}, f32[512,128]{1,0:T(8,128)}, u32[]{:S(2)}) copy-start(f32[512,128]{1,0:T(8,128)} %copy-done.4) | copy-start | bytes 786436
  139.6 4.5 %collective-permute-start.27 = (f32[8,512]{1,0:T(8,128)}, f32[8,512]{1,0:T(8,128)S(1)}, u32[]{:S(2)}, u32[]{:S(2)}) collective-permute-start(f32[8,512]{1,0:T(8,128)} %get-tuple-element.87.local_ref), channel_id=1, source_target_pairs={{0,8},{4,12},{1,9},{5,13},{2,10},{6,14},{3,11},{7,15}} | collective-permute-start | bytes 49160 | tf_op jit(solution)/shard_map/ppermute | solution.py:182
  144.1 0.6 copy-start.17
  147.1 0.7 collective-permute-start.28
  151.5 0.7 collective-permute-start.29
  156.4 5.8 %copy-start.23 = (f32[8,512]{1,0:T(8,128)S(1)}, f32[8,512]{1,0:T(8,128)}, u32[]{:S(2)}) copy-start(f32[8,512]{1,0:T(8,128)} %get-tuple-element.90) | copy-start | bytes 49156
  156.4 5.8 %collective-permute-start.30 = (f32[8,512]{1,0:T(8,128)}, f32[8,512]{1,0:T(8,128)S(1)}, u32[]{:S(2)}, u32[]{:S(2)}) collective-permute-start(f32[8,512]{1,0:T(8,128)} %get-tuple-element.90), channel_id=1, source_target_pairs={{0,4},{4,0},{8,12},{12,8},{16,20},{20,16},{24,28},{28,24},{1,5},{5... | collective-permute-start | bytes 49160 | tf_op jit(solution)/shard_map/ppermute | solution.py:179
  160.8 37.5 %copy-start.3 = (f32[512,128]{1,0:T(8,128)S(1)}, f32[512,128]{1,0:T(8,128)}, u32[]{:S(2)}) copy-start(f32[512,128]{1,0:T(8,128)} %add.35.got_ref) | copy-start | bytes 786436
  160.8 37.5 %collective-permute-start.26 = (f32[512,128]{1,0:T(8,128)}, f32[512,128]{1,0:T(8,128)S(1)}, u32[]{:S(2)}, u32[]{:S(2)}) collective-permute-start(f32[512,128]{1,0:T(8,128)} %noise_link.3), channel_id=1, source_target_pairs={{8,0},{12,4},{9,1},{13,5},{10,2},{14,6},{11,3},{15,7}} | collective-permute-start | bytes 786440 | tf_op jit(solution)/shard_map/ppermute | solution.py:182
  165.0 0.7 collective-permute-start.31
  165.7 0.6 copy-start.18
  168.5 0.7 collective-permute-start.32
  172.6 24.4 %collective-permute-start.33 = (f32[8,512]{1,0:T(8,128)}, f32[8,512]{1,0:T(8,128)S(1)}, u32[]{:S(2)}, u32[]{:S(2)}) collective-permute-start(f32[8,512]{1,0:T(8,128)} %backward_link.5), channel_id=1, source_target_pairs={{8,0},{12,4},{9,1},{13,5},{10,2},{14,6},{11,3},{15,7}} | collective-permute-start | bytes 49160 | tf_op jit(solution)/shard_map/ppermute | solution.py:182
  201.9 8.6 %collective-permute-start.34 = (f32[512,128]{1,0:T(8,128)}, f32[512,128]{1,0:T(8,128)S(1)}, u32[]{:S(2)}, u32[]{:S(2)}) collective-permute-start(f32[512,128]{1,0:T(8,128)} %get-tuple-element.92), channel_id=1, source_target_pairs={{0,4},{4,0},{8,12},{12,8},{16,20},{20,16},{24,28},{28,24},{1,5},{5... | collective-permute-start | bytes 786440 | tf_op jit(solution)/shard_map/ppermute | solution.py:179
  210.5 0.7 copy-start.13

commit v2 on v0

v2 whole, which is shorter than its diff:
```python
import functools

import jax
import jax.numpy as jnp
from jax import lax
from jax.experimental import pallas as pl
from jax.experimental.pallas import tpu as pltpu
from jax.sharding import PartitionSpec as P

F32 = jnp.float32
BF16 = jnp.bfloat16
CORES = 2
PAIR = 2
LINES = 8

NN = ((1,), (0,))
TN = ((0,), (0,))
NT = ((1,), (1,))


def split(value):
    high = value.astype(BF16)
    return high, (value - high.astype(F32)).astype(BF16)


def parts(ref):
    return ref[0], ref[1]


def dot_parts(left, right, dims):
    product = functools.partial(
        lax.dot_general, dimension_numbers=(dims, ((), ())), preferred_element_type=F32
    )
    return product(left[0], right[0]) + (product(left[0], right[1]) + product(left[1], right[0]))


def shape(*dims, dtype=F32):
    return jax.ShapeDtypeStruct(dims, dtype)


def in_vmem(value):
    return pltpu.with_memory_space_constraint(value, pltpu.VMEM)


def call(body, outs, name, scalars, arrays, work=1, scratch=(), out_specs=None):
    vmem = pl.BlockSpec(memory_space=pltpu.VMEM)
    out_shape = outs if out_specs else jax.tree.map(lambda o: pltpu.VMEM(o.shape, o.dtype), outs)
    return pl.pallas_call(
        body,
        out_shape=out_shape,
        in_specs=[pl.BlockSpec(memory_space=pltpu.SMEM)] * len(scalars) + [vmem] * len(arrays),
        out_specs=out_specs or jax.tree.map(lambda _: vmem, outs),
        scratch_shapes=list(scratch),
        compiler_params=pltpu.CompilerParams(vmem_limit_bytes=20 * 1024 * 1024),
        cost_estimate=pl.CostEstimate(
            flops=int(work * 1.0e9), transcendentals=0, bytes_accessed=1024
        ),
        name=name,
    )(*scalars, *map(in_vmem, arrays))


def bin_observations(obs_day, obs_node, obs_value, days, nodes):
    chunk = min(512, obs_day.shape[0])
    chunks = obs_day.shape[0] // chunk

    def body(day_ref, node_ref, value_ref, out_ref):
        total = jnp.zeros((3 * days, nodes), F32)
        for index in range(chunks):
            row = pl.ds(index, 1)
            value = value_ref[row, :]
            high = value.astype(BF16).astype(F32)
            middle = (value - high).astype(BF16).astype(F32)
            low = value - high - middle
            is_day = lax.broadcasted_iota(jnp.int32, (days, chunk), 0) == day_ref[row, :]
            marked = jnp.concatenate(
                [jnp.where(is_day, part, 0.0).astype(BF16) for part in (high, middle, low)], axis=0
            )
            is_node = lax.broadcasted_iota(jnp.int32, (nodes, chunk), 0) == node_ref[row, :]
            total += lax.dot_general(
                marked, is_node.astype(F32).astype(BF16), (NT, ((), ())), preferred_element_type=F32
            )
        out_ref[...] = total[:days] + (total[days : 2 * days] + total[2 * days :])

    return call(
        body,
        shape(days, nodes),
        "bin_observations",
        (),
        [value.reshape(chunks, chunk) for value in (obs_day, obs_node, obs_value)],
        work=2,
    )


def gather_rows(position_ref, refs, take, out_ref):
    share = refs[0].shape[-2]
    for offset, ref in enumerate(refs):
        at = pl.ds(pl.multiple_of((position_ref[0] ^ offset) * share, share), share)
        out_ref[0, at, :], out_ref[1, at, :] = split(ref[take(offset)])


def inverse_step(inverse, path, noise, wanted):
    moved = inverse if path is None else split(dot_parts(inverse, path, NN))
    current = dot_parts(split(wanted), inverse, NT)
    return moved, current, (
        dot_parts(moved, noise, TN),
        dot_parts(moved, moved, TN),
        dot_parts(split(current), moved, NN),
    )


def local(inv_diag, coupling, noise, obs_day, obs_node, obs_value):
    part_count = lax.axis_size("tm")
    row_count = lax.axis_size("row")
    my_part = lax.axis_index("tm")
    my_row = lax.axis_index("row")
    day_count, share, nodes = inv_diag.shape
    columns = noise.shape[2]
    half = columns // PAIR
    half_nodes = nodes // CORES
    groups = part_count // PAIR
    early = day_count // 2

    def to_row(value, distance):
        return lax.ppermute(value, "row", [(i, i ^ distance) for i in range(row_count)])

    def to_pair(value):
        return lax.ppermute(value, "tm", [(i, i ^ 1) for i in range(part_count)])

    def to_group(value, source, target):
        return lax.ppermute(
            value, "tm", [(PAIR * source + i, PAIR * target + i) for i in range(PAIR)]
        )

    position = jnp.reshape(my_row, (1,)).astype(jnp.int32)
    side = jnp.reshape(my_part % PAIR, (1,)).astype(jnp.int32)
    core = jnp.reshape(my_row % CORES, (1,)).astype(jnp.int32)

    line = shape(LINES, nodes)
    square = shape(nodes, nodes)
    map_parts = shape(2, nodes, nodes, dtype=BF16)
    columns_half = shape(nodes, half)
    columns_full = shape(nodes, columns)

    def after(value, *others):
        return lax.optimization_barrier((value, *others))[0]

    ranges = [(inv_diag, 0, early), (coupling, 0, early), (inv_diag, early, day_count)]
    ranges += [(coupling, day, day + 1) for day in range(early, day_count)]
    arrived = []
    for index, (values, start, stop) in enumerate(ranges):
        rows = values[start:stop]
        if index >= 2:
            rows = after(rows, *arrived[index - 2])
        arrived.append([to_row(rows, distance) for distance in range(CORES, row_count, CORES)])

    def shared(index, *ahead):
        pieces = []
        for got in arrived[index]:
            pieces += [got, to_row(after(got, *ahead) if ahead else got, 1)]
        return pieces

    own_inverse = [inv_diag, to_row(inv_diag, 1)]
    own_link = [coupling, to_row(coupling, 1)]

    def taking(start, day):
        return lambda offset: day if offset < CORES else day - start

    right_side = bin_observations(obs_day, obs_node, obs_value, part_count * day_count, nodes)
    distance = part_count // 2
    while distance:
        count = right_side.shape[0] // 2
        upper = (my_part // distance) % 2 == 1
        low, high = right_side[:count], right_side[count:]
        got = lax.ppermute(
            jnp.where(upper, low, high), "tm", [(i, i ^ distance) for i in range(part_count)]
        )
        right_side = jnp.where(upper, high, low) + got
        distance //= 2
    distance = 1
    while distance < row_count:
        right_side = right_side + to_row(right_side, distance)
        distance *= 2
    right_side = jnp.broadcast_to(right_side[:, None, :], (day_count, LINES, nodes))

    def early_body(position_ref, *refs):
        inverse_refs, link_refs = refs[:row_count], refs[row_count : 2 * row_count]
        noise_ref, source_ref = refs[2 * row_count : 2 * row_count + 2]
        path_out, gram_out, sum_out, applied_out, back_out = refs[2 * row_count + 2 :][:5]
        inverse_out, link_out, moved_out, current_out = refs[2 * row_count + 7 :]
        path = applied = None
        for day in range(early):
            gather_rows(position_ref, inverse_refs, taking(0, day), inverse_out.at[day])
            gather_rows(position_ref, link_refs, taking(0, day), link_out.at[day])
            wanted = source_ref[day] if day == 0 else source_ref[day] - applied
            moved, current, terms = inverse_step(
                parts(inverse_out.at[day]), path, split(noise_ref[day]), wanted
            )
            moved_out[day, 0], moved_out[day, 1] = moved
            current_out[day] = current
            link = parts(link_out.at[day])
            path_value = -dot_parts(link, moved, NN)
            path = split(path_value)
            applied = dot_parts(split(current), link, NT)
            for out, term in zip((sum_out, gram_out, back_out), terms, strict=True):
                out[...] = term if day == 0 else out[...] + term
        path_out[0], path_out[1] = path
        applied_out[...] = applied

    def several(count, value):
        return shape(count, *value.shape, dtype=value.dtype)

    (path, gram, summed, applied, back, inverses_0, links_0, moved_0, currents_0) = call(
        early_body,
        (
            map_parts, square, columns_full, line, line,
            several(early, map_parts), several(early, map_parts), several(early, map_parts),
            several(early, line),
        ),
        "early_days",
        (position,),
        [*own_inverse, *shared(0), *own_link, *shared(1), noise, right_side],
        work=6,
    )

    def late_body(position_ref, *refs):
        inverse_refs = refs[:row_count]
        noise_ref, source_ref, path_ref, gram_ref, sum_ref, applied_ref, back_ref = refs[
            row_count : row_count + 7
        ]
        gram_out, sum_out, back_out, inverse_out, moved_out, current_out = refs[row_count + 7 :]
        for day in range(early, day_count):
            gather_rows(
                position_ref, inverse_refs, taking(early, day), inverse_out.at[day - early]
            )
        moved, current, terms = inverse_step(
            parts(inverse_out.at[0]),
            parts(path_ref),
            split(noise_ref[early]),
            source_ref[early] - applied_ref[...],
        )
        moved_out[0], moved_out[1] = moved
        current_out[...] = current
        sum_out[...] = sum_ref[...] + terms[0]
        gram_out[...] = gram_ref[...] + terms[1]
        back_out[...] = back_ref[...] + terms[2]

    late = day_count - early
    gram, summed, back, inverses_1, moved, current = call(
        late_body,
        (square, columns_full, line, several(late, map_parts), map_parts, line),
        "late_inverses",
        (position,),
        [
            *own_inverse, *shared(2, path), noise, right_side, path, gram, summed, applied, back,
        ],
        work=3,
    )
    moved_late, current_late, links_late = [moved], [current], []

    def next_body(day, position_ref, *refs):
        link_refs = refs[:row_count]
        (noise_ref, source_ref, inverse_ref, gram_ref, sum_ref, back_ref, moved_ref, current_ref) = (
            refs[row_count : row_count + 8]
        )
        gram_out, sum_out, back_out, link_out, moved_out, current_out = refs[row_count + 8 :]
        gather_rows(position_ref, link_refs, taking(day, day), link_out)
        link = parts(link_out)
        path = split(-dot_parts(link, parts(moved_ref), NN))
        applied = dot_parts(split(current_ref[...]), link, NT)
        moved, current, terms = inverse_step(
            parts(inverse_ref.at[day + 1 - early]),
            path,
            split(noise_ref[day + 1]),
            source_ref[day + 1] - applied,
        )
        moved_out[0], moved_out[1] = moved
        current_out[...] = current
        sum_out[...] = sum_ref[...] + terms[0]
        gram_out[...] = gram_ref[...] + terms[1]
        back_out[...] = back_ref[...] + terms[2]

    for day in range(early, day_count - 1):
        gram, summed, back, link, moved, current = call(
            functools.partial(next_body, day),
            (square, columns_full, line, map_parts, map_parts, line),
            f"late_day_{day}",
            (position,),
            [
                *own_link, *shared(3 + day - early, moved), noise, right_side, inverses_1, gram, summed,
                back, moved, current,
            ],
            work=4,
        )
        moved_late.append(moved)
        current_late.append(current)
        links_late.append(link)

    def halves_body(side_ref, sum_ref, keep, send):
        low, high = sum_ref[:, :half], sum_ref[:, half:]
        first = side_ref[0] == 0
        keep[...] = jnp.where(first, low, high)
        send[...] = jnp.where(first, high, low)

    keep, send = call(
        halves_body, (columns_half, columns_half), "halves", (side,), [summed], work=0.1
    )
    other_sum = to_pair(send)

    def last_link_body(position_ref, core_ref, *refs):
        link_refs = refs[:row_count]
        moved_ref, current_ref, path_out, half_out, flux_out, link_out, whole = refs[row_count:]
        gather_rows(position_ref, link_refs, taking(day_count - 1, day_count - 1), link_out)
        link = parts(link_out)
        whole[...] = -dot_parts(link, parts(moved_ref), NN)
        half_out[...] = whole[
            pl.ds(pl.multiple_of(core_ref[0] * half_nodes, half_nodes), half_nodes), :
        ]
        path_out[0], path_out[1] = split(whole[...])
        flux_out[...] = dot_parts(split(current_ref[...]), link, NT)

    path, path_half, flux, link = call(
        last_link_body,
        (map_parts, shape(half_nodes, nodes), line, map_parts),
        "last_link",
        (position, core),
        [*own_link, *shared(2 + late, moved), moved, current],
        work=1.5,
        scratch=[pltpu.VMEM((nodes, nodes), F32)],
    )
    links_late.append(link)
    other_half = to_pair(after(path_half, other_sum))
    other_flux = to_pair(flux)
    other_rest = to_row(other_half, 1)

    def own_maps_body(noise_ref, inverse_0, inverse_1, link_0, *refs):
        link_refs, (map_out, local_out) = refs[:late], refs[late:]
        for day in range(day_count):
            inverse = parts(inverse_0.at[day] if day < early else inverse_1.at[day - early])
            link = parts(link_0.at[day] if day < early else link_refs[day - early])
            map_out[day, 0], map_out[day, 1] = split(-dot_parts(link, inverse, NN))
            local_out[day] = dot_parts(inverse, split(noise_ref[day]), TN)

    step_maps, local_terms = call(
        own_maps_body,
        (several(day_count, map_parts), several(day_count, columns_full)),
        "own_maps",
        (),
        [noise, inverses_0, inverses_1, links_0, *links_late],
        work=2 * day_count,
    )

    def pair_body(
        side_ref, core_ref, path_ref, half_ref, rest_ref, sum_ref, other_ref, flux_ref,
        other_flux_ref, maps_out, sum_out, high_sum_out, flux_out, low_flux_out,
    ):
        me, mate = side_ref[0], 1 - side_ref[0]
        mine = core_ref[0]
        maps_out[me] = path_ref[...]
        for which, ref in ((mine, half_ref), (1 - mine, rest_ref)):
            at = pl.ds(pl.multiple_of(which * half_nodes, half_nodes), half_nodes)
            maps_out[mate, 0, at, :], maps_out[mate, 1, at, :] = split(ref[...])
        first = me == 0
        low_sum = jnp.where(first, sum_ref[...], other_ref[...])
        high_sum = jnp.where(first, other_ref[...], sum_ref[...])
        low_flux = jnp.where(first, flux_ref[...], other_flux_ref[...])
        high_flux = jnp.where(first, other_flux_ref[...], flux_ref[...])
        sum_out[...] = dot_parts(parts(maps_out.at[0]), split(high_sum), TN) + low_sum
        high_sum_out[...] = high_sum
        flux_out[...] = dot_parts(split(low_flux), parts(maps_out.at[1]), NT) + high_flux
        low_flux_out[...] = low_flux

    pair_maps, pair_sum, high_sum, pair_flux, low_flux = call(
        pair_body,
        (several(PAIR, map_parts), columns_half, columns_half, line, line),
        "pair_maps",
        (side, core),
        [after(path, local_terms), other_half, other_rest, keep, other_sum, flux, other_flux],
        work=1.5,
    )

    def group_map_body(maps_ref, out_ref):
        out_ref[0], out_ref[1] = split(
            dot_parts(parts(maps_ref.at[1]), parts(maps_ref.at[0]), NN)
        )

    group_map = call(group_map_body, map_parts, "group_map", (), [pair_maps])

    def advance_body(map_ref, local_ref, got_ref, out_ref):
        out_ref[...] = dot_parts(parts(map_ref), split(got_ref[...]), TN) + local_ref[...]

    def line_body(dims, map_ref, local_ref, got_ref, out_ref):
        out_ref[...] = dot_parts(split(got_ref[...]), parts(map_ref), dims) + local_ref[...]

    leaving = None
    value = pair_sum
    for group in range(groups - 1, 0, -1):
        got = to_group(value, group, group - 1)
        leaving = got if leaving is None else leaving + got
        if group > 1:
            value = call(
                advance_body, columns_half, "noise_link", (), [group_map, pair_sum, leaving]
            )

    entering = None
    value = pair_flux
    for group in range(groups - 1):
        got = to_group(value, group, group + 1)
        entering = got if entering is None else entering + got
        if group < groups - 2:
            value = call(
                functools.partial(line_body, NT), line, "forward_link", (),
                [group_map, pair_flux, entering], work=0.5,
            )

    def turn_body(side_ref, maps_ref, flux_ref, entering_ref, gram_ref, back_ref, own_out, back_out):
        given = entering_ref[...]
        after = dot_parts(split(given), parts(maps_ref.at[0]), NT) + flux_ref[...]
        given = jnp.where(side_ref[0] == 0, given, after)
        own_out[...] = given
        back_out[...] = back_ref[...] - dot_parts(split(given), split(gram_ref[...]), NN)

    own_entering, own_back = call(
        turn_body, (line, line), "mean_turn", (side,),
        [pair_maps, low_flux, entering, gram, back],
    )
    other_back = to_pair(own_back)

    def pair_back_body(side_ref, maps_ref, own_ref, other_ref, pair_out, high_out):
        first = side_ref[0] == 0
        low = jnp.where(first, own_ref[...], other_ref[...])
        high = jnp.where(first, other_ref[...], own_ref[...])
        pair_out[...] = dot_parts(split(high), parts(maps_ref.at[0]), NN) + low
        high_out[...] = high

    pair_back, high_back = call(
        pair_back_body, (line, line), "pair_back", (side,), [pair_maps, own_back, other_back],
        work=0.5,
    )
    mean_leaving = None
    value = pair_back
    for group in range(groups - 1, 0, -1):
        got = to_group(value, group, group - 1)
        mean_leaving = got if mean_leaving is None else mean_leaving + got
        if group > 1:
            value = call(
                functools.partial(line_body, NN), line, "backward_link", (),
                [group_map, pair_back, mean_leaving], work=0.5,
            )

    def divide_body(side_ref, maps_ref, sum_ref, leaving_ref, keep_out, send_out):
        between = dot_parts(parts(maps_ref.at[1]), split(leaving_ref[...]), TN) + sum_ref[...]
        first = side_ref[0] == 0
        keep_out[...] = jnp.where(first, between, leaving_ref[...])
        send_out[...] = jnp.where(first, leaving_ref[...], between)

    kept_half, sent_half = call(
        divide_body, (columns_half, columns_half), "divide", (side,),
        [pair_maps, high_sum, leaving],
    )
    got_half = to_pair(sent_half)

    def as_columns(lines):
        spread = jnp.full((LINES, columns), 1.0 / LINES, BF16)
        return sum(
            lax.dot_general(part, spread, (TN, ((), ())), preferred_element_type=F32)
            for part in split(lines)
        )

    def terms_body(entering_ref, local_ref, inverse_0, inverse_1, moved_0_ref, current_0, *refs):
        out_ref = refs[-1]
        given = split(entering_ref[...])
        for day in range(day_count):
            if day < early:
                inverse, moved = inverse_0.at[day], moved_0_ref.at[day]
                current = current_0[day]
            else:
                inverse, moved = inverse_1.at[day - early], refs[day - early]
                current = refs[late + day - early][...]
            current = current - dot_parts(given, parts(moved), NT)
            term = dot_parts(split(current), parts(inverse), NN)
            out_ref[day] = local_ref[day] + as_columns(term)

    terms = call(
        terms_body, several(day_count, columns_full), "mean_terms", (),
        [
            own_entering, local_terms, inverses_0, inverses_1, moved_0, currents_0,
            *moved_late, *current_late,
        ],
        work=4,
    )

    def last_body(
        side_ref, keep_ref, got_ref, mean_ref, back_ref, pair_ref, map_ref, term_ref, out_ref,
        held, sems,
    ):
        first = side_ref[0] == 0
        between = dot_parts(split(mean_ref[...]), parts(pair_ref.at[1]), NN) + back_ref[...]
        mean = jnp.where(first, between, mean_ref[...])
        low = jnp.where(first, keep_ref[...], got_ref[...])
        high = jnp.where(first, got_ref[...], keep_ref[...])
        following = jnp.concatenate([low, high], axis=1) + as_columns(mean)
        copies = []
        for day in reversed(range(day_count)):
            following = dot_parts(parts(map_ref.at[day]), split(following), TN) + term_ref[day]
            held[day] = following
            copies.append(
                pltpu.make_async_copy(held.at[day], out_ref.at[day], sems.at[day])
            )
            copies[-1].start()
        for copy in copies:
            copy.wait()

    return call(
        last_body, shape(day_count, nodes, columns), "last_days", (side,),
        [kept_half, got_half, mean_leaving, high_back, pair_maps, step_maps, terms],
        work=4,
        scratch=[
            pltpu.VMEM((day_count, nodes, columns), F32), pltpu.SemaphoreType.DMA((day_count,)),
        ],
        out_specs=pl.BlockSpec(memory_space=pl.ANY),
    )


def solution(mesh):
    return jax.shard_map(
        local,
        mesh=mesh,
        in_specs=(
            P("tm", "row", None),
            P("tm", "row", None),
            P("tm", None, "row"),
            P(("tm", "row")),
            P(("tm", "row")),
            P(("tm", "row")),
        ),
        out_specs=P("tm", None, "row"),
        check_vma=False,
    )
```

time: 521 us -> 158 us (0.30); the launches traced: 511 us -> 155 us
  waiting for transfers between devices: 262 us -> 61.2 us
  matrix products: 153 us -> 0 us
  Pallas kernels: 0 us -> 44 us
  other arithmetic: 30.1 us -> 0.15 us
  between operations: 15.7 us -> 0.69 us
  local copies, waits for them, and re-layouts: 1.39 us -> 16.3 us
  starting transfers between devices: 41.8 us -> 32.7 us
  blocking collectives: 6.15 us -> 0 us
    unnamed x5 -> x0, waiting for transfers between devices: 157 us -> none
    dot_general x60 -> x0, matrix products: 153 us -> none  [the longest x37 82.2 us: matmul(): jnp.dot(left_side, right_side, precision=highest, preferred_element_type=...]
    pallas_call x0 -> x20, Pallas kernels: none -> 44 us  [call(): pl.pallas_call(body, out_shape=out_shape, in_specs=[pl.BlockSpec(memory_s...]
    ppermute x14 -> x32, waiting for transfers between devices: 105 us -> 61.2 us  [the longest x15 22.2 us: to_row(): lax.ppermute(value, 'row', [(i, i ^ distance) for i in range(row_count)])]
    unnamed x6 -> x0, other arithmetic: 23.7 us -> none
    unnamed x5 -> x52, local copies, waits for them, and re-layouts: 0.73 us -> 13 us
    ppermute x14 -> x32, starting transfers between devices: 41.5 us -> 32.7 us  [the longest x9 11.2 us: to_group(): lax.ppermute(value, 'tm', [(PAIR * source + i, PAIR * target + i) for i i...]
    all_gather x1 -> x0, blocking collectives: 6.15 us -> none  [local(): lax.all_gather(own_sources, 'row', axis=1, tiled=True)]
  transfers between devices with their start and end apart: 18 -> 32, of which waited for: 15 -> 15; matrix products, arithmetic and copies ran while one was open for 19% -> 1% of each run, Pallas kernels for 0% -> 24%
where the time goes in v2:
time: 158 us; the launch traced here: 155 us
  waiting for transfers between devices  61.2 us (39%)
  Pallas kernels  44 us (28%)
  starting transfers between devices  32.7 us (21%)
  local copies, waits for them, and re-layouts  16.3 us (10%)
    pallas_call x20, Pallas kernels, call(): pl.pallas_call(body, out_shape=out_shape, in_specs=[pl.BlockSpec(memory_s...  44 us
    ppermute x15, waiting for transfers between devices, to_row(): lax.ppermute(value, 'row', [(i, i ^ distance) for i in range(row_count)])  22.2 us
    ppermute x5, waiting for transfers between devices, to_pair(): return lax.ppermute(value, 'tm', [(i, i ^ 1) for i in range(part_count)])  18 us
    ppermute x9, waiting for transfers between devices, to_group(): lax.ppermute(value, 'tm', [(PAIR * source + i, PAIR * target + i) for i i...  17.7 us
    unnamed x52, local copies, waits for them, and re-layouts  13 us
    ppermute x9, starting transfers between devices, to_group(): lax.ppermute(value, 'tm', [(PAIR * source + i, PAIR * target + i) for i i...  11.2 us
    ppermute x15, starting transfers between devices, to_row(): lax.ppermute(value, 'row', [(i, i ^ distance) for i in range(row_count)])  7.73 us
    ppermute x3, starting transfers between devices, local(): lax.ppermute(jnp.where(upper, low, high), 'tm', [(i, i ^ distance) for i...  6.99 us
  transfers between devices with their start and end apart: 32, of which 15 were waited for; matrix products, arithmetic and copies ran while one was open for 1% of the time, Pallas kernels for 24%

profile of v2, /device:TPU:0, one launch (start us, length us, event | category | flops | bytes accessed | tf_op | source)
XLA Modules:
  0.0 155.0 jit_solution(2264328642200307614)
XLA Ops:
  0.0 2.3 %fusion.1 = (f32[2,128,512]{2,1,0:T(8,128)}, f32[2,128,512]{2,1,0:T(8,128)}) fusion(f32[4,128,512]{2,1,0:T(8,128)} %refs_0_.5), kind=kLoop, calls=%fused_computation.7 | loop fusion | bytes 2097152 | tf_op jit(solution)/shard_map/slice | solution.py:151
  2.3 2.9 %collective-permute-start.1 = (f32[2,128,512]{2,1,0:T(8,128)}, f32[2,128,512]{2,1,0:T(8,128)}, u32[]{:S(2)}, u32[]{:S(2)}) collective-permute-start(f32[2,128,512]{2,1,0:T(8,128)} %get-tuple-element.103), channel_id=1, source_target_pairs={{0,2},{1,3},{2,0},{3,1},{4,6},{5,7},{6,4},{7,5},{8,10},{9,11},{10,... | collective-permute-start | bytes 1572872 | tf_op jit(solution)/shard_map/ppermute | solution.py:124
  5.3 0.8 slice.37
  6.2 1.4 bin_observations.1
  7.6 3.2 %collective-permute-start.9 = (f32[16,512]{1,0:T(8,128)S(1)}, f32[16,512]{1,0:T(8,128)S(1)}, u32[]{:S(2)}, u32[]{:S(2)}) collective-permute-start(f32[16,512]{1,0:T(8,128)S(1)} %slice_select_fusion), channel_id=1, source_target_pairs={{0,16},{4,20},{8,24},{12,28},{16,0},{20,4},{24,8},{28,12},{1,17},{... | collective-permute-start | bytes 98312 | tf_op jit(solution)/shard_map/ppermute | solution.py:174
  10.8 0.5 collective-permute-start.6
  11.3 1.4 collective-permute-done.9
  12.7 2.0 %collective-permute-start.10 = (f32[8,512]{1,0:T(8,128)S(1)}, f32[8,512]{1,0:T(8,128)S(1)}, u32[]{:S(2)}, u32[]{:S(2)}) collective-permute-start(f32[8,512]{1,0:T(8,128)S(1)} %slice_select_fusion.1), channel_id=1, source_target_pairs={{0,8},{4,12},{8,0},{12,4},{16,24},{20,28},{24,16},{28,20},{1,9},{5... | collective-permute-start | bytes 49160 | tf_op jit(solution)/shard_map/ppermute | solution.py:174
  14.7 3.6 %collective-permute-done.1.refs_2_ = f32[2,128,512]{2,1,0:T(8,128)} collective-permute-done((f32[2,128,512]{2,1,0:T(8,128)}, f32[2,128,512]{2,1,0:T(8,128)}, u32[]{:S(2)}, u32[]{:S(2)}) %collective-permute-start.1) | collective-permute-done | bytes 524320 | tf_op jit(solution)/shard_map/ppermute | solution.py:124
  18.4 10.4 %collective-permute-done.4.refs_6_ = f32[2,128,512]{2,1,0:T(8,128)} collective-permute-done((f32[2,128,512]{2,1,0:T(8,128)}, f32[2,128,512]{2,1,0:T(8,128)}, u32[]{:S(2)}, u32[]{:S(2)}) %collective-permute-start.4) | collective-permute-done | bytes 524320 | tf_op jit(solution)/shard_map/ppermute | solution.py:124
  28.8 1.8 %collective-permute-start.11 = (f32[4,512]{1,0:T(4,128)S(1)}, f32[4,512]{1,0:T(4,128)S(1)}, u32[]{:S(2)}, u32[]{:S(2)}) collective-permute-start(f32[4,512]{1,0:T(4,128)S(1)} %slice_select_fusion.2), channel_id=1, source_target_pairs={{0,4},{4,0},{8,12},{12,8},{16,20},{20,16},{24,28},{28,24},{1,5},{5... | collective-permute-start | bytes 24584 | tf_op jit(solution)/shard_map/ppermute | solution.py:174
  30.6 1.9 %collective-permute-done.11 = f32[4,512]{1,0:T(4,128)S(1)} collective-permute-done((f32[4,512]{1,0:T(4,128)S(1)}, f32[4,512]{1,0:T(4,128)S(1)}, u32[]{:S(2)}, u32[]{:S(2)}) %collective-permute-start.11) | collective-permute-done | bytes 8224 | tf_op jit(solution)/shard_map/ppermute | solution.py:174
  32.5 1.2 collective-permute-done.12
  33.7 1.7 %collective-permute-start.13 = (f32[4,512]{1,0:T(4,128)S(1)}, f32[4,512]{1,0:T(4,128)S(1)}, u32[]{:S(2)}, u32[]{:S(2)}) collective-permute-start(f32[4,512]{1,0:T(4,128)S(1)} %add.57), channel_id=1, source_target_pairs={{0,2},{1,3},{2,0},{3,1},{4,6},{5,7},{6,4},{7,5},{8,10},{9,11},{10,... | collective-permute-start | bytes 24584 | tf_op jit(solution)/shard_map/ppermute | solution.py:124
  35.4 1.9 %collective-permute-done.13 = f32[4,512]{1,0:T(4,128)S(1)} collective-permute-done((f32[4,512]{1,0:T(4,128)S(1)}, f32[4,512]{1,0:T(4,128)S(1)}, u32[]{:S(2)}, u32[]{:S(2)}) %collective-permute-start.13) | collective-permute-done | bytes 8224 | tf_op jit(solution)/shard_map/ppermute | solution.py:124
  37.4 1.7 %collective-permute-start.2 = (f32[2,128,512]{2,1,0:T(8,128)}, f32[2,128,512]{2,1,0:T(8,128)S(1)}, u32[]{:S(2)}, u32[]{:S(2)}) collective-permute-start(f32[2,128,512]{2,1,0:T(8,128)} %get-tuple-element.53), channel_id=1, source_target_pairs={{0,2},{1,3},{2,0},{3,1},{4,6},{5,7},{6,4},{7,5},{8,10},{9,11},{10,... | collective-permute-start | bytes 1572872 | tf_op jit(solution)/shard_map/ppermute | solution.py:124
  39.1 1.6 %copy-done.2 = f32[4,512,256]{2,1,0:T(8,128)S(1)} copy-done((f32[4,512,256]{2,1,0:T(8,128)S(1)}, f32[4,512,256]{2,1,0:T(8,128)}, u32[]{:S(2)}) %copy-start.2) | copy-done | bytes 2097176
  40.7 10.5 %early_days.1 = (bf16[2,512,512]{2,1,0:T(8,128)(2,1)S(1)}, f32[512,512]{1,0:T(8,128)S(1)}, f32[512,256]{1,0:T(8,128)S(1)}, f32[8,512]{1,0:T(8,128)S(1)}, f32[8,5...) custom-call(s32[1]{0:T(128)} %bitcast.2.position_ref, ...), custom_call_target="tpu_custom_call" | custom-call | flops 6000000000 | bytes 1024 | tf_op jit(solution)/shard_map/early_days/pallas_call | solution.py:48
  51.3 1.3 copy-done.7
  52.6 1.3 copy-done.9
  53.9 1.4 copy-done.21
  55.7 1.5 collective-permute-done.14.refs_3_
  57.2 4.6 %late_inverses.1 = (f32[512,512]{1,0:T(8,128)S(1)}, f32[512,256]{1,0:T(8,128)S(1)}, f32[8,512]{1,0:T(8,128)S(1)}, bf16[2,2,512,512]{3,2,1,0:T(8,128)(2,1)S(1)}, ...) custom-call(s32[1]{0:T(128)} %bitcast.2.position_ref, f32[4,128,512]{2,1,0:T(8,128)S(1)} %copy-done, ...), custom_call_target="tpu_custom_call" | custom-call | flops 3000000000 | bytes 1024 | tf_op jit(solution)/shard_map/late_inverses/pallas_call | solution.py:48
  61.8 2.3 %collective-permute-done.5.refs_2_ = f32[1,128,512]{2,1,0:T(8,128)S(1)} collective-permute-done((f32[1,128,512]{2,1,0:T(8,128)S(1)}, f32[1,128,512]{2,1,0:T(8,128)S(1)}, u32[]{:S(2)}, u32[]{:S(2)}) %collective-permute-start.5) | collective-permute-done | bytes 262176 | tf_op jit(solution)/shard_map/ppermute | solution.py:124
  64.4 1.2 collective-permute-done.15.refs_3_
  65.6 4.5 %late_day_2.1 = (f32[512,512]{1,0:T(8,128)S(1)}, f32[512,256]{1,0:T(8,128)S(1)}, f32[8,512]{1,0:T(8,128)S(1)}, bf16[2,512,512]{2,1,0:T(8,128)(2,1)S(1)}, bf16[2,...) custom-call(s32[1]{0:T(128)} %bitcast.2.position_ref, f32[4,128,512]{2,1,0:T(8,128)S(1)} %copy-done.1, ...), custom_call_target="tpu_custom_call" | custom-call | flops 4000000000 | bytes 1024 | tf_op jit(solution)/shard_map/late_day_2/pallas_call | solution.py:48
  70.2 1.0 copy-done.5
  71.1 1.0 copy-done.14
  72.2 1.0 copy-done.19
  73.3 1.6 %collective-permute-start.17 = (f32[512,128]{1,0:T(8,128)S(1)}, f32[512,128]{1,0:T(8,128)S(1)}, u32[]{:S(2)}, u32[]{:S(2)}) collective-permute-start(f32[512,128]{1,0:T(8,128)S(1)} %get-tuple-element.81), channel_id=1, source_target_pairs={{0,4},{4,0},{8,12},{12,8},{16,20},{20,16},{24,28},{28,24},{1,5},{5... | collective-permute-start | bytes 786440 | tf_op jit(solution)/shard_map/ppermute | solution.py:127
  74.9 1.2 copy-done.15
  76.2 1.5 last_link.1
  77.7 4.3 %collective-permute-done.17.other_ref = f32[512,128]{1,0:T(8,128)S(1)} collective-permute-done((f32[512,128]{1,0:T(8,128)S(1)}, f32[512,128]{1,0:T(8,128)S(1)}, u32[]{:S(2)}, u32[]{:S(2)}) %collective-permute-start.17) | collective-permute-done | bytes 262176 | tf_op jit(solution)/shard_map/ppermute | solution.py:127
  82.0 1.5 collective-permute-start.18
  83.5 0.5 collective-permute-start.20
  84.0 11.5 %collective-permute-done.18.half_ref = f32[256,512]{1,0:T(8,128)S(1)} collective-permute-done((f32[256,512]{1,0:T(8,128)S(1)}, f32[256,512]{1,0:T(8,128)S(1)}, u32[]{:S(2)}, u32[]{:S(2)}) %collective-permute-start.18) | collective-permute-done | bytes 524320 | tf_op jit(solution)/shard_map/ppermute | solution.py:127
  95.6 1.6 %copy-done.12 = bf16[2,2,512,512]{3,2,1,0:T(8,128)(2,1)S(1)} copy-done((bf16[2,2,512,512]{3,2,1,0:T(8,128)(2,1)S(1)}, bf16[2,2,512,512]{3,2,1,0:T(8,128)(2,1)}, u32[]{:S(2)}) %copy-start.12) | copy-done | bytes 2097176
  97.2 1.6 %copy-done.22 = bf16[2,2,512,512]{3,2,1,0:T(8,128)(2,1)S(1)} copy-done((bf16[2,2,512,512]{3,2,1,0:T(8,128)(2,1)S(1)}, bf16[2,2,512,512]{3,2,1,0:T(8,128)(2,1)}, u32[]{:S(2)}) %copy-start.22) | copy-done | bytes 2097176
  98.7 5.1 %own_maps.1 = (bf16[4,2,512,512]{3,2,1,0:T(8,128)(2,1)S(1)}, f32[4,512,256]{2,1,0:T(8,128)S(1)}) custom-call(f32[4,512,256]{2,1,0:T(8,128)S(1)} %copy-done.4, bf16[2,2,512,512]{3,2,1,0:T(8,128)(2,1)S(1)} %copy-done.8, bf16[2,2,512,512]{3,2,1,0:T(8,128)(2,1)S(1)} %copy-done.12, bf16[2,2,512,512]{3,2,1,0:T(8,128)(2,1)S(1)} %copy-done.22, ...), custom_call_target="tpu_custom_call" | custom-call | flops 8000000000 | bytes 1024 | tf_op jit(solution)/shard_map/own_maps/pallas_call | solution.py:48
  103.8 1.3 pair_maps.1
  105.1 0.7 collective-permute-start.21
  105.8 1.0 group_map.1.map_ref
  106.8 0.6 noise_link.2
  107.4 0.7 collective-permute-start.22
  108.1 4.1 %collective-permute-start.25 = (f32[8,512]{1,0:T(8,128)S(1)}, f32[8,512]{1,0:T(8,128)S(1)}, u32[]{:S(2)}, u32[]{:S(2)}) collective-permute-start(f32[8,512]{1,0:T(8,128)S(1)} %get-tuple-element.91.local_ref), channel_id=1, source_target_pairs={{0,8},{4,12},{1,9},{5,13},{2,10},{6,14},{3,11},{7,15}} | collective-permute-start | bytes 49160 | tf_op jit(solution)/shard_map/ppermute | solution.py:130
  112.2 1.4 collective-permute-done.25.got_ref
  113.7 0.5 forward_link.2
  114.2 0.7 collective-permute-start.26
  114.9 0.5 forward_link.3
  115.4 0.7 collective-permute-start.27
  116.1 0.6 noise_link.3
  116.8 1.5 collective-permute-start.23
  118.3 0.8 mean_turn.1
  119.1 1.5 collective-permute-start.28
  120.6 2.2 %collective-permute-done.28.other_ref = f32[8,512]{1,0:T(8,128)S(1)} collective-permute-done((f32[8,512]{1,0:T(8,128)S(1)}, f32[8,512]{1,0:T(8,128)S(1)}, u32[]{:S(2)}, u32[]{:S(2)}) %collective-permute-start.28) | collective-permute-done | bytes 16416 | tf_op jit(solution)/shard_map/ppermute | solution.py:127
  123.1 0.7 collective-permute-start.29
  124.1 0.7 collective-permute-start.30
  125.2 1.6 %collective-permute-start.31 = (f32[8,512]{1,0:T(8,128)S(1)}, f32[8,512]{1,0:T(8,128)S(1)}, u32[]{:S(2)}, u32[]{:S(2)}) collective-permute-start(f32[8,512]{1,0:T(8,128)S(1)} %backward_link.3), channel_id=1, source_target_pairs={{8,0},{12,4},{9,1},{13,5},{10,2},{14,6},{11,3},{15,7}} | collective-permute-start | bytes 49160 | tf_op jit(solution)/shard_map/ppermute | solution.py:130
  126.7 7.8 %collective-permute-done.23 = f32[512,128]{1,0:T(8,128)S(1)} collective-permute-done((f32[512,128]{1,0:T(8,128)S(1)}, f32[512,128]{1,0:T(8,128)S(1)}, u32[]{:S(2)}, u32[]{:S(2)}) %collective-permute-start.23) | collective-permute-done | bytes 262176 | tf_op jit(solution)/shard_map/ppermute | solution.py:130
  134.6 0.6 divide.1
  135.2 1.6 %collective-permute-start.24 = (f32[512,128]{1,0:T(8,128)S(1)}, f32[512,128]{1,0:T(8,128)S(1)}, u32[]{:S(2)}, u32[]{:S(2)}) collective-permute-start(f32[512,128]{1,0:T(8,128)S(1)} %get-tuple-element.89), channel_id=1, source_target_pairs={{0,4},{4,0},{8,12},{12,8},{16,20},{20,16},{24,28},{28,24},{1,5},{5... | collective-permute-start | bytes 786440 | tf_op jit(solution)/shard_map/ppermute | solution.py:127
  136.8 4.7 %mean_terms.1.term_ref = f32[4,512,256]{2,1,0:T(8,128)S(1)} custom-call(f32[8,512]{1,0:T(8,128)S(1)} %get-tuple-element.98.entering_ref, f32[4,512,256]{2,1,0:T(8,128)S(1)} %get-tuple-element.77.local_ref, bf16[2,2,512,512]{3,2,1,0:T(8,128)(2,1)S(1)} %copy-done.8, bf16[2,2,512,512]{3,2,1,0:T(8,128)(2,1)S(1)} %copy-done.13, ...), custom_call_target="tpu_custom_call" | custom-call | flops 4000000000 | bytes 1024 | tf_op jit(solution)/shard_map/mean_terms/pallas_call | solution.py:48
  141.5 8.4 %collective-permute-done.31 = f32[8,512]{1,0:T(8,128)S(1)} collective-permute-done((f32[8,512]{1,0:T(8,128)S(1)}, f32[8,512]{1,0:T(8,128)S(1)}, u32[]{:S(2)}, u32[]{:S(2)}) %collective-permute-start.31) | collective-permute-done | bytes 16416 | tf_op jit(solution)/shard_map/ppermute | solution.py:130
  149.9 4.9 %last_days.1 = f32[4,512,256]{2,1,0:T(8,128)} custom-call(s32[1]{0:T(128)} %bitcast.side_ref, f32[512,128]{1,0:T(8,128)S(1)} %get-tuple-element.88.keep_ref, f32[512,128]{1,0:T(8,128)S(1)} %collective-permute-done.24.got_ref, f32[8,512]{1,0:T(8,128)S(1)} %add.64.mean_ref, f32[8,512]{1,0:T(8,128)S(1)} %get-tuple-element.96.back_ref, ...), custom_call_target="tpu_custom_call" | custom-call | flops 4000000000 | bytes 1024 | tf_op jit(solution)/shard_map/last_days/pallas_call | solution.py:48
  (93 shorter events, 2.1 us)
Async XLA Ops:
  0.0 5.3 %copy-start.1 = (f32[4,128,512]{2,1,0:T(8,128)S(1)}, f32[4,128,512]{2,1,0:T(8,128)}, u32[]{:S(2)}) copy-start(f32[4,128,512]{2,1,0:T(8,128)} %refs_0_.7) | copy-start | bytes 3145732
  0.0 6.1 %copy-start.23 = (s32[4096]{0:T(1024)S(1)}, s32[4096]{0:T(1024)}, u32[]{:S(2)}) copy-start(s32[4096]{0:T(1024)} %param.9) | copy-start | bytes 49156
  0.0 6.1 %copy-start.24 = (s32[4096]{0:T(1024)S(1)}, s32[4096]{0:T(1024)}, u32[]{:S(2)}) copy-start(s32[4096]{0:T(1024)} %param.10) | copy-start | bytes 49156
  0.0 6.2 %copy-start.25 = (f32[4096]{0:T(1024)S(1)}, f32[4096]{0:T(1024)}, u32[]{:S(2)}) copy-start(f32[4096]{0:T(1024)} %param.11) | copy-start | bytes 49156
  2.3 16.0 %collective-permute-start.1 = (f32[2,128,512]{2,1,0:T(8,128)}, f32[2,128,512]{2,1,0:T(8,128)}, u32[]{:S(2)}, u32[]{:S(2)}) collective-permute-start(f32[2,128,512]{2,1,0:T(8,128)} %get-tuple-element.103), channel_id=1, source_target_pairs={{0,2},{1,3},{2,0},{3,1},{4,6},{5,7},{6,4},{7,5},{8,10},{9,11},{10,... | collective-permute-start | bytes 1572872 | tf_op jit(solution)/shard_map/ppermute | solution.py:124
  6.1 22.6 %collective-permute-start.4 = (f32[2,128,512]{2,1,0:T(8,128)}, f32[2,128,512]{2,1,0:T(8,128)}, u32[]{:S(2)}, u32[]{:S(2)}) collective-permute-start(f32[2,128,512]{2,1,0:T(8,128)} %slice.37), channel_id=1, source_target_pairs={{0,2},{1,3},{2,0},{3,1},{4,6},{5,7},{6,4},{7,5},{8,10},{9,11},{10,... | collective-permute-start | bytes 1572872 | tf_op jit(solution)/shard_map/ppermute | solution.py:124
  6.2 4.6 %copy-start = (f32[4,128,512]{2,1,0:T(8,128)S(1)}, f32[4,128,512]{2,1,0:T(8,128)}, u32[]{:S(2)}) copy-start(f32[4,128,512]{2,1,0:T(8,128)} %refs_0_.5) | copy-start | bytes 3145732
  7.6 5.1 %collective-permute-start.9 = (f32[16,512]{1,0:T(8,128)S(1)}, f32[16,512]{1,0:T(8,128)S(1)}, u32[]{:S(2)}, u32[]{:S(2)}) collective-permute-start(f32[16,512]{1,0:T(8,128)S(1)} %slice_select_fusion), channel_id=1, source_target_pairs={{0,16},{4,20},{8,24},{12,28},{16,0},{20,4},{24,8},{28,12},{1,17},{... | collective-permute-start | bytes 98312 | tf_op jit(solution)/shard_map/ppermute | solution.py:174
  10.8 28.3 %collective-permute-start = (f32[4,128,512]{2,1,0:T(8,128)S(1)}, f32[4,128,512]{2,1,0:T(8,128)S(1)}, u32[]{:S(2)}, u32[]{:S(2)}) collective-permute-start(f32[4,128,512]{2,1,0:T(8,128)S(1)} %copy-done.1), channel_id=1, source_target_pairs={{0,1},{1,0},{2,3},{3,2},{4,5},{5,4},{6,7},{7,6},{8,9},{9,8},{10,11... | collective-permute-start | bytes 3145736 | tf_op jit(solution)/shard_map/ppermute | solution.py:124
  10.8 28.3 %collective-permute-start.6 = (f32[4,128,512]{2,1,0:T(8,128)S(1)}, f32[4,128,512]{2,1,0:T(8,128)}, u32[]{:S(2)}, u32[]{:S(2)}) collective-permute-start(f32[4,128,512]{2,1,0:T(8,128)S(1)} %copy-done), channel_id=1, source_target_pairs={{0,1},{1,0},{2,3},{3,2},{4,5},{5,4},{6,7},{7,6},{8,9},{9,8},{10,11... | collective-permute-start | bytes 3145736 | tf_op jit(solution)/shard_map/ppermute | solution.py:124
  12.7 16.0 %collective-permute-start.10 = (f32[8,512]{1,0:T(8,128)S(1)}, f32[8,512]{1,0:T(8,128)S(1)}, u32[]{:S(2)}, u32[]{:S(2)}) collective-permute-start(f32[8,512]{1,0:T(8,128)S(1)} %slice_select_fusion.1), channel_id=1, source_target_pairs={{0,8},{4,12},{8,0},{12,4},{16,24},{20,28},{24,16},{28,20},{1,9},{5... | collective-permute-start | bytes 49160 | tf_op jit(solution)/shard_map/ppermute | solution.py:174
  18.4 20.7 %collective-permute-start.7 = (f32[2,128,512]{2,1,0:T(8,128)}, f32[2,128,512]{2,1,0:T(8,128)}, u32[]{:S(2)}, u32[]{:S(2)}) collective-permute-start(f32[2,128,512]{2,1,0:T(8,128)} %collective-permute-done.1.refs_2_), channel_id=1, source_target_pairs={{0,1},{1,0},{2,3},{3,2},{4,5},{5,4},{6,7},{7,6},{8,9},{9,8},{10,11... | collective-permute-start | bytes 1572872 | tf_op jit(solution)/shard_map/ppermute | solution.py:124
  28.8 10.3 %collective-permute-start.8 = (f32[2,128,512]{2,1,0:T(8,128)}, f32[2,128,512]{2,1,0:T(8,128)}, u32[]{:S(2)}, u32[]{:S(2)}) collective-permute-start(f32[2,128,512]{2,1,0:T(8,128)} %collective-permute-done.4.refs_6_), channel_id=1, source_target_pairs={{0,1},{1,0},{2,3},{3,2},{4,5},{5,4},{6,7},{7,6},{8,9},{9,8},{10,11... | collective-permute-start | bytes 1572872 | tf_op jit(solution)/shard_map/ppermute | solution.py:124
  28.8 3.7 %collective-permute-start.11 = (f32[4,512]{1,0:T(4,128)S(1)}, f32[4,512]{1,0:T(4,128)S(1)}, u32[]{:S(2)}, u32[]{:S(2)}) collective-permute-start(f32[4,512]{1,0:T(4,128)S(1)} %slice_select_fusion.2), channel_id=1, source_target_pairs={{0,4},{4,0},{8,12},{12,8},{16,20},{20,16},{24,28},{28,24},{1,5},{5... | collective-permute-start | bytes 24584 | tf_op jit(solution)/shard_map/ppermute | solution.py:174
  32.5 1.2 collective-permute-start.12
  33.7 3.7 %collective-permute-start.13 = (f32[4,512]{1,0:T(4,128)S(1)}, f32[4,512]{1,0:T(4,128)S(1)}, u32[]{:S(2)}, u32[]{:S(2)}) collective-permute-start(f32[4,512]{1,0:T(4,128)S(1)} %add.57), channel_id=1, source_target_pairs={{0,2},{1,3},{2,0},{3,1},{4,6},{5,7},{6,4},{7,5},{8,10},{9,11},{10,... | collective-permute-start | bytes 24584 | tf_op jit(solution)/shard_map/ppermute | solution.py:124
  37.4 17.9 %collective-permute-start.2 = (f32[2,128,512]{2,1,0:T(8,128)}, f32[2,128,512]{2,1,0:T(8,128)S(1)}, u32[]{:S(2)}, u32[]{:S(2)}) collective-permute-start(f32[2,128,512]{2,1,0:T(8,128)} %get-tuple-element.53), channel_id=1, source_target_pairs={{0,2},{1,3},{2,0},{3,1},{4,6},{5,7},{6,4},{7,5},{8,10},{9,11},{10,... | collective-permute-start | bytes 1572872 | tf_op jit(solution)/shard_map/ppermute | solution.py:124
  39.1 1.6 %copy-start.2 = (f32[4,512,256]{2,1,0:T(8,128)S(1)}, f32[4,512,256]{2,1,0:T(8,128)}, u32[]{:S(2)}) copy-start(f32[4,512,256]{2,1,0:T(8,128)} %noise_ref.1) | copy-start | bytes 6291460
  40.7 16.5 %copy-start.3 = (f32[4,512,256]{2,1,0:T(8,128)S(1)}, f32[4,512,256]{2,1,0:T(8,128)}, u32[]{:S(2)}) copy-start(f32[4,512,256]{2,1,0:T(8,128)} %noise_ref.1) | copy-start | bytes 6291460
  51.2 1.3 copy-start.7
  52.6 1.3 copy-start.9
  53.9 1.4 copy-start.21
  55.3 1.9 %collective-permute-start.14 = (f32[2,128,512]{2,1,0:T(8,128)S(1)}, f32[2,128,512]{2,1,0:T(8,128)S(1)}, u32[]{:S(2)}, u32[]{:S(2)}) collective-permute-start(f32[2,128,512]{2,1,0:T(8,128)S(1)} %collective-permute-done.2.refs_2_), channel_id=1, source_target_pairs={{0,1},{1,0},{2,3},{3,2},{4,5},{5,4},{6,7},{7,6},{8,9},{9,8},{10,11... | collective-permute-start | bytes 1572872 | tf_op jit(solution)/shard_map/ppermute | solution.py:124
  55.3 8.8 %collective-permute-start.5 = (f32[1,128,512]{2,1,0:T(8,128)S(1)}, f32[1,128,512]{2,1,0:T(8,128)S(1)}, u32[]{:S(2)}, u32[]{:S(2)}) collective-permute-start(f32[1,128,512]{2,1,0:T(8,128)S(1)} %get-tuple-element.55), channel_id=1, source_target_pairs={{0,2},{1,3},{2,0},{3,1},{4,6},{5,7},{6,4},{7,5},{8,10},{9,11},{10,... | collective-permute-start | bytes 786440 | tf_op jit(solution)/shard_map/ppermute | solution.py:124
  61.8 8.4 %copy-start.11 = (bf16[2,2,512,512]{3,2,1,0:T(8,128)(2,1)}, bf16[2,2,512,512]{3,2,1,0:T(8,128)(2,1)S(1)}, u32[]{:S(2)}) copy-start(bf16[2,2,512,512]{3,2,1,0:T(8,128)(2,1)S(1)} %get-tuple-element.64.refs_6_.inverse_1) | copy-start | bytes 6291460
  61.8 8.4 %copy-start.17 = (bf16[2,512,512]{2,1,0:T(8,128)(2,1)}, bf16[2,512,512]{2,1,0:T(8,128)(2,1)S(1)}, u32[]{:S(2)}) copy-start(bf16[2,512,512]{2,1,0:T(8,128)(2,1)S(1)} %get-tuple-element.62.refs_10_.refs_0_) | copy-start | bytes 3145732
  64.1 1.5 collective-permute-start.15
  64.1 9.0 %collective-permute-start.3 = (f32[1,128,512]{2,1,0:T(8,128)S(1)}, f32[1,128,512]{2,1,0:T(8,128)S(1)}, u32[]{:S(2)}, u32[]{:S(2)}) collective-permute-start(f32[1,128,512]{2,1,0:T(8,128)S(1)} %get-tuple-element.54), channel_id=1, source_target_pairs={{0,2},{1,3},{2,0},{3,1},{4,6},{5,7},{6,4},{7,5},{8,10},{9,11},{10,... | collective-permute-start | bytes 786440 | tf_op jit(solution)/shard_map/ppermute | solution.py:124
  70.2 1.0 copy-start.5
  71.1 1.0 copy-start.14
  72.2 1.0 copy-start.19
  73.1 1.8 %collective-permute-start.16 = (f32[1,128,512]{2,1,0:T(8,128)S(1)}, f32[1,128,512]{2,1,0:T(8,128)S(1)}, u32[]{:S(2)}, u32[]{:S(2)}) collective-permute-start(f32[1,128,512]{2,1,0:T(8,128)S(1)} %collective-permute-done.3.refs_2_), channel_id=1, source_target_pairs={{0,1},{1,0},{2,3},{3,2},{4,5},{5,4},{6,7},{7,6},{8,9},{9,8},{10,11... | collective-permute-start | bytes 786440 | tf_op jit(solution)/shard_map/ppermute | solution.py:124
  73.3 8.7 %collective-permute-start.17 = (f32[512,128]{1,0:T(8,128)S(1)}, f32[512,128]{1,0:T(8,128)S(1)}, u32[]{:S(2)}, u32[]{:S(2)}) collective-permute-start(f32[512,128]{1,0:T(8,128)S(1)} %get-tuple-element.81), channel_id=1, source_target_pairs={{0,4},{4,0},{8,12},{12,8},{16,20},{20,16},{24,28},{28,24},{1,5},{5... | collective-permute-start | bytes 786440 | tf_op jit(solution)/shard_map/ppermute | solution.py:127
  74.9 1.2 copy-start.15
  76.2 19.4 %copy-start.4 = (f32[4,512,256]{2,1,0:T(8,128)S(1)}, f32[4,512,256]{2,1,0:T(8,128)}, u32[]{:S(2)}) copy-start(f32[4,512,256]{2,1,0:T(8,128)} %noise_ref.1) | copy-start | bytes 6291460
  76.2 19.4 %copy-start.8 = (bf16[2,2,512,512]{3,2,1,0:T(8,128)(2,1)S(1)}, bf16[2,2,512,512]{3,2,1,0:T(8,128)(2,1)}, u32[]{:S(2)}) copy-start(bf16[2,2,512,512]{3,2,1,0:T(8,128)(2,1)} %copy-done.7) | copy-start | bytes 6291460
  76.2 19.4 %copy-start.20 = (bf16[2,512,512]{2,1,0:T(8,128)(2,1)S(1)}, bf16[2,512,512]{2,1,0:T(8,128)(2,1)}, u32[]{:S(2)}) copy-start(bf16[2,512,512]{2,1,0:T(8,128)(2,1)} %copy-done.19) | copy-start | bytes 3145732
  82.0 13.6 %collective-permute-start.18 = (f32[256,512]{1,0:T(8,128)S(1)}, f32[256,512]{1,0:T(8,128)S(1)}, u32[]{:S(2)}, u32[]{:S(2)}) collective-permute-start(f32[256,512]{1,0:T(8,128)S(1)} %get-tuple-element.82), channel_id=1, source_target_pairs={{0,4},{4,0},{8,12},{12,8},{16,20},{20,16},{24,28},{28,24},{1,5},{5... | collective-permute-start | bytes 1572872 | tf_op jit(solution)/shard_map/ppermute | solution.py:127
  83.5 20.3 %collective-permute-start.20 = (f32[8,512]{1,0:T(8,128)S(1)}, f32[8,512]{1,0:T(8,128)S(1)}, u32[]{:S(2)}, u32[]{:S(2)}) collective-permute-start(f32[8,512]{1,0:T(8,128)S(1)} %get-tuple-element.84.flux_ref), channel_id=1, source_target_pairs={{0,4},{4,0},{8,12},{12,8},{16,20},{20,16},{24,28},{28,24},{1,5},{5... | collective-permute-start | bytes 49160 | tf_op jit(solution)/shard_map/ppermute | solution.py:127
  95.5 8.3 %collective-permute-start.19 = (f32[256,512]{1,0:T(8,128)S(1)}, f32[256,512]{1,0:T(8,128)S(1)}, u32[]{:S(2)}, u32[]{:S(2)}) collective-permute-start(f32[256,512]{1,0:T(8,128)S(1)} %collective-permute-done.18.half_ref), channel_id=1, source_target_pairs={{0,1},{1,0},{2,3},{3,2},{4,5},{5,4},{6,7},{7,6},{8,9},{9,8},{10,11... | collective-permute-start | bytes 1572872 | tf_op jit(solution)/shard_map/ppermute | solution.py:124
  95.6 1.6 %copy-start.12 = (bf16[2,2,512,512]{3,2,1,0:T(8,128)(2,1)S(1)}, bf16[2,2,512,512]{3,2,1,0:T(8,128)(2,1)}, u32[]{:S(2)}) copy-start(bf16[2,2,512,512]{3,2,1,0:T(8,128)(2,1)} %copy-done.11) | copy-start | bytes 6291460
  97.2 1.6 %copy-start.22 = (bf16[2,2,512,512]{3,2,1,0:T(8,128)(2,1)S(1)}, bf16[2,2,512,512]{3,2,1,0:T(8,128)(2,1)}, u32[]{:S(2)}) copy-start(bf16[2,2,512,512]{3,2,1,0:T(8,128)(2,1)} %copy-done.21) | copy-start | bytes 6291460
  105.1 1.7 %collective-permute-start.21 = (f32[512,128]{1,0:T(8,128)S(1)}, f32[512,128]{1,0:T(8,128)S(1)}, u32[]{:S(2)}, u32[]{:S(2)}) collective-permute-start(f32[512,128]{1,0:T(8,128)S(1)} %get-tuple-element.87.local_ref), channel_id=1, source_target_pairs={{24,16},{28,20},{25,17},{29,21},{26,18},{30,22},{27,19},{31,23}} | collective-permute-start | bytes 786440 | tf_op jit(solution)/shard_map/ppermute | solution.py:130
  107.4 8.6 %collective-permute-start.22 = (f32[512,128]{1,0:T(8,128)S(1)}, f32[512,128]{1,0:T(8,128)S(1)}, u32[]{:S(2)}, u32[]{:S(2)}) collective-permute-start(f32[512,128]{1,0:T(8,128)S(1)} %noise_link.2), channel_id=1, source_target_pairs={{16,8},{20,12},{17,9},{21,13},{18,10},{22,14},{19,11},{23,15}} | collective-permute-start | bytes 786440 | tf_op jit(solution)/shard_map/ppermute | solution.py:130
  108.1 5.5 %collective-permute-start.25 = (f32[8,512]{1,0:T(8,128)S(1)}, f32[8,512]{1,0:T(8,128)S(1)}, u32[]{:S(2)}, u32[]{:S(2)}) collective-permute-start(f32[8,512]{1,0:T(8,128)S(1)} %get-tuple-element.91.local_ref), channel_id=1, source_target_pairs={{0,8},{4,12},{1,9},{5,13},{2,10},{6,14},{3,11},{7,15}} | collective-permute-start | bytes 49160 | tf_op jit(solution)/shard_map/ppermute | solution.py:130
  114.2 0.7 collective-permute-start.26
  115.4 0.7 collective-permute-start.27
  116.1 2.2 %copy-start.6 = (f32[512,512]{1,0:T(8,128)S(1)}, f32[512,512]{1,0:T(8,128)}, u32[]{:S(2)}) copy-start(f32[512,512]{1,0:T(8,128)} %copy-done.5) | copy-start | bytes 3145732
  116.8 17.8 %collective-permute-start.23 = (f32[512,128]{1,0:T(8,128)S(1)}, f32[512,128]{1,0:T(8,128)S(1)}, u32[]{:S(2)}, u32[]{:S(2)}) collective-permute-start(f32[512,128]{1,0:T(8,128)S(1)} %noise_link.3), channel_id=1, source_target_pairs={{8,0},{12,4},{9,1},{13,5},{10,2},{14,6},{11,3},{15,7}} | collective-permute-start | bytes 786440 | tf_op jit(solution)/shard_map/ppermute | solution.py:130
  119.1 3.7 %collective-permute-start.28 = (f32[8,512]{1,0:T(8,128)S(1)}, f32[8,512]{1,0:T(8,128)S(1)}, u32[]{:S(2)}, u32[]{:S(2)}) collective-permute-start(f32[8,512]{1,0:T(8,128)S(1)} %get-tuple-element.94.own_ref), channel_id=1, source_target_pairs={{0,4},{4,0},{8,12},{12,8},{16,20},{20,16},{24,28},{28,24},{1,5},{5... | collective-permute-start | bytes 49160 | tf_op jit(solution)/shard_map/ppermute | solution.py:127
  123.1 0.7 collective-permute-start.29
  124.1 0.7 collective-permute-start.30
  124.8 12.0 %copy-start.16 = (bf16[2,512,512]{2,1,0:T(8,128)(2,1)S(1)}, bf16[2,512,512]{2,1,0:T(8,128)(2,1)}, u32[]{:S(2)}) copy-start(bf16[2,512,512]{2,1,0:T(8,128)(2,1)} %copy-done.14) | copy-start | bytes 3145732
  124.8 12.0 %copy-start.18 = (bf16[2,512,512]{2,1,0:T(8,128)(2,1)S(1)}, bf16[2,512,512]{2,1,0:T(8,128)(2,1)}, u32[]{:S(2)}) copy-start(bf16[2,512,512]{2,1,0:T(8,128)(2,1)} %copy-done.17) | copy-start | bytes 3145732
  125.1 11.6 %copy-start.10 = (bf16[2,2,512,512]{3,2,1,0:T(8,128)(2,1)S(1)}, bf16[2,2,512,512]{3,2,1,0:T(8,128)(2,1)}, u32[]{:S(2)}) copy-start(bf16[2,2,512,512]{3,2,1,0:T(8,128)(2,1)} %copy-done.9) | copy-start | bytes 6291460
  125.1 11.6 %copy-start.13 = (bf16[2,2,512,512]{3,2,1,0:T(8,128)(2,1)S(1)}, bf16[2,2,512,512]{3,2,1,0:T(8,128)(2,1)}, u32[]{:S(2)}) copy-start(bf16[2,2,512,512]{3,2,1,0:T(8,128)(2,1)} %copy-done.11) | copy-start | bytes 6291460
  125.2 24.7 %collective-permute-start.31 = (f32[8,512]{1,0:T(8,128)S(1)}, f32[8,512]{1,0:T(8,128)S(1)}, u32[]{:S(2)}, u32[]{:S(2)}) collective-permute-start(f32[8,512]{1,0:T(8,128)S(1)} %backward_link.3), channel_id=1, source_target_pairs={{8,0},{12,4},{9,1},{13,5},{10,2},{14,6},{11,3},{15,7}} | collective-permute-start | bytes 49160 | tf_op jit(solution)/shard_map/ppermute | solution.py:130
  135.2 14.7 %collective-permute-start.24 = (f32[512,128]{1,0:T(8,128)S(1)}, f32[512,128]{1,0:T(8,128)S(1)}, u32[]{:S(2)}, u32[]{:S(2)}) collective-permute-start(f32[512,128]{1,0:T(8,128)S(1)} %get-tuple-element.89), channel_id=1, source_target_pairs={{0,4},{4,0},{8,12},{12,8},{16,20},{20,16},{24,28},{28,24},{1,5},{5... | collective-permute-start | bytes 786440 | tf_op jit(solution)/shard_map/ppermute | solution.py:127

commit v3 on v0

v3 whole, which is shorter than its diff:
```python
import functools

import jax
import jax.numpy as jnp
from jax import lax
from jax.experimental import pallas as pl
from jax.experimental.pallas import tpu as pltpu
from jax.sharding import PartitionSpec as P

F32 = jnp.float32
BF16 = jnp.bfloat16
CORES = 2
PAIR = 2
LINES = 8

NN = ((1,), (0,))
TN = ((0,), (0,))
NT = ((1,), (1,))


def split(value):
    high = value.astype(BF16)
    return high, (value - high.astype(F32)).astype(BF16)


def parts(ref):
    return ref[0], ref[1]


def dot_parts(left, right, dims):
    product = functools.partial(
        lax.dot_general, dimension_numbers=(dims, ((), ())), preferred_element_type=F32
    )
    return product(left[0], right[0]) + (product(left[0], right[1]) + product(left[1], right[0]))


def shape(*dims, dtype=F32):
    return jax.ShapeDtypeStruct(dims, dtype)


def in_vmem(value):
    return pltpu.with_memory_space_constraint(value, pltpu.VMEM)


def call(body, outs, name, scalars, arrays, work=1, scratch=(), out_specs=None):
    vmem = pl.BlockSpec(memory_space=pltpu.VMEM)
    out_shape = outs if out_specs else jax.tree.map(lambda o: pltpu.VMEM(o.shape, o.dtype), outs)
    return pl.pallas_call(
        body,
        out_shape=out_shape,
        in_specs=[pl.BlockSpec(memory_space=pltpu.SMEM)] * len(scalars) + [vmem] * len(arrays),
        out_specs=out_specs or jax.tree.map(lambda _: vmem, outs),
        scratch_shapes=list(scratch),
        compiler_params=pltpu.CompilerParams(vmem_limit_bytes=12 * 1024 * 1024),
        cost_estimate=pl.CostEstimate(
            flops=int(work * 2.0e8), transcendentals=0, bytes_accessed=1024
        ),
        name=name,
    )(*scalars, *map(in_vmem, arrays))


def deal(where_ref, distance, total, keep_out, sent_out):
    count = total.shape[0] // 2
    upper = (where_ref[1] & distance) != 0
    keep_out[...] = jnp.where(upper, total[count:], total[:count])
    sent_out[...] = jnp.where(upper, total[:count], total[count:])


def halved(where, distance, keep, got):
    def body(where_ref, keep_ref, got_ref, *outs):
        total = keep_ref[...] + got_ref[...]
        if distance:
            deal(where_ref, distance, total, *outs)
        else:
            outs[0][...] = total

    days, nodes = keep.shape
    outs = [shape(days // 2, nodes)] * 2 if distance else [keep]
    outs = [shape(*out.shape) for out in outs]
    return (*call(body, outs, "halved", (where,), [keep, got], work=0.05), None)[:2]


def bin_observations(where, obs_day, obs_node, obs_value, days, nodes, distance):
    chunk = min(512, obs_day.shape[0])
    chunks = obs_day.shape[0] // chunk

    def body(where_ref, day_ref, node_ref, value_ref, keep_out, sent_out):
        total = jnp.zeros((3 * days, nodes), F32)
        for index in range(chunks):
            row = pl.ds(index, 1)
            value = value_ref[row, :]
            high = value.astype(BF16).astype(F32)
            middle = (value - high).astype(BF16).astype(F32)
            low = value - high - middle
            is_day = lax.broadcasted_iota(jnp.int32, (days, chunk), 0) == day_ref[row, :]
            marked = jnp.concatenate(
                [jnp.where(is_day, part, 0.0).astype(BF16) for part in (high, middle, low)], axis=0
            )
            is_node = lax.broadcasted_iota(jnp.int32, (nodes, chunk), 0) == node_ref[row, :]
            total += lax.dot_general(
                marked, is_node.astype(F32).astype(BF16), (NT, ((), ())), preferred_element_type=F32
            )
        total = total[:days] + (total[days : 2 * days] + total[2 * days :])
        deal(where_ref, distance, total, keep_out, sent_out)

    return call(
        body,
        [shape(days // 2, nodes)] * 2,
        "bin_observations",
        (where,),
        [value.reshape(chunks, chunk) for value in (obs_day, obs_node, obs_value)],
        work=2,
    )


def gather_rows(where_ref, refs, take, out_ref):
    share = refs[0].shape[-2]
    for offset, ref in enumerate(refs):
        at = pl.ds(pl.multiple_of((where_ref[0] ^ offset) * share, share), share)
        if len(ref.shape) == 3:
            ref = ref.at[take(offset) if callable(take) else take]
        out_ref[0, at, :], out_ref[1, at, :] = split(ref[...])


def local(inv_diag, coupling, noise, obs_day, obs_node, obs_value):
    part_count = lax.axis_size("tm")
    row_count = lax.axis_size("row")
    my_part = lax.axis_index("tm")
    my_row = lax.axis_index("row")
    day_count, share, nodes = inv_diag.shape
    columns = noise.shape[2]
    half = columns // PAIR
    half_nodes = nodes // CORES
    groups = part_count // PAIR
    early = day_count // 2
    late = day_count - early

    def to_row(value, distance):
        return lax.ppermute(value, "row", [(i, i ^ distance) for i in range(row_count)])

    def to_pair(value):
        return lax.ppermute(value, "tm", [(i, i ^ 1) for i in range(part_count)])

    def to_group(value, source, target):
        return lax.ppermute(
            value, "tm", [(PAIR * source + i, PAIR * target + i) for i in range(PAIR)]
        )

    def after(value, *others):
        return lax.optimization_barrier((value, *others))[0]

    where = jnp.stack([my_row, my_part]).astype(jnp.int32)

    line = shape(LINES, nodes)
    square = shape(nodes, nodes)
    map_parts = shape(2, nodes, nodes, dtype=BF16)
    samples_half = shape(half, nodes)
    samples_full = shape(columns, nodes)

    keep, sent = bin_observations(
        where, obs_day, obs_node, obs_value, part_count * day_count, nodes, part_count // 2
    )

    arrived = []

    def send_rows(rows):
        arrived.append([to_row(rows, distance) for distance in range(CORES, row_count, CORES)])

    for day in range(early):
        blocks = (inv_diag[day], coupling[day])
        if day:
            blocks = tuple(after(block, stacked) for block in blocks)
        stacked = jnp.stack(blocks)
        send_rows(stacked)
    late_rows = [inv_diag[early:], *(coupling[day : day + 1] for day in range(early, day_count))]
    where = after(where, keep, stacked, *late_rows)
    for index, rows in enumerate(late_rows):
        send_rows(after(rows, *arrived[index]))

    def shared(index, *ahead):
        pieces = []
        for got in arrived[index]:
            pieces += [got, to_row(after(got, *ahead) if ahead else got, 1)]
        return pieces

    own_inverse = [inv_diag, to_row(inv_diag, 1)]
    own_link = [coupling, to_row(coupling, 1)]

    def taking(start, day):
        return lambda offset: day if offset < CORES else day - start

    reduced = []
    distance = part_count // 2
    while distance:
        got = lax.ppermute(sent, "tm", [(i, i ^ distance) for i in range(part_count)])
        distance //= 2
        keep, sent = halved(where, distance, keep, got)
        reduced.append(keep)
    right_side = keep
    distance = 1
    while distance < row_count:
        right_side = right_side + to_row(right_side, distance)
        distance *= 2
    right_side = jnp.broadcast_to(right_side[:, None, :], (day_count, LINES, nodes))

    def store(out_ref, pair):
        out_ref[0], out_ref[1] = pair

    def early_body(day, where_ref, *refs):
        inverse_refs, link_refs = list(refs[:CORES]), list(refs[CORES : 2 * CORES])
        got_refs, refs = refs[2 * CORES : CORES + row_count], refs[CORES + row_count :]
        state_refs, refs = refs[: 3 if day else 0], refs[3 if day else 0 :]
        noise_ref, path_out, gram_out, sum_out, inverse_out, link_out, moved_out = refs[:7]
        map_out, term_out = refs[7:]
        gather_rows(
            where_ref, inverse_refs + [ref.at[0] for ref in got_refs], day, inverse_out
        )
        gather_rows(where_ref, link_refs + [ref.at[1] for ref in got_refs], day, link_out)
        inverse, link = parts(inverse_out), parts(link_out)
        given = split(noise_ref[day])
        term = dot_parts(given, inverse, TN)
        step = split(-dot_parts(link, inverse, NN))
        if day == 0:
            moved, path, total, gram = inverse, step, term, 0.0
        else:
            moved = split(dot_parts(inverse, parts(state_refs[0]), NN))
            path = split(-dot_parts(link, moved, NN))
            total = state_refs[1][...] + dot_parts(given, moved, TN)
            gram = state_refs[2][...]
        store(path_out, path)
        store(moved_out, moved)
        store(map_out, step)
        sum_out[...] = total
        gram_out[...] = gram + dot_parts(moved, moved, TN)
        term_out[...] = term

    state = []
    inverses, links, moveds, step_maps, local_terms = [], [], [], [], []
    for day in range(early):
        ahead = (right_side, *state[:1]) if day else (where, reduced[len(reduced) // 2])
        path, gram, summed, inverse, link, moved, step, term = call(
            functools.partial(early_body, day),
            (
                map_parts, square, samples_full, map_parts, map_parts, map_parts, map_parts,
                samples_full,
            ),
            f"day_{day}",
            (where,),
            [
                *own_inverse, *own_link,
                *(piece for piece in shared(day, *ahead)), *state, noise,
            ],
            work=5,
        )
        state = [path, summed, gram]
        for kept, value in zip(
            (inverses, links, moveds, step_maps, local_terms),
            (inverse, link, moved, step, term),
            strict=True,
        ):
            kept.append(value)

    def early_lines_body(source_ref, *refs):
        applied_out, back_out, current_out = refs[-3:]
        applied = back = None
        for day in range(early):
            inverse_ref, link_ref, moved_ref = refs[3 * day : 3 * day + 3]
            wanted = source_ref[day] if day == 0 else source_ref[day] - applied
            current = dot_parts(split(wanted), parts(inverse_ref), NT)
            current_out[day] = current
            applied = dot_parts(split(current), parts(link_ref), NT)
            term = dot_parts(split(current), parts(moved_ref), NN)
            back = term if day == 0 else back + term
        applied_out[...] = applied
        back_out[...] = back

    applied, back, early_currents = call(
        early_lines_body,
        (line, line, shape(early, LINES, nodes)),
        "early_lines",
        (),
        [
            right_side,
            *(ref for day in range(early) for ref in (inverses[day], links[day], moveds[day])),
        ],
        work=2,
    )

    def late_body(where_ref, *refs):
        inverse_refs, refs = refs[:row_count], refs[row_count:]
        noise_ref, source_ref, path_ref, sum_ref, gram_ref, applied_ref, back_ref = refs[:7]
        gram_out, sum_out, back_out, moved_out, current_out = refs[7:12]
        inverse_outs, term_outs = refs[12 : 12 + late], refs[12 + late :]
        for index in range(late):
            gather_rows(
                where_ref, inverse_refs, taking(early, early + index), inverse_outs[index]
            )
        inverse = parts(inverse_outs[0])
        moved = split(dot_parts(inverse, parts(path_ref), NN))
        store(moved_out, moved)
        current = dot_parts(split(source_ref[early] - applied_ref[...]), inverse, NT)
        current_out[...] = current
        for index in range(late):
            given = split(noise_ref[early + index])
            term_outs[index][...] = dot_parts(given, parts(inverse_outs[index]), TN)
            if index == 0:
                sum_out[...] = sum_ref[...] + dot_parts(given, moved, TN)
        gram_out[...] = gram_ref[...] + dot_parts(moved, moved, TN)
        back_out[...] = back_ref[...] + dot_parts(split(current), moved, NN)

    results = call(
        late_body,
        (square, samples_full, line, map_parts, line, *[map_parts] * late, *[samples_full] * late),
        "late_inverses",
        (where,),
        [*own_inverse, *shared(early, path), noise, right_side, *state, applied, back],
        work=4,
    )
    gram, summed, back, moved, current = results[:5]
    inverses += results[5 : 5 + late]
    local_terms += results[5 + late :]
    moveds.append(moved)
    late_currents = [current]

    def next_body(day, where_ref, *refs):
        link_refs, refs = refs[:row_count], refs[row_count:]
        noise_ref, source_ref, inverse_ref, gram_ref, sum_ref, back_ref, moved_ref, current_ref = (
            refs[:8]
        )
        gram_out, back_out, link_out, moved_out, current_out, *sum_outs = refs[8:]
        gather_rows(where_ref, link_refs, taking(day, day), link_out)
        link, inverse = parts(link_out), parts(inverse_ref)
        path = split(-dot_parts(link, parts(moved_ref), NN))
        moved = split(dot_parts(inverse, path, NN))
        store(moved_out, moved)
        total = sum_ref[...] + dot_parts(split(noise_ref[day + 1]), moved, TN)
        if len(sum_outs) == 1:
            sum_outs[0][...] = total
        else:
            first = (where_ref[1] & (PAIR - 1)) == 0
            sum_outs[0][...] = jnp.where(first, total[:half], total[half:])
            sum_outs[1][...] = jnp.where(first, total[half:], total[:half])
        applied = dot_parts(split(current_ref[...]), link, NT)
        current = dot_parts(split(source_ref[day + 1] - applied), inverse, NT)
        current_out[...] = current
        gram_out[...] = gram_ref[...] + dot_parts(moved, moved, TN)
        back_out[...] = back_ref[...] + dot_parts(split(current), moved, NN)

    for day in range(early, day_count - 1):
        sums = [samples_half] * 2 if day == day_count - 2 else [samples_full]
        gram, back, link, moved, current, *sums = call(
            functools.partial(next_body, day),
            (square, line, map_parts, map_parts, line, *sums),
            f"day_{day}",
            (where,),
            [
                *own_link, *shared(day + 1, moved), noise, right_side, inverses[day + 1], gram,
                summed, back, moved, current,
            ],
            work=4,
        )
        summed = sums[0]
        moveds.append(moved)
        late_currents.append(current)
        links.append(link)
    keep, send = sums
    other_sum = to_pair(send)

    def last_link_body(where_ref, *refs):
        link_refs, refs = refs[:row_count], refs[row_count:]
        moved_ref, current_ref, path_out, half_out, flux_out, link_out, whole = refs
        gather_rows(where_ref, link_refs, taking(day_count - 1, day_count - 1), link_out)
        link = parts(link_out)
        whole[...] = -dot_parts(link, parts(moved_ref), NN)
        half_out[...] = whole[
            pl.ds(pl.multiple_of((where_ref[0] & (CORES - 1)) * half_nodes, half_nodes), half_nodes), :
        ]
        store(path_out, split(whole[...]))
        flux_out[...] = dot_parts(split(current_ref[...]), link, NT)

    path, path_half, flux, link = call(
        last_link_body,
        (map_parts, shape(half_nodes, nodes), line, map_parts),
        "last_link",
        (where,),
        [*own_link, *shared(day_count, moved, send), moved, current],
        work=1.5,
        scratch=[pltpu.VMEM((nodes, nodes), F32)],
    )
    links.append(link)

    def late_maps_body(*refs):
        for index in range(late):
            store(
                refs[2 * late + index],
                split(-dot_parts(parts(refs[late + index]), parts(refs[index]), NN)),
            )

    step_maps += call(
        late_maps_body, [map_parts] * late, "late_maps", (), [*inverses[early:], *links[early:]],
        work=late,
    )
    other_half = to_pair(after(path_half, other_sum, *step_maps[early:]))
    other_flux = to_pair(flux)
    other_rest = to_row(other_half, 1)

    def pair_body(
        where_ref, path_ref, half_ref, rest_ref, sum_ref, other_ref, flux_ref,
        other_flux_ref, low_out, high_out, sum_out, high_sum_out, flux_out, low_flux_out, maps,
    ):
        me = where_ref[1] & (PAIR - 1)
        mate = 1 - me
        mine = (where_ref[0] & (CORES - 1))
        maps[me] = path_ref[...]
        for which, ref in ((mine, half_ref), (1 - mine, rest_ref)):
            at = pl.ds(pl.multiple_of(which * half_nodes, half_nodes), half_nodes)
            maps[mate, 0, at, :], maps[mate, 1, at, :] = split(ref[...])
        first = me == 0
        low_sum = jnp.where(first, sum_ref[...], other_ref[...])
        high_sum = jnp.where(first, other_ref[...], sum_ref[...])
        low_flux = jnp.where(first, flux_ref[...], other_flux_ref[...])
        high_flux = jnp.where(first, other_flux_ref[...], flux_ref[...])
        low_out[...] = maps[0]
        high_out[...] = maps[1]
        sum_out[...] = dot_parts(split(high_sum), parts(low_out), NN) + low_sum
        high_sum_out[...] = high_sum
        flux_out[...] = dot_parts(split(low_flux), parts(high_out), NT) + high_flux
        low_flux_out[...] = low_flux

    low_map, high_map, pair_sum, high_sum, pair_flux, low_flux = call(
        pair_body,
        (map_parts, map_parts, samples_half, samples_half, line, line),
        "pair_maps",
        (where,),
        [path, other_half, other_rest, keep, other_sum, flux, other_flux],
        work=1.5,
        scratch=[pltpu.VMEM((PAIR, 2, nodes, nodes), BF16)],
    )

    def group_map_body(low_ref, high_ref, out_ref):
        store(out_ref, split(dot_parts(parts(high_ref), parts(low_ref), NN)))

    group_map = call(
        group_map_body, map_parts, "group_map", (), [low_map, after(high_map, pair_sum)]
    )

    def link_body(dims, map_ref, local_ref, *refs):
        got = refs[0][...]
        for ref in refs[1:-1]:
            got = got + ref[...]
        refs[-1][...] = dot_parts(split(got), parts(map_ref), dims) + local_ref[...]

    def linked(dims, value_map, value, got, name):
        return call(
            functools.partial(link_body, dims), shape(*value.shape), name, (),
            [value_map, value, *got], work=0.6,
        )

    def turn_body(where_ref, low_ref, flux_ref, gram_ref, back_ref, *refs):
        own_out, back_out = refs[-2:]
        given = refs[0][...]
        for ref in refs[1:-2]:
            given = given + ref[...]
        behind = dot_parts(split(given), parts(low_ref), NT) + flux_ref[...]
        given = jnp.where((where_ref[1] & (PAIR - 1)) == 0, given, behind)
        own_out[...] = given
        back_out[...] = back_ref[...] - dot_parts(split(given), split(gram_ref[...]), NN)

    def pair_back_body(where_ref, map_ref, own_ref, other_ref, pair_out, high_out):
        first = (where_ref[1] & (PAIR - 1)) == 0
        low = jnp.where(first, own_ref[...], other_ref[...])
        high = jnp.where(first, other_ref[...], own_ref[...])
        pair_out[...] = dot_parts(split(high), parts(map_ref), NN) + low
        high_out[...] = high

    mean = {}

    def mean_hops():
        value, got = pair_flux, []
        ahead = yield
        for group in range(groups - 1):
            got.append(to_group(after(value, *ahead), group, group + 1))
            if group < groups - 2:
                value = linked(NT, group_map, pair_flux, got, "forward_link")
            ahead = yield (value if group < groups - 2 else got[-1])
        mean["entering"], own_back = call(
            turn_body, (line, line), "mean_turn", (where,),
            [low_map, low_flux, gram, back, *got],
        )
        other_back = to_pair(after(own_back, *ahead))
        value, mean["high_back"] = call(
            pair_back_body, (line, line), "pair_back", (where,), [low_map, own_back, other_back],
            work=0.6,
        )
        pair_back, got = value, []
        ahead = yield value
        for group in range(groups - 1, 0, -1):
            got.append(to_group(after(value, *ahead), group, group - 1))
            if group > 1:
                value = linked(NN, group_map, pair_back, got, "backward_link")
            mean["leaving"] = got
            ahead = yield (value if group > 1 else got[-1])

    hops = mean_hops()
    next(hops)

    leaving = []
    value = pair_sum
    for group in range(groups - 1, 0, -1):
        got = to_group(value, group, group - 1)
        hops.send((value,))
        brought = hops.send(())
        leaving.append(after(got, brought))
        if group > 1:
            value = linked(NN, group_map, pair_sum, leaving, "noise_link")

    def divide_body(where_ref, map_ref, sum_ref, *refs):
        keep_out, send_out = refs[-2:]
        given = refs[0][...]
        for ref in refs[1:-2]:
            given = given + ref[...]
        between = dot_parts(split(given), parts(map_ref), NN) + sum_ref[...]
        first = (where_ref[1] & (PAIR - 1)) == 0
        keep_out[...] = jnp.where(first, between, given)
        send_out[...] = jnp.where(first, given, between)

    kept_half, sent_half = call(
        divide_body, (samples_half, samples_half), "divide", (where,),
        [high_map, high_sum, *leaving],
    )
    got_half = to_pair(sent_half)
    hops.send((sent_half,))

    def terms_body(entering_ref, early_ref, *refs):
        outs = refs[-day_count:]
        given = split(entering_ref[...])
        for day in range(day_count):
            local_ref, inverse_ref, moved_ref = refs[3 * day : 3 * day + 3]
            current = early_ref[day] if day < early else refs[3 * day_count + day - early][...]
            current = current - dot_parts(given, parts(moved_ref), NT)
            term = dot_parts(split(current), parts(inverse_ref), NN)
            outs[day][...] = local_ref[...] + term[:1]

    terms = call(
        terms_body, [samples_full] * day_count, "mean_terms", (),
        [
            after(mean["entering"], sent_half), early_currents,
            *(
                value for day in range(day_count)
                for value in (local_terms[day], inverses[day], moveds[day])
            ),
            *late_currents,
        ],
        work=4,
    )

    def last_body(where_ref, keep_ref, got_ref, back_ref, high_ref, *refs):
        got_means, refs = refs[: groups - 1], refs[groups - 1 :]
        map_refs, term_refs = refs[:day_count], refs[day_count : 2 * day_count]
        out_ref, held, sems = refs[2 * day_count :]
        first = (where_ref[1] & (PAIR - 1)) == 0
        given = got_means[0][...]
        for ref in got_means[1:]:
            given = given + ref[...]
        between = dot_parts(split(given), parts(high_ref), NN) + back_ref[...]
        given = jnp.where(first, between, given)
        low = jnp.where(first, keep_ref[...], got_ref[...])
        high = jnp.where(first, got_ref[...], keep_ref[...])
        following = jnp.concatenate([low, high], axis=0) + given[:1]
        copies = []
        for day in reversed(range(day_count)):
            following = dot_parts(split(following), parts(map_refs[day]), NN) + term_refs[day][...]
            held[day] = following.T
            copies.append(pltpu.make_async_copy(held.at[day], out_ref.at[day], sems.at[day]))
            copies[-1].start()
        for copy in copies:
            copy.wait()

    return call(
        last_body, shape(day_count, nodes, columns), "last_days", (where,),
        [
            kept_half, got_half, mean["high_back"], high_map, *mean["leaving"], *step_maps,
            *terms,
        ],
        work=4,
        scratch=[
            pltpu.VMEM((day_count, nodes, columns), F32), pltpu.SemaphoreType.DMA((day_count,)),
        ],
        out_specs=pl.BlockSpec(memory_space=pl.ANY),
    )


def solution(mesh):
    return jax.shard_map(
        local,
        mesh=mesh,
        in_specs=(
            P("tm", "row", None),
            P("tm", "row", None),
            P("tm", None, "row"),
            P(("tm", "row")),
            P(("tm", "row")),
            P(("tm", "row")),
        ),
        out_specs=P("tm", None, "row"),
        check_vma=False,
    )
```

time: 521 us -> 144 us (0.28); the launches traced: 511 us -> 144 us
  waiting for transfers between devices: 262 us -> 55.7 us
  matrix products: 153 us -> 0 us
  Pallas kernels: 0 us -> 48.6 us
  other arithmetic: 30.1 us -> 1.9 us
  between operations: 15.7 us -> 0.52 us
  starting transfers between devices: 41.8 us -> 32.8 us
  blocking collectives: 6.15 us -> 0 us
    unnamed x5 -> x0, waiting for transfers between devices: 157 us -> none
    dot_general x60 -> x0, matrix products: 153 us -> none  [the longest x37 82.2 us: matmul(): jnp.dot(left_side, right_side, precision=highest, preferred_element_type=...]
    ppermute x14 -> x32, waiting for transfers between devices: 105 us -> 55.7 us  [the longest x5 19 us: to_pair(): return lax.ppermute(value, 'tm', [(i, i ^ 1) for i in range(part_count)])]
    pallas_call x0 -> x24, Pallas kernels: none -> 48.6 us  [call(): pl.pallas_call(body, out_shape=out_shape, in_specs=[pl.BlockSpec(memory_s...]
    unnamed x6 -> x0, other arithmetic: 23.7 us -> none
    ppermute x14 -> x32, starting transfers between devices: 41.5 us -> 32.8 us  [the longest x9 10.3 us: to_group(): lax.ppermute(value, 'tm', [(PAIR * source + i, PAIR * target + i) for i i...]
    all_gather x1 -> x0, blocking collectives: 6.15 us -> none  [local(): lax.all_gather(own_sources, 'row', axis=1, tiled=True)]
  transfers between devices with their start and end apart: 18 -> 32, of which waited for: 15 -> 16; matrix products, arithmetic and copies ran while one was open for 19% -> 2% of each run, Pallas kernels for 0% -> 29%
where the time goes in v3:
time: 144 us
  waiting for transfers between devices  55.7 us (39%)
  Pallas kernels  48.6 us (34%)
  starting transfers between devices  32.8 us (23%)
  local copies, waits for them, and re-layouts  4.37 us (3%)
  other arithmetic  1.9 us (1%)
    pallas_call x24, Pallas kernels, call(): pl.pallas_call(body, out_shape=out_shape, in_specs=[pl.BlockSpec(memory_s...  48.6 us
    ppermute x5, waiting for transfers between devices, to_pair(): return lax.ppermute(value, 'tm', [(i, i ^ 1) for i in range(part_count)])  19 us
    ppermute x15, waiting for transfers between devices, to_row(): lax.ppermute(value, 'row', [(i, i ^ distance) for i in range(row_count)])  16.5 us
    ppermute x9, waiting for transfers between devices, to_group(): lax.ppermute(value, 'tm', [(PAIR * source + i, PAIR * target + i) for i i...  15.1 us
    ppermute x9, starting transfers between devices, to_group(): lax.ppermute(value, 'tm', [(PAIR * source + i, PAIR * target + i) for i i...  10.3 us
    ppermute x15, starting transfers between devices, to_row(): lax.ppermute(value, 'row', [(i, i ^ distance) for i in range(row_count)])  9.4 us
    ppermute x5, starting transfers between devices, to_pair(): return lax.ppermute(value, 'tm', [(i, i ^ 1) for i in range(part_count)])  7.65 us
    ppermute x3, starting transfers between devices, local(): lax.ppermute(sent, 'tm', [(i, i ^ distance) for i in range(part_count)])  5.45 us
  transfers between devices with their start and end apart: 32, of which 16 were waited for; matrix products, arithmetic and copies ran while one was open for 2% of the time, Pallas kernels for 29%

profile of v3, /device:TPU:0, one launch (start us, length us, event | category | flops | bytes accessed | tf_op | source)
XLA Modules:
  0.0 143.9 jit_solution(9931573680368199890)
XLA Ops:
  0.0 1.2 slice_bitcast_fusion.1
  1.2 2.1 %fusion = (f32[1,128,512]{2,1,0:T(8,128)}, f32[1,128,512]{2,1,0:T(8,128)}, f32[128,512]{1,0:T(8,128)}, f32[1,128,512]{2,1,0:T(8,128)S(1)}) fusion(f32[4,128,512]{2,1,0:T(8,128)} %refs_0_.9), kind=kLoop, calls=%fused_computation.5 | loop fusion | bytes 2097152 | tf_op jit(solution)/shard_map/slice | solution.py:175
  3.3 0.8 pad_maximum_fusion
  4.1 3.0 %collective-permute-start.1 = (f32[2,128,512]{2,1,0:T(8,128)}, f32[2,128,512]{2,1,0:T(8,128)}, u32[]{:S(2)}, u32[]{:S(2)}) collective-permute-start(f32[2,128,512]{2,1,0:T(8,128)} %pad_maximum_fusion), channel_id=1, source_target_pairs={{0,2},{1,3},{2,0},{3,1},{4,6},{5,7},{6,4},{7,5},{8,10},{9,11},{10,... | collective-permute-start | bytes 1572872 | tf_op jit(solution)/shard_map/ppermute | solution.py:139
  7.1 0.5 collective-permute-start
  7.7 1.9 %bin_observations.1 = (f32[16,512]{1,0:T(8,128)S(1)}, f32[16,512]{1,0:T(8,128)S(1)}) custom-call(s32[2]{0:T(128)S(1)} %pad_add_fusion.where_ref, s32[8,512]{1,0:T(8,128)S(1)} %reshape.10.day_ref, s32[8,512]{1,0:T(8,128)S(1)} %reshape.11.node_ref, f32[8,512]{1,0:T(8,128)S(1)} %reshape.12.value_ref), custom_call_target="tpu_custom_call" | custom-call | flops 400000000 | bytes 1024 | tf_op jit(solution)/shard_map/bin_observations/pallas_call | solution.py:48
  9.6 2.6 %collective-permute-start.7 = (f32[16,512]{1,0:T(8,128)S(1)}, f32[16,512]{1,0:T(8,128)S(1)}, u32[]{:S(2)}, u32[]{:S(2)}) collective-permute-start(f32[16,512]{1,0:T(8,128)S(1)} %get-tuple-element.96), channel_id=1, source_target_pairs={{0,16},{4,20},{8,24},{12,28},{16,0},{20,4},{24,8},{28,12},{1,17},{... | collective-permute-start | bytes 98312 | tf_op jit(solution)/shard_map/ppermute | solution.py:195
  12.2 1.0 pad_maximum_fusion.1
  13.2 1.1 slice.25
  14.3 0.5 collective-permute-done.7.got_ref
  14.8 0.5 halved.3
  15.4 1.3 collective-permute-start.8
  16.7 2.5 %collective-permute-done.8.got_ref = f32[8,512]{1,0:T(8,128)S(1)} collective-permute-done((f32[8,512]{1,0:T(8,128)S(1)}, f32[8,512]{1,0:T(8,128)S(1)}, u32[]{:S(2)}, u32[]{:S(2)}) %collective-permute-start.8) | collective-permute-done | bytes 16416 | tf_op jit(solution)/shard_map/ppermute | solution.py:195
  19.2 0.5 halved.4
  19.8 1.2 collective-permute-start.4
  21.0 1.5 %collective-permute-start.9 = (f32[4,512]{1,0:T(4,128)S(1)}, f32[4,512]{1,0:T(4,128)S(1)}, u32[]{:S(2)}, u32[]{:S(2)}) collective-permute-start(f32[4,512]{1,0:T(4,128)S(1)} %get-tuple-element.100), channel_id=1, source_target_pairs={{0,4},{4,0},{8,12},{12,8},{16,20},{20,16},{24,28},{28,24},{1,5},{5... | collective-permute-start | bytes 24584 | tf_op jit(solution)/shard_map/ppermute | solution.py:195
  22.5 2.1 %collective-permute-done.9.got_ref = f32[4,512]{1,0:T(4,128)S(1)} collective-permute-done((f32[4,512]{1,0:T(4,128)S(1)}, f32[4,512]{1,0:T(4,128)S(1)}, u32[]{:S(2)}, u32[]{:S(2)}) %collective-permute-start.9) | collective-permute-done | bytes 8224 | tf_op jit(solution)/shard_map/ppermute | solution.py:195
  24.7 0.5 halved.5
  25.3 1.2 collective-permute-done.10
  26.5 0.9 collective-permute-start.11
  27.4 7.0 %collective-permute-done.11 = f32[4,512]{1,0:T(4,128)S(1)} collective-permute-done((f32[4,512]{1,0:T(4,128)S(1)}, f32[4,512]{1,0:T(4,128)S(1)}, u32[]{:S(2)}, u32[]{:S(2)}) %collective-permute-start.11) | collective-permute-done | bytes 8224 | tf_op jit(solution)/shard_map/ppermute | solution.py:139
  34.4 4.7 %day_0.1 = (bf16[2,512,512]{2,1,0:T(8,128)(2,1)S(1)}, f32[512,512]{1,0:T(8,128)S(1)}, f32[256,512]{1,0:T(8,128)S(1)}, bf16[2,512,512]{2,1,0:T(8,128)(2,1)S(1)}, ...) custom-call(s32[2]{0:T(128)S(1)} %pad_add_fusion.where_ref, ...), custom_call_target="tpu_custom_call" | custom-call | flops 1000000000 | bytes 1024 | tf_op jit(solution)/shard_map/day_0/pallas_call | solution.py:48
  39.2 1.3 collective-permute-start.2
  40.5 0.6 collective-permute-done.13.refs_5_
  41.1 6.7 %day_1.1 = (bf16[2,512,512]{2,1,0:T(8,128)(2,1)S(1)}, f32[512,512]{1,0:T(8,128)S(1)}, f32[256,512]{1,0:T(8,128)S(1)}, bf16[2,512,512]{2,1,0:T(8,128)(2,1)S(1)}, ...) custom-call(s32[2]{0:T(128)S(1)} %pad_add_fusion.where_ref, ...), custom_call_target="tpu_custom_call" | custom-call | flops 1000000000 | bytes 1024 | tf_op jit(solution)/shard_map/day_1/pallas_call | solution.py:48
  47.8 5.7 %collective-permute-done.2.refs_2_ = f32[2,128,512]{2,1,0:T(8,128)S(1)} collective-permute-done((f32[2,128,512]{2,1,0:T(8,128)S(1)}, f32[2,128,512]{2,1,0:T(8,128)S(1)}, u32[]{:S(2)}, u32[]{:S(2)}) %collective-permute-start.2) | collective-permute-done | bytes 524320 | tf_op jit(solution)/shard_map/ppermute | solution.py:139
  53.5 1.2 collective-permute-start.5
  54.8 2.2 %early_lines.1 = (f32[8,512]{1,0:T(8,128)S(1)}, f32[8,512]{1,0:T(8,128)S(1)}, f32[2,8,512]{2,1,0:T(8,128)S(1)}) custom-call(f32[4,8,512]{2,1,0:T(8,128)S(1)} %broadcast_in_dim.2.source_ref.refs_5_, bf16[2,512,512]{2,1,0:T(8,128)(2,1)S(1)} %get-tuple-element.110.refs_0_.refs_1_, bf16[2,512,512]{2,1,0:T(8,128)(2,1)S(1)} %get-tuple-element.111.refs_1_, ...), custom_call_target="tpu_custom_call" | custom-call | flops 400000000 | bytes 1024 | tf_op jit(solution)/shard_map/early_lines/pallas_call | solution.py:48
  57.0 5.7 %late_inverses.1 = (f32[512,512]{1,0:T(8,128)S(1)}, f32[256,512]{1,0:T(8,128)S(1)}, f32[8,512]{1,0:T(8,128)S(1)}, bf16[2,512,512]{2,1,0:T(8,128)(2,1)S(1)}, f32[...) custom-call(s32[2]{0:T(128)S(1)} %pad_add_fusion.where_ref, ...), custom_call_target="tpu_custom_call" | custom-call | flops 800000000 | bytes 1024 | tf_op jit(solution)/shard_map/late_inverses/pallas_call | solution.py:48
  63.0 0.9 collective-permute-start.3
  63.8 0.4 collective-permute-done.15.refs_3_
  64.3 5.7 %day_2.1 = (f32[512,512]{1,0:T(8,128)S(1)}, f32[8,512]{1,0:T(8,128)S(1)}, bf16[2,512,512]{2,1,0:T(8,128)(2,1)S(1)}, bf16[2,512,512]{2,1,0:T(8,128)(2,1)S(1)}, f3...) custom-call(s32[2]{0:T(128)S(1)} %pad_add_fusion.where_ref, f32[4,128,512]{2,1,0:T(8,128)S(1)} %copy-done.1, ...), custom_call_target="tpu_custom_call" | custom-call | flops 800000000 | bytes 1024 | tf_op jit(solution)/shard_map/day_2/pallas_call | solution.py:48
  70.0 1.5 %collective-permute-done.3.refs_2_ = f32[1,128,512]{2,1,0:T(8,128)S(1)} collective-permute-done((f32[1,128,512]{2,1,0:T(8,128)S(1)}, f32[1,128,512]{2,1,0:T(8,128)S(1)}, u32[]{:S(2)}, u32[]{:S(2)}) %collective-permute-start.3) | collective-permute-done | bytes 262176 | tf_op jit(solution)/shard_map/ppermute | solution.py:139
  71.5 1.5 %collective-permute-start.17 = (f32[128,512]{1,0:T(8,128)S(1)}, f32[128,512]{1,0:T(8,128)S(1)}, u32[]{:S(2)}, u32[]{:S(2)}) collective-permute-start(f32[128,512]{1,0:T(8,128)S(1)} %get-tuple-element.126), channel_id=1, source_target_pairs={{0,4},{4,0},{8,12},{12,8},{16,20},{20,16},{24,28},{28,24},{1,5},{5... | collective-permute-start | bytes 786440 | tf_op jit(solution)/shard_map/ppermute | solution.py:142
  73.0 2.8 %last_link.1 = (bf16[2,512,512]{2,1,0:T(8,128)(2,1)S(1)}, f32[256,512]{1,0:T(8,128)S(1)}, f32[8,512]{1,0:T(8,128)S(1)}, bf16[2,512,512]{2,1,0:T(8,128)(2,1)S(1)}) custom-call(s32[2]{0:T(128)S(1)} %pad_add_fusion.where_ref, f32[4,128,512]{2,1,0:T(8,128)S(1)} %copy-done.1, f32[4,128,512]{2,1,0:T(8,128)} %collective-permute-done.refs_3_.refs_1_, ...), custom_call_target="tpu_custom_call" | custom-call | flops 300000000 | bytes 1024 | tf_op jit(solution)/shard_map/last_link/pallas_call | solution.py:48
  75.8 1.8 %late_maps.1 = (bf16[2,512,512]{2,1,0:T(8,128)(2,1)S(1)}, bf16[2,512,512]{2,1,0:T(8,128)(2,1)S(1)}) custom-call(bf16[2,512,512]{2,1,0:T(8,128)(2,1)S(1)} %get-tuple-element.131.refs_0_.refs_7_, bf16[2,512,512]{2,1,0:T(8,128)(2,1)S(1)} %get-tuple-element.120.refs_6_.refs_1_.refs_10_, bf16[2,512,512]{2,1,0:T(8,128)(2,1)S(1)} %get-tuple-element.132.refs_2_, ...), custom_call_target="tpu_custom_call" | custom-call | flops 400000000 | bytes 1024 | tf_op jit(solution)/shard_map/late_maps/pallas_call | solution.py:48
  77.7 2.5 %collective-permute-done.17.other_ref = f32[128,512]{1,0:T(8,128)S(1)} collective-permute-done((f32[128,512]{1,0:T(8,128)S(1)}, f32[128,512]{1,0:T(8,128)S(1)}, u32[]{:S(2)}, u32[]{:S(2)}) %collective-permute-start.17) | collective-permute-done | bytes 262176 | tf_op jit(solution)/shard_map/ppermute | solution.py:142
  80.2 1.5 %collective-permute-start.18 = (f32[256,512]{1,0:T(8,128)S(1)}, f32[256,512]{1,0:T(8,128)S(1)}, u32[]{:S(2)}, u32[]{:S(2)}) collective-permute-start(f32[256,512]{1,0:T(8,128)S(1)} %get-tuple-element.136), channel_id=1, source_target_pairs={{0,4},{4,0},{8,12},{12,8},{16,20},{20,16},{24,28},{28,24},{1,5},{5... | collective-permute-start | bytes 1572872 | tf_op jit(solution)/shard_map/ppermute | solution.py:142
  81.7 12.0 %collective-permute-done.18.half_ref = f32[256,512]{1,0:T(8,128)S(1)} collective-permute-done((f32[256,512]{1,0:T(8,128)S(1)}, f32[256,512]{1,0:T(8,128)S(1)}, u32[]{:S(2)}, u32[]{:S(2)}) %collective-permute-start.18) | collective-permute-done | bytes 524320 | tf_op jit(solution)/shard_map/ppermute | solution.py:142
  93.7 1.5 %collective-permute-start.20 = (f32[8,512]{1,0:T(8,128)S(1)}, f32[8,512]{1,0:T(8,128)S(1)}, u32[]{:S(2)}, u32[]{:S(2)}) collective-permute-start(f32[8,512]{1,0:T(8,128)S(1)} %get-tuple-element.138.flux_ref), channel_id=1, source_target_pairs={{0,4},{4,0},{8,12},{12,8},{16,20},{20,16},{24,28},{28,24},{1,5},{5... | collective-permute-start | bytes 49160 | tf_op jit(solution)/shard_map/ppermute | solution.py:142
  95.3 2.2 %collective-permute-done.20.other_flux_ref = f32[8,512]{1,0:T(8,128)S(1)} collective-permute-done((f32[8,512]{1,0:T(8,128)S(1)}, f32[8,512]{1,0:T(8,128)S(1)}, u32[]{:S(2)}, u32[]{:S(2)}) %collective-permute-start.20) | collective-permute-done | bytes 16416 | tf_op jit(solution)/shard_map/ppermute | solution.py:142
  97.5 1.8 %pair_maps.1 = (bf16[2,512,512]{2,1,0:T(8,128)(2,1)S(1)}, bf16[2,512,512]{2,1,0:T(8,128)(2,1)S(1)}, f32[128,512]{1,0:T(8,128)S(1)}, f32[128,512]{1,0:T(8,128)S(1...) custom-call(s32[2]{0:T(128)S(1)} %pad_add_fusion.where_ref, bf16[2,512,512]{2,1,0:T(8,128)(2,1)S(1)} %get-tuple-element.129.path_ref, ...), custom_call_target="tpu_custom_call" | custom-call | flops 300000000 | bytes 1024 | tf_op jit(solution)/shard_map/pair_maps/pallas_call | solution.py:48
  99.2 0.7 collective-permute-start.21
  99.9 3.5 %collective-permute-start.22 = (f32[8,512]{1,0:T(8,128)S(1)}, f32[8,512]{1,0:T(8,128)S(1)}, u32[]{:S(2)}, u32[]{:S(2)}) collective-permute-start(f32[8,512]{1,0:T(8,128)S(1)} %get-tuple-element.145.local_ref), channel_id=1, source_target_pairs={{0,8},{4,12},{1,9},{5,13},{2,10},{6,14},{3,11},{7,15}} | collective-permute-start | bytes 49160 | tf_op jit(solution)/shard_map/ppermute | solution.py:145
  103.4 1.0 group_map.1.map_ref
  104.8 0.5 forward_link.2
  105.3 0.7 collective-permute-start.23
  106.0 0.5 forward_link.3
  106.9 0.7 collective-permute-start.24
  107.6 0.7 collective-permute-start.25
  108.3 1.3 mean_turn.1
  109.7 1.5 %collective-permute-start.26 = (f32[8,512]{1,0:T(8,128)S(1)}, f32[8,512]{1,0:T(8,128)S(1)}, u32[]{:S(2)}, u32[]{:S(2)}) collective-permute-start(f32[8,512]{1,0:T(8,128)S(1)} %get-tuple-element.151.own_ref), channel_id=1, source_target_pairs={{0,4},{4,0},{8,12},{12,8},{16,20},{20,16},{24,28},{28,24},{1,5},{5... | collective-permute-start | bytes 49160 | tf_op jit(solution)/shard_map/ppermute | solution.py:142
  111.2 2.2 %collective-permute-done.26.other_ref = f32[8,512]{1,0:T(8,128)S(1)} collective-permute-done((f32[8,512]{1,0:T(8,128)S(1)}, f32[8,512]{1,0:T(8,128)S(1)}, u32[]{:S(2)}, u32[]{:S(2)}) %collective-permute-start.26) | collective-permute-done | bytes 16416 | tf_op jit(solution)/shard_map/ppermute | solution.py:142
  113.4 0.9 pair_back.1
  114.7 1.3 collective-permute-start.27
  116.0 0.7 collective-permute-start.28
  117.0 0.7 collective-permute-start.29
  118.0 7.6 %collective-permute-done.27.refs_2_ = f32[128,512]{1,0:T(8,128)S(1)} collective-permute-done((f32[128,512]{1,0:T(8,128)S(1)}, f32[128,512]{1,0:T(8,128)S(1)}, u32[]{:S(2)}, u32[]{:S(2)}) %collective-permute-start.27) | collective-permute-done | bytes 262176 | tf_op jit(solution)/shard_map/ppermute | solution.py:145
  125.6 0.9 divide.1
  126.5 1.6 %collective-permute-start.30 = (f32[128,512]{1,0:T(8,128)S(1)}, f32[128,512]{1,0:T(8,128)S(1)}, u32[]{:S(2)}, u32[]{:S(2)}) collective-permute-start(f32[128,512]{1,0:T(8,128)S(1)} %get-tuple-element.157), channel_id=1, source_target_pairs={{0,4},{4,0},{8,12},{12,8},{16,20},{20,16},{24,28},{28,24},{1,5},{5... | collective-permute-start | bytes 786440 | tf_op jit(solution)/shard_map/ppermute | solution.py:142
  128.1 1.5 %collective-permute-start.31 = (f32[8,512]{1,0:T(8,128)S(1)}, f32[8,512]{1,0:T(8,128)S(1)}, u32[]{:S(2)}, u32[]{:S(2)}) collective-permute-start(f32[8,512]{1,0:T(8,128)S(1)} %backward_link.3), channel_id=1, source_target_pairs={{8,0},{12,4},{9,1},{13,5},{10,2},{14,6},{11,3},{15,7}} | collective-permute-start | bytes 49160 | tf_op jit(solution)/shard_map/ppermute | solution.py:145
  129.6 3.1 %mean_terms.1 = (f32[256,512]{1,0:T(8,128)S(1)}, f32[256,512]{1,0:T(8,128)S(1)}, f32[256,512]{1,0:T(8,128)S(1)}, f32[256,512]{1,0:T(8,128)S(1)}) custom-call(f32[8,512]{1,0:T(8,128)S(1)} %get-tuple-element.163.entering_ref, f32[2,8,512]{2,1,0:T(8,128)S(1)} %get-tuple-element.164.early_ref, f32[256,512]{1,0:T(8,128)S(1)} %get-tuple-element.165.refs_0_, ...), custom_call_target="tpu_custom_call" | custom-call | flops 800000000 | bytes 1024 | tf_op jit(solution)/shard_map/mean_terms/pallas_call | solution.py:48
  132.7 7.1 %collective-permute-done.31.refs_2_ = f32[8,512]{1,0:T(8,128)S(1)} collective-permute-done((f32[8,512]{1,0:T(8,128)S(1)}, f32[8,512]{1,0:T(8,128)S(1)}, u32[]{:S(2)}, u32[]{:S(2)}) %collective-permute-start.31) | collective-permute-done | bytes 16416 | tf_op jit(solution)/shard_map/ppermute | solution.py:145
  139.8 3.9 %last_days.1 = f32[4,512,256]{2,1,0:T(8,128)} custom-call(s32[2]{0:T(128)S(1)} %pad_add_fusion.where_ref, f32[128,512]{1,0:T(8,128)S(1)} %get-tuple-element.156.keep_ref, f32[128,512]{1,0:T(8,128)S(1)} %collective-permute-done.30.got_ref, f32[8,512]{1,0:T(8,128)S(1)} %get-tuple-element.158.back_ref, ...), custom_call_target="tpu_custom_call" | custom-call | flops 800000000 | bytes 1024 | tf_op jit(solution)/shard_map/last_days/pallas_call | solution.py:48
  (50 shorter events, 2.6 us)
Async XLA Ops:
  0.0 7.0 %copy-start.1 = (f32[4,128,512]{2,1,0:T(8,128)S(1)}, f32[4,128,512]{2,1,0:T(8,128)}, u32[]{:S(2)}) copy-start(f32[4,128,512]{2,1,0:T(8,128)} %refs_0_.9) | copy-start | bytes 3145732
  0.0 7.6 %copy-start.4 = (s32[4096]{0:T(1024)S(1)}, s32[4096]{0:T(1024)}, u32[]{:S(2)}) copy-start(s32[4096]{0:T(1024)} %param.9) | copy-start | bytes 49156
  0.0 7.6 %copy-start.5 = (s32[4096]{0:T(1024)S(1)}, s32[4096]{0:T(1024)}, u32[]{:S(2)}) copy-start(s32[4096]{0:T(1024)} %param.10) | copy-start | bytes 49156
  0.0 7.6 %copy-start.6 = (f32[4096]{0:T(1024)S(1)}, f32[4096]{0:T(1024)}, u32[]{:S(2)}) copy-start(f32[4096]{0:T(1024)} %param.11) | copy-start | bytes 49156
  4.1 30.3 %copy-start = (f32[4,512,256]{2,1,0:T(8,128)S(1)}, f32[4,512,256]{2,1,0:T(8,128)}, u32[]{:S(2)}) copy-start(f32[4,512,256]{2,1,0:T(8,128)} %refs_4_.3) | copy-start | bytes 6291460
  4.1 15.6 %collective-permute-start.1 = (f32[2,128,512]{2,1,0:T(8,128)}, f32[2,128,512]{2,1,0:T(8,128)}, u32[]{:S(2)}, u32[]{:S(2)}) collective-permute-start(f32[2,128,512]{2,1,0:T(8,128)} %pad_maximum_fusion), channel_id=1, source_target_pairs={{0,2},{1,3},{2,0},{3,1},{4,6},{5,7},{6,4},{7,5},{8,10},{9,11},{10,... | collective-permute-start | bytes 1572872 | tf_op jit(solution)/shard_map/ppermute | solution.py:139
  7.0 27.3 %collective-permute-start.6 = (f32[4,128,512]{2,1,0:T(8,128)}, f32[4,128,512]{2,1,0:T(8,128)}, u32[]{:S(2)}, u32[]{:S(2)}) collective-permute-start(f32[4,128,512]{2,1,0:T(8,128)} %refs_0_.7), channel_id=1, source_target_pairs={{0,1},{1,0},{2,3},{3,2},{4,5},{5,4},{6,7},{7,6},{8,9},{9,8},{10,11... | collective-permute-start | bytes 3145736 | tf_op jit(solution)/shard_map/ppermute | solution.py:139
  7.1 27.3 %collective-permute-start = (f32[4,128,512]{2,1,0:T(8,128)S(1)}, f32[4,128,512]{2,1,0:T(8,128)}, u32[]{:S(2)}, u32[]{:S(2)}) collective-permute-start(f32[4,128,512]{2,1,0:T(8,128)S(1)} %copy-done.1), channel_id=1, source_target_pairs={{0,1},{1,0},{2,3},{3,2},{4,5},{5,4},{6,7},{7,6},{8,9},{9,8},{10,11... | collective-permute-start | bytes 3145736 | tf_op jit(solution)/shard_map/ppermute | solution.py:139
  9.6 5.2 %collective-permute-start.7 = (f32[16,512]{1,0:T(8,128)S(1)}, f32[16,512]{1,0:T(8,128)S(1)}, u32[]{:S(2)}, u32[]{:S(2)}) collective-permute-start(f32[16,512]{1,0:T(8,128)S(1)} %get-tuple-element.96), channel_id=1, source_target_pairs={{0,16},{4,20},{8,24},{12,28},{16,0},{20,4},{24,8},{28,12},{1,17},{... | collective-permute-start | bytes 98312 | tf_op jit(solution)/shard_map/ppermute | solution.py:195
  15.4 3.8 %collective-permute-start.8 = (f32[8,512]{1,0:T(8,128)S(1)}, f32[8,512]{1,0:T(8,128)S(1)}, u32[]{:S(2)}, u32[]{:S(2)}) collective-permute-start(f32[8,512]{1,0:T(8,128)S(1)} %get-tuple-element.98), channel_id=1, source_target_pairs={{0,8},{4,12},{8,0},{12,4},{16,24},{20,28},{24,16},{28,20},{1,9},{5... | collective-permute-start | bytes 49160 | tf_op jit(solution)/shard_map/ppermute | solution.py:195
  19.7 14.6 %collective-permute-start.12 = (f32[2,128,512]{2,1,0:T(8,128)}, f32[2,128,512]{2,1,0:T(8,128)S(1)}, u32[]{:S(2)}, u32[]{:S(2)}) collective-permute-start(f32[2,128,512]{2,1,0:T(8,128)} %collective-permute-done.1.refs_4_), channel_id=1, source_target_pairs={{0,1},{1,0},{2,3},{3,2},{4,5},{5,4},{6,7},{7,6},{8,9},{9,8},{10,11... | collective-permute-start | bytes 1572872 | tf_op jit(solution)/shard_map/ppermute | solution.py:139
  19.8 19.3 %collective-permute-start.4 = (f32[2,128,512]{2,1,0:T(8,128)S(1)}, f32[2,128,512]{2,1,0:T(8,128)S(1)}, u32[]{:S(2)}, u32[]{:S(2)}) collective-permute-start(f32[2,128,512]{2,1,0:T(8,128)S(1)} %pad_maximum_fusion.1), channel_id=1, source_target_pairs={{0,2},{1,3},{2,0},{3,1},{4,6},{5,7},{6,4},{7,5},{8,10},{9,11},{10,... | collective-permute-start | bytes 1572872 | tf_op jit(solution)/shard_map/ppermute | solution.py:139
  21.0 3.7 %collective-permute-start.9 = (f32[4,512]{1,0:T(4,128)S(1)}, f32[4,512]{1,0:T(4,128)S(1)}, u32[]{:S(2)}, u32[]{:S(2)}) collective-permute-start(f32[4,512]{1,0:T(4,128)S(1)} %get-tuple-element.100), channel_id=1, source_target_pairs={{0,4},{4,0},{8,12},{12,8},{16,20},{20,16},{24,28},{28,24},{1,5},{5... | collective-permute-start | bytes 24584 | tf_op jit(solution)/shard_map/ppermute | solution.py:195
  25.2 1.2 collective-permute-start.10
  26.5 7.9 %collective-permute-start.11 = (f32[4,512]{1,0:T(4,128)S(1)}, f32[4,512]{1,0:T(4,128)S(1)}, u32[]{:S(2)}, u32[]{:S(2)}) collective-permute-start(f32[4,512]{1,0:T(4,128)S(1)} %add.6), channel_id=1, source_target_pairs={{0,2},{1,3},{2,0},{3,1},{4,6},{5,7},{6,4},{7,5},{8,10},{9,11},{10,... | collective-permute-start | bytes 24584 | tf_op jit(solution)/shard_map/ppermute | solution.py:139
  39.1 2.0 %collective-permute-start.13 = (f32[2,128,512]{2,1,0:T(8,128)S(1)}, f32[2,128,512]{2,1,0:T(8,128)S(1)}, u32[]{:S(2)}, u32[]{:S(2)}) collective-permute-start(f32[2,128,512]{2,1,0:T(8,128)S(1)} %collective-permute-done.4.refs_4_), channel_id=1, source_target_pairs={{0,1},{1,0},{2,3},{3,2},{4,5},{5,4},{6,7},{7,6},{8,9},{9,8},{10,11... | collective-permute-start | bytes 1572872 | tf_op jit(solution)/shard_map/ppermute | solution.py:139
  39.2 14.3 %collective-permute-start.2 = (f32[2,128,512]{2,1,0:T(8,128)S(1)}, f32[2,128,512]{2,1,0:T(8,128)S(1)}, u32[]{:S(2)}, u32[]{:S(2)}) collective-permute-start(f32[2,128,512]{2,1,0:T(8,128)S(1)} %slice.25), channel_id=1, source_target_pairs={{0,2},{1,3},{2,0},{3,1},{4,6},{5,7},{6,4},{7,5},{8,10},{9,11},{10,... | collective-permute-start | bytes 1572872 | tf_op jit(solution)/shard_map/ppermute | solution.py:139
  41.1 12.4 %copy-start.3 = (f32[1,128,512]{2,1,0:T(8,128)S(1)}, f32[1,128,512]{2,1,0:T(8,128)}, u32[]{:S(2)}) copy-start(f32[1,128,512]{2,1,0:T(8,128)} %get-tuple-element.95) | copy-start | bytes 786436
  53.5 3.5 %collective-permute-start.14 = (f32[2,128,512]{2,1,0:T(8,128)S(1)}, f32[2,128,512]{2,1,0:T(8,128)S(1)}, u32[]{:S(2)}, u32[]{:S(2)}) collective-permute-start(f32[2,128,512]{2,1,0:T(8,128)S(1)} %collective-permute-done.2.refs_2_), channel_id=1, source_target_pairs={{0,1},{1,0},{2,3},{3,2},{4,5},{5,4},{6,7},{7,6},{8,9},{9,8},{10,11... | collective-permute-start | bytes 1572872 | tf_op jit(solution)/shard_map/ppermute | solution.py:139
  53.5 9.1 %collective-permute-start.5 = (f32[1,128,512]{2,1,0:T(8,128)S(1)}, f32[1,128,512]{2,1,0:T(8,128)S(1)}, u32[]{:S(2)}, u32[]{:S(2)}) collective-permute-start(f32[1,128,512]{2,1,0:T(8,128)S(1)} %copy-done.3), channel_id=1, source_target_pairs={{0,2},{1,3},{2,0},{3,1},{4,6},{5,7},{6,4},{7,5},{8,10},{9,11},{10,... | collective-permute-start | bytes 786440 | tf_op jit(solution)/shard_map/ppermute | solution.py:139
  57.0 6.0 %copy-start.2 = (f32[1,128,512]{2,1,0:T(8,128)S(1)}, f32[1,128,512]{2,1,0:T(8,128)}, u32[]{:S(2)}) copy-start(f32[1,128,512]{2,1,0:T(8,128)} %get-tuple-element.94) | copy-start | bytes 786436
  62.7 1.6 %collective-permute-start.15 = (f32[1,128,512]{2,1,0:T(8,128)S(1)}, f32[1,128,512]{2,1,0:T(8,128)S(1)}, u32[]{:S(2)}, u32[]{:S(2)}) collective-permute-start(f32[1,128,512]{2,1,0:T(8,128)S(1)} %collective-permute-done.5.refs_2_), channel_id=1, source_target_pairs={{0,1},{1,0},{2,3},{3,2},{4,5},{5,4},{6,7},{7,6},{8,9},{9,8},{10,11... | collective-permute-start | bytes 786440 | tf_op jit(solution)/shard_map/ppermute | solution.py:139
  63.0 8.5 %collective-permute-start.3 = (f32[1,128,512]{2,1,0:T(8,128)S(1)}, f32[1,128,512]{2,1,0:T(8,128)S(1)}, u32[]{:S(2)}, u32[]{:S(2)}) collective-permute-start(f32[1,128,512]{2,1,0:T(8,128)S(1)} %copy-done.2), channel_id=1, source_target_pairs={{0,2},{1,3},{2,0},{3,1},{4,6},{5,7},{6,4},{7,5},{8,10},{9,11},{10,... | collective-permute-start | bytes 786440 | tf_op jit(solution)/shard_map/ppermute | solution.py:139
  71.5 1.5 %collective-permute-start.16 = (f32[1,128,512]{2,1,0:T(8,128)S(1)}, f32[1,128,512]{2,1,0:T(8,128)S(1)}, u32[]{:S(2)}, u32[]{:S(2)}) collective-permute-start(f32[1,128,512]{2,1,0:T(8,128)S(1)} %collective-permute-done.3.refs_2_), channel_id=1, source_target_pairs={{0,1},{1,0},{2,3},{3,2},{4,5},{5,4},{6,7},{7,6},{8,9},{9,8},{10,11... | collective-permute-start | bytes 786440 | tf_op jit(solution)/shard_map/ppermute | solution.py:139
  71.5 8.7 %collective-permute-start.17 = (f32[128,512]{1,0:T(8,128)S(1)}, f32[128,512]{1,0:T(8,128)S(1)}, u32[]{:S(2)}, u32[]{:S(2)}) collective-permute-start(f32[128,512]{1,0:T(8,128)S(1)} %get-tuple-element.126), channel_id=1, source_target_pairs={{0,4},{4,0},{8,12},{12,8},{16,20},{20,16},{24,28},{28,24},{1,5},{5... | collective-permute-start | bytes 786440 | tf_op jit(solution)/shard_map/ppermute | solution.py:142
  80.2 13.6 %collective-permute-start.18 = (f32[256,512]{1,0:T(8,128)S(1)}, f32[256,512]{1,0:T(8,128)S(1)}, u32[]{:S(2)}, u32[]{:S(2)}) collective-permute-start(f32[256,512]{1,0:T(8,128)S(1)} %get-tuple-element.136), channel_id=1, source_target_pairs={{0,4},{4,0},{8,12},{12,8},{16,20},{20,16},{24,28},{28,24},{1,5},{5... | collective-permute-start | bytes 1572872 | tf_op jit(solution)/shard_map/ppermute | solution.py:142
  93.7 3.7 %collective-permute-start.19 = (f32[256,512]{1,0:T(8,128)S(1)}, f32[256,512]{1,0:T(8,128)S(1)}, u32[]{:S(2)}, u32[]{:S(2)}) collective-permute-start(f32[256,512]{1,0:T(8,128)S(1)} %collective-permute-done.18.half_ref), channel_id=1, source_target_pairs={{0,1},{1,0},{2,3},{3,2},{4,5},{5,4},{6,7},{7,6},{8,9},{9,8},{10,11... | collective-permute-start | bytes 1572872 | tf_op jit(solution)/shard_map/ppermute | solution.py:139
  93.7 3.7 %collective-permute-start.20 = (f32[8,512]{1,0:T(8,128)S(1)}, f32[8,512]{1,0:T(8,128)S(1)}, u32[]{:S(2)}, u32[]{:S(2)}) collective-permute-start(f32[8,512]{1,0:T(8,128)S(1)} %get-tuple-element.138.flux_ref), channel_id=1, source_target_pairs={{0,4},{4,0},{8,12},{12,8},{16,20},{20,16},{24,28},{28,24},{1,5},{5... | collective-permute-start | bytes 49160 | tf_op jit(solution)/shard_map/ppermute | solution.py:142
  99.2 7.3 %collective-permute-start.21 = (f32[128,512]{1,0:T(8,128)S(1)}, f32[128,512]{1,0:T(8,128)S(1)}, u32[]{:S(2)}, u32[]{:S(2)}) collective-permute-start(f32[128,512]{1,0:T(8,128)S(1)} %get-tuple-element.141.local_ref), channel_id=1, source_target_pairs={{24,16},{28,20},{25,17},{29,21},{26,18},{30,22},{27,19},{31,23}} | collective-permute-start | bytes 786440 | tf_op jit(solution)/shard_map/ppermute | solution.py:145
  99.9 4.9 %collective-permute-start.22 = (f32[8,512]{1,0:T(8,128)S(1)}, f32[8,512]{1,0:T(8,128)S(1)}, u32[]{:S(2)}, u32[]{:S(2)}) collective-permute-start(f32[8,512]{1,0:T(8,128)S(1)} %get-tuple-element.145.local_ref), channel_id=1, source_target_pairs={{0,8},{4,12},{1,9},{5,13},{2,10},{6,14},{3,11},{7,15}} | collective-permute-start | bytes 49160 | tf_op jit(solution)/shard_map/ppermute | solution.py:145
  105.3 0.7 collective-permute-start.23
  106.9 7.3 %collective-permute-start.24 = (f32[128,512]{1,0:T(8,128)S(1)}, f32[128,512]{1,0:T(8,128)S(1)}, u32[]{:S(2)}, u32[]{:S(2)}) collective-permute-start(f32[128,512]{1,0:T(8,128)S(1)} %noise_link.2), channel_id=1, source_target_pairs={{16,8},{20,12},{17,9},{21,13},{18,10},{22,14},{19,11},{23,15}} | collective-permute-start | bytes 786440 | tf_op jit(solution)/shard_map/ppermute | solution.py:145
  107.6 0.7 collective-permute-start.25
  109.7 3.7 %collective-permute-start.26 = (f32[8,512]{1,0:T(8,128)S(1)}, f32[8,512]{1,0:T(8,128)S(1)}, u32[]{:S(2)}, u32[]{:S(2)}) collective-permute-start(f32[8,512]{1,0:T(8,128)S(1)} %get-tuple-element.151.own_ref), channel_id=1, source_target_pairs={{0,4},{4,0},{8,12},{12,8},{16,20},{20,16},{24,28},{28,24},{1,5},{5... | collective-permute-start | bytes 49160 | tf_op jit(solution)/shard_map/ppermute | solution.py:142
  114.7 10.9 %collective-permute-start.27 = (f32[128,512]{1,0:T(8,128)S(1)}, f32[128,512]{1,0:T(8,128)S(1)}, u32[]{:S(2)}, u32[]{:S(2)}) collective-permute-start(f32[128,512]{1,0:T(8,128)S(1)} %noise_link.3), channel_id=1, source_target_pairs={{8,0},{12,4},{9,1},{13,5},{10,2},{14,6},{11,3},{15,7}} | collective-permute-start | bytes 786440 | tf_op jit(solution)/shard_map/ppermute | solution.py:145
  116.0 0.7 collective-permute-start.28
  117.0 0.7 collective-permute-start.29
  126.5 13.3 %collective-permute-start.30 = (f32[128,512]{1,0:T(8,128)S(1)}, f32[128,512]{1,0:T(8,128)S(1)}, u32[]{:S(2)}, u32[]{:S(2)}) collective-permute-start(f32[128,512]{1,0:T(8,128)S(1)} %get-tuple-element.157), channel_id=1, source_target_pairs={{0,4},{4,0},{8,12},{12,8},{16,20},{20,16},{24,28},{28,24},{1,5},{5... | collective-permute-start | bytes 786440 | tf_op jit(solution)/shard_map/ppermute | solution.py:142
  128.1 11.7 %collective-permute-start.31 = (f32[8,512]{1,0:T(8,128)S(1)}, f32[8,512]{1,0:T(8,128)S(1)}, u32[]{:S(2)}, u32[]{:S(2)}) collective-permute-start(f32[8,512]{1,0:T(8,128)S(1)} %backward_link.3), channel_id=1, source_target_pairs={{8,0},{12,4},{9,1},{13,5},{10,2},{14,6},{11,3},{15,7}} | collective-permute-start | bytes 49160 | tf_op jit(solution)/shard_map/ppermute | solution.py:145

commit v4 on v3

v4 whole, which is shorter than its diff:
```python
import functools

import jax
import jax.numpy as jnp
from jax import lax
from jax.experimental import pallas as pl
from jax.experimental.pallas import tpu as pltpu
from jax.sharding import PartitionSpec as P

F32 = jnp.float32
BF16 = jnp.bfloat16
CORES = 2
PAIR = 2
LINES = 8

NN = ((1,), (0,))
TN = ((0,), (0,))
NT = ((1,), (1,))


def split(value):
    high = value.astype(BF16)
    return high, (value - high.astype(F32)).astype(BF16)


def parts(ref):
    return ref[0], ref[1]


def dot_parts(left, right, dims):
    product = functools.partial(
        lax.dot_general, dimension_numbers=(dims, ((), ())), preferred_element_type=F32
    )
    return product(left[0], right[0]) + (product(left[0], right[1]) + product(left[1], right[0]))


def shape(*dims, dtype=F32):
    return jax.ShapeDtypeStruct(dims, dtype)


def in_vmem(value):
    return pltpu.with_memory_space_constraint(value, pltpu.VMEM)


def call(body, outs, name, scalars, arrays, work=1, scratch=(), out_specs=None):
    vmem = pl.BlockSpec(memory_space=pltpu.VMEM)
    out_shape = outs if out_specs else jax.tree.map(lambda o: pltpu.VMEM(o.shape, o.dtype), outs)
    return pl.pallas_call(
        body,
        out_shape=out_shape,
        in_specs=[vmem] * (len(scalars) + len(arrays)),
        out_specs=out_specs or jax.tree.map(lambda _: vmem, outs),
        scratch_shapes=list(scratch),
        compiler_params=pltpu.CompilerParams(vmem_limit_bytes=12 * 1024 * 1024),
        cost_estimate=pl.CostEstimate(
            flops=int(work * 2.0e8), transcendentals=0, bytes_accessed=1024
        ),
        name=name,
    )(*map(in_vmem, (*scalars, *arrays)))


def deal(where_ref, distance, total, keep_out, sent_out):
    count = total.shape[0] // 2
    upper = (where_ref[1, 0] & distance) != 0
    keep_out[...] = jnp.where(upper, total[count:], total[:count])
    sent_out[...] = jnp.where(upper, total[:count], total[count:])


def halved(where, distance, keep, got):
    def body(where_ref, keep_ref, got_ref, *outs):
        total = keep_ref[...] + got_ref[...]
        if distance:
            deal(where_ref, distance, total, *outs)
        else:
            outs[0][...] = total

    days, nodes = keep.shape
    outs = [shape(days // 2, nodes)] * 2 if distance else [keep]
    outs = [shape(*out.shape) for out in outs]
    return (*call(body, outs, "halved", (where,), [keep, got], work=0.05), None)[:2]


def bin_observations(where, obs_day, obs_node, obs_value, days, nodes, distance):
    chunk = min(512, obs_day.shape[0])
    chunks = obs_day.shape[0] // chunk

    def body(where_ref, day_ref, node_ref, value_ref, keep_out, sent_out):
        total = jnp.zeros((3 * days, nodes), F32)
        for index in range(chunks):
            row = pl.ds(index, 1)
            value = value_ref[row, :]
            high = value.astype(BF16).astype(F32)
            middle = (value - high).astype(BF16).astype(F32)
            low = value - high - middle
            is_day = lax.broadcasted_iota(jnp.int32, (days, chunk), 0) == day_ref[row, :]
            marked = jnp.concatenate(
                [jnp.where(is_day, part, 0.0).astype(BF16) for part in (high, middle, low)], axis=0
            )
            is_node = lax.broadcasted_iota(jnp.int32, (nodes, chunk), 0) == node_ref[row, :]
            total += lax.dot_general(
                marked, is_node.astype(F32).astype(BF16), (NT, ((), ())), preferred_element_type=F32
            )
        total = total[:days] + (total[days : 2 * days] + total[2 * days :])
        deal(where_ref, distance, total, keep_out, sent_out)

    return call(
        body,
        [shape(days // 2, nodes)] * 2,
        "bin_observations",
        (where,),
        [value.reshape(chunks, chunk) for value in (obs_day, obs_node, obs_value)],
        work=2,
    )


def gather_rows(where_ref, refs, take, out_ref):
    share = refs[0].shape[-2]
    for offset, ref in enumerate(refs):
        at = pl.ds(pl.multiple_of((where_ref[0, 0] ^ offset) * share, share), share)
        if len(ref.shape) == 3:
            ref = ref.at[take(offset) if callable(take) else take]
        out_ref[0, at, :], out_ref[1, at, :] = split(ref[...])


def local(inv_diag, coupling, noise, obs_day, obs_node, obs_value):
    part_count = lax.axis_size("tm")
    row_count = lax.axis_size("row")
    my_part = lax.axis_index("tm")
    my_row = lax.axis_index("row")
    day_count, share, nodes = inv_diag.shape
    columns = noise.shape[2]
    half = columns // PAIR
    half_nodes = nodes // CORES
    groups = part_count // PAIR
    chips = row_count // CORES
    early = day_count // 2
    late = day_count - early

    def to_row(value, distance):
        return lax.ppermute(value, "row", [(i, i ^ distance) for i in range(row_count)])

    def to_pair(value):
        return lax.ppermute(value, "tm", [(i, i ^ 1) for i in range(part_count)])

    def to_group(value, source, target):
        return lax.ppermute(
            value, "tm", [(PAIR * source + i, PAIR * target + i) for i in range(PAIR)]
        )

    def after(value, *others):
        return lax.optimization_barrier((value, *others))[0]

    where = jnp.broadcast_to(jnp.stack([my_row, my_part]).astype(jnp.int32)[:, None], (2, 128))

    line = shape(LINES, nodes)
    square = shape(nodes, nodes)
    map_parts = shape(2, nodes, nodes, dtype=BF16)
    samples_half = shape(half, nodes)
    samples_full = shape(columns, nodes)

    keep, sent = bin_observations(
        where, obs_day, obs_node, obs_value, part_count * day_count, nodes, part_count // 2
    )

    def over_chips(rows):
        return [to_row(rows, distance) for distance in range(CORES, row_count, CORES)]

    def shared(arrived, *ahead):
        return [piece for got in arrived for piece in (got, to_row(after(got, *ahead), 1))]

    early_rows = coupling[:early]
    late_rows = [coupling[day : day + 1] for day in range(early, day_count)]
    got_inverses = over_chips(inv_diag)
    got_links = [over_chips(early_rows)]
    for index, rows in enumerate(late_rows[:-1]):
        got_links.append(over_chips(after(rows, *(got_inverses, *got_links)[index])))
    own_inverse = [inv_diag, to_row(inv_diag, 1)]
    own_link = [coupling, to_row(coupling, 1)]
    where = after(where, keep, early_rows, *late_rows)

    distance = part_count // 2
    while distance:
        got = lax.ppermute(sent, "tm", [(i, i ^ distance) for i in range(part_count)])
        distance //= 2
        keep, sent = halved(where, distance, keep, got)
    right_side = keep + to_row(keep, 1)

    def pack_body(rows_ref, source_ref, out_ref):
        out_ref[:share, :] = rows_ref[0]
        out_ref[share:, :] = jnp.zeros((LINES, nodes), F32)
        out_ref[share : share + day_count, :] = source_ref[...]

    packed = call(
        pack_body, shape(share + LINES, nodes), "pack", (), [late_rows[-1], right_side], work=0.1
    )
    got_links.append(over_chips(after(packed, *(got_inverses, *got_links)[late - 1])))

    def store(out_ref, pair):
        out_ref[0], out_ref[1] = pair

    def inverses_body(where_ref, *refs):
        row_refs, noise_ref, gram_out, outs = (
            refs[:row_count], refs[row_count], refs[row_count + 1], refs[row_count + 2 :],
        )
        for day in range(day_count):
            gather_rows(where_ref, row_refs, lambda offset: day, outs[day])
            outs[day_count + day][...] = dot_parts(
                split(noise_ref[day]), parts(outs[day]), TN
            )
        gram_out[...] = dot_parts(parts(outs[0]), parts(outs[0]), TN)

    gram, *results = call(
        inverses_body,
        [square, *[map_parts] * day_count, *[samples_full] * day_count],
        "inverses",
        (where,),
        [*own_inverse, *shared(got_inverses, where, packed), noise],
        work=4,
    )
    inverses, local_terms = results[:day_count], results[day_count:]

    def early_body(where_ref, *refs):
        own_refs, got_refs, refs = refs[:CORES], refs[CORES:row_count], refs[row_count:]
        noise_ref, term_ref, refs = refs[0], refs[1], refs[2:]
        inverse_refs, refs = refs[: early + 1], refs[early + 1 :]
        sum_out, *outs = refs
        link_outs, moved_outs, map_outs = outs[:early], outs[early : 2 * early], outs[2 * early :]
        for day in range(early):
            gather_rows(where_ref, (*own_refs, *got_refs), lambda offset: day, link_outs[day])
        total = term_ref[...]
        moved = parts(inverse_refs[0])
        for day in range(early):
            link = parts(link_outs[day])
            path = split(-dot_parts(link, moved, NN))
            if day == 0:
                store(map_outs[0], path)
            else:
                store(map_outs[day], split(-dot_parts(link, parts(inverse_refs[day]), NN)))
            moved = split(dot_parts(parts(inverse_refs[day + 1]), path, NN))
            store(moved_outs[day], moved)
            total = total + dot_parts(split(noise_ref[day + 1]), moved, TN)
        sum_out[...] = total

    summed, *results = call(
        early_body,
        [samples_full, *[map_parts] * (3 * early)],
        "early_days",
        (where,),
        [*own_link, *shared(got_links[0], gram), noise, local_terms[0], *inverses[: early + 1]],
        work=6,
    )
    links, step_maps = list(results[:early]), list(results[2 * early :])
    moveds = [inverses[0], *results[early : 2 * early]]

    def next_body(day, where_ref, *refs):
        own_refs, got_refs, refs = refs[:CORES], refs[CORES:row_count], refs[row_count:]
        noise_ref, inverse_ref, sum_ref, moved_ref, link_out, moved_out, *sum_outs = refs
        gather_rows(
            where_ref, (*own_refs, *got_refs), lambda offset: day if offset < CORES else 0, link_out
        )
        path = split(-dot_parts(parts(link_out), parts(moved_ref), NN))
        moved = split(dot_parts(parts(inverse_ref), path, NN))
        store(moved_out, moved)
        total = sum_ref[...] + dot_parts(split(noise_ref[day + 1]), moved, TN)
        if len(sum_outs) == 1:
            sum_outs[0][...] = total
        else:
            first = (where_ref[1, 0] & (PAIR - 1)) == 0
            sum_outs[0][...] = jnp.where(first, total[:half], total[half:])
            sum_outs[1][...] = jnp.where(first, total[half:], total[:half])

    for day in range(early, day_count - 1):
        sums = [samples_half] * 2 if day == day_count - 2 else [samples_full]
        link, moved, *sums = call(
            functools.partial(next_body, day),
            [map_parts, map_parts, *sums],
            f"day_{day}",
            (where,),
            [
                *own_link, *shared(got_links[1 + day - early], summed), noise, inverses[day + 1],
                summed, moveds[day],
            ],
            work=3,
        )
        summed = sums[0]
        moveds.append(moved)
        links.append(link)
    keep, send = sums
    other_sum = to_pair(send)

    def last_link_body(where_ref, *refs):
        own_refs, got_refs, refs = refs[:CORES], refs[CORES:row_count], refs[row_count:]
        moved_ref, whole_out, half_out, link_out = refs
        gather_rows(
            where_ref,
            (*own_refs, *(ref.at[pl.ds(0, share)] for ref in got_refs)),
            lambda offset: day_count - 1,
            link_out,
        )
        whole_out[...] = -dot_parts(parts(link_out), parts(moved_ref), NN)
        half_out[...] = whole_out[
            pl.ds(pl.multiple_of((where_ref[0, 0] & (CORES - 1)) * half_nodes, half_nodes), half_nodes), :
        ]

    path, path_half, link = call(
        last_link_body,
        (square, shape(half_nodes, nodes), map_parts),
        "last_link",
        (where,),
        [*own_link, *shared(got_links[-1], send), moveds[-1]],
        work=1.5,
    )
    links.append(link)
    other_half = to_pair(after(path_half, other_sum))

    def lines_body(source_ref, *refs):
        got_refs, refs = refs[: chips - 1], refs[chips - 1 :]
        flux_out, back_out, current_out = refs[-3:]
        source = source_ref[...]
        for ref in got_refs:
            source = source + ref[share : share + day_count, :]
        applied = jnp.zeros((LINES, nodes), F32)
        back = applied
        for day in range(day_count):
            inverse_ref, link_ref, moved_ref = refs[3 * day : 3 * day + 3]
            wanted = source[day : day + 1] - applied
            current = dot_parts(split(wanted), parts(inverse_ref), NT)
            current_out[day] = current
            current = split(current)
            applied = dot_parts(current, parts(link_ref), NT)
            back = back + dot_parts(current, parts(moved_ref), NN)
        flux_out[...] = applied
        back_out[...] = back

    flux, back, currents = call(
        lines_body,
        (line, line, shape(day_count, LINES, nodes)),
        "lines",
        (),
        [
            right_side,
            *got_links[-1],
            *(
                ref for day in range(day_count)
                for ref in (inverses[day], links[day], moveds[day])
            ),
        ],
        work=5,
    )
    other_flux = to_pair(flux)

    def grams_body(gram_ref, *refs):
        total = gram_ref[...]
        for ref in refs[:-1]:
            total = total + dot_parts(parts(ref), parts(ref), TN)
        store(refs[-1], split(total))

    gram = call(grams_body, map_parts, "grams", (), [after(gram, flux), *moveds[1:]], work=3)

    def late_maps_body(*refs):
        for index in range(late):
            store(
                refs[2 * late + index],
                split(-dot_parts(parts(refs[late + index]), parts(refs[index]), NN)),
            )

    step_maps += call(
        late_maps_body,
        [map_parts] * late,
        "late_maps",
        (),
        [after(inverses[early], gram), *inverses[early + 1 :], *links[early:]],
        work=late,
    )

    other_rest = to_row(after(other_half, other_flux, *step_maps), 1)

    def pair_body(
        where_ref, path_ref, half_ref, rest_ref, sum_ref, other_ref, flux_ref, other_flux_ref,
        low_out, high_out, sum_out, high_sum_out, flux_out, low_flux_out,
    ):
        first = (where_ref[1, 0] & (PAIR - 1)) == 0
        lead = (where_ref[0, 0] & (CORES - 1)) == 0
        half_rows, rest_rows = half_ref[...], rest_ref[...]
        for at, rows in (
            (slice(0, half_nodes), jnp.where(lead, half_rows, rest_rows)),
            (slice(half_nodes, nodes), jnp.where(lead, rest_rows, half_rows)),
        ):
            own = path_ref[at, :]
            low_out[0, at, :], low_out[1, at, :] = split(jnp.where(first, own, rows))
            high_out[0, at, :], high_out[1, at, :] = split(jnp.where(first, rows, own))
        low_sum = jnp.where(first, sum_ref[...], other_ref[...])
        high_sum = jnp.where(first, other_ref[...], sum_ref[...])
        low_flux = jnp.where(first, flux_ref[...], other_flux_ref[...])
        high_flux = jnp.where(first, other_flux_ref[...], flux_ref[...])
        flux_out[...] = dot_parts(split(low_flux), parts(high_out), NT) + high_flux
        low_flux_out[...] = low_flux
        sum_out[...] = dot_parts(split(high_sum), parts(low_out), NN) + low_sum
        high_sum_out[...] = high_sum

    low_map, high_map, pair_sum, high_sum, pair_flux, low_flux = call(
        pair_body,
        (map_parts, map_parts, samples_half, samples_half, line, line),
        "pair_maps",
        (where,),
        [path, other_half, other_rest, keep, other_sum, flux, other_flux],
        work=1.5,
    )

    def group_map_body(low_ref, high_ref, out_ref):
        store(out_ref, split(dot_parts(parts(high_ref), parts(low_ref), NN)))

    group_map = call(
        group_map_body, map_parts, "group_map", (), [low_map, after(high_map, pair_sum)]
    )

    def link_body(dims, map_ref, local_ref, *refs):
        got = refs[0][...]
        for ref in refs[1:-1]:
            got = got + ref[...]
        refs[-1][...] = dot_parts(split(got), parts(map_ref), dims) + local_ref[...]

    def linked(dims, value_map, value, got, name):
        return call(
            functools.partial(link_body, dims), shape(*value.shape), name, (),
            [value_map, value, *got], work=0.6,
        )

    def added(refs):
        total = refs[0][...]
        for ref in refs[1:]:
            total = total + ref[...]
        return total

    def turn_body(where_ref, low_ref, flux_ref, gram_ref, back_ref, *refs):
        own_out, back_out, part_out = refs[-3:]
        given = added(refs[:-3])
        behind = dot_parts(split(given), parts(low_ref), NT) + flux_ref[...]
        first = (where_ref[1, 0] & (PAIR - 1)) == 0
        given = jnp.where(first, given, behind)
        own_out[...] = given
        own_back = back_ref[...] - dot_parts(split(given), parts(gram_ref), NN)
        back_out[...] = own_back
        part_out[...] = jnp.where(first, own_back, dot_parts(split(own_back), parts(low_ref), NN))

    def first_back_body(where_ref, map_ref, own_ref, other_ref, part_ref, mate_ref, *refs):
        value_out, pair_out, high_out = refs[-3:]
        first = (where_ref[1, 0] & (PAIR - 1)) == 0
        pair_back = part_ref[...] + mate_ref[...]
        pair_out[...] = pair_back
        high_out[...] = jnp.where(first, other_ref[...], own_ref[...])
        value_out[...] = dot_parts(split(added(refs[:-3])), parts(map_ref), NN) + pair_back

    mean = {}

    def mean_hops():
        value, got = pair_flux, []
        yield value
        for group in range(groups - 1):
            got.append(to_group(value, group, group + 1))
            if group < groups - 2:
                value = linked(NT, group_map, pair_flux, got, "forward_link")
                yield value
        mean["entering"], own_back, part = call(
            turn_body, (line, line, line), "mean_turn", (where,),
            [low_map, low_flux, gram, back, *got],
        )
        yield part
        last = PAIR * (groups - 1)
        got = [
            lax.ppermute(part, "tm", [(last + i, last - PAIR + (i ^ cross)) for i in range(PAIR)])
            for cross in range(PAIR)
        ]
        both = to_pair(jnp.concatenate([own_back, part], axis=0))
        value, pair_back, mean["high_back"] = call(
            first_back_body, (line, line, line), "first_back", (where,),
            [group_map, own_back, both[:LINES], part, both[LINES:], *got], work=0.6,
        )
        mean["leaving"] = got
        for group in range(groups - 2, 0, -1):
            yield value
            got.append(to_group(value, group, group - 1))
            if group > 1:
                value = linked(NN, group_map, pair_back, got, "backward_link")
        yield got[-1]

    hops = mean_hops()
    ahead = next(hops)

    leaving = []
    value = pair_sum
    for group in range(groups - 1, 0, -1):
        got = to_group(after(value, ahead), group, group - 1)
        next(hops)
        ahead = next(hops, ahead)
        leaving.append(after(got, ahead))
        if group > 1:
            value = linked(NN, group_map, pair_sum, leaving, "noise_link")
    for ahead in hops:
        pass

    def divide_body(where_ref, map_ref, sum_ref, *refs):
        keep_out, send_out = refs[-2:]
        given = refs[0][...]
        for ref in refs[1:-2]:
            given = given + ref[...]
        between = dot_parts(split(given), parts(map_ref), NN) + sum_ref[...]
        first = (where_ref[1, 0] & (PAIR - 1)) == 0
        keep_out[...] = jnp.where(first, between, given)
        send_out[...] = jnp.where(first, given, between)

    kept_half, sent_half = call(
        divide_body, (samples_half, samples_half), "divide", (where,),
        [high_map, high_sum, *leaving],
    )
    got_half = to_pair(sent_half)

    def terms_body(entering_ref, current_ref, *refs):
        outs = refs[-day_count:]
        given = split(entering_ref[...])
        for day in range(day_count):
            local_ref, inverse_ref, moved_ref = refs[3 * day : 3 * day + 3]
            current = current_ref[day] - dot_parts(given, parts(moved_ref), NT)
            term = dot_parts(split(current), parts(inverse_ref), NN)
            outs[day][...] = local_ref[...] + term[:1]

    terms = call(
        terms_body, [samples_full] * day_count, "mean_terms", (),
        [
            after(mean["entering"], sent_half), currents,
            *(
                value for day in range(day_count)
                for value in (local_terms[day], inverses[day], moveds[day])
            ),
        ],
        work=4,
    )

    def last_body(where_ref, keep_ref, got_ref, back_ref, high_ref, *refs):
        count = len(mean["leaving"])
        got_means, refs = refs[:count], refs[count:]
        map_refs, term_refs = refs[:day_count], refs[day_count : 2 * day_count]
        out_ref, held, sems = refs[2 * day_count :]
        first = (where_ref[1, 0] & (PAIR - 1)) == 0
        given = got_means[0][...]
        for ref in got_means[1:]:
            given = given + ref[...]
        between = dot_parts(split(given), parts(high_ref), NN) + back_ref[...]
        given = jnp.where(first, between, given)
        low = jnp.where(first, keep_ref[...], got_ref[...])
        high = jnp.where(first, got_ref[...], keep_ref[...])
        following = jnp.concatenate([low, high], axis=0) + given[:1]
        copies = []
        for day in reversed(range(day_count)):
            following = dot_parts(split(following), parts(map_refs[day]), NN) + term_refs[day][...]
            held[day] = following.T
            copies.append(pltpu.make_async_copy(held.at[day], out_ref.at[day], sems.at[day]))
            copies[-1].start()
        for copy in copies:
            copy.wait()

    return call(
        last_body, shape(day_count, nodes, columns), "last_days", (where,),
        [
            kept_half, got_half, mean["high_back"], high_map, *mean["leaving"], *step_maps,
            *terms,
        ],
        work=4,
        scratch=[
            pltpu.VMEM((day_count, nodes, columns), F32), pltpu.SemaphoreType.DMA((day_count,)),
        ],
        out_specs=pl.BlockSpec(memory_space=pl.ANY),
    )


def solution(mesh):
    return jax.shard_map(
        local,
        mesh=mesh,
        in_specs=(
            P("tm", "row", None),
            P("tm", "row", None),
            P("tm", None, "row"),
            P(("tm", "row")),
            P(("tm", "row")),
            P(("tm", "row")),
        ),
        out_specs=P("tm", None, "row"),
        check_vma=False,
    )
```

time: 144 us -> 131 us (0.910)
  Pallas kernels: 48.6 us -> 36.4 us
  waiting for transfers between devices: 55.7 us -> 58.4 us
  other arithmetic: 1.9 us -> 0.08 us
    pallas_call x24, Pallas kernels: 48.6 us -> 36.4 us  [call(): pl.pallas_call(body, out_shape=out_shape, in_specs=[vmem] * (len(scalars)...]
    ppermute x5, waiting for transfers between devices: 19 us -> 10.7 us  [to_pair(): return lax.ppermute(value, 'tm', [(i, i ^ 1) for i in range(part_count)])]
    ppermute x15 -> x12, waiting for transfers between devices: 16.5 us -> 23.2 us  [to_row(): lax.ppermute(value, 'row', [(i, i ^ distance) for i in range(row_count)])]
    ppermute x9 -> x8, waiting for transfers between devices: 15.1 us -> 19 us  [to_group(): lax.ppermute(value, 'tm', [(PAIR * source + i, PAIR * target + i) for i i...]
    reshape x3, local copies, waits for them, and re-layouts: 0.01 us -> 2.16 us  [bin_observations(): value.reshape(chunks, chunk)]
    slice x2 -> x3, local copies, waits for them, and re-layouts: 3.18 us -> 1.1 us  [the longest x1 1.06 us: local(): late_rows = [coupling[day:day + 1] for day in range(early, day_count)]]
    another operation x3 -> x1, other arithmetic: 1.89 us -> 0.07 us  [local(): jnp.stack([my_row, my_part]).astype(jnp.int32)[:, None]]
    ppermute x15 -> x12, starting transfers between devices: 9.4 us -> 8.71 us  [to_row(): lax.ppermute(value, 'row', [(i, i ^ distance) for i in range(row_count)])]
  transfers between devices with their start and end apart: 32 -> 30, of which waited for: 16 -> 16; matrix products, arithmetic and copies ran while one was open for 2% -> 3% of each run, Pallas kernels for 29% -> 24%
where the time goes in v4:
time: 131 us
  waiting for transfers between devices  58.4 us (45%)
  Pallas kernels  36.4 us (28%)
  starting transfers between devices  32 us (24%)
  local copies, waits for them, and re-layouts  3.35 us (3%)
    pallas_call x24, Pallas kernels, call(): pl.pallas_call(body, out_shape=out_shape, in_specs=[vmem] * (len(scalars)...  36.4 us
    ppermute x12, waiting for transfers between devices, to_row(): lax.ppermute(value, 'row', [(i, i ^ distance) for i in range(row_count)])  23.2 us
    ppermute x8, waiting for transfers between devices, to_group(): lax.ppermute(value, 'tm', [(PAIR * source + i, PAIR * target + i) for i i...  19 us
    ppermute x5, waiting for transfers between devices, to_pair(): return lax.ppermute(value, 'tm', [(i, i ^ 1) for i in range(part_count)])  10.7 us
    ppermute x8, starting transfers between devices, to_group(): lax.ppermute(value, 'tm', [(PAIR * source + i, PAIR * target + i) for i i...  9.62 us
    ppermute x12, starting transfers between devices, to_row(): lax.ppermute(value, 'row', [(i, i ^ distance) for i in range(row_count)])  8.71 us
    ppermute x5, starting transfers between devices, to_pair(): return lax.ppermute(value, 'tm', [(i, i ^ 1) for i in range(part_count)])  6.47 us
    ppermute x3, starting transfers between devices, local(): lax.ppermute(sent, 'tm', [(i, i ^ distance) for i in range(part_count)])  5.85 us
  transfers between devices with their start and end apart: 30, of which 16 were waited for; matrix products, arithmetic and copies ran while one was open for 3% of the time, Pallas kernels for 24%

profile of v4, /device:TPU:0, one launch (start us, length us, event | category | flops | bytes accessed | tf_op | source)
XLA Modules:
  0.0 130.7 jit_solution(11392857004126254250)
XLA Ops:
  0.0 2.9 %collective-permute-start.7 = (f32[4,128,512]{2,1,0:T(8,128)}, f32[4,128,512]{2,1,0:T(8,128)S(1)}, u32[]{:S(2)}, u32[]{:S(2)}) collective-permute-start(f32[4,128,512]{2,1,0:T(8,128)} %refs_0_.4), channel_id=1, source_target_pairs={{0,2},{1,3},{2,0},{3,1},{4,6},{5,7},{6,4},{7,5},{8,10},{9,11},{10,... | collective-permute-start | bytes 3145736 | tf_op jit(solution)/shard_map/ppermute | solution.py:140
  2.9 0.7 reshape.10.day_ref
  3.7 0.7 reshape.11.node_ref
  4.4 0.7 reshape.12.value_ref
  5.3 1.4 %bin_observations.1 = (f32[16,512]{1,0:T(8,128)S(1)}, f32[16,512]{1,0:T(8,128)S(1)}) custom-call(s32[2,128]{1,0:T(2,128)S(1)} %broadcast_in_dim.2.where_ref, s32[8,512]{1,0:T(8,128)S(1)} %reshape.10.day_ref, s32[8,512]{1,0:T(8,128)S(1)} %reshape.11.node_ref, f32[8,512]{1,0:T(8,128)S(1)} %reshape.12.value_ref), custom_call_target="tpu_custom_call" | custom-call | flops 400000000 | bytes 1024 | tf_op jit(solution)/shard_map/bin_observations/pallas_call | solution.py:48
  6.6 2.6 %collective-permute-start.1 = (f32[16,512]{1,0:T(8,128)S(1)}, f32[16,512]{1,0:T(8,128)S(1)}, u32[]{:S(2)}, u32[]{:S(2)}) collective-permute-start(f32[16,512]{1,0:T(8,128)S(1)} %get-tuple-element.78), channel_id=1, source_target_pairs={{0,16},{4,20},{8,24},{12,28},{16,0},{20,4},{24,8},{28,12},{1,17},{... | collective-permute-start | bytes 98312 | tf_op jit(solution)/shard_map/ppermute | solution.py:183
  9.3 1.1 fusion
  10.4 1.1 collective-permute-done.1.got_ref
  11.5 1.6 %collective-permute-start.2 = (f32[8,512]{1,0:T(8,128)S(1)}, f32[8,512]{1,0:T(8,128)S(1)}, u32[]{:S(2)}, u32[]{:S(2)}) collective-permute-start(f32[8,512]{1,0:T(8,128)S(1)} %get-tuple-element.80), channel_id=1, source_target_pairs={{0,8},{4,12},{8,0},{12,4},{16,24},{20,28},{24,16},{28,20},{1,9},{5... | collective-permute-start | bytes 49160 | tf_op jit(solution)/shard_map/ppermute | solution.py:183
  13.2 2.2 %collective-permute-done.2.got_ref = f32[8,512]{1,0:T(8,128)S(1)} collective-permute-done((f32[8,512]{1,0:T(8,128)S(1)}, f32[8,512]{1,0:T(8,128)S(1)}, u32[]{:S(2)}, u32[]{:S(2)}) %collective-permute-start.2) | collective-permute-done | bytes 16416 | tf_op jit(solution)/shard_map/ppermute | solution.py:183
  15.4 1.6 %collective-permute-start.3 = (f32[4,512]{1,0:T(4,128)S(1)}, f32[4,512]{1,0:T(4,128)S(1)}, u32[]{:S(2)}, u32[]{:S(2)}) collective-permute-start(f32[4,512]{1,0:T(4,128)S(1)} %get-tuple-element.82), channel_id=1, source_target_pairs={{0,4},{4,0},{8,12},{12,8},{16,20},{20,16},{24,28},{28,24},{1,5},{5... | collective-permute-start | bytes 24584 | tf_op jit(solution)/shard_map/ppermute | solution.py:183
  17.0 2.1 %collective-permute-done.3.got_ref = f32[4,512]{1,0:T(4,128)S(1)} collective-permute-done((f32[4,512]{1,0:T(4,128)S(1)}, f32[4,512]{1,0:T(4,128)S(1)}, u32[]{:S(2)}, u32[]{:S(2)}) %collective-permute-start.3) | collective-permute-done | bytes 8224 | tf_op jit(solution)/shard_map/ppermute | solution.py:183
  19.1 0.5 collective-permute-start.9
  19.6 0.7 collective-permute-done.4
  20.3 6.1 %collective-permute-done.7.refs_2_ = f32[4,128,512]{2,1,0:T(8,128)S(1)} collective-permute-done((f32[4,128,512]{2,1,0:T(8,128)}, f32[4,128,512]{2,1,0:T(8,128)S(1)}, u32[]{:S(2)}, u32[]{:S(2)}) %collective-permute-start.7) | collective-permute-done | bytes 1048608 | tf_op jit(solution)/shard_map/ppermute | solution.py:140
  26.4 1.7 %collective-permute-start.5 = (f32[2,128,512]{2,1,0:T(8,128)S(1)}, f32[2,128,512]{2,1,0:T(8,128)S(1)}, u32[]{:S(2)}, u32[]{:S(2)}) collective-permute-start(f32[2,128,512]{2,1,0:T(8,128)S(1)} %slice.15), channel_id=1, source_target_pairs={{0,2},{1,3},{2,0},{3,1},{4,6},{5,7},{6,4},{7,5},{8,10},{9,11},{10,... | collective-permute-start | bytes 1572872 | tf_op jit(solution)/shard_map/ppermute | solution.py:140
  28.1 0.2 collective-permute-start
  28.3 0.8 collective-permute-done.10.refs_3_
  29.0 3.7 %inverses.1 = (f32[512,512]{1,0:T(8,128)S(1)}, bf16[2,512,512]{2,1,0:T(8,128)(2,1)S(1)}, bf16[2,512,512]{2,1,0:T(8,128)(2,1)S(1)}, bf16[2,512,512]{2,1,0:T(8,128...) custom-call(s32[2,128]{1,0:T(2,128)S(1)} %broadcast_in_dim.2.where_r, ...), custom_call_target="tpu_custom_call" | custom-call | flops 800000000 | bytes 1024 | tf_op jit(solution)/shard_map/inverses/pallas_call | solution.py:48
  32.8 8.0 %collective-permute-done.5.refs_2_ = f32[2,128,512]{2,1,0:T(8,128)S(1)} collective-permute-done((f32[2,128,512]{2,1,0:T(8,128)S(1)}, f32[2,128,512]{2,1,0:T(8,128)S(1)}, u32[]{:S(2)}, u32[]{:S(2)}) %collective-permute-start.5) | collective-permute-done | bytes 524320 | tf_op jit(solution)/shard_map/ppermute | solution.py:140
  40.7 1.7 %collective-permute-start.8 = (f32[1,128,512]{2,1,0:T(8,128)S(1)}, f32[1,128,512]{2,1,0:T(8,128)S(1)}, u32[]{:S(2)}, u32[]{:S(2)}) collective-permute-start(f32[1,128,512]{2,1,0:T(8,128)S(1)} %get-tuple-element.84), channel_id=1, source_target_pairs={{0,2},{1,3},{2,0},{3,1},{4,6},{5,7},{6,4},{7,5},{8,10},{9,11},{10,... | collective-permute-start | bytes 786440 | tf_op jit(solution)/shard_map/ppermute | solution.py:140
  42.4 0.2 collective-permute-done.11.refs_3_
  42.6 5.9 %early_days.1 = (f32[256,512]{1,0:T(8,128)S(1)}, bf16[2,512,512]{2,1,0:T(8,128)(2,1)S(1)}, bf16[2,512,512]{2,1,0:T(8,128)(2,1)S(1)}, bf16[2,512,512]{2,1,0:T(8,1...) custom-call(s32[2,128]{1,0:T(2,128)S(1)} %broadcast_in_dim.2.where_r, ...), custom_call_target="tpu_custom_call" | custom-call | flops 1200000000 | bytes 1024 | tf_op jit(solution)/shard_map/early_days/pallas_call | solution.py:48
  48.5 0.9 collective-permute-done.8.refs_2_
  49.4 1.7 %collective-permute-start.6 = (f32[136,512]{1,0:T(8,128)S(1)}, f32[136,512]{1,0:T(8,128)S(1)}, u32[]{:S(2)}, u32[]{:S(2)}) collective-permute-start(f32[136,512]{1,0:T(8,128)S(1)} %pack.1), channel_id=1, source_target_pairs={{0,2},{1,3},{2,0},{3,1},{4,6},{5,7},{6,4},{7,5},{8,10},{9,11},{10,... | collective-permute-start | bytes 835592 | tf_op jit(solution)/shard_map/ppermute | solution.py:140
  51.1 2.7 %day_2.1 = (bf16[2,512,512]{2,1,0:T(8,128)(2,1)S(1)}, bf16[2,512,512]{2,1,0:T(8,128)(2,1)S(1)}, f32[128,512]{1,0:T(8,128)S(1)}, f32[128,512]{1,0:T(8,128)S(1)}) custom-call(s32[2,128]{1,0:T(2,128)S(1)} %broadcast_in_dim.2.where_ref, f32[4,128,512]{2,1,0:T(8,128)S(1)} %copy-done.1, f32[4,128,512]{2,1,0:T(8,128)S(1)} %collective-permute-done.refs_1_, ...), custom_call_target="tpu_custom_call" | custom-call | flops 600000000 | bytes 1024 | tf_op jit(solution)/shard_map/day_2/pallas_call | solution.py:48
  53.8 4.7 %collective-permute-done.6.refs_2_.refs_0_ = f32[136,512]{1,0:T(8,128)S(1)} collective-permute-done((f32[136,512]{1,0:T(8,128)S(1)}, f32[136,512]{1,0:T(8,128)S(1)}, u32[]{:S(2)}, u32[]{:S(2)}) %collective-permute-start.6) | collective-permute-done | bytes 278560 | tf_op jit(solution)/shard_map/ppermute | solution.py:140
  58.5 1.7 %collective-permute-start.14 = (f32[128,512]{1,0:T(8,128)S(1)}, f32[128,512]{1,0:T(8,128)S(1)}, u32[]{:S(2)}, u32[]{:S(2)}) collective-permute-start(f32[128,512]{1,0:T(8,128)S(1)} %get-tuple-element.96), channel_id=1, source_target_pairs={{0,4},{4,0},{8,12},{12,8},{16,20},{20,16},{24,28},{28,24},{1,5},{5... | collective-permute-start | bytes 786440 | tf_op jit(solution)/shard_map/ppermute | solution.py:143
  60.2 1.3 last_link.1
  61.5 5.7 %collective-permute-done.14.other_ref = f32[128,512]{1,0:T(8,128)S(1)} collective-permute-done((f32[128,512]{1,0:T(8,128)S(1)}, f32[128,512]{1,0:T(8,128)S(1)}, u32[]{:S(2)}, u32[]{:S(2)}) %collective-permute-start.14) | collective-permute-done | bytes 262176 | tf_op jit(solution)/shard_map/ppermute | solution.py:143
  67.2 1.7 %collective-permute-start.15 = (f32[256,512]{1,0:T(8,128)S(1)}, f32[256,512]{1,0:T(8,128)S(1)}, u32[]{:S(2)}, u32[]{:S(2)}) collective-permute-start(f32[256,512]{1,0:T(8,128)S(1)} %get-tuple-element.101), channel_id=1, source_target_pairs={{0,4},{4,0},{8,12},{12,8},{16,20},{20,16},{24,28},{28,24},{1,5},{5... | collective-permute-start | bytes 1572872 | tf_op jit(solution)/shard_map/ppermute | solution.py:143
  68.9 4.5 %lines.1 = (f32[8,512]{1,0:T(8,128)S(1)}, f32[8,512]{1,0:T(8,128)S(1)}, f32[4,8,512]{2,1,0:T(8,128)S(1)}) custom-call(f32[4,512]{1,0:T(4,128)S(1)} %add.3.source_ref, f32[136,512]{1,0:T(8,128)S(1)} %collective-permute-done.6.refs_2_.refs_0_, bf16[2,512,512]{2,1,0:T(8,128)(2,1)S(1)} %get-tuple-element.89.refs_6_.refs_1_.refs_3_.refs_2_, ...), custom_call_target="tpu_custom_call" | custom-call | flops 1000000000 | bytes 1024 | tf_op jit(solution)/shard_map/lines/pallas_call | solution.py:48
  73.5 0.3 collective-permute-start.16
  73.8 2.7 %grams.1.gram_ref = bf16[2,512,512]{2,1,0:T(8,128)(2,1)S(1)} custom-call(f32[512,512]{1,0:T(8,128)S(1)} %get-tuple-element.110.gram_ref, bf16[2,512,512]{2,1,0:T(8,128)(2,1)S(1)} %get-tuple-element.104.refs_6_.refs_0_.refs_5_, bf16[2,512,512]{2,1,0:T(8,128)(2,1)S(1)} %get-tuple-element.95.refs_7_.refs_9_.refs_1_.refs_8_, ...), custom_call_target="tpu_custom_call" | custom-call | flops 600000000 | bytes 1024 | tf_op jit(solution)/shard_map/grams/pallas_call | solution.py:48
  76.5 1.8 %late_maps.1 = (bf16[2,512,512]{2,1,0:T(8,128)(2,1)S(1)}, bf16[2,512,512]{2,1,0:T(8,128)(2,1)S(1)}) custom-call(bf16[2,512,512]{2,1,0:T(8,128)(2,1)S(1)} %get-tuple-element.111.refs_8_.refs_7_.refs_0_, bf16[2,512,512]{2,1,0:T(8,128)(2,1)S(1)} %get-tuple-element.94.refs_5_.refs_10_.refs_1_, bf16[2,512,512]{2,1,0:T(8,128)(2,1)S(1)} %get-tuple-element.105.refs_8_.refs_2_, ...), custom_call_target="tpu_custom_call" | custom-call | flops 400000000 | bytes 1024 | tf_op jit(solution)/shard_map/late_maps/pallas_call | solution.py:48
  78.3 2.8 %collective-permute-done.16.other_flux_ref = f32[8,512]{1,0:T(8,128)S(1)} collective-permute-done((f32[8,512]{1,0:T(8,128)S(1)}, f32[8,512]{1,0:T(8,128)S(1)}, u32[]{:S(2)}, u32[]{:S(2)}) %collective-permute-start.16) | collective-permute-done | bytes 16416 | tf_op jit(solution)/shard_map/ppermute | solution.py:143
  81.1 1.9 %collective-permute-done.17.rest_ref = f32[256,512]{1,0:T(8,128)S(1)} collective-permute-done((f32[256,512]{1,0:T(8,128)S(1)}, f32[256,512]{1,0:T(8,128)S(1)}, u32[]{:S(2)}, u32[]{:S(2)}) %collective-permute-start.17) | collective-permute-done | bytes 524320 | tf_op jit(solution)/shard_map/ppermute | solution.py:140
  83.1 1.1 pair_maps.1
  84.1 0.7 collective-permute-start.18
  84.8 3.7 %collective-permute-start.19 = (f32[8,512]{1,0:T(8,128)S(1)}, f32[8,512]{1,0:T(8,128)S(1)}, u32[]{:S(2)}, u32[]{:S(2)}) collective-permute-start(f32[8,512]{1,0:T(8,128)S(1)} %get-tuple-element.119.local_ref), channel_id=1, source_target_pairs={{0,8},{4,12},{1,9},{5,13},{2,10},{6,14},{3,11},{7,15}} | collective-permute-start | bytes 49160 | tf_op jit(solution)/shard_map/ppermute | solution.py:146
  88.5 1.0 group_map.1.map_ref
  89.5 0.4 collective-permute-done.19.refs_0_
  89.9 0.5 forward_link.2
  90.4 0.7 collective-permute-start.20
  91.1 0.5 forward_link.3
  91.6 0.7 collective-permute-start.22
  92.3 1.1 mean_turn.1
  93.4 1.5 %collective-permute-start.23 = (f32[16,512]{1,0:T(8,128)S(1)}, f32[16,512]{1,0:T(8,128)S(1)}, u32[]{:S(2)}, u32[]{:S(2)}) collective-permute-start(f32[16,512]{1,0:T(8,128)S(1)} %pad_maximum_fusion), channel_id=1, source_target_pairs={{0,4},{4,0},{8,12},{12,8},{16,20},{20,16},{24,28},{28,24},{1,5},{5... | collective-permute-start | bytes 98312 | tf_op jit(solution)/shard_map/ppermute | solution.py:143
  94.9 0.4 noise_link.2
  95.3 0.7 collective-permute-start.21
  96.0 0.7 collective-permute-start.25
  96.7 0.7 collective-permute-start.24
  97.4 0.3 first_back.1
  97.7 0.4 noise_link.3
  98.1 1.3 collective-permute-start.26
  99.4 0.7 collective-permute-start.27
  100.1 0.3 backward_link.1
  100.4 1.3 collective-permute-start.28
  101.7 18.6 %collective-permute-done.28.refs_3_ = f32[8,512]{1,0:T(8,128)S(1)} collective-permute-done((f32[8,512]{1,0:T(8,128)S(1)}, f32[8,512]{1,0:T(8,128)S(1)}, u32[]{:S(2)}, u32[]{:S(2)}) %collective-permute-start.28) | collective-permute-done | bytes 16416 | tf_op jit(solution)/shard_map/ppermute | solution.py:146
  120.3 0.4 divide.1
  120.7 1.2 collective-permute-start.29
  121.9 3.1 %mean_terms.1 = (f32[256,512]{1,0:T(8,128)S(1)}, f32[256,512]{1,0:T(8,128)S(1)}, f32[256,512]{1,0:T(8,128)S(1)}, f32[256,512]{1,0:T(8,128)S(1)}) custom-call(f32[8,512]{1,0:T(8,128)S(1)} %get-tuple-element.138.entering_ref, f32[4,8,512]{2,1,0:T(8,128)S(1)} %get-tuple-element.139.current_ref, f32[256,512]{1,0:T(8,128)S(1)} %get-tuple-element.88.refs_5_.refs_0_, ...), custom_call_target="tpu_custom_call" | custom-call | flops 800000000 | bytes 1024 | tf_op jit(solution)/shard_map/mean_terms/pallas_call | solution.py:48
  125.0 2.1 %collective-permute-done.29.got_ref = f32[128,512]{1,0:T(8,128)S(1)} collective-permute-done((f32[128,512]{1,0:T(8,128)S(1)}, f32[128,512]{1,0:T(8,128)S(1)}, u32[]{:S(2)}, u32[]{:S(2)}) %collective-permute-start.29) | collective-permute-done | bytes 262176 | tf_op jit(solution)/shard_map/ppermute | solution.py:143
  127.1 3.4 %last_days.1 = f32[4,512,256]{2,1,0:T(8,128)} custom-call(s32[2,128]{1,0:T(2,128)S(1)} %broadcast_in_dim.2.where_ref, f32[128,512]{1,0:T(8,128)S(1)} %get-tuple-element.134.keep_ref, f32[128,512]{1,0:T(8,128)S(1)} %collective-permute-done.29.got_ref, f32[8,512]{1,0:T(8,128)S(1)} %get-tuple-element.136.back_ref, ...), custom_call_target="tpu_custom_call" | custom-call | flops 800000000 | bytes 1024 | tf_op jit(solution)/shard_map/last_days/pallas_call | solution.py:48
  (36 shorter events, 0.4 us)
Async XLA Ops:
  0.0 19.1 %copy-start.2 = (f32[4,128,512]{2,1,0:T(8,128)S(1)}, f32[4,128,512]{2,1,0:T(8,128)}, u32[]{:S(2)}) copy-start(f32[4,128,512]{2,1,0:T(8,128)} %refs_0_.4) | copy-start | bytes 3145732
  0.0 10.3 %copy-start.1 = (f32[4,128,512]{2,1,0:T(8,128)S(1)}, f32[4,128,512]{2,1,0:T(8,128)}, u32[]{:S(2)}) copy-start(f32[4,128,512]{2,1,0:T(8,128)} %refs_0_.7) | copy-start | bytes 3145732
  0.0 26.4 %collective-permute-start.7 = (f32[4,128,512]{2,1,0:T(8,128)}, f32[4,128,512]{2,1,0:T(8,128)S(1)}, u32[]{:S(2)}, u32[]{:S(2)}) collective-permute-start(f32[4,128,512]{2,1,0:T(8,128)} %refs_0_.4), channel_id=1, source_target_pairs={{0,2},{1,3},{2,0},{3,1},{4,6},{5,7},{6,4},{7,5},{8,10},{9,11},{10,... | collective-permute-start | bytes 3145736 | tf_op jit(solution)/shard_map/ppermute | solution.py:140
  5.3 23.8 %copy-start = (f32[4,512,256]{2,1,0:T(8,128)S(1)}, f32[4,512,256]{2,1,0:T(8,128)}, u32[]{:S(2)}) copy-start(f32[4,512,256]{2,1,0:T(8,128)} %refs_4_.5) | copy-start | bytes 6291460
  6.6 4.9 %collective-permute-start.1 = (f32[16,512]{1,0:T(8,128)S(1)}, f32[16,512]{1,0:T(8,128)S(1)}, u32[]{:S(2)}, u32[]{:S(2)}) collective-permute-start(f32[16,512]{1,0:T(8,128)S(1)} %get-tuple-element.78), channel_id=1, source_target_pairs={{0,16},{4,20},{8,24},{12,28},{16,0},{20,4},{24,8},{28,12},{1,17},{... | collective-permute-start | bytes 98312 | tf_op jit(solution)/shard_map/ppermute | solution.py:183
  11.5 3.8 %collective-permute-start.2 = (f32[8,512]{1,0:T(8,128)S(1)}, f32[8,512]{1,0:T(8,128)S(1)}, u32[]{:S(2)}, u32[]{:S(2)}) collective-permute-start(f32[8,512]{1,0:T(8,128)S(1)} %get-tuple-element.80), channel_id=1, source_target_pairs={{0,8},{4,12},{8,0},{12,4},{16,24},{20,28},{24,16},{28,20},{1,9},{5... | collective-permute-start | bytes 49160 | tf_op jit(solution)/shard_map/ppermute | solution.py:183
  15.4 3.7 %collective-permute-start.3 = (f32[4,512]{1,0:T(4,128)S(1)}, f32[4,512]{1,0:T(4,128)S(1)}, u32[]{:S(2)}, u32[]{:S(2)}) collective-permute-start(f32[4,512]{1,0:T(4,128)S(1)} %get-tuple-element.82), channel_id=1, source_target_pairs={{0,4},{4,0},{8,12},{12,8},{16,20},{20,16},{24,28},{28,24},{1,5},{5... | collective-permute-start | bytes 24584 | tf_op jit(solution)/shard_map/ppermute | solution.py:183
  19.1 1.2 collective-permute-start.4
  19.1 9.2 %collective-permute-start.9 = (f32[4,128,512]{2,1,0:T(8,128)S(1)}, f32[4,128,512]{2,1,0:T(8,128)S(1)}, u32[]{:S(2)}, u32[]{:S(2)}) collective-permute-start(f32[4,128,512]{2,1,0:T(8,128)S(1)} %copy-done.2), channel_id=1, source_target_pairs={{0,1},{1,0},{2,3},{3,2},{4,5},{5,4},{6,7},{7,6},{8,9},{9,8},{10,11... | collective-permute-start | bytes 3145736 | tf_op jit(solution)/shard_map/ppermute | solution.py:140
  26.4 2.7 %collective-permute-start.10 = (f32[4,128,512]{2,1,0:T(8,128)S(1)}, f32[4,128,512]{2,1,0:T(8,128)S(1)}, u32[]{:S(2)}, u32[]{:S(2)}) collective-permute-start(f32[4,128,512]{2,1,0:T(8,128)S(1)} %collective-permute-done.7.refs_2_), channel_id=1, source_target_pairs={{0,1},{1,0},{2,3},{3,2},{4,5},{5,4},{6,7},{7,6},{8,9},{9,8},{10,11... | collective-permute-start | bytes 3145736 | tf_op jit(solution)/shard_map/ppermute | solution.py:140
  26.4 14.3 %collective-permute-start.5 = (f32[2,128,512]{2,1,0:T(8,128)S(1)}, f32[2,128,512]{2,1,0:T(8,128)S(1)}, u32[]{:S(2)}, u32[]{:S(2)}) collective-permute-start(f32[2,128,512]{2,1,0:T(8,128)S(1)} %slice.15), channel_id=1, source_target_pairs={{0,2},{1,3},{2,0},{3,1},{4,6},{5,7},{6,4},{7,5},{8,10},{9,11},{10,... | collective-permute-start | bytes 1572872 | tf_op jit(solution)/shard_map/ppermute | solution.py:140
  28.1 14.3 %collective-permute-start = (f32[4,128,512]{2,1,0:T(8,128)S(1)}, f32[4,128,512]{2,1,0:T(8,128)S(1)}, u32[]{:S(2)}, u32[]{:S(2)}) collective-permute-start(f32[4,128,512]{2,1,0:T(8,128)S(1)} %copy-done.1), channel_id=1, source_target_pairs={{0,1},{1,0},{2,3},{3,2},{4,5},{5,4},{6,7},{7,6},{8,9},{9,8},{10,11... | collective-permute-start | bytes 3145736 | tf_op jit(solution)/shard_map/ppermute | solution.py:140
  40.7 1.9 %collective-permute-start.11 = (f32[2,128,512]{2,1,0:T(8,128)S(1)}, f32[2,128,512]{2,1,0:T(8,128)S(1)}, u32[]{:S(2)}, u32[]{:S(2)}) collective-permute-start(f32[2,128,512]{2,1,0:T(8,128)S(1)} %collective-permute-done.5.refs_2_), channel_id=1, source_target_pairs={{0,1},{1,0},{2,3},{3,2},{4,5},{5,4},{6,7},{7,6},{8,9},{9,8},{10,11... | collective-permute-start | bytes 1572872 | tf_op jit(solution)/shard_map/ppermute | solution.py:140
  40.7 8.7 %collective-permute-start.8 = (f32[1,128,512]{2,1,0:T(8,128)S(1)}, f32[1,128,512]{2,1,0:T(8,128)S(1)}, u32[]{:S(2)}, u32[]{:S(2)}) collective-permute-start(f32[1,128,512]{2,1,0:T(8,128)S(1)} %get-tuple-element.84), channel_id=1, source_target_pairs={{0,2},{1,3},{2,0},{3,1},{4,6},{5,7},{6,4},{7,5},{8,10},{9,11},{10,... | collective-permute-start | bytes 786440 | tf_op jit(solution)/shard_map/ppermute | solution.py:140
  49.4 1.7 %collective-permute-start.12 = (f32[1,128,512]{2,1,0:T(8,128)S(1)}, f32[1,128,512]{2,1,0:T(8,128)S(1)}, u32[]{:S(2)}, u32[]{:S(2)}) collective-permute-start(f32[1,128,512]{2,1,0:T(8,128)S(1)} %collective-permute-done.8.refs_2_), channel_id=1, source_target_pairs={{0,1},{1,0},{2,3},{3,2},{4,5},{5,4},{6,7},{7,6},{8,9},{9,8},{10,11... | collective-permute-start | bytes 786440 | tf_op jit(solution)/shard_map/ppermute | solution.py:140
  49.4 9.1 %collective-permute-start.6 = (f32[136,512]{1,0:T(8,128)S(1)}, f32[136,512]{1,0:T(8,128)S(1)}, u32[]{:S(2)}, u32[]{:S(2)}) collective-permute-start(f32[136,512]{1,0:T(8,128)S(1)} %pack.1), channel_id=1, source_target_pairs={{0,2},{1,3},{2,0},{3,1},{4,6},{5,7},{6,4},{7,5},{8,10},{9,11},{10,... | collective-permute-start | bytes 835592 | tf_op jit(solution)/shard_map/ppermute | solution.py:140
  58.5 1.7 %collective-permute-start.13 = (f32[136,512]{1,0:T(8,128)S(1)}, f32[136,512]{1,0:T(8,128)S(1)}, u32[]{:S(2)}, u32[]{:S(2)}) collective-permute-start(f32[136,512]{1,0:T(8,128)S(1)} %collective-permute-done.6.refs_2_.refs_0_), channel_id=1, source_target_pairs={{0,1},{1,0},{2,3},{3,2},{4,5},{5,4},{6,7},{7,6},{8,9},{9,8},{10,11... | collective-permute-start | bytes 835592 | tf_op jit(solution)/shard_map/ppermute | solution.py:140
  58.5 8.7 %collective-permute-start.14 = (f32[128,512]{1,0:T(8,128)S(1)}, f32[128,512]{1,0:T(8,128)S(1)}, u32[]{:S(2)}, u32[]{:S(2)}) collective-permute-start(f32[128,512]{1,0:T(8,128)S(1)} %get-tuple-element.96), channel_id=1, source_target_pairs={{0,4},{4,0},{8,12},{12,8},{16,20},{20,16},{24,28},{28,24},{1,5},{5... | collective-permute-start | bytes 786440 | tf_op jit(solution)/shard_map/ppermute | solution.py:143
  67.2 13.9 %collective-permute-start.15 = (f32[256,512]{1,0:T(8,128)S(1)}, f32[256,512]{1,0:T(8,128)S(1)}, u32[]{:S(2)}, u32[]{:S(2)}) collective-permute-start(f32[256,512]{1,0:T(8,128)S(1)} %get-tuple-element.101), channel_id=1, source_target_pairs={{0,4},{4,0},{8,12},{12,8},{16,20},{20,16},{24,28},{28,24},{1,5},{5... | collective-permute-start | bytes 1572872 | tf_op jit(solution)/shard_map/ppermute | solution.py:143
  73.5 7.7 %collective-permute-start.16 = (f32[8,512]{1,0:T(8,128)S(1)}, f32[8,512]{1,0:T(8,128)S(1)}, u32[]{:S(2)}, u32[]{:S(2)}) collective-permute-start(f32[8,512]{1,0:T(8,128)S(1)} %get-tuple-element.107.flux_ref), channel_id=1, source_target_pairs={{0,4},{4,0},{8,12},{12,8},{16,20},{20,16},{24,28},{28,24},{1,5},{5... | collective-permute-start | bytes 49160 | tf_op jit(solution)/shard_map/ppermute | solution.py:143
  81.1 1.9 %collective-permute-start.17 = (f32[256,512]{1,0:T(8,128)S(1)}, f32[256,512]{1,0:T(8,128)S(1)}, u32[]{:S(2)}, u32[]{:S(2)}) collective-permute-start(f32[256,512]{1,0:T(8,128)S(1)} %collective-permute-done.15.half_ref), channel_id=1, source_target_pairs={{0,1},{1,0},{2,3},{3,2},{4,5},{5,4},{6,7},{7,6},{8,9},{9,8},{10,11... | collective-permute-start | bytes 1572872 | tf_op jit(solution)/shard_map/ppermute | solution.py:140
  84.1 10.8 %collective-permute-start.18 = (f32[128,512]{1,0:T(8,128)S(1)}, f32[128,512]{1,0:T(8,128)S(1)}, u32[]{:S(2)}, u32[]{:S(2)}) collective-permute-start(f32[128,512]{1,0:T(8,128)S(1)} %get-tuple-element.120.local_ref), channel_id=1, source_target_pairs={{24,16},{28,20},{25,17},{29,21},{26,18},{30,22},{27,19},{31,23}} | collective-permute-start | bytes 786440 | tf_op jit(solution)/shard_map/ppermute | solution.py:146
  84.8 5.1 %collective-permute-start.19 = (f32[8,512]{1,0:T(8,128)S(1)}, f32[8,512]{1,0:T(8,128)S(1)}, u32[]{:S(2)}, u32[]{:S(2)}) collective-permute-start(f32[8,512]{1,0:T(8,128)S(1)} %get-tuple-element.119.local_ref), channel_id=1, source_target_pairs={{0,8},{4,12},{1,9},{5,13},{2,10},{6,14},{3,11},{7,15}} | collective-permute-start | bytes 49160 | tf_op jit(solution)/shard_map/ppermute | solution.py:146
  90.4 0.7 collective-permute-start.20
  91.6 0.7 collective-permute-start.22
  93.4 4.0 %collective-permute-start.23 = (f32[16,512]{1,0:T(8,128)S(1)}, f32[16,512]{1,0:T(8,128)S(1)}, u32[]{:S(2)}, u32[]{:S(2)}) collective-permute-start(f32[16,512]{1,0:T(8,128)S(1)} %pad_maximum_fusion), channel_id=1, source_target_pairs={{0,4},{4,0},{8,12},{12,8},{16,20},{20,16},{24,28},{28,24},{1,5},{5... | collective-permute-start | bytes 98312 | tf_op jit(solution)/shard_map/ppermute | solution.py:143
  95.3 2.4 %collective-permute-start.21 = (f32[128,512]{1,0:T(8,128)S(1)}, f32[128,512]{1,0:T(8,128)S(1)}, u32[]{:S(2)}, u32[]{:S(2)}) collective-permute-start(f32[128,512]{1,0:T(8,128)S(1)} %noise_link.2), channel_id=1, source_target_pairs={{16,8},{20,12},{17,9},{21,13},{18,10},{22,14},{19,11},{23,15}} | collective-permute-start | bytes 786440 | tf_op jit(solution)/shard_map/ppermute | solution.py:146
  96.0 1.4 %collective-permute-start.25 = (f32[8,512]{1,0:T(8,128)S(1)}, f32[8,512]{1,0:T(8,128)S(1)}, u32[]{:S(2)}, u32[]{:S(2)}) collective-permute-start(f32[8,512]{1,0:T(8,128)S(1)} %get-tuple-element.128.part_ref), channel_id=1, source_target_pairs={{24,20},{28,16},{25,21},{29,17},{26,22},{30,18},{27,23},{31,19}} | collective-permute-start | bytes 49160 | tf_op jit(solution)/shard_map/ppermute | solution.py:471
  96.7 0.7 collective-permute-start.24
  98.1 22.2 %collective-permute-start.26 = (f32[128,512]{1,0:T(8,128)S(1)}, f32[128,512]{1,0:T(8,128)S(1)}, u32[]{:S(2)}, u32[]{:S(2)}) collective-permute-start(f32[128,512]{1,0:T(8,128)S(1)} %noise_link.3), channel_id=1, source_target_pairs={{8,0},{12,4},{9,1},{13,5},{10,2},{14,6},{11,3},{15,7}} | collective-permute-start | bytes 786440 | tf_op jit(solution)/shard_map/ppermute | solution.py:146
  99.4 0.7 collective-permute-start.27
  100.4 19.9 %collective-permute-start.28 = (f32[8,512]{1,0:T(8,128)S(1)}, f32[8,512]{1,0:T(8,128)S(1)}, u32[]{:S(2)}, u32[]{:S(2)}) collective-permute-start(f32[8,512]{1,0:T(8,128)S(1)} %backward_link.1), channel_id=1, source_target_pairs={{8,0},{12,4},{9,1},{13,5},{10,2},{14,6},{11,3},{15,7}} | collective-permute-start | bytes 49160 | tf_op jit(solution)/shard_map/ppermute | solution.py:146
  120.7 6.4 %collective-permute-start.29 = (f32[128,512]{1,0:T(8,128)S(1)}, f32[128,512]{1,0:T(8,128)S(1)}, u32[]{:S(2)}, u32[]{:S(2)}) collective-permute-start(f32[128,512]{1,0:T(8,128)S(1)} %get-tuple-element.135), channel_id=1, source_target_pairs={{0,4},{4,0},{8,12},{12,8},{16,20},{20,16},{24,28},{28,24},{1,5},{5... | collective-permute-start | bytes 786440 | tf_op jit(solution)/shard_map/ppermute | solution.py:143

commit v5 on v4

--- a/solution.py
+++ b/solution.py
@@ -452,6 +452,7 @@
         value_out[...] = dot_parts(split(added(refs[:-3])), parts(map_ref), NN) + pair_back
 
     mean = {}
+    noise_step = []
 
     def mean_hops():
         value, got = pair_flux, []
@@ -463,7 +464,7 @@
                 yield value
         mean["entering"], own_back, part = call(
             turn_body, (line, line, line), "mean_turn", (where,),
-            [low_map, low_flux, gram, back, *got],
+            [low_map, low_flux, gram, back, after(got[0], *noise_step), *got[1:]],
         )
         yield part
         last = PAIR * (groups - 1)
@@ -481,8 +482,9 @@
             yield value
             got.append(to_group(value, group, group - 1))
             if group > 1:
-                value = linked(NN, group_map, pair_back, got, "backward_link")
-        yield got[-1]
+                gated = [after(got[0], *noise_step), *got[1:]]
+                value = linked(NN, group_map, pair_back, gated, "backward_link")
+        yield value
 
     hops = mean_hops()
     ahead = next(hops)
@@ -491,12 +493,14 @@
     value = pair_sum
     for group in range(groups - 1, 0, -1):
         got = to_group(after(value, ahead), group, group - 1)
-        next(hops)
-        ahead = next(hops, ahead)
+        ahead = next(hops)
+        if group > 1:
+            ahead = next(hops)
         leaving.append(after(got, ahead))
         if group > 1:
             value = linked(NN, group_map, pair_sum, leaving, "noise_link")
-    for ahead in hops:
+            noise_step[:] = [value]
+    for _ in hops:
         pass
 
     def divide_body(where_ref, map_ref, sum_ref, *refs):

time: 131 us -> 126 us (0.962)
  waiting for transfers between devices: 58.4 us -> 54 us
    ppermute x8, waiting for transfers between devices: 19 us -> 16.1 us  [to_group(): lax.ppermute(value, 'tm', [(PAIR * source + i, PAIR * target + i) for i i...]
    ppermute x5, waiting for transfers between devices: 10.7 us -> 9.22 us  [to_pair(): return lax.ppermute(value, 'tm', [(i, i ^ 1) for i in range(part_count)])]
  transfers between devices with their start and end apart: 30 -> 30, of which waited for: 16 -> 18; matrix products, arithmetic and copies ran while one was open for 3% -> 3% of each run, Pallas kernels for 24% -> 24%
where the time goes in v5:
time: 126 us
  waiting for transfers between devices  54 us (43%)
  Pallas kernels  36.4 us (29%)
  starting transfers between devices  31.3 us (25%)
  local copies, waits for them, and re-layouts  3.35 us (3%)
    pallas_call x24, Pallas kernels, call(): pl.pallas_call(body, out_shape=out_shape, in_specs=[vmem] * (len(scalars)...  36.4 us
    ppermute x12, waiting for transfers between devices, to_row(): lax.ppermute(value, 'row', [(i, i ^ distance) for i in range(row_count)])  23.2 us
    ppermute x8, waiting for transfers between devices, to_group(): lax.ppermute(value, 'tm', [(PAIR * source + i, PAIR * target + i) for i i...  16.1 us
    ppermute x8, starting transfers between devices, to_group(): lax.ppermute(value, 'tm', [(PAIR * source + i, PAIR * target + i) for i i...  9.59 us
    ppermute x5, waiting for transfers between devices, to_pair(): return lax.ppermute(value, 'tm', [(i, i ^ 1) for i in range(part_count)])  9.22 us
    ppermute x12, starting transfers between devices, to_row(): lax.ppermute(value, 'row', [(i, i ^ distance) for i in range(row_count)])  8.71 us
    ppermute x3, starting transfers between devices, local(): lax.ppermute(sent, 'tm', [(i, i ^ distance) for i in range(part_count)])  5.85 us
    ppermute x5, starting transfers between devices, to_pair(): return lax.ppermute(value, 'tm', [(i, i ^ 1) for i in range(part_count)])  5.84 us
  transfers between devices with their start and end apart: 30, of which 18 were waited for; matrix products, arithmetic and copies ran while one was open for 3% of the time, Pallas kernels for 24%

profile of v5, /device:TPU:0, one launch (start us, length us, event | category | flops | bytes accessed | tf_op | source)
XLA Modules:
  0.0 125.6 jit_solution(14800488144877206095)
XLA Ops:
  0.0 2.9 %collective-permute-start.7 = (f32[4,128,512]{2,1,0:T(8,128)}, f32[4,128,512]{2,1,0:T(8,128)S(1)}, u32[]{:S(2)}, u32[]{:S(2)}) collective-permute-start(f32[4,128,512]{2,1,0:T(8,128)} %refs_0_.4), channel_id=1, source_target_pairs={{0,2},{1,3},{2,0},{3,1},{4,6},{5,7},{6,4},{7,5},{8,10},{9,11},{10,... | collective-permute-start | bytes 3145736 | tf_op jit(solution)/shard_map/ppermute | solution.py:140
  2.9 0.7 reshape.10.day_ref
  3.7 0.7 reshape.11.node_ref
  4.4 0.7 reshape.12.value_ref
  5.3 1.4 %bin_observations.1 = (f32[16,512]{1,0:T(8,128)S(1)}, f32[16,512]{1,0:T(8,128)S(1)}) custom-call(s32[2,128]{1,0:T(2,128)S(1)} %broadcast_in_dim.2.where_ref, s32[8,512]{1,0:T(8,128)S(1)} %reshape.10.day_ref, s32[8,512]{1,0:T(8,128)S(1)} %reshape.11.node_ref, f32[8,512]{1,0:T(8,128)S(1)} %reshape.12.value_ref), custom_call_target="tpu_custom_call" | custom-call | flops 400000000 | bytes 1024 | tf_op jit(solution)/shard_map/bin_observations/pallas_call | solution.py:48
  6.6 2.6 %collective-permute-start.1 = (f32[16,512]{1,0:T(8,128)S(1)}, f32[16,512]{1,0:T(8,128)S(1)}, u32[]{:S(2)}, u32[]{:S(2)}) collective-permute-start(f32[16,512]{1,0:T(8,128)S(1)} %get-tuple-element.80), channel_id=1, source_target_pairs={{0,16},{4,20},{8,24},{12,28},{16,0},{20,4},{24,8},{28,12},{1,17},{... | collective-permute-start | bytes 98312 | tf_op jit(solution)/shard_map/ppermute | solution.py:183
  9.3 1.1 fusion
  10.4 1.1 collective-permute-done.1.got_ref
  11.5 1.6 %collective-permute-start.2 = (f32[8,512]{1,0:T(8,128)S(1)}, f32[8,512]{1,0:T(8,128)S(1)}, u32[]{:S(2)}, u32[]{:S(2)}) collective-permute-start(f32[8,512]{1,0:T(8,128)S(1)} %get-tuple-element.82), channel_id=1, source_target_pairs={{0,8},{4,12},{8,0},{12,4},{16,24},{20,28},{24,16},{28,20},{1,9},{5... | collective-permute-start | bytes 49160 | tf_op jit(solution)/shard_map/ppermute | solution.py:183
  13.2 2.2 %collective-permute-done.2.got_ref = f32[8,512]{1,0:T(8,128)S(1)} collective-permute-done((f32[8,512]{1,0:T(8,128)S(1)}, f32[8,512]{1,0:T(8,128)S(1)}, u32[]{:S(2)}, u32[]{:S(2)}) %collective-permute-start.2) | collective-permute-done | bytes 16416 | tf_op jit(solution)/shard_map/ppermute | solution.py:183
  15.4 1.6 %collective-permute-start.3 = (f32[4,512]{1,0:T(4,128)S(1)}, f32[4,512]{1,0:T(4,128)S(1)}, u32[]{:S(2)}, u32[]{:S(2)}) collective-permute-start(f32[4,512]{1,0:T(4,128)S(1)} %get-tuple-element.84), channel_id=1, source_target_pairs={{0,4},{4,0},{8,12},{12,8},{16,20},{20,16},{24,28},{28,24},{1,5},{5... | collective-permute-start | bytes 24584 | tf_op jit(solution)/shard_map/ppermute | solution.py:183
  17.0 2.1 %collective-permute-done.3.got_ref = f32[4,512]{1,0:T(4,128)S(1)} collective-permute-done((f32[4,512]{1,0:T(4,128)S(1)}, f32[4,512]{1,0:T(4,128)S(1)}, u32[]{:S(2)}, u32[]{:S(2)}) %collective-permute-start.3) | collective-permute-done | bytes 8224 | tf_op jit(solution)/shard_map/ppermute | solution.py:183
  19.1 0.5 collective-permute-start.9
  19.6 0.7 collective-permute-done.4
  20.3 6.1 %collective-permute-done.7.refs_2_ = f32[4,128,512]{2,1,0:T(8,128)S(1)} collective-permute-done((f32[4,128,512]{2,1,0:T(8,128)}, f32[4,128,512]{2,1,0:T(8,128)S(1)}, u32[]{:S(2)}, u32[]{:S(2)}) %collective-permute-start.7) | collective-permute-done | bytes 1048608 | tf_op jit(solution)/shard_map/ppermute | solution.py:140
  26.4 1.7 %collective-permute-start.5 = (f32[2,128,512]{2,1,0:T(8,128)S(1)}, f32[2,128,512]{2,1,0:T(8,128)S(1)}, u32[]{:S(2)}, u32[]{:S(2)}) collective-permute-start(f32[2,128,512]{2,1,0:T(8,128)S(1)} %slice.15), channel_id=1, source_target_pairs={{0,2},{1,3},{2,0},{3,1},{4,6},{5,7},{6,4},{7,5},{8,10},{9,11},{10,... | collective-permute-start | bytes 1572872 | tf_op jit(solution)/shard_map/ppermute | solution.py:140
  28.3 0.8 collective-permute-done.10.refs_3_
  29.0 3.7 %inverses.1 = (f32[512,512]{1,0:T(8,128)S(1)}, bf16[2,512,512]{2,1,0:T(8,128)(2,1)S(1)}, bf16[2,512,512]{2,1,0:T(8,128)(2,1)S(1)}, bf16[2,512,512]{2,1,0:T(8,128...) custom-call(s32[2,128]{1,0:T(2,128)S(1)} %broadcast_in_dim.2.where_r, ...), custom_call_target="tpu_custom_call" | custom-call | flops 800000000 | bytes 1024 | tf_op jit(solution)/shard_map/inverses/pallas_call | solution.py:48
  32.8 8.0 %collective-permute-done.5.refs_2_ = f32[2,128,512]{2,1,0:T(8,128)S(1)} collective-permute-done((f32[2,128,512]{2,1,0:T(8,128)S(1)}, f32[2,128,512]{2,1,0:T(8,128)S(1)}, u32[]{:S(2)}, u32[]{:S(2)}) %collective-permute-start.5) | collective-permute-done | bytes 524320 | tf_op jit(solution)/shard_map/ppermute | solution.py:140
  40.7 1.7 %collective-permute-start.8 = (f32[1,128,512]{2,1,0:T(8,128)S(1)}, f32[1,128,512]{2,1,0:T(8,128)S(1)}, u32[]{:S(2)}, u32[]{:S(2)}) collective-permute-start(f32[1,128,512]{2,1,0:T(8,128)S(1)} %get-tuple-element.86), channel_id=1, source_target_pairs={{0,2},{1,3},{2,0},{3,1},{4,6},{5,7},{6,4},{7,5},{8,10},{9,11},{10,... | collective-permute-start | bytes 786440 | tf_op jit(solution)/shard_map/ppermute | solution.py:140
  42.6 5.9 %early_days.1 = (f32[256,512]{1,0:T(8,128)S(1)}, bf16[2,512,512]{2,1,0:T(8,128)(2,1)S(1)}, bf16[2,512,512]{2,1,0:T(8,128)(2,1)S(1)}, bf16[2,512,512]{2,1,0:T(8,1...) custom-call(s32[2,128]{1,0:T(2,128)S(1)} %broadcast_in_dim.2.where_r, ...), custom_call_target="tpu_custom_call" | custom-call | flops 1200000000 | bytes 1024 | tf_op jit(solution)/shard_map/early_days/pallas_call | solution.py:48
  48.5 0.9 collective-permute-done.8.refs_2_
  49.4 1.7 %collective-permute-start.6 = (f32[136,512]{1,0:T(8,128)S(1)}, f32[136,512]{1,0:T(8,128)S(1)}, u32[]{:S(2)}, u32[]{:S(2)}) collective-permute-start(f32[136,512]{1,0:T(8,128)S(1)} %pack.1), channel_id=1, source_target_pairs={{0,2},{1,3},{2,0},{3,1},{4,6},{5,7},{6,4},{7,5},{8,10},{9,11},{10,... | collective-permute-start | bytes 835592 | tf_op jit(solution)/shard_map/ppermute | solution.py:140
  51.1 2.7 %day_2.1 = (bf16[2,512,512]{2,1,0:T(8,128)(2,1)S(1)}, bf16[2,512,512]{2,1,0:T(8,128)(2,1)S(1)}, f32[128,512]{1,0:T(8,128)S(1)}, f32[128,512]{1,0:T(8,128)S(1)}) custom-call(s32[2,128]{1,0:T(2,128)S(1)} %broadcast_in_dim.2.where_ref, f32[4,128,512]{2,1,0:T(8,128)S(1)} %copy-done.1, f32[4,128,512]{2,1,0:T(8,128)S(1)} %collective-permute-done.refs_1_, ...), custom_call_target="tpu_custom_call" | custom-call | flops 600000000 | bytes 1024 | tf_op jit(solution)/shard_map/day_2/pallas_call | solution.py:48
  53.8 4.7 %collective-permute-done.6.refs_2_.refs_0_ = f32[136,512]{1,0:T(8,128)S(1)} collective-permute-done((f32[136,512]{1,0:T(8,128)S(1)}, f32[136,512]{1,0:T(8,128)S(1)}, u32[]{:S(2)}, u32[]{:S(2)}) %collective-permute-start.6) | collective-permute-done | bytes 278560 | tf_op jit(solution)/shard_map/ppermute | solution.py:140
  58.5 1.7 %collective-permute-start.14 = (f32[128,512]{1,0:T(8,128)S(1)}, f32[128,512]{1,0:T(8,128)S(1)}, u32[]{:S(2)}, u32[]{:S(2)}) collective-permute-start(f32[128,512]{1,0:T(8,128)S(1)} %get-tuple-element.98), channel_id=1, source_target_pairs={{0,4},{4,0},{8,12},{12,8},{16,20},{20,16},{24,28},{28,24},{1,5},{5... | collective-permute-start | bytes 786440 | tf_op jit(solution)/shard_map/ppermute | solution.py:143
  60.2 1.3 %last_link.1 = (f32[512,512]{1,0:T(8,128)S(1)}, f32[256,512]{1,0:T(8,128)S(1)}, bf16[2,512,512]{2,1,0:T(8,128)(2,1)S(1)}) custom-call(s32[2,128]{1,0:T(2,128)S(1)} %broadcast_in_dim.2.where_ref, f32[4,128,512]{2,1,0:T(8,128)S(1)} %copy-done.1, f32[4,128,512]{2,1,0:T(8,128)S(1)} %collective-permute-done.refs_1_, ...), custom_call_target="tpu_custom_call" | custom-call | flops 300000000 | bytes 1024 | tf_op jit(solution)/shard_map/last_link/pallas_call | solution.py:48
  61.5 5.7 %collective-permute-done.14.other_ref = f32[128,512]{1,0:T(8,128)S(1)} collective-permute-done((f32[128,512]{1,0:T(8,128)S(1)}, f32[128,512]{1,0:T(8,128)S(1)}, u32[]{:S(2)}, u32[]{:S(2)}) %collective-permute-start.14) | collective-permute-done | bytes 262176 | tf_op jit(solution)/shard_map/ppermute | solution.py:143
  67.2 1.7 %collective-permute-start.15 = (f32[256,512]{1,0:T(8,128)S(1)}, f32[256,512]{1,0:T(8,128)S(1)}, u32[]{:S(2)}, u32[]{:S(2)}) collective-permute-start(f32[256,512]{1,0:T(8,128)S(1)} %get-tuple-element.103), channel_id=1, source_target_pairs={{0,4},{4,0},{8,12},{12,8},{16,20},{20,16},{24,28},{28,24},{1,5},{5... | collective-permute-start | bytes 1572872 | tf_op jit(solution)/shard_map/ppermute | solution.py:143
  68.9 4.5 %lines.1 = (f32[8,512]{1,0:T(8,128)S(1)}, f32[8,512]{1,0:T(8,128)S(1)}, f32[4,8,512]{2,1,0:T(8,128)S(1)}) custom-call(f32[4,512]{1,0:T(4,128)S(1)} %add.3.source_ref, f32[136,512]{1,0:T(8,128)S(1)} %collective-permute-done.6.refs_2_.refs_0_, bf16[2,512,512]{2,1,0:T(8,128)(2,1)S(1)} %get-tuple-element.91.refs_6_.refs_1_.refs_3_.refs_2_, ...), custom_call_target="tpu_custom_call" | custom-call | flops 1000000000 | bytes 1024 | tf_op jit(solution)/shard_map/lines/pallas_call | solution.py:48
  73.5 0.3 collective-permute-start.16
  73.8 2.7 %grams.1.gram_ref = bf16[2,512,512]{2,1,0:T(8,128)(2,1)S(1)} custom-call(f32[512,512]{1,0:T(8,128)S(1)} %get-tuple-element.112.gram_ref, bf16[2,512,512]{2,1,0:T(8,128)(2,1)S(1)} %get-tuple-element.106.refs_6_.refs_0_.refs_5_, bf16[2,512,512]{2,1,0:T(8,128)(2,1)S(1)} %get-tuple-element.97.refs_7_.refs_9_.refs_1_.refs_8_, ...), custom_call_target="tpu_custom_call" | custom-call | flops 600000000 | bytes 1024 | tf_op jit(solution)/shard_map/grams/pallas_call | solution.py:48
  76.5 1.8 %late_maps.1 = (bf16[2,512,512]{2,1,0:T(8,128)(2,1)S(1)}, bf16[2,512,512]{2,1,0:T(8,128)(2,1)S(1)}) custom-call(bf16[2,512,512]{2,1,0:T(8,128)(2,1)S(1)} %get-tuple-element.113.refs_8_.refs_7_.refs_0_, bf16[2,512,512]{2,1,0:T(8,128)(2,1)S(1)} %get-tuple-element.96.refs_5_.refs_10_.refs_1_, bf16[2,512,512]{2,1,0:T(8,128)(2,1)S(1)} %get-tuple-element.107.refs_8_.refs_2_, ...), custom_call_target="tpu_custom_call" | custom-call | flops 400000000 | bytes 1024 | tf_op jit(solution)/shard_map/late_maps/pallas_call | solution.py:48
  78.3 2.8 %collective-permute-done.16.other_flux_ref = f32[8,512]{1,0:T(8,128)S(1)} collective-permute-done((f32[8,512]{1,0:T(8,128)S(1)}, f32[8,512]{1,0:T(8,128)S(1)}, u32[]{:S(2)}, u32[]{:S(2)}) %collective-permute-start.16) | collective-permute-done | bytes 16416 | tf_op jit(solution)/shard_map/ppermute | solution.py:143
  81.1 1.9 %collective-permute-done.17.rest_ref = f32[256,512]{1,0:T(8,128)S(1)} collective-permute-done((f32[256,512]{1,0:T(8,128)S(1)}, f32[256,512]{1,0:T(8,128)S(1)}, u32[]{:S(2)}, u32[]{:S(2)}) %collective-permute-start.17) | collective-permute-done | bytes 524320 | tf_op jit(solution)/shard_map/ppermute | solution.py:140
  83.1 1.1 pair_maps.1
  84.1 0.7 collective-permute-start.18
  84.8 3.7 %collective-permute-start.19 = (f32[8,512]{1,0:T(8,128)S(1)}, f32[8,512]{1,0:T(8,128)S(1)}, u32[]{:S(2)}, u32[]{:S(2)}) collective-permute-start(f32[8,512]{1,0:T(8,128)S(1)} %get-tuple-element.121.local_ref), channel_id=1, source_target_pairs={{0,8},{4,12},{1,9},{5,13},{2,10},{6,14},{3,11},{7,15}} | collective-permute-start | bytes 49160 | tf_op jit(solution)/shard_map/ppermute | solution.py:146
  88.5 1.0 group_map.1.map_ref
  89.5 0.4 collective-permute-done.19.refs_0_
  89.9 0.5 forward_link.2
  90.4 0.7 collective-permute-start.20
  91.1 0.5 forward_link.3
  91.6 0.7 collective-permute-start.22
  92.3 0.4 noise_link.2
  92.7 1.1 mean_turn.1
  93.8 1.5 %collective-permute-start.23 = (f32[16,512]{1,0:T(8,128)S(1)}, f32[16,512]{1,0:T(8,128)S(1)}, u32[]{:S(2)}, u32[]{:S(2)}) collective-permute-start(f32[16,512]{1,0:T(8,128)S(1)} %pad_maximum_fusion), channel_id=1, source_target_pairs={{0,4},{4,0},{8,12},{12,8},{16,20},{20,16},{24,28},{28,24},{1,5},{5... | collective-permute-start | bytes 98312 | tf_op jit(solution)/shard_map/ppermute | solution.py:143
  95.3 0.7 collective-permute-start.21
  96.0 0.7 collective-permute-start.25
  96.7 0.7 collective-permute-start.24
  97.4 0.4 collective-permute-done.23
  97.7 0.3 first_back.1
  98.1 0.4 noise_link.3
  98.5 1.3 %collective-permute-start.26 = (f32[128,512]{1,0:T(8,128)S(1)}, f32[128,512]{1,0:T(8,128)S(1)}, u32[]{:S(2)}, u32[]{:S(2)}) collective-permute-start(f32[128,512]{1,0:T(8,128)S(1)} %noise_link.3), channel_id=1, source_target_pairs={{8,0},{12,4},{9,1},{13,5},{10,2},{14,6},{11,3},{15,7}} | collective-permute-start | bytes 786440 | tf_op jit(solution)/shard_map/ppermute | solution.py:146
  99.8 0.7 collective-permute-start.27
  100.4 0.3 backward_link.1
  100.8 14.5 %collective-permute-done.26.refs_2_ = f32[128,512]{1,0:T(8,128)S(1)} collective-permute-done((f32[128,512]{1,0:T(8,128)S(1)}, f32[128,512]{1,0:T(8,128)S(1)}, u32[]{:S(2)}, u32[]{:S(2)}) %collective-permute-start.26) | collective-permute-done | bytes 262176 | tf_op jit(solution)/shard_map/ppermute | solution.py:146
  115.2 0.4 divide.1
  115.6 0.6 collective-permute-start.28
  116.2 1.3 %collective-permute-start.29 = (f32[8,512]{1,0:T(8,128)S(1)}, f32[8,512]{1,0:T(8,128)S(1)}, u32[]{:S(2)}, u32[]{:S(2)}) collective-permute-start(f32[8,512]{1,0:T(8,128)S(1)} %backward_link.1), channel_id=1, source_target_pairs={{8,0},{12,4},{9,1},{13,5},{10,2},{14,6},{11,3},{15,7}} | collective-permute-start | bytes 49160 | tf_op jit(solution)/shard_map/ppermute | solution.py:146
  117.5 3.1 %mean_terms.1 = (f32[256,512]{1,0:T(8,128)S(1)}, f32[256,512]{1,0:T(8,128)S(1)}, f32[256,512]{1,0:T(8,128)S(1)}, f32[256,512]{1,0:T(8,128)S(1)}) custom-call(f32[8,512]{1,0:T(8,128)S(1)} %get-tuple-element.142.entering_ref, f32[4,8,512]{2,1,0:T(8,128)S(1)} %get-tuple-element.143.current_ref, f32[256,512]{1,0:T(8,128)S(1)} %get-tuple-element.90.refs_5_.refs_0_, ...), custom_call_target="tpu_custom_call" | custom-call | flops 800000000 | bytes 1024 | tf_op jit(solution)/shard_map/mean_terms/pallas_call | solution.py:48
  120.6 1.2 collective-permute-done.29.refs_3_
  121.8 0.3 collective-permute-done.28.got_ref
  122.1 3.4 %last_days.1 = f32[4,512,256]{2,1,0:T(8,128)} custom-call(s32[2,128]{1,0:T(2,128)S(1)} %broadcast_in_dim.2.where_ref, f32[128,512]{1,0:T(8,128)S(1)} %get-tuple-element.138.keep_ref, f32[128,512]{1,0:T(8,128)S(1)} %collective-permute-done.28.got_ref, f32[8,512]{1,0:T(8,128)S(1)} %get-tuple-element.140.back_ref, ...), custom_call_target="tpu_custom_call" | custom-call | flops 800000000 | bytes 1024 | tf_op jit(solution)/shard_map/last_days/pallas_call | solution.py:48
  (36 shorter events, 0.8 us)
Async XLA Ops:
  0.0 19.1 %copy-start.2 = (f32[4,128,512]{2,1,0:T(8,128)S(1)}, f32[4,128,512]{2,1,0:T(8,128)}, u32[]{:S(2)}) copy-start(f32[4,128,512]{2,1,0:T(8,128)} %refs_0_.4) | copy-start | bytes 3145732
  0.0 10.3 %copy-start.1 = (f32[4,128,512]{2,1,0:T(8,128)S(1)}, f32[4,128,512]{2,1,0:T(8,128)}, u32[]{:S(2)}) copy-start(f32[4,128,512]{2,1,0:T(8,128)} %refs_0_.7) | copy-start | bytes 3145732
  0.0 26.4 %collective-permute-start.7 = (f32[4,128,512]{2,1,0:T(8,128)}, f32[4,128,512]{2,1,0:T(8,128)S(1)}, u32[]{:S(2)}, u32[]{:S(2)}) collective-permute-start(f32[4,128,512]{2,1,0:T(8,128)} %refs_0_.4), channel_id=1, source_target_pairs={{0,2},{1,3},{2,0},{3,1},{4,6},{5,7},{6,4},{7,5},{8,10},{9,11},{10,... | collective-permute-start | bytes 3145736 | tf_op jit(solution)/shard_map/ppermute | solution.py:140
  5.3 23.8 %copy-start = (f32[4,512,256]{2,1,0:T(8,128)S(1)}, f32[4,512,256]{2,1,0:T(8,128)}, u32[]{:S(2)}) copy-start(f32[4,512,256]{2,1,0:T(8,128)} %refs_4_.5) | copy-start | bytes 6291460
  6.6 4.9 %collective-permute-start.1 = (f32[16,512]{1,0:T(8,128)S(1)}, f32[16,512]{1,0:T(8,128)S(1)}, u32[]{:S(2)}, u32[]{:S(2)}) collective-permute-start(f32[16,512]{1,0:T(8,128)S(1)} %get-tuple-element.80), channel_id=1, source_target_pairs={{0,16},{4,20},{8,24},{12,28},{16,0},{20,4},{24,8},{28,12},{1,17},{... | collective-permute-start | bytes 98312 | tf_op jit(solution)/shard_map/ppermute | solution.py:183
  11.5 3.8 %collective-permute-start.2 = (f32[8,512]{1,0:T(8,128)S(1)}, f32[8,512]{1,0:T(8,128)S(1)}, u32[]{:S(2)}, u32[]{:S(2)}) collective-permute-start(f32[8,512]{1,0:T(8,128)S(1)} %get-tuple-element.82), channel_id=1, source_target_pairs={{0,8},{4,12},{8,0},{12,4},{16,24},{20,28},{24,16},{28,20},{1,9},{5... | collective-permute-start | bytes 49160 | tf_op jit(solution)/shard_map/ppermute | solution.py:183
  15.4 3.7 %collective-permute-start.3 = (f32[4,512]{1,0:T(4,128)S(1)}, f32[4,512]{1,0:T(4,128)S(1)}, u32[]{:S(2)}, u32[]{:S(2)}) collective-permute-start(f32[4,512]{1,0:T(4,128)S(1)} %get-tuple-element.84), channel_id=1, source_target_pairs={{0,4},{4,0},{8,12},{12,8},{16,20},{20,16},{24,28},{28,24},{1,5},{5... | collective-permute-start | bytes 24584 | tf_op jit(solution)/shard_map/ppermute | solution.py:183
  19.1 1.2 collective-permute-start.4
  19.1 9.2 %collective-permute-start.9 = (f32[4,128,512]{2,1,0:T(8,128)S(1)}, f32[4,128,512]{2,1,0:T(8,128)S(1)}, u32[]{:S(2)}, u32[]{:S(2)}) collective-permute-start(f32[4,128,512]{2,1,0:T(8,128)S(1)} %copy-done.2), channel_id=1, source_target_pairs={{0,1},{1,0},{2,3},{3,2},{4,5},{5,4},{6,7},{7,6},{8,9},{9,8},{10,11... | collective-permute-start | bytes 3145736 | tf_op jit(solution)/shard_map/ppermute | solution.py:140
  26.4 2.7 %collective-permute-start.10 = (f32[4,128,512]{2,1,0:T(8,128)S(1)}, f32[4,128,512]{2,1,0:T(8,128)S(1)}, u32[]{:S(2)}, u32[]{:S(2)}) collective-permute-start(f32[4,128,512]{2,1,0:T(8,128)S(1)} %collective-permute-done.7.refs_2_), channel_id=1, source_target_pairs={{0,1},{1,0},{2,3},{3,2},{4,5},{5,4},{6,7},{7,6},{8,9},{9,8},{10,11... | collective-permute-start | bytes 3145736 | tf_op jit(solution)/shard_map/ppermute | solution.py:140
  26.4 14.3 %collective-permute-start.5 = (f32[2,128,512]{2,1,0:T(8,128)S(1)}, f32[2,128,512]{2,1,0:T(8,128)S(1)}, u32[]{:S(2)}, u32[]{:S(2)}) collective-permute-start(f32[2,128,512]{2,1,0:T(8,128)S(1)} %slice.15), channel_id=1, source_target_pairs={{0,2},{1,3},{2,0},{3,1},{4,6},{5,7},{6,4},{7,5},{8,10},{9,11},{10,... | collective-permute-start | bytes 1572872 | tf_op jit(solution)/shard_map/ppermute | solution.py:140
  28.1 14.3 %collective-permute-start = (f32[4,128,512]{2,1,0:T(8,128)S(1)}, f32[4,128,512]{2,1,0:T(8,128)S(1)}, u32[]{:S(2)}, u32[]{:S(2)}) collective-permute-start(f32[4,128,512]{2,1,0:T(8,128)S(1)} %copy-done.1), channel_id=1, source_target_pairs={{0,1},{1,0},{2,3},{3,2},{4,5},{5,4},{6,7},{7,6},{8,9},{9,8},{10,11... | collective-permute-start | bytes 3145736 | tf_op jit(solution)/shard_map/ppermute | solution.py:140
  40.7 1.9 %collective-permute-start.11 = (f32[2,128,512]{2,1,0:T(8,128)S(1)}, f32[2,128,512]{2,1,0:T(8,128)S(1)}, u32[]{:S(2)}, u32[]{:S(2)}) collective-permute-start(f32[2,128,512]{2,1,0:T(8,128)S(1)} %collective-permute-done.5.refs_2_), channel_id=1, source_target_pairs={{0,1},{1,0},{2,3},{3,2},{4,5},{5,4},{6,7},{7,6},{8,9},{9,8},{10,11... | collective-permute-start | bytes 1572872 | tf_op jit(solution)/shard_map/ppermute | solution.py:140
  40.7 8.7 %collective-permute-start.8 = (f32[1,128,512]{2,1,0:T(8,128)S(1)}, f32[1,128,512]{2,1,0:T(8,128)S(1)}, u32[]{:S(2)}, u32[]{:S(2)}) collective-permute-start(f32[1,128,512]{2,1,0:T(8,128)S(1)} %get-tuple-element.86), channel_id=1, source_target_pairs={{0,2},{1,3},{2,0},{3,1},{4,6},{5,7},{6,4},{7,5},{8,10},{9,11},{10,... | collective-permute-start | bytes 786440 | tf_op jit(solution)/shard_map/ppermute | solution.py:140
  49.4 1.7 %collective-permute-start.12 = (f32[1,128,512]{2,1,0:T(8,128)S(1)}, f32[1,128,512]{2,1,0:T(8,128)S(1)}, u32[]{:S(2)}, u32[]{:S(2)}) collective-permute-start(f32[1,128,512]{2,1,0:T(8,128)S(1)} %collective-permute-done.8.refs_2_), channel_id=1, source_target_pairs={{0,1},{1,0},{2,3},{3,2},{4,5},{5,4},{6,7},{7,6},{8,9},{9,8},{10,11... | collective-permute-start | bytes 786440 | tf_op jit(solution)/shard_map/ppermute | solution.py:140
  49.4 9.1 %collective-permute-start.6 = (f32[136,512]{1,0:T(8,128)S(1)}, f32[136,512]{1,0:T(8,128)S(1)}, u32[]{:S(2)}, u32[]{:S(2)}) collective-permute-start(f32[136,512]{1,0:T(8,128)S(1)} %pack.1), channel_id=1, source_target_pairs={{0,2},{1,3},{2,0},{3,1},{4,6},{5,7},{6,4},{7,5},{8,10},{9,11},{10,... | collective-permute-start | bytes 835592 | tf_op jit(solution)/shard_map/ppermute | solution.py:140
  58.5 1.7 %collective-permute-start.13 = (f32[136,512]{1,0:T(8,128)S(1)}, f32[136,512]{1,0:T(8,128)S(1)}, u32[]{:S(2)}, u32[]{:S(2)}) collective-permute-start(f32[136,512]{1,0:T(8,128)S(1)} %collective-permute-done.6.refs_2_.refs_0_), channel_id=1, source_target_pairs={{0,1},{1,0},{2,3},{3,2},{4,5},{5,4},{6,7},{7,6},{8,9},{9,8},{10,11... | collective-permute-start | bytes 835592 | tf_op jit(solution)/shard_map/ppermute | solution.py:140
  58.5 8.7 %collective-permute-start.14 = (f32[128,512]{1,0:T(8,128)S(1)}, f32[128,512]{1,0:T(8,128)S(1)}, u32[]{:S(2)}, u32[]{:S(2)}) collective-permute-start(f32[128,512]{1,0:T(8,128)S(1)} %get-tuple-element.98), channel_id=1, source_target_pairs={{0,4},{4,0},{8,12},{12,8},{16,20},{20,16},{24,28},{28,24},{1,5},{5... | collective-permute-start | bytes 786440 | tf_op jit(solution)/shard_map/ppermute | solution.py:143
  67.2 13.9 %collective-permute-start.15 = (f32[256,512]{1,0:T(8,128)S(1)}, f32[256,512]{1,0:T(8,128)S(1)}, u32[]{:S(2)}, u32[]{:S(2)}) collective-permute-start(f32[256,512]{1,0:T(8,128)S(1)} %get-tuple-element.103), channel_id=1, source_target_pairs={{0,4},{4,0},{8,12},{12,8},{16,20},{20,16},{24,28},{28,24},{1,5},{5... | collective-permute-start | bytes 1572872 | tf_op jit(solution)/shard_map/ppermute | solution.py:143
  73.5 7.7 %collective-permute-start.16 = (f32[8,512]{1,0:T(8,128)S(1)}, f32[8,512]{1,0:T(8,128)S(1)}, u32[]{:S(2)}, u32[]{:S(2)}) collective-permute-start(f32[8,512]{1,0:T(8,128)S(1)} %get-tuple-element.109.flux_ref), channel_id=1, source_target_pairs={{0,4},{4,0},{8,12},{12,8},{16,20},{20,16},{24,28},{28,24},{1,5},{5... | collective-permute-start | bytes 49160 | tf_op jit(solution)/shard_map/ppermute | solution.py:143
  81.1 1.9 %collective-permute-start.17 = (f32[256,512]{1,0:T(8,128)S(1)}, f32[256,512]{1,0:T(8,128)S(1)}, u32[]{:S(2)}, u32[]{:S(2)}) collective-permute-start(f32[256,512]{1,0:T(8,128)S(1)} %collective-permute-done.15.half_ref), channel_id=1, source_target_pairs={{0,1},{1,0},{2,3},{3,2},{4,5},{5,4},{6,7},{7,6},{8,9},{9,8},{10,11... | collective-permute-start | bytes 1572872 | tf_op jit(solution)/shard_map/ppermute | solution.py:140
  84.1 8.2 %collective-permute-start.18 = (f32[128,512]{1,0:T(8,128)S(1)}, f32[128,512]{1,0:T(8,128)S(1)}, u32[]{:S(2)}, u32[]{:S(2)}) collective-permute-start(f32[128,512]{1,0:T(8,128)S(1)} %get-tuple-element.122.local_ref), channel_id=1, source_target_pairs={{24,16},{28,20},{25,17},{29,21},{26,18},{30,22},{27,19},{31,23}} | collective-permute-start | bytes 786440 | tf_op jit(solution)/shard_map/ppermute | solution.py:146
  84.8 5.1 %collective-permute-start.19 = (f32[8,512]{1,0:T(8,128)S(1)}, f32[8,512]{1,0:T(8,128)S(1)}, u32[]{:S(2)}, u32[]{:S(2)}) collective-permute-start(f32[8,512]{1,0:T(8,128)S(1)} %get-tuple-element.121.local_ref), channel_id=1, source_target_pairs={{0,8},{4,12},{1,9},{5,13},{2,10},{6,14},{3,11},{7,15}} | collective-permute-start | bytes 49160 | tf_op jit(solution)/shard_map/ppermute | solution.py:146
  90.4 0.7 collective-permute-start.20
  91.6 1.1 collective-permute-start.22
  93.8 3.9 %collective-permute-start.23 = (f32[16,512]{1,0:T(8,128)S(1)}, f32[16,512]{1,0:T(8,128)S(1)}, u32[]{:S(2)}, u32[]{:S(2)}) collective-permute-start(f32[16,512]{1,0:T(8,128)S(1)} %pad_maximum_fusion), channel_id=1, source_target_pairs={{0,4},{4,0},{8,12},{12,8},{16,20},{20,16},{24,28},{28,24},{1,5},{5... | collective-permute-start | bytes 98312 | tf_op jit(solution)/shard_map/ppermute | solution.py:143
  95.3 2.7 %collective-permute-start.21 = (f32[128,512]{1,0:T(8,128)S(1)}, f32[128,512]{1,0:T(8,128)S(1)}, u32[]{:S(2)}, u32[]{:S(2)}) collective-permute-start(f32[128,512]{1,0:T(8,128)S(1)} %noise_link.2), channel_id=1, source_target_pairs={{16,8},{20,12},{17,9},{21,13},{18,10},{22,14},{19,11},{23,15}} | collective-permute-start | bytes 786440 | tf_op jit(solution)/shard_map/ppermute | solution.py:146
  96.0 1.7 %collective-permute-start.25 = (f32[8,512]{1,0:T(8,128)S(1)}, f32[8,512]{1,0:T(8,128)S(1)}, u32[]{:S(2)}, u32[]{:S(2)}) collective-permute-start(f32[8,512]{1,0:T(8,128)S(1)} %get-tuple-element.131.part_ref), channel_id=1, source_target_pairs={{24,20},{28,16},{25,21},{29,17},{26,22},{30,18},{27,23},{31,19}} | collective-permute-start | bytes 49160 | tf_op jit(solution)/shard_map/ppermute | solution.py:472
  96.7 1.1 collective-permute-start.24
  98.5 16.8 %collective-permute-start.26 = (f32[128,512]{1,0:T(8,128)S(1)}, f32[128,512]{1,0:T(8,128)S(1)}, u32[]{:S(2)}, u32[]{:S(2)}) collective-permute-start(f32[128,512]{1,0:T(8,128)S(1)} %noise_link.3), channel_id=1, source_target_pairs={{8,0},{12,4},{9,1},{13,5},{10,2},{14,6},{11,3},{15,7}} | collective-permute-start | bytes 786440 | tf_op jit(solution)/shard_map/ppermute | solution.py:146
  99.8 0.7 collective-permute-start.27
  115.6 6.4 %collective-permute-start.28 = (f32[128,512]{1,0:T(8,128)S(1)}, f32[128,512]{1,0:T(8,128)S(1)}, u32[]{:S(2)}, u32[]{:S(2)}) collective-permute-start(f32[128,512]{1,0:T(8,128)S(1)} %get-tuple-element.139), channel_id=1, source_target_pairs={{0,4},{4,0},{8,12},{12,8},{16,20},{20,16},{24,28},{28,24},{1,5},{5... | collective-permute-start | bytes 786440 | tf_op jit(solution)/shard_map/ppermute | solution.py:143
  116.2 5.6 %collective-permute-start.29 = (f32[8,512]{1,0:T(8,128)S(1)}, f32[8,512]{1,0:T(8,128)S(1)}, u32[]{:S(2)}, u32[]{:S(2)}) collective-permute-start(f32[8,512]{1,0:T(8,128)S(1)} %backward_link.1), channel_id=1, source_target_pairs={{8,0},{12,4},{9,1},{13,5},{10,2},{14,6},{11,3},{15,7}} | collective-permute-start | bytes 49160 | tf_op jit(solution)/shard_map/ppermute | solution.py:146

commit v6 on v5

--- a/solution.py
+++ b/solution.py
@@ -168,15 +168,22 @@
     def shared(arrived, *ahead):
         return [piece for got in arrived for piece in (got, to_row(after(got, *ahead), 1))]
 
-    early_rows = coupling[:early]
-    late_rows = [coupling[day : day + 1] for day in range(early, day_count)]
-    got_inverses = over_chips(inv_diag)
-    got_links = [over_chips(early_rows)]
-    for index, rows in enumerate(late_rows[:-1]):
-        got_links.append(over_chips(after(rows, *(got_inverses, *got_links)[index])))
+    arrived = []
+
+    def send_rows(*rows):
+        for piece in rows:
+            if len(arrived) >= 2:
+                piece = after(piece, *arrived[len(arrived) - 2][-1])
+            pieces.append(over_chips(piece))
+        arrived.append(pieces[-len(rows) :])
+
+    pieces = []
+    link_rows = [coupling[day : day + 1] for day in range(day_count)]
+    for rows in (inv_diag, *link_rows[:-1]):
+        send_rows(rows)
     own_inverse = [inv_diag, to_row(inv_diag, 1)]
     own_link = [coupling, to_row(coupling, 1)]
-    where = after(where, keep, early_rows, *late_rows)
+    where = after(where, keep, *link_rows)
 
     distance = part_count // 2
     while distance:
@@ -185,23 +192,31 @@
         keep, sent = halved(where, distance, keep, got)
     right_side = keep + to_row(keep, 1)
 
-    def pack_body(rows_ref, source_ref, out_ref):
-        out_ref[:share, :] = rows_ref[0]
-        out_ref[share:, :] = jnp.zeros((LINES, nodes), F32)
-        out_ref[share : share + day_count, :] = source_ref[...]
+    first_rows = share // 2
+
+    def pack_body(rows_ref, source_ref, first_out, rest_out):
+        first_out[...] = rows_ref[0, :first_rows, :]
+        rest_out[: share - first_rows, :] = rows_ref[0, first_rows:, :]
+        rest_out[share - first_rows :, :] = jnp.zeros((LINES, nodes), F32)
+        rest_out[share - first_rows : share - first_rows + day_count, :] = source_ref[...]
 
     packed = call(
-        pack_body, shape(share + LINES, nodes), "pack", (), [late_rows[-1], right_side], work=0.1
-    )
-    got_links.append(over_chips(after(packed, *(got_inverses, *got_links)[late - 1])))
+        pack_body,
+        (shape(first_rows, nodes), shape(share - first_rows + LINES, nodes)),
+        "pack",
+        (),
+        [link_rows[-1], right_side],
+        work=0.1,
+    )
+    send_rows(*packed)
+    got_inverses, got_links = pieces[0], pieces[1:]
 
     def store(out_ref, pair):
         out_ref[0], out_ref[1] = pair
 
     def inverses_body(where_ref, *refs):
-        row_refs, noise_ref, gram_out, outs = (
-            refs[:row_count], refs[row_count], refs[row_count + 1], refs[row_count + 2 :],
-        )
+        row_refs, refs = refs[:row_count], refs[row_count:]
+        noise_ref, gram_out, outs = refs[0], refs[1], refs[2:]
         for day in range(day_count):
             gather_rows(where_ref, row_refs, lambda offset: day, outs[day])
             outs[day_count + day][...] = dot_parts(
@@ -214,19 +229,24 @@
         [square, *[map_parts] * day_count, *[samples_full] * day_count],
         "inverses",
         (where,),
-        [*own_inverse, *shared(got_inverses, where, packed), noise],
+        [*own_inverse, *shared(got_inverses, where, *packed), noise],
         work=4,
     )
     inverses, local_terms = results[:day_count], results[day_count:]
 
     def early_body(where_ref, *refs):
-        own_refs, got_refs, refs = refs[:CORES], refs[CORES:row_count], refs[row_count:]
+        own_refs, refs = refs[:CORES], refs[CORES:]
+        count = row_count - CORES
+        got_refs, refs = refs[: count * early], refs[count * early :]
         noise_ref, term_ref, refs = refs[0], refs[1], refs[2:]
         inverse_refs, refs = refs[: early + 1], refs[early + 1 :]
         sum_out, *outs = refs
         link_outs, moved_outs, map_outs = outs[:early], outs[early : 2 * early], outs[2 * early :]
         for day in range(early):
-            gather_rows(where_ref, (*own_refs, *got_refs), lambda offset: day, link_outs[day])
+            row_refs = (*own_refs, *got_refs[count * day : count * (day + 1)])
+            gather_rows(
+                where_ref, row_refs, lambda offset: day if offset < CORES else 0, link_outs[day]
+            )
         total = term_ref[...]
         moved = parts(inverse_refs[0])
         for day in range(early):
@@ -246,7 +266,11 @@
         [samples_full, *[map_parts] * (3 * early)],
         "early_days",
         (where,),
-        [*own_link, *shared(got_links[0], gram), noise, local_terms[0], *inverses[: early + 1]],
+        [
+            *own_link,
+            *(piece for got in got_links[:early] for piece in shared(got, gram)),
+            noise, local_terms[0], *inverses[: early + 1],
+        ],
         work=6,
     )
     links, step_maps = list(results[:early]), list(results[2 * early :])
@@ -277,7 +301,7 @@
             f"day_{day}",
             (where,),
             [
-                *own_link, *shared(got_links[1 + day - early], summed), noise, inverses[day + 1],
+                *own_link, *shared(got_links[day], summed), noise, inverses[day + 1],
                 summed, moveds[day],
             ],
             work=3,
@@ -289,14 +313,22 @@
     other_sum = to_pair(send)
 
     def last_link_body(where_ref, *refs):
-        own_refs, got_refs, refs = refs[:CORES], refs[CORES:row_count], refs[row_count:]
+        own_refs, refs = refs[:CORES], refs[CORES:]
+        count = row_count - CORES
+        first_refs, rest_refs, refs = refs[:count], refs[count : 2 * count], refs[2 * count :]
         moved_ref, whole_out, half_out, link_out = refs
-        gather_rows(
-            where_ref,
-            (*own_refs, *(ref.at[pl.ds(0, share)] for ref in got_refs)),
-            lambda offset: day_count - 1,
-            link_out,
-        )
+        rest_refs = [ref.at[pl.ds(0, share - first_rows)] for ref in rest_refs]
+        pairs = [
+            (ref.at[day_count - 1, pl.ds(0, first_rows)], ref.at[day_count - 1, pl.ds(first_rows, share - first_rows)])
+            for ref in own_refs
+        ] + list(zip(first_refs, rest_refs, strict=True))
+        for offset, pair in enumerate(pairs):
+            for ref, start, size in zip(
+                pair, (0, first_rows), (first_rows, share - first_rows), strict=True
+            ):
+                start = (where_ref[0, 0] ^ offset) * share + start
+                at = pl.ds(pl.multiple_of(start, first_rows), size)
+                link_out[0, at, :], link_out[1, at, :] = split(ref[...])
         whole_out[...] = -dot_parts(parts(link_out), parts(moved_ref), NN)
         half_out[...] = whole_out[
             pl.ds(pl.multiple_of((where_ref[0, 0] & (CORES - 1)) * half_nodes, half_nodes), half_nodes), :
@@ -307,7 +339,7 @@
         (square, shape(half_nodes, nodes), map_parts),
         "last_link",
         (where,),
-        [*own_link, *shared(got_links[-1], send), moveds[-1]],
+        [*own_link, *shared(got_links[-2], send), *shared(got_links[-1], send), moveds[-1]],
         work=1.5,
     )
     links.append(link)
@@ -318,7 +350,7 @@
         flux_out, back_out, current_out = refs[-3:]
         source = source_ref[...]
         for ref in got_refs:
-            source = source + ref[share : share + day_count, :]
+            source = source + ref[share - first_rows : share - first_rows + day_count, :]
         applied = jnp.zeros((LINES, nodes), F32)
         back = applied
         for day in range(day_count):

time: 126 us -> 121 us (0.960)
  waiting for transfers between devices: 54 us -> 45.5 us
  starting transfers between devices: 31.3 us -> 33 us
    ppermute x5, waiting for transfers between devices: 9.22 us -> 4.19 us  [to_pair(): return lax.ppermute(value, 'tm', [(i, i ^ 1) for i in range(part_count)])]
    ppermute x12 -> x16, waiting for transfers between devices: 23.2 us -> 18.8 us  [to_row(): lax.ppermute(value, 'row', [(i, i ^ distance) for i in range(row_count)])]
    ppermute x12 -> x16, starting transfers between devices: 8.71 us -> 10.3 us  [to_row(): lax.ppermute(value, 'row', [(i, i ^ distance) for i in range(row_count)])]
  transfers between devices with their start and end apart: 30 -> 34, of which waited for: 18 -> 19; matrix products, arithmetic and copies ran while one was open for 3% -> 2% of each run, Pallas kernels for 24% -> 26%
where the time goes in v6:
time: 121 us; the launch traced here: 120 us
  waiting for transfers between devices  45.5 us (38%)
  Pallas kernels  37.6 us (31%)
  starting transfers between devices  33 us (27%)
  local copies, waits for them, and re-layouts  3.55 us (3%)
    pallas_call x24, Pallas kernels, call(): pl.pallas_call(body, out_shape=out_shape, in_specs=[vmem] * (len(scalars)...  37.6 us
    ppermute x16, waiting for transfers between devices, to_row(): lax.ppermute(value, 'row', [(i, i ^ distance) for i in range(row_count)])  18.8 us
    ppermute x8, waiting for transfers between devices, to_group(): lax.ppermute(value, 'tm', [(PAIR * source + i, PAIR * target + i) for i i...  16.1 us
    ppermute x16, starting transfers between devices, to_row(): lax.ppermute(value, 'row', [(i, i ^ distance) for i in range(row_count)])  10.3 us
    ppermute x8, starting transfers between devices, to_group(): lax.ppermute(value, 'tm', [(PAIR * source + i, PAIR * target + i) for i i...  9.6 us
    ppermute x3, waiting for transfers between devices, local(): lax.ppermute(sent, 'tm', [(i, i ^ distance) for i in range(part_count)])  6.42 us
    ppermute x5, starting transfers between devices, to_pair(): return lax.ppermute(value, 'tm', [(i, i ^ 1) for i in range(part_count)])  5.97 us
    ppermute x3, starting transfers between devices, local(): lax.ppermute(sent, 'tm', [(i, i ^ distance) for i in range(part_count)])  5.86 us
  transfers between devices with their start and end apart: 34, of which 19 were waited for; matrix products, arithmetic and copies ran while one was open for 2% of the time, Pallas kernels for 26%

profile of v6, /device:TPU:0, one launch (start us, length us, event | category | flops | bytes accessed | tf_op | source)
XLA Modules:
  0.0 120.2 jit_solution(14956847437791318524)
XLA Ops:
  0.0 2.9 %collective-permute-start.5 = (f32[4,128,512]{2,1,0:T(8,128)}, f32[4,128,512]{2,1,0:T(8,128)}, u32[]{:S(2)}, u32[]{:S(2)}) collective-permute-start(f32[4,128,512]{2,1,0:T(8,128)} %refs_0_.4), channel_id=1, source_target_pairs={{0,2},{1,3},{2,0},{3,1},{4,6},{5,7},{6,4},{7,5},{8,10},{9,11},{10,... | collective-permute-start | bytes 3145736 | tf_op jit(solution)/shard_map/ppermute | solution.py:140
  2.9 0.7 reshape.10.day_ref
  3.7 0.7 reshape.11.node_ref
  4.4 0.7 reshape.12.value_ref
  5.3 1.4 %bin_observations.1 = (f32[16,512]{1,0:T(8,128)S(1)}, f32[16,512]{1,0:T(8,128)S(1)}) custom-call(s32[2,128]{1,0:T(2,128)S(1)} %broadcast_in_dim.2.where_ref, s32[8,512]{1,0:T(8,128)S(1)} %reshape.10.day_ref, s32[8,512]{1,0:T(8,128)S(1)} %reshape.11.node_ref, f32[8,512]{1,0:T(8,128)S(1)} %reshape.12.value_ref), custom_call_target="tpu_custom_call" | custom-call | flops 400000000 | bytes 1024 | tf_op jit(solution)/shard_map/bin_observations/pallas_call | solution.py:48
  6.6 2.6 %collective-permute-start.1 = (f32[16,512]{1,0:T(8,128)S(1)}, f32[16,512]{1,0:T(8,128)S(1)}, u32[]{:S(2)}, u32[]{:S(2)}) collective-permute-start(f32[16,512]{1,0:T(8,128)S(1)} %get-tuple-element.86), channel_id=1, source_target_pairs={{0,16},{4,20},{8,24},{12,28},{16,0},{20,4},{24,8},{28,12},{1,17},{... | collective-permute-start | bytes 98312 | tf_op jit(solution)/shard_map/ppermute | solution.py:190
  9.4 2.1 %collective-permute-done.1.got_ref = f32[16,512]{1,0:T(8,128)S(1)} collective-permute-done((f32[16,512]{1,0:T(8,128)S(1)}, f32[16,512]{1,0:T(8,128)S(1)}, u32[]{:S(2)}, u32[]{:S(2)}) %collective-permute-start.1) | collective-permute-done | bytes 32800 | tf_op jit(solution)/shard_map/ppermute | solution.py:190
  11.5 1.6 %collective-permute-start.2 = (f32[8,512]{1,0:T(8,128)S(1)}, f32[8,512]{1,0:T(8,128)S(1)}, u32[]{:S(2)}, u32[]{:S(2)}) collective-permute-start(f32[8,512]{1,0:T(8,128)S(1)} %get-tuple-element.88), channel_id=1, source_target_pairs={{0,8},{4,12},{8,0},{12,4},{16,24},{20,28},{24,16},{28,20},{1,9},{5... | collective-permute-start | bytes 49160 | tf_op jit(solution)/shard_map/ppermute | solution.py:190
  13.2 2.2 %collective-permute-done.2.got_ref = f32[8,512]{1,0:T(8,128)S(1)} collective-permute-done((f32[8,512]{1,0:T(8,128)S(1)}, f32[8,512]{1,0:T(8,128)S(1)}, u32[]{:S(2)}, u32[]{:S(2)}) %collective-permute-start.2) | collective-permute-done | bytes 16416 | tf_op jit(solution)/shard_map/ppermute | solution.py:190
  15.4 1.6 %collective-permute-start.3 = (f32[4,512]{1,0:T(4,128)S(1)}, f32[4,512]{1,0:T(4,128)S(1)}, u32[]{:S(2)}, u32[]{:S(2)}) collective-permute-start(f32[4,512]{1,0:T(4,128)S(1)} %get-tuple-element.90), channel_id=1, source_target_pairs={{0,4},{4,0},{8,12},{12,8},{16,20},{20,16},{24,28},{28,24},{1,5},{5... | collective-permute-start | bytes 24584 | tf_op jit(solution)/shard_map/ppermute | solution.py:190
  17.0 2.1 %collective-permute-done.3.got_ref = f32[4,512]{1,0:T(4,128)S(1)} collective-permute-done((f32[4,512]{1,0:T(4,128)S(1)}, f32[4,512]{1,0:T(4,128)S(1)}, u32[]{:S(2)}, u32[]{:S(2)}) %collective-permute-start.3) | collective-permute-done | bytes 8224 | tf_op jit(solution)/shard_map/ppermute | solution.py:190
  19.1 0.5 collective-permute-start.10
  19.6 0.7 collective-permute-done.4
  20.3 6.1 %collective-permute-done.5.refs_2_ = f32[4,128,512]{2,1,0:T(8,128)} collective-permute-done((f32[4,128,512]{2,1,0:T(8,128)}, f32[4,128,512]{2,1,0:T(8,128)}, u32[]{:S(2)}, u32[]{:S(2)}) %collective-permute-start.5) | collective-permute-done | bytes 1048608 | tf_op jit(solution)/shard_map/ppermute | solution.py:140
  26.4 0.5 collective-permute-start
  26.9 1.7 %collective-permute-start.6 = (f32[1,128,512]{2,1,0:T(8,128)S(1)}, f32[1,128,512]{2,1,0:T(8,128)S(1)}, u32[]{:S(2)}, u32[]{:S(2)}) collective-permute-start(f32[1,128,512]{2,1,0:T(8,128)S(1)} %get-tuple-element.92), channel_id=1, source_target_pairs={{0,2},{1,3},{2,0},{3,1},{4,6},{5,7},{6,4},{7,5},{8,10},{9,11},{10,... | collective-permute-start | bytes 786440 | tf_op jit(solution)/shard_map/ppermute | solution.py:140
  29.0 1.8 %collective-permute-done.11.refs_3_ = f32[4,128,512]{2,1,0:T(8,128)S(1)} collective-permute-done((f32[4,128,512]{2,1,0:T(8,128)}, f32[4,128,512]{2,1,0:T(8,128)S(1)}, u32[]{:S(2)}, u32[]{:S(2)}) %collective-permute-start.11) | collective-permute-done | bytes 1048608 | tf_op jit(solution)/shard_map/ppermute | solution.py:140
  30.8 1.2 %copy-done.2 = f32[4,128,512]{2,1,0:T(8,128)S(1)} copy-done((f32[4,128,512]{2,1,0:T(8,128)S(1)}, f32[4,128,512]{2,1,0:T(8,128)}, u32[]{:S(2)}) %copy-start.2) | copy-done | bytes 1048600
  32.0 4.9 %inverses.1 = (f32[512,512]{1,0:T(8,128)S(1)}, bf16[2,512,512]{2,1,0:T(8,128)(2,1)S(1)}, bf16[2,512,512]{2,1,0:T(8,128)(2,1)S(1)}, bf16[2,512,512]{2,1,0:T(8,128...) custom-call(s32[2,128]{1,0:T(2,128)S(1)} %broadcast_in_dim.2.where_r, ...), custom_call_target="tpu_custom_call" | custom-call | flops 800000000 | bytes 1024 | tf_op jit(solution)/shard_map/inverses/pallas_call | solution.py:48
  36.9 3.8 %collective-permute-done.8.refs_2_ = f32[1,128,512]{2,1,0:T(8,128)S(1)} collective-permute-done((f32[1,128,512]{2,1,0:T(8,128)S(1)}, f32[1,128,512]{2,1,0:T(8,128)S(1)}, u32[]{:S(2)}, u32[]{:S(2)}) %collective-permute-start.8) | collective-permute-done | bytes 262176 | tf_op jit(solution)/shard_map/ppermute | solution.py:140
  40.8 0.5 collective-permute-start.13
  41.3 1.7 %collective-permute-start.9 = (f32[1,128,512]{2,1,0:T(8,128)S(1)}, f32[1,128,512]{2,1,0:T(8,128)S(1)}, u32[]{:S(2)}, u32[]{:S(2)}) collective-permute-start(f32[1,128,512]{2,1,0:T(8,128)S(1)} %get-tuple-element.94), channel_id=1, source_target_pairs={{0,2},{1,3},{2,0},{3,1},{4,6},{5,7},{6,4},{7,5},{8,10},{9,11},{10,... | collective-permute-start | bytes 786440 | tf_op jit(solution)/shard_map/ppermute | solution.py:140
  43.0 5.9 %early_days.1 = (f32[256,512]{1,0:T(8,128)S(1)}, bf16[2,512,512]{2,1,0:T(8,128)(2,1)S(1)}, bf16[2,512,512]{2,1,0:T(8,128)(2,1)S(1)}, bf16[2,512,512]{2,1,0:T(8,1...) custom-call(s32[2,128]{1,0:T(2,128)S(1)} %broadcast_in_dim.2.where_r, ...), custom_call_target="tpu_custom_call" | custom-call | flops 1200000000 | bytes 1024 | tf_op jit(solution)/shard_map/early_days/pallas_call | solution.py:48
  48.9 0.6 collective-permute-done.9.refs_2_
  49.5 1.7 %collective-permute-start.16 = (f32[72,512]{1,0:T(8,128)S(1)}, f32[72,512]{1,0:T(8,128)S(1)}, u32[]{:S(2)}, u32[]{:S(2)}) collective-permute-start(f32[72,512]{1,0:T(8,128)S(1)} %get-tuple-element.110), channel_id=1, source_target_pairs={{0,2},{1,3},{2,0},{3,1},{4,6},{5,7},{6,4},{7,5},{8,10},{9,11},{10,... | collective-permute-start | bytes 442376 | tf_op jit(solution)/shard_map/ppermute | solution.py:140
  51.5 2.7 %day_2.1 = (bf16[2,512,512]{2,1,0:T(8,128)(2,1)S(1)}, bf16[2,512,512]{2,1,0:T(8,128)(2,1)S(1)}, f32[128,512]{1,0:T(8,128)S(1)}, f32[128,512]{1,0:T(8,128)S(1)}) custom-call(s32[2,128]{1,0:T(2,128)S(1)} %broadcast_in_dim.2.where_ref, f32[4,128,512]{2,1,0:T(8,128)S(1)} %copy-done.1, f32[4,128,512]{2,1,0:T(8,128)S(1)} %collective-permute-done.refs_1_, ...), custom_call_target="tpu_custom_call" | custom-call | flops 600000000 | bytes 1024 | tf_op jit(solution)/shard_map/day_2/pallas_call | solution.py:48
  54.2 1.8 %collective-permute-start.18 = (f32[128,512]{1,0:T(8,128)S(1)}, f32[128,512]{1,0:T(8,128)S(1)}, u32[]{:S(2)}, u32[]{:S(2)}) collective-permute-start(f32[128,512]{1,0:T(8,128)S(1)} %get-tuple-element.108), channel_id=1, source_target_pairs={{0,4},{4,0},{8,12},{12,8},{16,20},{20,16},{24,28},{28,24},{1,5},{5... | collective-permute-start | bytes 786440 | tf_op jit(solution)/shard_map/ppermute | solution.py:143
  56.1 2.4 %collective-permute-done.7.refs_2_ = f32[64,512]{1,0:T(8,128)S(1)} collective-permute-done((f32[64,512]{1,0:T(8,128)S(1)}, f32[64,512]{1,0:T(8,128)S(1)}, u32[]{:S(2)}, u32[]{:S(2)}) %collective-permute-start.7) | collective-permute-done | bytes 131104 | tf_op jit(solution)/shard_map/ppermute | solution.py:140
  58.6 1.3 %collective-permute-done.15.refs_3_ = f32[64,512]{1,0:T(8,128)S(1)} collective-permute-done((f32[64,512]{1,0:T(8,128)S(1)}, f32[64,512]{1,0:T(8,128)S(1)}, u32[]{:S(2)}, u32[]{:S(2)}) %collective-permute-start.15) | collective-permute-done | bytes 131104 | tf_op jit(solution)/shard_map/ppermute | solution.py:140
  59.9 1.2 last_link.1
  61.1 1.3 %collective-permute-done.18.other_ref = f32[128,512]{1,0:T(8,128)S(1)} collective-permute-done((f32[128,512]{1,0:T(8,128)S(1)}, f32[128,512]{1,0:T(8,128)S(1)}, u32[]{:S(2)}, u32[]{:S(2)}) %collective-permute-start.18) | collective-permute-done | bytes 262176 | tf_op jit(solution)/shard_map/ppermute | solution.py:143
  62.4 1.7 %collective-permute-start.19 = (f32[256,512]{1,0:T(8,128)S(1)}, f32[256,512]{1,0:T(8,128)S(1)}, u32[]{:S(2)}, u32[]{:S(2)}) collective-permute-start(f32[256,512]{1,0:T(8,128)S(1)} %get-tuple-element.115), channel_id=1, source_target_pairs={{0,4},{4,0},{8,12},{12,8},{16,20},{20,16},{24,28},{28,24},{1,5},{5... | collective-permute-start | bytes 1572872 | tf_op jit(solution)/shard_map/ppermute | solution.py:143
  64.2 4.5 %lines.1 = (f32[8,512]{1,0:T(8,128)S(1)}, f32[8,512]{1,0:T(8,128)S(1)}, f32[4,8,512]{2,1,0:T(8,128)S(1)}) custom-call(f32[4,512]{1,0:T(4,128)S(1)} %add.3.source_ref, f32[72,512]{1,0:T(8,128)S(1)} %collective-permute-done.16.refs_4_.refs_0_, bf16[2,512,512]{2,1,0:T(8,128)(2,1)S(1)} %get-tuple-element.101.refs_8_.refs_1_.refs_3_.refs_2_, ...), custom_call_target="tpu_custom_call" | custom-call | flops 1000000000 | bytes 1024 | tf_op jit(solution)/shard_map/lines/pallas_call | solution.py:48
  69.0 2.7 %grams.1.gram_ref = bf16[2,512,512]{2,1,0:T(8,128)(2,1)S(1)} custom-call(f32[512,512]{1,0:T(8,128)S(1)} %get-tuple-element.124.gram_ref, bf16[2,512,512]{2,1,0:T(8,128)(2,1)S(1)} %get-tuple-element.118.refs_6_.refs_0_.refs_5_, bf16[2,512,512]{2,1,0:T(8,128)(2,1)S(1)} %get-tuple-element.107.refs_7_.refs_9_.refs_1_.refs_8_, ...), custom_call_target="tpu_custom_call" | custom-call | flops 600000000 | bytes 1024 | tf_op jit(solution)/shard_map/grams/pallas_call | solution.py:48
  71.7 1.8 %late_maps.1 = (bf16[2,512,512]{2,1,0:T(8,128)(2,1)S(1)}, bf16[2,512,512]{2,1,0:T(8,128)(2,1)S(1)}) custom-call(bf16[2,512,512]{2,1,0:T(8,128)(2,1)S(1)} %get-tuple-element.125.refs_10_.refs_7_.refs_0_, bf16[2,512,512]{2,1,0:T(8,128)(2,1)S(1)} %get-tuple-element.106.refs_5_.refs_10_.refs_1_, bf16[2,512,512]{2,1,0:T(8,128)(2,1)S(1)} %get-tuple-element.119.refs_8_.refs_2_, ...), custom_call_target="tpu_custom_call" | custom-call | flops 400000000 | bytes 1024 | tf_op jit(solution)/shard_map/late_maps/pallas_call | solution.py:48
  73.5 2.2 %collective-permute-done.20.other_flux_ref = f32[8,512]{1,0:T(8,128)S(1)} collective-permute-done((f32[8,512]{1,0:T(8,128)S(1)}, f32[8,512]{1,0:T(8,128)S(1)}, u32[]{:S(2)}, u32[]{:S(2)}) %collective-permute-start.20) | collective-permute-done | bytes 16416 | tf_op jit(solution)/shard_map/ppermute | solution.py:143
  75.7 1.9 %collective-permute-done.21.rest_ref = f32[256,512]{1,0:T(8,128)S(1)} collective-permute-done((f32[256,512]{1,0:T(8,128)S(1)}, f32[256,512]{1,0:T(8,128)S(1)}, u32[]{:S(2)}, u32[]{:S(2)}) %collective-permute-start.21) | collective-permute-done | bytes 524320 | tf_op jit(solution)/shard_map/ppermute | solution.py:140
  77.7 1.1 pair_maps.1
  78.7 0.7 collective-permute-start.22
  79.4 3.7 %collective-permute-start.23 = (f32[8,512]{1,0:T(8,128)S(1)}, f32[8,512]{1,0:T(8,128)S(1)}, u32[]{:S(2)}, u32[]{:S(2)}) collective-permute-start(f32[8,512]{1,0:T(8,128)S(1)} %get-tuple-element.133.local_ref), channel_id=1, source_target_pairs={{0,8},{4,12},{1,9},{5,13},{2,10},{6,14},{3,11},{7,15}} | collective-permute-start | bytes 49160 | tf_op jit(solution)/shard_map/ppermute | solution.py:146
  83.1 1.0 group_map.1.map_ref
  84.1 0.4 collective-permute-done.23.refs_0_
  84.5 0.5 forward_link.2
  85.0 0.7 collective-permute-start.24
  85.7 0.5 forward_link.3
  86.2 0.7 collective-permute-start.26
  86.9 0.4 noise_link.2
  87.3 1.1 mean_turn.1
  88.4 1.5 %collective-permute-start.27 = (f32[16,512]{1,0:T(8,128)S(1)}, f32[16,512]{1,0:T(8,128)S(1)}, u32[]{:S(2)}, u32[]{:S(2)}) collective-permute-start(f32[16,512]{1,0:T(8,128)S(1)} %pad_maximum_fusion), channel_id=1, source_target_pairs={{0,4},{4,0},{8,12},{12,8},{16,20},{20,16},{24,28},{28,24},{1,5},{5... | collective-permute-start | bytes 98312 | tf_op jit(solution)/shard_map/ppermute | solution.py:143
  89.9 0.7 collective-permute-start.25
  90.6 0.7 collective-permute-start.29
  91.3 0.7 collective-permute-start.28
  91.9 0.4 collective-permute-done.27
  92.3 0.3 first_back.1
  92.7 0.4 noise_link.3
  93.1 1.3 %collective-permute-start.30 = (f32[128,512]{1,0:T(8,128)S(1)}, f32[128,512]{1,0:T(8,128)S(1)}, u32[]{:S(2)}, u32[]{:S(2)}) collective-permute-start(f32[128,512]{1,0:T(8,128)S(1)} %noise_link.3), channel_id=1, source_target_pairs={{8,0},{12,4},{9,1},{13,5},{10,2},{14,6},{11,3},{15,7}} | collective-permute-start | bytes 786440 | tf_op jit(solution)/shard_map/ppermute | solution.py:146
  94.4 0.7 collective-permute-start.31
  95.4 14.5 %collective-permute-done.30.refs_2_ = f32[128,512]{1,0:T(8,128)S(1)} collective-permute-done((f32[128,512]{1,0:T(8,128)S(1)}, f32[128,512]{1,0:T(8,128)S(1)}, u32[]{:S(2)}, u32[]{:S(2)}) %collective-permute-start.30) | collective-permute-done | bytes 262176 | tf_op jit(solution)/shard_map/ppermute | solution.py:146
  109.8 0.4 divide.1
  110.2 0.6 collective-permute-start.32
  110.8 1.3 %collective-permute-start.33 = (f32[8,512]{1,0:T(8,128)S(1)}, f32[8,512]{1,0:T(8,128)S(1)}, u32[]{:S(2)}, u32[]{:S(2)}) collective-permute-start(f32[8,512]{1,0:T(8,128)S(1)} %backward_link.1), channel_id=1, source_target_pairs={{8,0},{12,4},{9,1},{13,5},{10,2},{14,6},{11,3},{15,7}} | collective-permute-start | bytes 49160 | tf_op jit(solution)/shard_map/ppermute | solution.py:146
  112.1 3.1 %mean_terms.1 = (f32[256,512]{1,0:T(8,128)S(1)}, f32[256,512]{1,0:T(8,128)S(1)}, f32[256,512]{1,0:T(8,128)S(1)}, f32[256,512]{1,0:T(8,128)S(1)}) custom-call(f32[8,512]{1,0:T(8,128)S(1)} %get-tuple-element.154.entering_ref, f32[4,8,512]{2,1,0:T(8,128)S(1)} %get-tuple-element.155.current_ref, f32[256,512]{1,0:T(8,128)S(1)} %get-tuple-element.100.refs_7_.refs_0_, ...), custom_call_target="tpu_custom_call" | custom-call | flops 800000000 | bytes 1024 | tf_op jit(solution)/shard_map/mean_terms/pallas_call | solution.py:48
  115.2 1.2 %collective-permute-done.33.refs_3_ = f32[8,512]{1,0:T(8,128)S(1)} collective-permute-done((f32[8,512]{1,0:T(8,128)S(1)}, f32[8,512]{1,0:T(8,128)S(1)}, u32[]{:S(2)}, u32[]{:S(2)}) %collective-permute-start.33) | collective-permute-done | bytes 16416 | tf_op jit(solution)/shard_map/ppermute | solution.py:146
  116.7 3.4 %last_days.1 = f32[4,512,256]{2,1,0:T(8,128)} custom-call(s32[2,128]{1,0:T(2,128)S(1)} %broadcast_in_dim.2.where_ref, f32[128,512]{1,0:T(8,128)S(1)} %get-tuple-element.150.keep_ref, f32[128,512]{1,0:T(8,128)S(1)} %collective-permute-done.32.got_ref, f32[8,512]{1,0:T(8,128)S(1)} %get-tuple-element.152.back_ref, ...), custom_call_target="tpu_custom_call" | custom-call | flops 800000000 | bytes 1024 | tf_op jit(solution)/shard_map/last_days/pallas_call | solution.py:48
  (43 shorter events, 1.9 us)
Async XLA Ops:
  0.0 9.3 %copy-start.1 = (f32[4,128,512]{2,1,0:T(8,128)S(1)}, f32[4,128,512]{2,1,0:T(8,128)}, u32[]{:S(2)}) copy-start(f32[4,128,512]{2,1,0:T(8,128)} %refs_0_.7) | copy-start | bytes 3145732
  0.0 30.7 %copy-start = (f32[4,512,256]{2,1,0:T(8,128)S(1)}, f32[4,512,256]{2,1,0:T(8,128)}, u32[]{:S(2)}) copy-start(f32[4,512,256]{2,1,0:T(8,128)} %refs_4_.3) | copy-start | bytes 6291460
  0.0 26.4 %collective-permute-start.5 = (f32[4,128,512]{2,1,0:T(8,128)}, f32[4,128,512]{2,1,0:T(8,128)}, u32[]{:S(2)}, u32[]{:S(2)}) collective-permute-start(f32[4,128,512]{2,1,0:T(8,128)} %refs_0_.4), channel_id=1, source_target_pairs={{0,2},{1,3},{2,0},{3,1},{4,6},{5,7},{6,4},{7,5},{8,10},{9,11},{10,... | collective-permute-start | bytes 3145736 | tf_op jit(solution)/shard_map/ppermute | solution.py:140
  6.6 4.9 %collective-permute-start.1 = (f32[16,512]{1,0:T(8,128)S(1)}, f32[16,512]{1,0:T(8,128)S(1)}, u32[]{:S(2)}, u32[]{:S(2)}) collective-permute-start(f32[16,512]{1,0:T(8,128)S(1)} %get-tuple-element.86), channel_id=1, source_target_pairs={{0,16},{4,20},{8,24},{12,28},{16,0},{20,4},{24,8},{28,12},{1,17},{... | collective-permute-start | bytes 98312 | tf_op jit(solution)/shard_map/ppermute | solution.py:190
  11.5 3.8 %collective-permute-start.2 = (f32[8,512]{1,0:T(8,128)S(1)}, f32[8,512]{1,0:T(8,128)S(1)}, u32[]{:S(2)}, u32[]{:S(2)}) collective-permute-start(f32[8,512]{1,0:T(8,128)S(1)} %get-tuple-element.88), channel_id=1, source_target_pairs={{0,8},{4,12},{8,0},{12,4},{16,24},{20,28},{24,16},{28,20},{1,9},{5... | collective-permute-start | bytes 49160 | tf_op jit(solution)/shard_map/ppermute | solution.py:190
  15.4 3.7 %collective-permute-start.3 = (f32[4,512]{1,0:T(4,128)S(1)}, f32[4,512]{1,0:T(4,128)S(1)}, u32[]{:S(2)}, u32[]{:S(2)}) collective-permute-start(f32[4,512]{1,0:T(4,128)S(1)} %get-tuple-element.90), channel_id=1, source_target_pairs={{0,4},{4,0},{8,12},{12,8},{16,20},{20,16},{24,28},{28,24},{1,5},{5... | collective-permute-start | bytes 24584 | tf_op jit(solution)/shard_map/ppermute | solution.py:190
  19.1 1.2 collective-permute-start.4
  19.1 9.8 %collective-permute-start.10 = (f32[4,128,512]{2,1,0:T(8,128)}, f32[4,128,512]{2,1,0:T(8,128)S(1)}, u32[]{:S(2)}, u32[]{:S(2)}) collective-permute-start(f32[4,128,512]{2,1,0:T(8,128)} %refs_0_.4), channel_id=1, source_target_pairs={{0,1},{1,0},{2,3},{3,2},{4,5},{5,4},{6,7},{7,6},{8,9},{9,8},{10,11... | collective-permute-start | bytes 3145736 | tf_op jit(solution)/shard_map/ppermute | solution.py:140
  26.4 4.3 %collective-permute-start.11 = (f32[4,128,512]{2,1,0:T(8,128)}, f32[4,128,512]{2,1,0:T(8,128)S(1)}, u32[]{:S(2)}, u32[]{:S(2)}) collective-permute-start(f32[4,128,512]{2,1,0:T(8,128)} %collective-permute-done.5.refs_2_), channel_id=1, source_target_pairs={{0,1},{1,0},{2,3},{3,2},{4,5},{5,4},{6,7},{7,6},{8,9},{9,8},{10,11... | collective-permute-start | bytes 3145736 | tf_op jit(solution)/shard_map/ppermute | solution.py:140
  26.4 16.6 %collective-permute-start = (f32[4,128,512]{2,1,0:T(8,128)S(1)}, f32[4,128,512]{2,1,0:T(8,128)S(1)}, u32[]{:S(2)}, u32[]{:S(2)}) collective-permute-start(f32[4,128,512]{2,1,0:T(8,128)S(1)} %copy-done.1), channel_id=1, source_target_pairs={{0,1},{1,0},{2,3},{3,2},{4,5},{5,4},{6,7},{7,6},{8,9},{9,8},{10,11... | collective-permute-start | bytes 3145736 | tf_op jit(solution)/shard_map/ppermute | solution.py:140
  26.9 10.0 %collective-permute-start.6 = (f32[1,128,512]{2,1,0:T(8,128)S(1)}, f32[1,128,512]{2,1,0:T(8,128)S(1)}, u32[]{:S(2)}, u32[]{:S(2)}) collective-permute-start(f32[1,128,512]{2,1,0:T(8,128)S(1)} %get-tuple-element.92), channel_id=1, source_target_pairs={{0,2},{1,3},{2,0},{3,1},{4,6},{5,7},{6,4},{7,5},{8,10},{9,11},{10,... | collective-permute-start | bytes 786440 | tf_op jit(solution)/shard_map/ppermute | solution.py:140
  28.7 12.1 %collective-permute-start.8 = (f32[1,128,512]{2,1,0:T(8,128)S(1)}, f32[1,128,512]{2,1,0:T(8,128)S(1)}, u32[]{:S(2)}, u32[]{:S(2)}) collective-permute-start(f32[1,128,512]{2,1,0:T(8,128)S(1)} %get-tuple-element.166), channel_id=1, source_target_pairs={{0,2},{1,3},{2,0},{3,1},{4,6},{5,7},{6,4},{7,5},{8,10},{9,11},{10,... | collective-permute-start | bytes 786440 | tf_op jit(solution)/shard_map/ppermute | solution.py:140
  30.8 1.2 %copy-start.2 = (f32[4,128,512]{2,1,0:T(8,128)S(1)}, f32[4,128,512]{2,1,0:T(8,128)}, u32[]{:S(2)}) copy-start(f32[4,128,512]{2,1,0:T(8,128)} %refs_0_.4) | copy-start | bytes 3145732
  40.8 2.3 %collective-permute-start.12 = (f32[1,128,512]{2,1,0:T(8,128)S(1)}, f32[1,128,512]{2,1,0:T(8,128)S(1)}, u32[]{:S(2)}, u32[]{:S(2)}) collective-permute-start(f32[1,128,512]{2,1,0:T(8,128)S(1)} %collective-permute-done.8.refs_2_), channel_id=1, source_target_pairs={{0,1},{1,0},{2,3},{3,2},{4,5},{5,4},{6,7},{7,6},{8,9},{9,8},{10,11... | collective-permute-start | bytes 786440 | tf_op jit(solution)/shard_map/ppermute | solution.py:140
  40.8 2.3 %collective-permute-start.13 = (f32[1,128,512]{2,1,0:T(8,128)S(1)}, f32[1,128,512]{2,1,0:T(8,128)S(1)}, u32[]{:S(2)}, u32[]{:S(2)}) collective-permute-start(f32[1,128,512]{2,1,0:T(8,128)S(1)} %collective-permute-done.6.refs_4_), channel_id=1, source_target_pairs={{0,1},{1,0},{2,3},{3,2},{4,5},{5,4},{6,7},{7,6},{8,9},{9,8},{10,11... | collective-permute-start | bytes 786440 | tf_op jit(solution)/shard_map/ppermute | solution.py:140
  41.3 8.2 %collective-permute-start.9 = (f32[1,128,512]{2,1,0:T(8,128)S(1)}, f32[1,128,512]{2,1,0:T(8,128)S(1)}, u32[]{:S(2)}, u32[]{:S(2)}) collective-permute-start(f32[1,128,512]{2,1,0:T(8,128)S(1)} %get-tuple-element.94), channel_id=1, source_target_pairs={{0,2},{1,3},{2,0},{3,1},{4,6},{5,7},{6,4},{7,5},{8,10},{9,11},{10,... | collective-permute-start | bytes 786440 | tf_op jit(solution)/shard_map/ppermute | solution.py:140
  49.5 2.0 %collective-permute-start.14 = (f32[1,128,512]{2,1,0:T(8,128)S(1)}, f32[1,128,512]{2,1,0:T(8,128)S(1)}, u32[]{:S(2)}, u32[]{:S(2)}) collective-permute-start(f32[1,128,512]{2,1,0:T(8,128)S(1)} %collective-permute-done.9.refs_2_), channel_id=1, source_target_pairs={{0,1},{1,0},{2,3},{3,2},{4,5},{5,4},{6,7},{7,6},{8,9},{9,8},{10,11... | collective-permute-start | bytes 786440 | tf_op jit(solution)/shard_map/ppermute | solution.py:140
  49.5 6.6 %collective-permute-start.16 = (f32[72,512]{1,0:T(8,128)S(1)}, f32[72,512]{1,0:T(8,128)S(1)}, u32[]{:S(2)}, u32[]{:S(2)}) collective-permute-start(f32[72,512]{1,0:T(8,128)S(1)} %get-tuple-element.110), channel_id=1, source_target_pairs={{0,2},{1,3},{2,0},{3,1},{4,6},{5,7},{6,4},{7,5},{8,10},{9,11},{10,... | collective-permute-start | bytes 442376 | tf_op jit(solution)/shard_map/ppermute | solution.py:140
  51.2 7.3 %collective-permute-start.7 = (f32[64,512]{1,0:T(8,128)S(1)}, f32[64,512]{1,0:T(8,128)S(1)}, u32[]{:S(2)}, u32[]{:S(2)}) collective-permute-start(f32[64,512]{1,0:T(8,128)S(1)} %get-tuple-element.93), channel_id=1, source_target_pairs={{0,2},{1,3},{2,0},{3,1},{4,6},{5,7},{6,4},{7,5},{8,10},{9,11},{10,... | collective-permute-start | bytes 393224 | tf_op jit(solution)/shard_map/ppermute | solution.py:140
  54.2 8.3 %collective-permute-start.18 = (f32[128,512]{1,0:T(8,128)S(1)}, f32[128,512]{1,0:T(8,128)S(1)}, u32[]{:S(2)}, u32[]{:S(2)}) collective-permute-start(f32[128,512]{1,0:T(8,128)S(1)} %get-tuple-element.108), channel_id=1, source_target_pairs={{0,4},{4,0},{8,12},{12,8},{16,20},{20,16},{24,28},{28,24},{1,5},{5... | collective-permute-start | bytes 786440 | tf_op jit(solution)/shard_map/ppermute | solution.py:143
  56.1 3.8 %collective-permute-start.17 = (f32[72,512]{1,0:T(8,128)S(1)}, f32[72,512]{1,0:T(8,128)S(1)}, u32[]{:S(2)}, u32[]{:S(2)}) collective-permute-start(f32[72,512]{1,0:T(8,128)S(1)} %collective-permute-done.16.refs_4_.refs_0_), channel_id=1, source_target_pairs={{0,1},{1,0},{2,3},{3,2},{4,5},{5,4},{6,7},{7,6},{8,9},{9,8},{10,11... | collective-permute-start | bytes 442376 | tf_op jit(solution)/shard_map/ppermute | solution.py:140
  58.6 1.3 %collective-permute-start.15 = (f32[64,512]{1,0:T(8,128)S(1)}, f32[64,512]{1,0:T(8,128)S(1)}, u32[]{:S(2)}, u32[]{:S(2)}) collective-permute-start(f32[64,512]{1,0:T(8,128)S(1)} %collective-permute-done.7.refs_2_), channel_id=1, source_target_pairs={{0,1},{1,0},{2,3},{3,2},{4,5},{5,4},{6,7},{7,6},{8,9},{9,8},{10,11... | collective-permute-start | bytes 393224 | tf_op jit(solution)/shard_map/ppermute | solution.py:140
  62.4 13.3 %collective-permute-start.19 = (f32[256,512]{1,0:T(8,128)S(1)}, f32[256,512]{1,0:T(8,128)S(1)}, u32[]{:S(2)}, u32[]{:S(2)}) collective-permute-start(f32[256,512]{1,0:T(8,128)S(1)} %get-tuple-element.115), channel_id=1, source_target_pairs={{0,4},{4,0},{8,12},{12,8},{16,20},{20,16},{24,28},{28,24},{1,5},{5... | collective-permute-start | bytes 1572872 | tf_op jit(solution)/shard_map/ppermute | solution.py:143
  68.7 7.0 %collective-permute-start.20 = (f32[8,512]{1,0:T(8,128)S(1)}, f32[8,512]{1,0:T(8,128)S(1)}, u32[]{:S(2)}, u32[]{:S(2)}) collective-permute-start(f32[8,512]{1,0:T(8,128)S(1)} %get-tuple-element.121.flux_ref), channel_id=1, source_target_pairs={{0,4},{4,0},{8,12},{12,8},{16,20},{20,16},{24,28},{28,24},{1,5},{5... | collective-permute-start | bytes 49160 | tf_op jit(solution)/shard_map/ppermute | solution.py:143
  75.7 1.9 %collective-permute-start.21 = (f32[256,512]{1,0:T(8,128)S(1)}, f32[256,512]{1,0:T(8,128)S(1)}, u32[]{:S(2)}, u32[]{:S(2)}) collective-permute-start(f32[256,512]{1,0:T(8,128)S(1)} %collective-permute-done.19.half_ref), channel_id=1, source_target_pairs={{0,1},{1,0},{2,3},{3,2},{4,5},{5,4},{6,7},{7,6},{8,9},{9,8},{10,11... | collective-permute-start | bytes 1572872 | tf_op jit(solution)/shard_map/ppermute | solution.py:140
  78.7 8.2 %collective-permute-start.22 = (f32[128,512]{1,0:T(8,128)S(1)}, f32[128,512]{1,0:T(8,128)S(1)}, u32[]{:S(2)}, u32[]{:S(2)}) collective-permute-start(f32[128,512]{1,0:T(8,128)S(1)} %get-tuple-element.134.local_ref), channel_id=1, source_target_pairs={{24,16},{28,20},{25,17},{29,21},{26,18},{30,22},{27,19},{31,23}} | collective-permute-start | bytes 786440 | tf_op jit(solution)/shard_map/ppermute | solution.py:146
  79.4 5.1 %collective-permute-start.23 = (f32[8,512]{1,0:T(8,128)S(1)}, f32[8,512]{1,0:T(8,128)S(1)}, u32[]{:S(2)}, u32[]{:S(2)}) collective-permute-start(f32[8,512]{1,0:T(8,128)S(1)} %get-tuple-element.133.local_ref), channel_id=1, source_target_pairs={{0,8},{4,12},{1,9},{5,13},{2,10},{6,14},{3,11},{7,15}} | collective-permute-start | bytes 49160 | tf_op jit(solution)/shard_map/ppermute | solution.py:146
  85.0 0.7 collective-permute-start.24
  86.2 1.1 collective-permute-start.26
  88.4 3.9 %collective-permute-start.27 = (f32[16,512]{1,0:T(8,128)S(1)}, f32[16,512]{1,0:T(8,128)S(1)}, u32[]{:S(2)}, u32[]{:S(2)}) collective-permute-start(f32[16,512]{1,0:T(8,128)S(1)} %pad_maximum_fusion), channel_id=1, source_target_pairs={{0,4},{4,0},{8,12},{12,8},{16,20},{20,16},{24,28},{28,24},{1,5},{5... | collective-permute-start | bytes 98312 | tf_op jit(solution)/shard_map/ppermute | solution.py:143
  89.9 2.7 %collective-permute-start.25 = (f32[128,512]{1,0:T(8,128)S(1)}, f32[128,512]{1,0:T(8,128)S(1)}, u32[]{:S(2)}, u32[]{:S(2)}) collective-permute-start(f32[128,512]{1,0:T(8,128)S(1)} %noise_link.2), channel_id=1, source_target_pairs={{16,8},{20,12},{17,9},{21,13},{18,10},{22,14},{19,11},{23,15}} | collective-permute-start | bytes 786440 | tf_op jit(solution)/shard_map/ppermute | solution.py:146
  90.6 1.7 %collective-permute-start.29 = (f32[8,512]{1,0:T(8,128)S(1)}, f32[8,512]{1,0:T(8,128)S(1)}, u32[]{:S(2)}, u32[]{:S(2)}) collective-permute-start(f32[8,512]{1,0:T(8,128)S(1)} %get-tuple-element.143.part_ref), channel_id=1, source_target_pairs={{24,20},{28,16},{25,21},{29,17},{26,22},{30,18},{27,23},{31,19}} | collective-permute-start | bytes 49160 | tf_op jit(solution)/shard_map/ppermute | solution.py:504
  91.3 1.1 collective-permute-start.28
  93.1 16.8 %collective-permute-start.30 = (f32[128,512]{1,0:T(8,128)S(1)}, f32[128,512]{1,0:T(8,128)S(1)}, u32[]{:S(2)}, u32[]{:S(2)}) collective-permute-start(f32[128,512]{1,0:T(8,128)S(1)} %noise_link.3), channel_id=1, source_target_pairs={{8,0},{12,4},{9,1},{13,5},{10,2},{14,6},{11,3},{15,7}} | collective-permute-start | bytes 786440 | tf_op jit(solution)/shard_map/ppermute | solution.py:146
  94.4 0.7 collective-permute-start.31
  110.2 6.4 %collective-permute-start.32 = (f32[128,512]{1,0:T(8,128)S(1)}, f32[128,512]{1,0:T(8,128)S(1)}, u32[]{:S(2)}, u32[]{:S(2)}) collective-permute-start(f32[128,512]{1,0:T(8,128)S(1)} %get-tuple-element.151), channel_id=1, source_target_pairs={{0,4},{4,0},{8,12},{12,8},{16,20},{20,16},{24,28},{28,24},{1,5},{5... | collective-permute-start | bytes 786440 | tf_op jit(solution)/shard_map/ppermute | solution.py:143
  110.8 5.6 %collective-permute-start.33 = (f32[8,512]{1,0:T(8,128)S(1)}, f32[8,512]{1,0:T(8,128)S(1)}, u32[]{:S(2)}, u32[]{:S(2)}) collective-permute-start(f32[8,512]{1,0:T(8,128)S(1)} %backward_link.1), channel_id=1, source_target_pairs={{8,0},{12,4},{9,1},{13,5},{10,2},{14,6},{11,3},{15,7}} | collective-permute-start | bytes 49160 | tf_op jit(solution)/shard_map/ppermute | solution.py:146

commit v7 on v6

--- a/solution.py
+++ b/solution.py
@@ -229,7 +229,7 @@
         [square, *[map_parts] * day_count, *[samples_full] * day_count],
         "inverses",
         (where,),
-        [*own_inverse, *shared(got_inverses, where, *packed), noise],
+        [*own_inverse, *shared(got_inverses, where, *packed, *got_links[0]), noise],
         work=4,
     )
     inverses, local_terms = results[:day_count], results[day_count:]
@@ -301,7 +301,7 @@
             f"day_{day}",
             (where,),
             [
-                *own_link, *shared(got_links[day], summed), noise, inverses[day + 1],
+                *own_link, *shared(got_links[day], summed, *got_links[day + 1]), noise, inverses[day + 1],
                 summed, moveds[day],
             ],
             work=3,

time: 121 us -> 125 us (1.033)
  starting transfers between devices: 33 us -> 34.7 us
  waiting for transfers between devices: 45.5 us -> 47.2 us
    ppermute x5, waiting for transfers between devices: 4.19 us -> 7.04 us  [to_pair(): return lax.ppermute(value, 'tm', [(i, i ^ 1) for i in range(part_count)])]
    reshape x3, local copies, waits for them, and re-layouts: 2.16 us -> 0.01 us  [bin_observations(): value.reshape(chunks, chunk)]
    slice x1, local copies, waits for them, and re-layouts: 0.08 us -> 2.08 us  [local(): link_rows = [coupling[day:day + 1] for day in range(day_count)]]
    ppermute x3, starting transfers between devices: 5.86 us -> 7.24 us  [local(): lax.ppermute(sent, 'tm', [(i, i ^ distance) for i in range(part_count)])]
  transfers between devices with their start and end apart: 34 -> 34, of which waited for: 19 -> 18; matrix products, arithmetic and copies ran while one was open for 2% -> 2% of each run, Pallas kernels for 26% -> 26%
where the time goes in v7:
time: 125 us; the launch traced here: 124 us
  waiting for transfers between devices  47.2 us (38%)
  Pallas kernels  38.6 us (31%)
  starting transfers between devices  34.7 us (28%)
  local copies, waits for them, and re-layouts  3.41 us (3%)
    pallas_call x24, Pallas kernels, call(): pl.pallas_call(body, out_shape=out_shape, in_specs=[vmem] * (len(scalars)...  38.6 us
    ppermute x16, waiting for transfers between devices, to_row(): lax.ppermute(value, 'row', [(i, i ^ distance) for i in range(row_count)])  18.7 us
    ppermute x8, waiting for transfers between devices, to_group(): lax.ppermute(value, 'tm', [(PAIR * source + i, PAIR * target + i) for i i...  15.9 us
    ppermute x16, starting transfers between devices, to_row(): lax.ppermute(value, 'row', [(i, i ^ distance) for i in range(row_count)])  10.8 us
    ppermute x8, starting transfers between devices, to_group(): lax.ppermute(value, 'tm', [(PAIR * source + i, PAIR * target + i) for i i...  9.59 us
    ppermute x3, starting transfers between devices, local(): lax.ppermute(sent, 'tm', [(i, i ^ distance) for i in range(part_count)])  7.24 us
    ppermute x5, waiting for transfers between devices, to_pair(): return lax.ppermute(value, 'tm', [(i, i ^ 1) for i in range(part_count)])  7.04 us
    ppermute x5, starting transfers between devices, to_pair(): return lax.ppermute(value, 'tm', [(i, i ^ 1) for i in range(part_count)])  5.75 us
  transfers between devices with their start and end apart: 34, of which 18 were waited for; matrix products, arithmetic and copies ran while one was open for 2% of the time, Pallas kernels for 26%

profile of v7, /device:TPU:0, one launch (start us, length us, event | category | flops | bytes accessed | tf_op | source)
XLA Modules:
  0.0 124.5 jit_solution(4276272334040426331)
XLA Ops:
  0.0 3.0 %collective-permute-start.5 = (f32[4,128,512]{2,1,0:T(8,128)}, f32[4,128,512]{2,1,0:T(8,128)}, u32[]{:S(2)}, u32[]{:S(2)}) collective-permute-start(f32[4,128,512]{2,1,0:T(8,128)} %refs_0_.4), channel_id=1, source_target_pairs={{0,2},{1,3},{2,0},{3,1},{4,6},{5,7},{6,4},{7,5},{8,10},{9,11},{10,... | collective-permute-start | bytes 3145736 | tf_op jit(solution)/shard_map/ppermute | solution.py:140
  3.0 2.1 %fusion = (f32[1,128,512]{2,1,0:T(8,128)S(1)}, f32[1,128,512]{2,1,0:T(8,128)}, f32[1,128,512]{2,1,0:T(8,128)}, f32[1,128,512]{2,1,0:T(8,128)}) fusion(f32[4,128,512]{2,1,0:T(8,128)} %refs_0_.7), kind=kLoop, calls=%fused_computation.2 | loop fusion | bytes 2097152 | tf_op jit(solution)/shard_map/slice | solution.py:181
  5.5 1.4 %bin_observations.1 = (f32[16,512]{1,0:T(8,128)S(1)}, f32[16,512]{1,0:T(8,128)S(1)}) custom-call(s32[2,128]{1,0:T(2,128)S(1)} %broadcast_in_dim.2.where_ref, s32[8,512]{1,0:T(8,128)S(1)} %reshape.10.day_ref, s32[8,512]{1,0:T(8,128)S(1)} %reshape.11.node_ref, f32[8,512]{1,0:T(8,128)S(1)} %reshape.12.value_ref), custom_call_target="tpu_custom_call" | custom-call | flops 400000000 | bytes 1024 | tf_op jit(solution)/shard_map/bin_observations/pallas_call | solution.py:48
  6.9 3.3 %collective-permute-start.1 = (f32[16,512]{1,0:T(8,128)S(1)}, f32[16,512]{1,0:T(8,128)S(1)}, u32[]{:S(2)}, u32[]{:S(2)}) collective-permute-start(f32[16,512]{1,0:T(8,128)S(1)} %get-tuple-element.86), channel_id=1, source_target_pairs={{0,16},{4,20},{8,24},{12,28},{16,0},{20,4},{24,8},{28,12},{1,17},{... | collective-permute-start | bytes 98312 | tf_op jit(solution)/shard_map/ppermute | solution.py:190
  10.2 1.9 %collective-permute-done.1.got_ref = f32[16,512]{1,0:T(8,128)S(1)} collective-permute-done((f32[16,512]{1,0:T(8,128)S(1)}, f32[16,512]{1,0:T(8,128)S(1)}, u32[]{:S(2)}, u32[]{:S(2)}) %collective-permute-start.1) | collective-permute-done | bytes 32800 | tf_op jit(solution)/shard_map/ppermute | solution.py:190
  12.1 2.0 %collective-permute-start.2 = (f32[8,512]{1,0:T(8,128)S(1)}, f32[8,512]{1,0:T(8,128)S(1)}, u32[]{:S(2)}, u32[]{:S(2)}) collective-permute-start(f32[8,512]{1,0:T(8,128)S(1)} %get-tuple-element.88), channel_id=1, source_target_pairs={{0,8},{4,12},{8,0},{12,4},{16,24},{20,28},{24,16},{28,20},{1,9},{5... | collective-permute-start | bytes 49160 | tf_op jit(solution)/shard_map/ppermute | solution.py:190
  14.1 1.8 %collective-permute-done.2.got_ref = f32[8,512]{1,0:T(8,128)S(1)} collective-permute-done((f32[8,512]{1,0:T(8,128)S(1)}, f32[8,512]{1,0:T(8,128)S(1)}, u32[]{:S(2)}, u32[]{:S(2)}) %collective-permute-start.2) | collective-permute-done | bytes 16416 | tf_op jit(solution)/shard_map/ppermute | solution.py:190
  16.0 1.9 %collective-permute-start.3 = (f32[4,512]{1,0:T(4,128)S(1)}, f32[4,512]{1,0:T(4,128)S(1)}, u32[]{:S(2)}, u32[]{:S(2)}) collective-permute-start(f32[4,512]{1,0:T(4,128)S(1)} %get-tuple-element.90), channel_id=1, source_target_pairs={{0,4},{4,0},{8,12},{12,8},{16,20},{20,16},{24,28},{28,24},{1,5},{5... | collective-permute-start | bytes 24584 | tf_op jit(solution)/shard_map/ppermute | solution.py:190
  17.9 1.8 %collective-permute-done.3.got_ref = f32[4,512]{1,0:T(4,128)S(1)} collective-permute-done((f32[4,512]{1,0:T(4,128)S(1)}, f32[4,512]{1,0:T(4,128)S(1)}, u32[]{:S(2)}, u32[]{:S(2)}) %collective-permute-start.3) | collective-permute-done | bytes 8224 | tf_op jit(solution)/shard_map/ppermute | solution.py:190
  19.7 0.5 collective-permute-start.10
  20.2 0.7 collective-permute-done.4
  20.9 11.2 %collective-permute-done.8.refs_2_ = f32[1,128,512]{2,1,0:T(8,128)} collective-permute-done((f32[1,128,512]{2,1,0:T(8,128)}, f32[1,128,512]{2,1,0:T(8,128)}, u32[]{:S(2)}, u32[]{:S(2)}) %collective-permute-start.8) | collective-permute-done | bytes 262176 | tf_op jit(solution)/shard_map/ppermute | solution.py:140
  32.1 0.5 collective-permute-start
  32.6 1.7 %collective-permute-start.6 = (f32[1,128,512]{2,1,0:T(8,128)}, f32[1,128,512]{2,1,0:T(8,128)S(1)}, u32[]{:S(2)}, u32[]{:S(2)}) collective-permute-start(f32[1,128,512]{2,1,0:T(8,128)} %get-tuple-element.92), channel_id=1, source_target_pairs={{0,2},{1,3},{2,0},{3,1},{4,6},{5,7},{6,4},{7,5},{8,10},{9,11},{10,... | collective-permute-start | bytes 786440 | tf_op jit(solution)/shard_map/ppermute | solution.py:140
  34.4 1.4 %collective-permute-done.11.refs_3_ = f32[4,128,512]{2,1,0:T(8,128)S(1)} collective-permute-done((f32[4,128,512]{2,1,0:T(8,128)}, f32[4,128,512]{2,1,0:T(8,128)S(1)}, u32[]{:S(2)}, u32[]{:S(2)}) %collective-permute-start.11) | collective-permute-done | bytes 1048608 | tf_op jit(solution)/shard_map/ppermute | solution.py:140
  35.8 1.2 copy-done.2
  37.0 5.0 %inverses.1 = (f32[512,512]{1,0:T(8,128)S(1)}, bf16[2,512,512]{2,1,0:T(8,128)(2,1)S(1)}, bf16[2,512,512]{2,1,0:T(8,128)(2,1)S(1)}, bf16[2,512,512]{2,1,0:T(8,128...) custom-call(s32[2,128]{1,0:T(2,128)S(1)} %broadcast_in_dim.2.where_r, ...), custom_call_target="tpu_custom_call" | custom-call | flops 800000000 | bytes 1024 | tf_op jit(solution)/shard_map/inverses/pallas_call | solution.py:48
  42.2 0.4 collective-permute-start.13
  42.6 1.7 %collective-permute-start.9 = (f32[1,128,512]{2,1,0:T(8,128)S(1)}, f32[1,128,512]{2,1,0:T(8,128)S(1)}, u32[]{:S(2)}, u32[]{:S(2)}) collective-permute-start(f32[1,128,512]{2,1,0:T(8,128)S(1)} %copy-done.3), channel_id=1, source_target_pairs={{0,2},{1,3},{2,0},{3,1},{4,6},{5,7},{6,4},{7,5},{8,10},{9,11},{10,... | collective-permute-start | bytes 786440 | tf_op jit(solution)/shard_map/ppermute | solution.py:140
  44.3 0.3 collective-permute-start.7
  44.6 6.8 %early_days.1 = (f32[256,512]{1,0:T(8,128)S(1)}, bf16[2,512,512]{2,1,0:T(8,128)(2,1)S(1)}, bf16[2,512,512]{2,1,0:T(8,128)(2,1)S(1)}, bf16[2,512,512]{2,1,0:T(8,1...) custom-call(s32[2,128]{1,0:T(2,128)S(1)} %broadcast_in_dim.2.where_r, ...), custom_call_target="tpu_custom_call" | custom-call | flops 1200000000 | bytes 1024 | tf_op jit(solution)/shard_map/early_days/pallas_call | solution.py:48
  51.7 2.0 %collective-permute-done.7.refs_2_ = f32[64,512]{1,0:T(8,128)S(1)} collective-permute-done((f32[64,512]{1,0:T(8,128)S(1)}, f32[64,512]{1,0:T(8,128)S(1)}, u32[]{:S(2)}, u32[]{:S(2)}) %collective-permute-start.7) | collective-permute-done | bytes 131104 | tf_op jit(solution)/shard_map/ppermute | solution.py:140
  53.7 1.7 %collective-permute-start.16 = (f32[72,512]{1,0:T(8,128)S(1)}, f32[72,512]{1,0:T(8,128)S(1)}, u32[]{:S(2)}, u32[]{:S(2)}) collective-permute-start(f32[72,512]{1,0:T(8,128)S(1)} %get-tuple-element.110), channel_id=1, source_target_pairs={{0,2},{1,3},{2,0},{3,1},{4,6},{5,7},{6,4},{7,5},{8,10},{9,11},{10,... | collective-permute-start | bytes 442376 | tf_op jit(solution)/shard_map/ppermute | solution.py:140
  55.5 2.7 %day_2.1 = (bf16[2,512,512]{2,1,0:T(8,128)(2,1)S(1)}, bf16[2,512,512]{2,1,0:T(8,128)(2,1)S(1)}, f32[128,512]{1,0:T(8,128)S(1)}, f32[128,512]{1,0:T(8,128)S(1)}) custom-call(s32[2,128]{1,0:T(2,128)S(1)} %broadcast_in_dim.2.where_ref, f32[4,128,512]{2,1,0:T(8,128)S(1)} %copy-done.1, f32[4,128,512]{2,1,0:T(8,128)S(1)} %collective-permute-done.refs_1_, ...), custom_call_target="tpu_custom_call" | custom-call | flops 600000000 | bytes 1024 | tf_op jit(solution)/shard_map/day_2/pallas_call | solution.py:48
  58.1 1.6 %collective-permute-start.18 = (f32[128,512]{1,0:T(8,128)S(1)}, f32[128,512]{1,0:T(8,128)S(1)}, u32[]{:S(2)}, u32[]{:S(2)}) collective-permute-start(f32[128,512]{1,0:T(8,128)S(1)} %get-tuple-element.108), channel_id=1, source_target_pairs={{0,4},{4,0},{8,12},{12,8},{16,20},{20,16},{24,28},{28,24},{1,5},{5... | collective-permute-start | bytes 786440 | tf_op jit(solution)/shard_map/ppermute | solution.py:143
  60.0 0.5 collective-permute-start.15
  60.5 1.0 collective-permute-done.15.refs_3_
  61.6 1.2 last_link.1
  62.8 3.9 %collective-permute-done.18.other_ref = f32[128,512]{1,0:T(8,128)S(1)} collective-permute-done((f32[128,512]{1,0:T(8,128)S(1)}, f32[128,512]{1,0:T(8,128)S(1)}, u32[]{:S(2)}, u32[]{:S(2)}) %collective-permute-start.18) | collective-permute-done | bytes 262176 | tf_op jit(solution)/shard_map/ppermute | solution.py:143
  66.7 1.5 %collective-permute-start.19 = (f32[256,512]{1,0:T(8,128)S(1)}, f32[256,512]{1,0:T(8,128)S(1)}, u32[]{:S(2)}, u32[]{:S(2)}) collective-permute-start(f32[256,512]{1,0:T(8,128)S(1)} %get-tuple-element.115), channel_id=1, source_target_pairs={{0,4},{4,0},{8,12},{12,8},{16,20},{20,16},{24,28},{28,24},{1,5},{5... | collective-permute-start | bytes 1572872 | tf_op jit(solution)/shard_map/ppermute | solution.py:143
  68.2 4.5 %lines.1 = (f32[8,512]{1,0:T(8,128)S(1)}, f32[8,512]{1,0:T(8,128)S(1)}, f32[4,8,512]{2,1,0:T(8,128)S(1)}) custom-call(f32[4,512]{1,0:T(4,128)S(1)} %add.3.source_ref, f32[72,512]{1,0:T(8,128)S(1)} %collective-permute-done.16.refs_4_.refs_0_, bf16[2,512,512]{2,1,0:T(8,128)(2,1)S(1)} %get-tuple-element.101.refs_8_.refs_1_.refs_3_.refs_2_, ...), custom_call_target="tpu_custom_call" | custom-call | flops 1000000000 | bytes 1024 | tf_op jit(solution)/shard_map/lines/pallas_call | solution.py:48
  72.7 0.5 collective-permute-start.20
  73.2 2.7 %grams.1.gram_ref = bf16[2,512,512]{2,1,0:T(8,128)(2,1)S(1)} custom-call(f32[512,512]{1,0:T(8,128)S(1)} %get-tuple-element.124.gram_ref, bf16[2,512,512]{2,1,0:T(8,128)(2,1)S(1)} %get-tuple-element.118.refs_6_.refs_0_.refs_5_, bf16[2,512,512]{2,1,0:T(8,128)(2,1)S(1)} %get-tuple-element.107.refs_7_.refs_9_.refs_1_.refs_8_, ...), custom_call_target="tpu_custom_call" | custom-call | flops 600000000 | bytes 1024 | tf_op jit(solution)/shard_map/grams/pallas_call | solution.py:48
  75.9 1.8 %late_maps.1 = (bf16[2,512,512]{2,1,0:T(8,128)(2,1)S(1)}, bf16[2,512,512]{2,1,0:T(8,128)(2,1)S(1)}) custom-call(bf16[2,512,512]{2,1,0:T(8,128)(2,1)S(1)} %get-tuple-element.125.refs_10_.refs_7_.refs_0_, bf16[2,512,512]{2,1,0:T(8,128)(2,1)S(1)} %get-tuple-element.106.refs_5_.refs_10_.refs_1_, bf16[2,512,512]{2,1,0:T(8,128)(2,1)S(1)} %get-tuple-element.119.refs_8_.refs_2_, ...), custom_call_target="tpu_custom_call" | custom-call | flops 400000000 | bytes 1024 | tf_op jit(solution)/shard_map/late_maps/pallas_call | solution.py:48
  77.7 2.5 %collective-permute-done.20.other_flux_ref = f32[8,512]{1,0:T(8,128)S(1)} collective-permute-done((f32[8,512]{1,0:T(8,128)S(1)}, f32[8,512]{1,0:T(8,128)S(1)}, u32[]{:S(2)}, u32[]{:S(2)}) %collective-permute-start.20) | collective-permute-done | bytes 16416 | tf_op jit(solution)/shard_map/ppermute | solution.py:143
  80.2 1.9 %collective-permute-done.21.rest_ref = f32[256,512]{1,0:T(8,128)S(1)} collective-permute-done((f32[256,512]{1,0:T(8,128)S(1)}, f32[256,512]{1,0:T(8,128)S(1)}, u32[]{:S(2)}, u32[]{:S(2)}) %collective-permute-start.21) | collective-permute-done | bytes 524320 | tf_op jit(solution)/shard_map/ppermute | solution.py:140
  82.2 1.1 pair_maps.1
  83.2 0.7 collective-permute-start.22
  83.9 3.4 %collective-permute-start.23 = (f32[8,512]{1,0:T(8,128)S(1)}, f32[8,512]{1,0:T(8,128)S(1)}, u32[]{:S(2)}, u32[]{:S(2)}) collective-permute-start(f32[8,512]{1,0:T(8,128)S(1)} %get-tuple-element.133.local_ref), channel_id=1, source_target_pairs={{0,8},{4,12},{1,9},{5,13},{2,10},{6,14},{3,11},{7,15}} | collective-permute-start | bytes 49160 | tf_op jit(solution)/shard_map/ppermute | solution.py:146
  87.4 1.0 group_map.1.map_ref
  88.4 0.4 collective-permute-done.23.refs_0_
  88.8 0.5 forward_link.2
  89.3 0.7 collective-permute-start.24
  90.0 0.5 forward_link.3
  90.5 0.7 collective-permute-start.26
  91.2 0.4 noise_link.2
  91.6 1.1 mean_turn.1
  92.7 1.5 %collective-permute-start.27 = (f32[16,512]{1,0:T(8,128)S(1)}, f32[16,512]{1,0:T(8,128)S(1)}, u32[]{:S(2)}, u32[]{:S(2)}) collective-permute-start(f32[16,512]{1,0:T(8,128)S(1)} %pad_maximum_fusion), channel_id=1, source_target_pairs={{0,4},{4,0},{8,12},{12,8},{16,20},{20,16},{24,28},{28,24},{1,5},{5... | collective-permute-start | bytes 98312 | tf_op jit(solution)/shard_map/ppermute | solution.py:143
  94.2 0.7 collective-permute-start.25
  94.9 0.7 collective-permute-start.29
  95.5 0.7 collective-permute-start.28
  96.2 0.4 collective-permute-done.27
  96.6 0.3 first_back.1
  96.9 0.4 noise_link.3
  97.3 1.3 %collective-permute-start.30 = (f32[128,512]{1,0:T(8,128)S(1)}, f32[128,512]{1,0:T(8,128)S(1)}, u32[]{:S(2)}, u32[]{:S(2)}) collective-permute-start(f32[128,512]{1,0:T(8,128)S(1)} %noise_link.3), channel_id=1, source_target_pairs={{8,0},{12,4},{9,1},{13,5},{10,2},{14,6},{11,3},{15,7}} | collective-permute-start | bytes 786440 | tf_op jit(solution)/shard_map/ppermute | solution.py:146
  98.6 0.7 collective-permute-start.31
  99.3 0.3 backward_link.1
  99.6 14.5 %collective-permute-done.30.refs_2_ = f32[128,512]{1,0:T(8,128)S(1)} collective-permute-done((f32[128,512]{1,0:T(8,128)S(1)}, f32[128,512]{1,0:T(8,128)S(1)}, u32[]{:S(2)}, u32[]{:S(2)}) %collective-permute-start.30) | collective-permute-done | bytes 262176 | tf_op jit(solution)/shard_map/ppermute | solution.py:146
  114.1 0.4 divide.1
  114.5 0.6 collective-permute-start.32
  115.1 1.5 %collective-permute-start.33 = (f32[8,512]{1,0:T(8,128)S(1)}, f32[8,512]{1,0:T(8,128)S(1)}, u32[]{:S(2)}, u32[]{:S(2)}) collective-permute-start(f32[8,512]{1,0:T(8,128)S(1)} %backward_link.1), channel_id=1, source_target_pairs={{8,0},{12,4},{9,1},{13,5},{10,2},{14,6},{11,3},{15,7}} | collective-permute-start | bytes 49160 | tf_op jit(solution)/shard_map/ppermute | solution.py:146
  116.6 3.1 %mean_terms.1 = (f32[256,512]{1,0:T(8,128)S(1)}, f32[256,512]{1,0:T(8,128)S(1)}, f32[256,512]{1,0:T(8,128)S(1)}, f32[256,512]{1,0:T(8,128)S(1)}) custom-call(f32[8,512]{1,0:T(8,128)S(1)} %get-tuple-element.154.entering_ref, f32[4,8,512]{2,1,0:T(8,128)S(1)} %get-tuple-element.155.current_ref, f32[256,512]{1,0:T(8,128)S(1)} %get-tuple-element.100.refs_7_.refs_0_, ...), custom_call_target="tpu_custom_call" | custom-call | flops 800000000 | bytes 1024 | tf_op jit(solution)/shard_map/mean_terms/pallas_call | solution.py:48
  119.7 1.0 collective-permute-done.33.refs_3_
  120.9 3.4 %last_days.1 = f32[4,512,256]{2,1,0:T(8,128)} custom-call(s32[2,128]{1,0:T(2,128)S(1)} %broadcast_in_dim.2.where_ref, f32[128,512]{1,0:T(8,128)S(1)} %get-tuple-element.150.keep_ref, f32[128,512]{1,0:T(8,128)S(1)} %collective-permute-done.32.got_ref, f32[8,512]{1,0:T(8,128)S(1)} %get-tuple-element.152.back_ref, ...), custom_call_target="tpu_custom_call" | custom-call | flops 800000000 | bytes 1024 | tf_op jit(solution)/shard_map/last_days/pallas_call | solution.py:48
  (51 shorter events, 1.5 us)
Async XLA Ops:
  0.0 32.1 %copy-start.1 = (f32[4,128,512]{2,1,0:T(8,128)S(1)}, f32[4,128,512]{2,1,0:T(8,128)}, u32[]{:S(2)}) copy-start(f32[4,128,512]{2,1,0:T(8,128)} %refs_0_.7) | copy-start | bytes 3145732
  0.0 5.3 %copy-start.4 = (s32[4096]{0:T(1024)S(1)}, s32[4096]{0:T(1024)}, u32[]{:S(2)}) copy-start(s32[4096]{0:T(1024)} %param.9) | copy-start | bytes 49156
  0.0 5.3 %copy-start.5 = (s32[4096]{0:T(1024)S(1)}, s32[4096]{0:T(1024)}, u32[]{:S(2)}) copy-start(s32[4096]{0:T(1024)} %param.10) | copy-start | bytes 49156
  0.0 5.3 %copy-start.6 = (f32[4096]{0:T(1024)S(1)}, f32[4096]{0:T(1024)}, u32[]{:S(2)}) copy-start(f32[4096]{0:T(1024)} %param.11) | copy-start | bytes 49156
  0.0 35.8 %copy-start = (f32[4,512,256]{2,1,0:T(8,128)S(1)}, f32[4,512,256]{2,1,0:T(8,128)}, u32[]{:S(2)}) copy-start(f32[4,512,256]{2,1,0:T(8,128)} %refs_4_.3) | copy-start | bytes 6291460
  0.0 32.1 %collective-permute-start.5 = (f32[4,128,512]{2,1,0:T(8,128)}, f32[4,128,512]{2,1,0:T(8,128)}, u32[]{:S(2)}, u32[]{:S(2)}) collective-permute-start(f32[4,128,512]{2,1,0:T(8,128)} %refs_0_.4), channel_id=1, source_target_pairs={{0,2},{1,3},{2,0},{3,1},{4,6},{5,7},{6,4},{7,5},{8,10},{9,11},{10,... | collective-permute-start | bytes 3145736 | tf_op jit(solution)/shard_map/ppermute | solution.py:140
  5.1 27.0 %collective-permute-start.8 = (f32[1,128,512]{2,1,0:T(8,128)}, f32[1,128,512]{2,1,0:T(8,128)}, u32[]{:S(2)}, u32[]{:S(2)}) collective-permute-start(f32[1,128,512]{2,1,0:T(8,128)} %get-tuple-element.166), channel_id=1, source_target_pairs={{0,2},{1,3},{2,0},{3,1},{4,6},{5,7},{6,4},{7,5},{8,10},{9,11},{10,... | collective-permute-start | bytes 786440 | tf_op jit(solution)/shard_map/ppermute | solution.py:140
  6.9 5.2 %collective-permute-start.1 = (f32[16,512]{1,0:T(8,128)S(1)}, f32[16,512]{1,0:T(8,128)S(1)}, u32[]{:S(2)}, u32[]{:S(2)}) collective-permute-start(f32[16,512]{1,0:T(8,128)S(1)} %get-tuple-element.86), channel_id=1, source_target_pairs={{0,16},{4,20},{8,24},{12,28},{16,0},{20,4},{24,8},{28,12},{1,17},{... | collective-permute-start | bytes 98312 | tf_op jit(solution)/shard_map/ppermute | solution.py:190
  12.1 3.8 %collective-permute-start.2 = (f32[8,512]{1,0:T(8,128)S(1)}, f32[8,512]{1,0:T(8,128)S(1)}, u32[]{:S(2)}, u32[]{:S(2)}) collective-permute-start(f32[8,512]{1,0:T(8,128)S(1)} %get-tuple-element.88), channel_id=1, source_target_pairs={{0,8},{4,12},{8,0},{12,4},{16,24},{20,28},{24,16},{28,20},{1,9},{5... | collective-permute-start | bytes 49160 | tf_op jit(solution)/shard_map/ppermute | solution.py:190
  16.0 3.7 %collective-permute-start.3 = (f32[4,512]{1,0:T(4,128)S(1)}, f32[4,512]{1,0:T(4,128)S(1)}, u32[]{:S(2)}, u32[]{:S(2)}) collective-permute-start(f32[4,512]{1,0:T(4,128)S(1)} %get-tuple-element.90), channel_id=1, source_target_pairs={{0,4},{4,0},{8,12},{12,8},{16,20},{20,16},{24,28},{28,24},{1,5},{5... | collective-permute-start | bytes 24584 | tf_op jit(solution)/shard_map/ppermute | solution.py:190
  19.7 1.2 collective-permute-start.4
  19.7 14.7 %collective-permute-start.10 = (f32[4,128,512]{2,1,0:T(8,128)}, f32[4,128,512]{2,1,0:T(8,128)S(1)}, u32[]{:S(2)}, u32[]{:S(2)}) collective-permute-start(f32[4,128,512]{2,1,0:T(8,128)} %refs_0_.4), channel_id=1, source_target_pairs={{0,1},{1,0},{2,3},{3,2},{4,5},{5,4},{6,7},{7,6},{8,9},{9,8},{10,11... | collective-permute-start | bytes 3145736 | tf_op jit(solution)/shard_map/ppermute | solution.py:140
  32.1 3.6 %collective-permute-start.11 = (f32[4,128,512]{2,1,0:T(8,128)}, f32[4,128,512]{2,1,0:T(8,128)S(1)}, u32[]{:S(2)}, u32[]{:S(2)}) collective-permute-start(f32[4,128,512]{2,1,0:T(8,128)} %collective-permute-done.5.refs_2_), channel_id=1, source_target_pairs={{0,1},{1,0},{2,3},{3,2},{4,5},{5,4},{6,7},{7,6},{8,9},{9,8},{10,11... | collective-permute-start | bytes 3145736 | tf_op jit(solution)/shard_map/ppermute | solution.py:140
  32.1 12.5 %collective-permute-start = (f32[4,128,512]{2,1,0:T(8,128)S(1)}, f32[4,128,512]{2,1,0:T(8,128)S(1)}, u32[]{:S(2)}, u32[]{:S(2)}) collective-permute-start(f32[4,128,512]{2,1,0:T(8,128)S(1)} %copy-done.1), channel_id=1, source_target_pairs={{0,1},{1,0},{2,3},{3,2},{4,5},{5,4},{6,7},{7,6},{8,9},{9,8},{10,11... | collective-permute-start | bytes 3145736 | tf_op jit(solution)/shard_map/ppermute | solution.py:140
  32.6 9.3 %collective-permute-start.6 = (f32[1,128,512]{2,1,0:T(8,128)}, f32[1,128,512]{2,1,0:T(8,128)S(1)}, u32[]{:S(2)}, u32[]{:S(2)}) collective-permute-start(f32[1,128,512]{2,1,0:T(8,128)} %get-tuple-element.92), channel_id=1, source_target_pairs={{0,2},{1,3},{2,0},{3,1},{4,6},{5,7},{6,4},{7,5},{8,10},{9,11},{10,... | collective-permute-start | bytes 786440 | tf_op jit(solution)/shard_map/ppermute | solution.py:140
  35.8 1.2 copy-start.2
  37.0 5.6 %copy-start.3 = (f32[1,128,512]{2,1,0:T(8,128)S(1)}, f32[1,128,512]{2,1,0:T(8,128)}, u32[]{:S(2)}) copy-start(f32[1,128,512]{2,1,0:T(8,128)} %get-tuple-element.94) | copy-start | bytes 786436
  42.0 2.6 %collective-permute-start.12 = (f32[1,128,512]{2,1,0:T(8,128)}, f32[1,128,512]{2,1,0:T(8,128)S(1)}, u32[]{:S(2)}, u32[]{:S(2)}) collective-permute-start(f32[1,128,512]{2,1,0:T(8,128)} %collective-permute-done.8.refs_2_), channel_id=1, source_target_pairs={{0,1},{1,0},{2,3},{3,2},{4,5},{5,4},{6,7},{7,6},{8,9},{9,8},{10,11... | collective-permute-start | bytes 786440 | tf_op jit(solution)/shard_map/ppermute | solution.py:140
  42.2 2.4 %collective-permute-start.13 = (f32[1,128,512]{2,1,0:T(8,128)S(1)}, f32[1,128,512]{2,1,0:T(8,128)S(1)}, u32[]{:S(2)}, u32[]{:S(2)}) collective-permute-start(f32[1,128,512]{2,1,0:T(8,128)S(1)} %collective-permute-done.6.refs_4_), channel_id=1, source_target_pairs={{0,1},{1,0},{2,3},{3,2},{4,5},{5,4},{6,7},{7,6},{8,9},{9,8},{10,11... | collective-permute-start | bytes 786440 | tf_op jit(solution)/shard_map/ppermute | solution.py:140
  42.6 9.1 %collective-permute-start.9 = (f32[1,128,512]{2,1,0:T(8,128)S(1)}, f32[1,128,512]{2,1,0:T(8,128)S(1)}, u32[]{:S(2)}, u32[]{:S(2)}) collective-permute-start(f32[1,128,512]{2,1,0:T(8,128)S(1)} %copy-done.3), channel_id=1, source_target_pairs={{0,2},{1,3},{2,0},{3,1},{4,6},{5,7},{6,4},{7,5},{8,10},{9,11},{10,... | collective-permute-start | bytes 786440 | tf_op jit(solution)/shard_map/ppermute | solution.py:140
  44.3 9.4 %collective-permute-start.7 = (f32[64,512]{1,0:T(8,128)S(1)}, f32[64,512]{1,0:T(8,128)S(1)}, u32[]{:S(2)}, u32[]{:S(2)}) collective-permute-start(f32[64,512]{1,0:T(8,128)S(1)} %get-tuple-element.93), channel_id=1, source_target_pairs={{0,2},{1,3},{2,0},{3,1},{4,6},{5,7},{6,4},{7,5},{8,10},{9,11},{10,... | collective-permute-start | bytes 393224 | tf_op jit(solution)/shard_map/ppermute | solution.py:140
  53.7 1.7 %collective-permute-start.14 = (f32[1,128,512]{2,1,0:T(8,128)S(1)}, f32[1,128,512]{2,1,0:T(8,128)S(1)}, u32[]{:S(2)}, u32[]{:S(2)}) collective-permute-start(f32[1,128,512]{2,1,0:T(8,128)S(1)} %collective-permute-done.9.refs_2_), channel_id=1, source_target_pairs={{0,1},{1,0},{2,3},{3,2},{4,5},{5,4},{6,7},{7,6},{8,9},{9,8},{10,11... | collective-permute-start | bytes 786440 | tf_op jit(solution)/shard_map/ppermute | solution.py:140
  53.7 6.3 %collective-permute-start.16 = (f32[72,512]{1,0:T(8,128)S(1)}, f32[72,512]{1,0:T(8,128)S(1)}, u32[]{:S(2)}, u32[]{:S(2)}) collective-permute-start(f32[72,512]{1,0:T(8,128)S(1)} %get-tuple-element.110), channel_id=1, source_target_pairs={{0,2},{1,3},{2,0},{3,1},{4,6},{5,7},{6,4},{7,5},{8,10},{9,11},{10,... | collective-permute-start | bytes 442376 | tf_op jit(solution)/shard_map/ppermute | solution.py:140
  58.1 8.5 %collective-permute-start.18 = (f32[128,512]{1,0:T(8,128)S(1)}, f32[128,512]{1,0:T(8,128)S(1)}, u32[]{:S(2)}, u32[]{:S(2)}) collective-permute-start(f32[128,512]{1,0:T(8,128)S(1)} %get-tuple-element.108), channel_id=1, source_target_pairs={{0,4},{4,0},{8,12},{12,8},{16,20},{20,16},{24,28},{28,24},{1,5},{5... | collective-permute-start | bytes 786440 | tf_op jit(solution)/shard_map/ppermute | solution.py:143
  60.0 1.6 %collective-permute-start.17 = (f32[72,512]{1,0:T(8,128)S(1)}, f32[72,512]{1,0:T(8,128)S(1)}, u32[]{:S(2)}, u32[]{:S(2)}) collective-permute-start(f32[72,512]{1,0:T(8,128)S(1)} %collective-permute-done.16.refs_4_.refs_0_), channel_id=1, source_target_pairs={{0,1},{1,0},{2,3},{3,2},{4,5},{5,4},{6,7},{7,6},{8,9},{9,8},{10,11... | collective-permute-start | bytes 442376 | tf_op jit(solution)/shard_map/ppermute | solution.py:140
  60.0 1.6 %collective-permute-start.15 = (f32[64,512]{1,0:T(8,128)S(1)}, f32[64,512]{1,0:T(8,128)S(1)}, u32[]{:S(2)}, u32[]{:S(2)}) collective-permute-start(f32[64,512]{1,0:T(8,128)S(1)} %collective-permute-done.7.refs_2_), channel_id=1, source_target_pairs={{0,1},{1,0},{2,3},{3,2},{4,5},{5,4},{6,7},{7,6},{8,9},{9,8},{10,11... | collective-permute-start | bytes 393224 | tf_op jit(solution)/shard_map/ppermute | solution.py:140
  66.7 13.6 %collective-permute-start.19 = (f32[256,512]{1,0:T(8,128)S(1)}, f32[256,512]{1,0:T(8,128)S(1)}, u32[]{:S(2)}, u32[]{:S(2)}) collective-permute-start(f32[256,512]{1,0:T(8,128)S(1)} %get-tuple-element.115), channel_id=1, source_target_pairs={{0,4},{4,0},{8,12},{12,8},{16,20},{20,16},{24,28},{28,24},{1,5},{5... | collective-permute-start | bytes 1572872 | tf_op jit(solution)/shard_map/ppermute | solution.py:143
  72.7 7.5 %collective-permute-start.20 = (f32[8,512]{1,0:T(8,128)S(1)}, f32[8,512]{1,0:T(8,128)S(1)}, u32[]{:S(2)}, u32[]{:S(2)}) collective-permute-start(f32[8,512]{1,0:T(8,128)S(1)} %get-tuple-element.121.flux_ref), channel_id=1, source_target_pairs={{0,4},{4,0},{8,12},{12,8},{16,20},{20,16},{24,28},{28,24},{1,5},{5... | collective-permute-start | bytes 49160 | tf_op jit(solution)/shard_map/ppermute | solution.py:143
  80.2 1.9 %collective-permute-start.21 = (f32[256,512]{1,0:T(8,128)S(1)}, f32[256,512]{1,0:T(8,128)S(1)}, u32[]{:S(2)}, u32[]{:S(2)}) collective-permute-start(f32[256,512]{1,0:T(8,128)S(1)} %collective-permute-done.19.half_ref), channel_id=1, source_target_pairs={{0,1},{1,0},{2,3},{3,2},{4,5},{5,4},{6,7},{7,6},{8,9},{9,8},{10,11... | collective-permute-start | bytes 1572872 | tf_op jit(solution)/shard_map/ppermute | solution.py:140
  83.2 7.9 %collective-permute-start.22 = (f32[128,512]{1,0:T(8,128)S(1)}, f32[128,512]{1,0:T(8,128)S(1)}, u32[]{:S(2)}, u32[]{:S(2)}) collective-permute-start(f32[128,512]{1,0:T(8,128)S(1)} %get-tuple-element.134.local_ref), channel_id=1, source_target_pairs={{24,16},{28,20},{25,17},{29,21},{26,18},{30,22},{27,19},{31,23}} | collective-permute-start | bytes 786440 | tf_op jit(solution)/shard_map/ppermute | solution.py:146
  83.9 4.9 %collective-permute-start.23 = (f32[8,512]{1,0:T(8,128)S(1)}, f32[8,512]{1,0:T(8,128)S(1)}, u32[]{:S(2)}, u32[]{:S(2)}) collective-permute-start(f32[8,512]{1,0:T(8,128)S(1)} %get-tuple-element.133.local_ref), channel_id=1, source_target_pairs={{0,8},{4,12},{1,9},{5,13},{2,10},{6,14},{3,11},{7,15}} | collective-permute-start | bytes 49160 | tf_op jit(solution)/shard_map/ppermute | solution.py:146
  89.3 0.7 collective-permute-start.24
  90.5 1.1 collective-permute-start.26
  92.7 3.9 %collective-permute-start.27 = (f32[16,512]{1,0:T(8,128)S(1)}, f32[16,512]{1,0:T(8,128)S(1)}, u32[]{:S(2)}, u32[]{:S(2)}) collective-permute-start(f32[16,512]{1,0:T(8,128)S(1)} %pad_maximum_fusion), channel_id=1, source_target_pairs={{0,4},{4,0},{8,12},{12,8},{16,20},{20,16},{24,28},{28,24},{1,5},{5... | collective-permute-start | bytes 98312 | tf_op jit(solution)/shard_map/ppermute | solution.py:143
  94.2 2.7 %collective-permute-start.25 = (f32[128,512]{1,0:T(8,128)S(1)}, f32[128,512]{1,0:T(8,128)S(1)}, u32[]{:S(2)}, u32[]{:S(2)}) collective-permute-start(f32[128,512]{1,0:T(8,128)S(1)} %noise_link.2), channel_id=1, source_target_pairs={{16,8},{20,12},{17,9},{21,13},{18,10},{22,14},{19,11},{23,15}} | collective-permute-start | bytes 786440 | tf_op jit(solution)/shard_map/ppermute | solution.py:146
  94.9 1.7 %collective-permute-start.29 = (f32[8,512]{1,0:T(8,128)S(1)}, f32[8,512]{1,0:T(8,128)S(1)}, u32[]{:S(2)}, u32[]{:S(2)}) collective-permute-start(f32[8,512]{1,0:T(8,128)S(1)} %get-tuple-element.143.part_ref), channel_id=1, source_target_pairs={{24,20},{28,16},{25,21},{29,17},{26,22},{30,18},{27,23},{31,19}} | collective-permute-start | bytes 49160 | tf_op jit(solution)/shard_map/ppermute | solution.py:504
  95.5 1.1 collective-permute-start.28
  97.3 16.8 %collective-permute-start.30 = (f32[128,512]{1,0:T(8,128)S(1)}, f32[128,512]{1,0:T(8,128)S(1)}, u32[]{:S(2)}, u32[]{:S(2)}) collective-permute-start(f32[128,512]{1,0:T(8,128)S(1)} %noise_link.3), channel_id=1, source_target_pairs={{8,0},{12,4},{9,1},{13,5},{10,2},{14,6},{11,3},{15,7}} | collective-permute-start | bytes 786440 | tf_op jit(solution)/shard_map/ppermute | solution.py:146
  98.6 0.7 collective-permute-start.31
  114.5 6.4 %collective-permute-start.32 = (f32[128,512]{1,0:T(8,128)S(1)}, f32[128,512]{1,0:T(8,128)S(1)}, u32[]{:S(2)}, u32[]{:S(2)}) collective-permute-start(f32[128,512]{1,0:T(8,128)S(1)} %get-tuple-element.151), channel_id=1, source_target_pairs={{0,4},{4,0},{8,12},{12,8},{16,20},{20,16},{24,28},{28,24},{1,5},{5... | collective-permute-start | bytes 786440 | tf_op jit(solution)/shard_map/ppermute | solution.py:143
  115.1 5.6 %collective-permute-start.33 = (f32[8,512]{1,0:T(8,128)S(1)}, f32[8,512]{1,0:T(8,128)S(1)}, u32[]{:S(2)}, u32[]{:S(2)}) collective-permute-start(f32[8,512]{1,0:T(8,128)S(1)} %backward_link.1), channel_id=1, source_target_pairs={{8,0},{12,4},{9,1},{13,5},{10,2},{14,6},{11,3},{15,7}} | collective-permute-start | bytes 49160 | tf_op jit(solution)/shard_map/ppermute | solution.py:146

commit v8 on v6

--- a/solution.py
+++ b/solution.py
@@ -183,7 +183,7 @@
         send_rows(rows)
     own_inverse = [inv_diag, to_row(inv_diag, 1)]
     own_link = [coupling, to_row(coupling, 1)]
-    where = after(where, keep, *link_rows)
+    where = after(where, keep, own_link[1], *link_rows)
 
     distance = part_count // 2
     while distance:
@@ -507,7 +507,10 @@
         both = to_pair(jnp.concatenate([own_back, part], axis=0))
         value, pair_back, mean["high_back"] = call(
             first_back_body, (line, line, line), "first_back", (where,),
-            [group_map, own_back, both[:LINES], part, both[LINES:], *got], work=0.6,
+            [
+                group_map, after(own_back, *noise_step), both[:LINES], part, both[LINES:], *got,
+            ],
+            work=0.6,
         )
         mean["leaving"] = got
         for group in range(groups - 2, 0, -1):
@@ -526,12 +529,14 @@
     for group in range(groups - 1, 0, -1):
         got = to_group(after(value, ahead), group, group - 1)
         ahead = next(hops)
-        if group > 1:
-            ahead = next(hops)
+        if group == groups - 1:
+            ahead = next(hops, ahead)
         leaving.append(after(got, ahead))
         if group > 1:
             value = linked(NN, group_map, pair_sum, leaving, "noise_link")
             noise_step[:] = [value]
+            if group < groups - 1:
+                ahead = next(hops, ahead)
     for _ in hops:
         pass
 

time: 121 us -> 121 us (level)
  Pallas kernels: 37.6 us -> 41.2 us
  waiting for transfers between devices: 45.5 us -> 42.1 us
    ppermute x8, waiting for transfers between devices: 16.1 us -> 12.5 us  [to_group(): lax.ppermute(value, 'tm', [(PAIR * source + i, PAIR * target + i) for i i...]
    pallas_call x24, Pallas kernels: 37.6 us -> 41.2 us  [call(): pl.pallas_call(body, out_shape=out_shape, in_specs=[vmem] * (len(scalars)...]
  transfers between devices with their start and end apart: 34 -> 34, of which waited for: 19 -> 17; matrix products, arithmetic and copies ran while one was open for 2% -> 2% of each run, Pallas kernels for 26% -> 30%
where the time goes in v8:
time: 121 us
  waiting for transfers between devices  42.1 us (35%)
  Pallas kernels  41.2 us (34%)
  starting transfers between devices  33.1 us (27%)
  local copies, waits for them, and re-layouts  3.56 us (3%)
    pallas_call x24, Pallas kernels, call(): pl.pallas_call(body, out_shape=out_shape, in_specs=[vmem] * (len(scalars)...  41.2 us
    ppermute x16, waiting for transfers between devices, to_row(): lax.ppermute(value, 'row', [(i, i ^ distance) for i in range(row_count)])  17.9 us
    ppermute x8, waiting for transfers between devices, to_group(): lax.ppermute(value, 'tm', [(PAIR * source + i, PAIR * target + i) for i i...  12.5 us
    ppermute x16, starting transfers between devices, to_row(): lax.ppermute(value, 'row', [(i, i ^ distance) for i in range(row_count)])  9.98 us
    ppermute x8, starting transfers between devices, to_group(): lax.ppermute(value, 'tm', [(PAIR * source + i, PAIR * target + i) for i i...  9.64 us
    ppermute x3, waiting for transfers between devices, local(): lax.ppermute(sent, 'tm', [(i, i ^ distance) for i in range(part_count)])  7.1 us
    ppermute x5, starting transfers between devices, to_pair(): return lax.ppermute(value, 'tm', [(i, i ^ 1) for i in range(part_count)])  6.69 us
    ppermute x3, starting transfers between devices, local(): lax.ppermute(sent, 'tm', [(i, i ^ distance) for i in range(part_count)])  5.51 us
  transfers between devices with their start and end apart: 34, of which 17 were waited for; matrix products, arithmetic and copies ran while one was open for 2% of the time, Pallas kernels for 30%

profile of v8, /device:TPU:0, one launch (start us, length us, event | category | flops | bytes accessed | tf_op | source)
XLA Modules:
  0.0 120.5 jit_solution(9205854383072542605)
XLA Ops:
  0.0 0.5 collective-permute-start
  0.5 2.6 %collective-permute-start.5 = (f32[4,128,512]{2,1,0:T(8,128)}, f32[4,128,512]{2,1,0:T(8,128)}, u32[]{:S(2)}, u32[]{:S(2)}) collective-permute-start(f32[4,128,512]{2,1,0:T(8,128)} %refs_0_.4), channel_id=1, source_target_pairs={{0,2},{1,3},{2,0},{3,1},{4,6},{5,7},{6,4},{7,5},{8,10},{9,11},{10,... | collective-permute-start | bytes 3145736 | tf_op jit(solution)/shard_map/ppermute | solution.py:140
  3.0 0.7 reshape.10.day_ref
  3.7 0.7 reshape.11.node_ref
  4.5 0.7 reshape.12.value_ref
  5.3 1.4 %bin_observations.1 = (f32[16,512]{1,0:T(8,128)S(1)}, f32[16,512]{1,0:T(8,128)S(1)}) custom-call(s32[2,128]{1,0:T(2,128)S(1)} %broadcast_in_dim.2.where_ref, s32[8,512]{1,0:T(8,128)S(1)} %reshape.10.day_ref, s32[8,512]{1,0:T(8,128)S(1)} %reshape.11.node_ref, f32[8,512]{1,0:T(8,128)S(1)} %reshape.12.value_ref), custom_call_target="tpu_custom_call" | custom-call | flops 400000000 | bytes 1024 | tf_op jit(solution)/shard_map/bin_observations/pallas_call | solution.py:48
  6.7 2.6 %collective-permute-start.1 = (f32[16,512]{1,0:T(8,128)S(1)}, f32[16,512]{1,0:T(8,128)S(1)}, u32[]{:S(2)}, u32[]{:S(2)}) collective-permute-start(f32[16,512]{1,0:T(8,128)S(1)} %get-tuple-element.87), channel_id=1, source_target_pairs={{0,16},{4,20},{8,24},{12,28},{16,0},{20,4},{24,8},{28,12},{1,17},{... | collective-permute-start | bytes 98312 | tf_op jit(solution)/shard_map/ppermute | solution.py:190
  9.5 2.5 %collective-permute-done.1.got_ref = f32[16,512]{1,0:T(8,128)S(1)} collective-permute-done((f32[16,512]{1,0:T(8,128)S(1)}, f32[16,512]{1,0:T(8,128)S(1)}, u32[]{:S(2)}, u32[]{:S(2)}) %collective-permute-start.1) | collective-permute-done | bytes 32800 | tf_op jit(solution)/shard_map/ppermute | solution.py:190
  12.0 1.3 %collective-permute-start.2 = (f32[8,512]{1,0:T(8,128)S(1)}, f32[8,512]{1,0:T(8,128)S(1)}, u32[]{:S(2)}, u32[]{:S(2)}) collective-permute-start(f32[8,512]{1,0:T(8,128)S(1)} %get-tuple-element.89), channel_id=1, source_target_pairs={{0,8},{4,12},{8,0},{12,4},{16,24},{20,28},{24,16},{28,20},{1,9},{5... | collective-permute-start | bytes 49160 | tf_op jit(solution)/shard_map/ppermute | solution.py:190
  13.3 2.5 %collective-permute-done.2.got_ref = f32[8,512]{1,0:T(8,128)S(1)} collective-permute-done((f32[8,512]{1,0:T(8,128)S(1)}, f32[8,512]{1,0:T(8,128)S(1)}, u32[]{:S(2)}, u32[]{:S(2)}) %collective-permute-start.2) | collective-permute-done | bytes 16416 | tf_op jit(solution)/shard_map/ppermute | solution.py:190
  15.8 1.6 %collective-permute-start.3 = (f32[4,512]{1,0:T(4,128)S(1)}, f32[4,512]{1,0:T(4,128)S(1)}, u32[]{:S(2)}, u32[]{:S(2)}) collective-permute-start(f32[4,512]{1,0:T(4,128)S(1)} %get-tuple-element.91), channel_id=1, source_target_pairs={{0,4},{4,0},{8,12},{12,8},{16,20},{20,16},{24,28},{28,24},{1,5},{5... | collective-permute-start | bytes 24584 | tf_op jit(solution)/shard_map/ppermute | solution.py:190
  17.4 2.1 %collective-permute-done.3.got_ref = f32[4,512]{1,0:T(4,128)S(1)} collective-permute-done((f32[4,512]{1,0:T(4,128)S(1)}, f32[4,512]{1,0:T(4,128)S(1)}, u32[]{:S(2)}, u32[]{:S(2)}) %collective-permute-start.3) | collective-permute-done | bytes 8224 | tf_op jit(solution)/shard_map/ppermute | solution.py:190
  19.5 0.5 collective-permute-start.10
  20.0 0.7 collective-permute-done.4
  20.7 6.4 %collective-permute-done.5.refs_2_ = f32[4,128,512]{2,1,0:T(8,128)} collective-permute-done((f32[4,128,512]{2,1,0:T(8,128)}, f32[4,128,512]{2,1,0:T(8,128)}, u32[]{:S(2)}, u32[]{:S(2)}) %collective-permute-start.5) | collective-permute-done | bytes 1048608 | tf_op jit(solution)/shard_map/ppermute | solution.py:140
  27.1 1.7 %collective-permute-start.6 = (f32[1,128,512]{2,1,0:T(8,128)S(1)}, f32[1,128,512]{2,1,0:T(8,128)S(1)}, u32[]{:S(2)}, u32[]{:S(2)}) collective-permute-start(f32[1,128,512]{2,1,0:T(8,128)S(1)} %get-tuple-element.93), channel_id=1, source_target_pairs={{0,2},{1,3},{2,0},{3,1},{4,6},{5,7},{6,4},{7,5},{8,10},{9,11},{10,... | collective-permute-start | bytes 786440 | tf_op jit(solution)/shard_map/ppermute | solution.py:140
  29.1 0.8 collective-permute-done.11.refs_3_
  30.0 1.2 %copy-done.2 = f32[4,128,512]{2,1,0:T(8,128)S(1)} copy-done((f32[4,128,512]{2,1,0:T(8,128)S(1)}, f32[4,128,512]{2,1,0:T(8,128)}, u32[]{:S(2)}) %copy-start.2) | copy-done | bytes 1048600
  31.2 4.9 %inverses.1 = (f32[512,512]{1,0:T(8,128)S(1)}, bf16[2,512,512]{2,1,0:T(8,128)(2,1)S(1)}, bf16[2,512,512]{2,1,0:T(8,128)(2,1)S(1)}, bf16[2,512,512]{2,1,0:T(8,128...) custom-call(s32[2,128]{1,0:T(2,128)S(1)} %broadcast_in_dim.2.where_r, ...), custom_call_target="tpu_custom_call" | custom-call | flops 800000000 | bytes 1024 | tf_op jit(solution)/shard_map/inverses/pallas_call | solution.py:48
  36.2 5.2 %collective-permute-done.8.refs_2_ = f32[1,128,512]{2,1,0:T(8,128)S(1)} collective-permute-done((f32[1,128,512]{2,1,0:T(8,128)S(1)}, f32[1,128,512]{2,1,0:T(8,128)S(1)}, u32[]{:S(2)}, u32[]{:S(2)}) %collective-permute-start.8) | collective-permute-done | bytes 262176 | tf_op jit(solution)/shard_map/ppermute | solution.py:140
  41.4 0.5 collective-permute-start.13
  41.9 1.7 %collective-permute-start.9 = (f32[1,128,512]{2,1,0:T(8,128)S(1)}, f32[1,128,512]{2,1,0:T(8,128)S(1)}, u32[]{:S(2)}, u32[]{:S(2)}) collective-permute-start(f32[1,128,512]{2,1,0:T(8,128)S(1)} %get-tuple-element.95), channel_id=1, source_target_pairs={{0,2},{1,3},{2,0},{3,1},{4,6},{5,7},{6,4},{7,5},{8,10},{9,11},{10,... | collective-permute-start | bytes 786440 | tf_op jit(solution)/shard_map/ppermute | solution.py:140
  43.7 7.1 %early_days.1 = (f32[256,512]{1,0:T(8,128)S(1)}, bf16[2,512,512]{2,1,0:T(8,128)(2,1)S(1)}, bf16[2,512,512]{2,1,0:T(8,128)(2,1)S(1)}, bf16[2,512,512]{2,1,0:T(8,1...) custom-call(s32[2,128]{1,0:T(2,128)S(1)} %broadcast_in_dim.2.where_r, ...), custom_call_target="tpu_custom_call" | custom-call | flops 1200000000 | bytes 1024 | tf_op jit(solution)/shard_map/early_days/pallas_call | solution.py:48
  50.9 1.5 %collective-permute-start.16 = (f32[72,512]{1,0:T(8,128)S(1)}, f32[72,512]{1,0:T(8,128)S(1)}, u32[]{:S(2)}, u32[]{:S(2)}) collective-permute-start(f32[72,512]{1,0:T(8,128)S(1)} %get-tuple-element.111), channel_id=1, source_target_pairs={{0,2},{1,3},{2,0},{3,1},{4,6},{5,7},{6,4},{7,5},{8,10},{9,11},{10,... | collective-permute-start | bytes 442376 | tf_op jit(solution)/shard_map/ppermute | solution.py:140
  52.4 0.6 collective-permute-start.7
  53.0 3.9 %day_2.1 = (bf16[2,512,512]{2,1,0:T(8,128)(2,1)S(1)}, bf16[2,512,512]{2,1,0:T(8,128)(2,1)S(1)}, f32[128,512]{1,0:T(8,128)S(1)}, f32[128,512]{1,0:T(8,128)S(1)}) custom-call(s32[2,128]{1,0:T(2,128)S(1)} %broadcast_in_dim.2.where_ref, f32[4,128,512]{2,1,0:T(8,128)S(1)} %copy-done.1, f32[4,128,512]{2,1,0:T(8,128)} %collective-permute-done.refs_1_, ...), custom_call_target="tpu_custom_call" | custom-call | flops 600000000 | bytes 1024 | tf_op jit(solution)/shard_map/day_2/pallas_call | solution.py:48
  56.9 1.6 %collective-permute-start.18 = (f32[128,512]{1,0:T(8,128)S(1)}, f32[128,512]{1,0:T(8,128)S(1)}, u32[]{:S(2)}, u32[]{:S(2)}) collective-permute-start(f32[128,512]{1,0:T(8,128)S(1)} %get-tuple-element.109), channel_id=1, source_target_pairs={{0,4},{4,0},{8,12},{12,8},{16,20},{20,16},{24,28},{28,24},{1,5},{5... | collective-permute-start | bytes 786440 | tf_op jit(solution)/shard_map/ppermute | solution.py:143
  58.5 1.5 %collective-permute-done.7.refs_2_ = f32[64,512]{1,0:T(8,128)S(1)} collective-permute-done((f32[64,512]{1,0:T(8,128)S(1)}, f32[64,512]{1,0:T(8,128)S(1)}, u32[]{:S(2)}, u32[]{:S(2)}) %collective-permute-start.7) | collective-permute-done | bytes 131104 | tf_op jit(solution)/shard_map/ppermute | solution.py:140
  60.0 1.3 %collective-permute-done.15.refs_3_ = f32[64,512]{1,0:T(8,128)S(1)} collective-permute-done((f32[64,512]{1,0:T(8,128)S(1)}, f32[64,512]{1,0:T(8,128)S(1)}, u32[]{:S(2)}, u32[]{:S(2)}) %collective-permute-start.15) | collective-permute-done | bytes 131104 | tf_op jit(solution)/shard_map/ppermute | solution.py:140
  61.3 2.4 %last_link.1 = (f32[512,512]{1,0:T(8,128)S(1)}, f32[256,512]{1,0:T(8,128)S(1)}, bf16[2,512,512]{2,1,0:T(8,128)(2,1)S(1)}) custom-call(s32[2,128]{1,0:T(2,128)S(1)} %broadcast_in_dim.2.where_ref, f32[4,128,512]{2,1,0:T(8,128)S(1)} %copy-done.1, f32[4,128,512]{2,1,0:T(8,128)} %collective-permute-done.refs_1_, f32[64,512]{1,0:T(8,128)S(1)} %collective-permute-done.7.refs_2_, ...), custom_call_target="tpu_custom_call" | custom-call | flops 300000000 | bytes 1024 | tf_op jit(solution)/shard_map/last_link/pallas_call | solution.py:48
  63.7 1.3 %collective-permute-done.18.other_ref = f32[128,512]{1,0:T(8,128)S(1)} collective-permute-done((f32[128,512]{1,0:T(8,128)S(1)}, f32[128,512]{1,0:T(8,128)S(1)}, u32[]{:S(2)}, u32[]{:S(2)}) %collective-permute-start.18) | collective-permute-done | bytes 262176 | tf_op jit(solution)/shard_map/ppermute | solution.py:143
  65.0 1.5 %collective-permute-start.19 = (f32[256,512]{1,0:T(8,128)S(1)}, f32[256,512]{1,0:T(8,128)S(1)}, u32[]{:S(2)}, u32[]{:S(2)}) collective-permute-start(f32[256,512]{1,0:T(8,128)S(1)} %get-tuple-element.116), channel_id=1, source_target_pairs={{0,4},{4,0},{8,12},{12,8},{16,20},{20,16},{24,28},{28,24},{1,5},{5... | collective-permute-start | bytes 1572872 | tf_op jit(solution)/shard_map/ppermute | solution.py:143
  66.6 4.5 %lines.1 = (f32[8,512]{1,0:T(8,128)S(1)}, f32[8,512]{1,0:T(8,128)S(1)}, f32[4,8,512]{2,1,0:T(8,128)S(1)}) custom-call(f32[4,512]{1,0:T(4,128)S(1)} %add.3.source_ref, f32[72,512]{1,0:T(8,128)S(1)} %collective-permute-done.16.refs_4_.refs_0_, bf16[2,512,512]{2,1,0:T(8,128)(2,1)S(1)} %get-tuple-element.102.refs_8_.refs_1_.refs_3_.refs_2_, ...), custom_call_target="tpu_custom_call" | custom-call | flops 1000000000 | bytes 1024 | tf_op jit(solution)/shard_map/lines/pallas_call | solution.py:48
  71.1 0.5 collective-permute-start.20
  71.6 2.7 %grams.1.gram_ref = bf16[2,512,512]{2,1,0:T(8,128)(2,1)S(1)} custom-call(f32[512,512]{1,0:T(8,128)S(1)} %get-tuple-element.125.gram_ref, bf16[2,512,512]{2,1,0:T(8,128)(2,1)S(1)} %get-tuple-element.119.refs_6_.refs_0_.refs_5_, bf16[2,512,512]{2,1,0:T(8,128)(2,1)S(1)} %get-tuple-element.108.refs_7_.refs_9_.refs_1_.refs_8_, ...), custom_call_target="tpu_custom_call" | custom-call | flops 600000000 | bytes 1024 | tf_op jit(solution)/shard_map/grams/pallas_call | solution.py:48
  74.3 1.8 %late_maps.1 = (bf16[2,512,512]{2,1,0:T(8,128)(2,1)S(1)}, bf16[2,512,512]{2,1,0:T(8,128)(2,1)S(1)}) custom-call(bf16[2,512,512]{2,1,0:T(8,128)(2,1)S(1)} %get-tuple-element.126.refs_10_.refs_7_.refs_0_, bf16[2,512,512]{2,1,0:T(8,128)(2,1)S(1)} %get-tuple-element.107.refs_5_.refs_10_.refs_1_, bf16[2,512,512]{2,1,0:T(8,128)(2,1)S(1)} %get-tuple-element.120.refs_8_.refs_2_, ...), custom_call_target="tpu_custom_call" | custom-call | flops 400000000 | bytes 1024 | tf_op jit(solution)/shard_map/late_maps/pallas_call | solution.py:48
  76.1 2.1 %collective-permute-done.20.other_flux_ref = f32[8,512]{1,0:T(8,128)S(1)} collective-permute-done((f32[8,512]{1,0:T(8,128)S(1)}, f32[8,512]{1,0:T(8,128)S(1)}, u32[]{:S(2)}, u32[]{:S(2)}) %collective-permute-start.20) | collective-permute-done | bytes 16416 | tf_op jit(solution)/shard_map/ppermute | solution.py:143
  78.2 1.9 %collective-permute-done.21.rest_ref = f32[256,512]{1,0:T(8,128)S(1)} collective-permute-done((f32[256,512]{1,0:T(8,128)S(1)}, f32[256,512]{1,0:T(8,128)S(1)}, u32[]{:S(2)}, u32[]{:S(2)}) %collective-permute-start.21) | collective-permute-done | bytes 524320 | tf_op jit(solution)/shard_map/ppermute | solution.py:140
  80.2 1.0 pair_maps.1
  81.2 0.7 collective-permute-start.22
  81.9 3.5 %collective-permute-start.23 = (f32[8,512]{1,0:T(8,128)S(1)}, f32[8,512]{1,0:T(8,128)S(1)}, u32[]{:S(2)}, u32[]{:S(2)}) collective-permute-start(f32[8,512]{1,0:T(8,128)S(1)} %get-tuple-element.134.local_ref), channel_id=1, source_target_pairs={{0,8},{4,12},{1,9},{5,13},{2,10},{6,14},{3,11},{7,15}} | collective-permute-start | bytes 49160 | tf_op jit(solution)/shard_map/ppermute | solution.py:146
  85.4 1.0 group_map.1.map_ref
  86.4 0.4 collective-permute-done.23.refs_0_
  86.8 0.5 forward_link.2
  87.3 0.7 collective-permute-start.24
  88.0 0.5 forward_link.3
  88.5 0.7 collective-permute-start.26
  89.2 0.4 noise_link.2
  89.6 0.7 collective-permute-start.25
  90.3 1.1 mean_turn.1
  91.4 1.5 %collective-permute-start.27 = (f32[16,512]{1,0:T(8,128)S(1)}, f32[16,512]{1,0:T(8,128)S(1)}, u32[]{:S(2)}, u32[]{:S(2)}) collective-permute-start(f32[16,512]{1,0:T(8,128)S(1)} %pad_maximum_fusion), channel_id=1, source_target_pairs={{0,4},{4,0},{8,12},{12,8},{16,20},{20,16},{24,28},{28,24},{1,5},{5... | collective-permute-start | bytes 98312 | tf_op jit(solution)/shard_map/ppermute | solution.py:143
  92.9 0.7 collective-permute-start.29
  93.6 0.7 collective-permute-start.28
  94.2 1.1 collective-permute-done.27
  95.3 0.4 noise_link.3
  96.0 1.3 %collective-permute-start.30 = (f32[128,512]{1,0:T(8,128)S(1)}, f32[128,512]{1,0:T(8,128)S(1)}, u32[]{:S(2)}, u32[]{:S(2)}) collective-permute-start(f32[128,512]{1,0:T(8,128)S(1)} %noise_link.3), channel_id=1, source_target_pairs={{8,0},{12,4},{9,1},{13,5},{10,2},{14,6},{11,3},{15,7}} | collective-permute-start | bytes 786440 | tf_op jit(solution)/shard_map/ppermute | solution.py:146
  97.3 0.7 collective-permute-start.31
  98.3 11.0 %collective-permute-done.30.refs_2_ = f32[128,512]{1,0:T(8,128)S(1)} collective-permute-done((f32[128,512]{1,0:T(8,128)S(1)}, f32[128,512]{1,0:T(8,128)S(1)}, u32[]{:S(2)}, u32[]{:S(2)}) %collective-permute-start.30) | collective-permute-done | bytes 262176 | tf_op jit(solution)/shard_map/ppermute | solution.py:146
  109.4 0.4 divide.1
  109.8 1.6 %collective-permute-start.32 = (f32[128,512]{1,0:T(8,128)S(1)}, f32[128,512]{1,0:T(8,128)S(1)}, u32[]{:S(2)}, u32[]{:S(2)}) collective-permute-start(f32[128,512]{1,0:T(8,128)S(1)} %get-tuple-element.153), channel_id=1, source_target_pairs={{0,4},{4,0},{8,12},{12,8},{16,20},{20,16},{24,28},{28,24},{1,5},{5... | collective-permute-start | bytes 786440 | tf_op jit(solution)/shard_map/ppermute | solution.py:143
  111.4 1.5 %collective-permute-start.33 = (f32[8,512]{1,0:T(8,128)S(1)}, f32[8,512]{1,0:T(8,128)S(1)}, u32[]{:S(2)}, u32[]{:S(2)}) collective-permute-start(f32[8,512]{1,0:T(8,128)S(1)} %backward_link.1), channel_id=1, source_target_pairs={{8,0},{12,4},{9,1},{13,5},{10,2},{14,6},{11,3},{15,7}} | collective-permute-start | bytes 49160 | tf_op jit(solution)/shard_map/ppermute | solution.py:146
  112.9 3.1 %mean_terms.1 = (f32[256,512]{1,0:T(8,128)S(1)}, f32[256,512]{1,0:T(8,128)S(1)}, f32[256,512]{1,0:T(8,128)S(1)}, f32[256,512]{1,0:T(8,128)S(1)}) custom-call(f32[8,512]{1,0:T(8,128)S(1)} %get-tuple-element.156.entering_ref, f32[4,8,512]{2,1,0:T(8,128)S(1)} %get-tuple-element.157.current_ref, f32[256,512]{1,0:T(8,128)S(1)} %get-tuple-element.101.refs_7_.refs_0_, ...), custom_call_target="tpu_custom_call" | custom-call | flops 800000000 | bytes 1024 | tf_op jit(solution)/shard_map/mean_terms/pallas_call | solution.py:48
  116.0 1.0 collective-permute-done.33.refs_3_
  117.0 3.4 %last_days.1 = f32[4,512,256]{2,1,0:T(8,128)} custom-call(s32[2,128]{1,0:T(2,128)S(1)} %broadcast_in_dim.2.where_ref, f32[128,512]{1,0:T(8,128)S(1)} %get-tuple-element.152.keep_ref, f32[128,512]{1,0:T(8,128)S(1)} %collective-permute-done.32.got_ref, f32[8,512]{1,0:T(8,128)S(1)} %get-tuple-element.154.back_ref, ...), custom_call_target="tpu_custom_call" | custom-call | flops 800000000 | bytes 1024 | tf_op jit(solution)/shard_map/last_days/pallas_call | solution.py:48
  (43 shorter events, 1.5 us)
Async XLA Ops:
  0.0 9.3 %copy-start.1 = (f32[4,128,512]{2,1,0:T(8,128)S(1)}, f32[4,128,512]{2,1,0:T(8,128)}, u32[]{:S(2)}) copy-start(f32[4,128,512]{2,1,0:T(8,128)} %refs_0_.7) | copy-start | bytes 3145732
  0.0 30.0 %copy-start = (f32[4,512,256]{2,1,0:T(8,128)S(1)}, f32[4,512,256]{2,1,0:T(8,128)}, u32[]{:S(2)}) copy-start(f32[4,512,256]{2,1,0:T(8,128)} %refs_4_.3) | copy-start | bytes 6291460
  0.0 9.4 %collective-permute-start = (f32[4,128,512]{2,1,0:T(8,128)}, f32[4,128,512]{2,1,0:T(8,128)}, u32[]{:S(2)}, u32[]{:S(2)}) collective-permute-start(f32[4,128,512]{2,1,0:T(8,128)} %refs_0_.7), channel_id=1, source_target_pairs={{0,1},{1,0},{2,3},{3,2},{4,5},{5,4},{6,7},{7,6},{8,9},{9,8},{10,11... | collective-permute-start | bytes 3145736 | tf_op jit(solution)/shard_map/ppermute | solution.py:140
  0.5 26.6 %collective-permute-start.5 = (f32[4,128,512]{2,1,0:T(8,128)}, f32[4,128,512]{2,1,0:T(8,128)}, u32[]{:S(2)}, u32[]{:S(2)}) collective-permute-start(f32[4,128,512]{2,1,0:T(8,128)} %refs_0_.4), channel_id=1, source_target_pairs={{0,2},{1,3},{2,0},{3,1},{4,6},{5,7},{6,4},{7,5},{8,10},{9,11},{10,... | collective-permute-start | bytes 3145736 | tf_op jit(solution)/shard_map/ppermute | solution.py:140
  6.7 5.2 %collective-permute-start.1 = (f32[16,512]{1,0:T(8,128)S(1)}, f32[16,512]{1,0:T(8,128)S(1)}, u32[]{:S(2)}, u32[]{:S(2)}) collective-permute-start(f32[16,512]{1,0:T(8,128)S(1)} %get-tuple-element.87), channel_id=1, source_target_pairs={{0,16},{4,20},{8,24},{12,28},{16,0},{20,4},{24,8},{28,12},{1,17},{... | collective-permute-start | bytes 98312 | tf_op jit(solution)/shard_map/ppermute | solution.py:190
  12.0 3.8 %collective-permute-start.2 = (f32[8,512]{1,0:T(8,128)S(1)}, f32[8,512]{1,0:T(8,128)S(1)}, u32[]{:S(2)}, u32[]{:S(2)}) collective-permute-start(f32[8,512]{1,0:T(8,128)S(1)} %get-tuple-element.89), channel_id=1, source_target_pairs={{0,8},{4,12},{8,0},{12,4},{16,24},{20,28},{24,16},{28,20},{1,9},{5... | collective-permute-start | bytes 49160 | tf_op jit(solution)/shard_map/ppermute | solution.py:190
  15.8 3.7 %collective-permute-start.3 = (f32[4,512]{1,0:T(4,128)S(1)}, f32[4,512]{1,0:T(4,128)S(1)}, u32[]{:S(2)}, u32[]{:S(2)}) collective-permute-start(f32[4,512]{1,0:T(4,128)S(1)} %get-tuple-element.91), channel_id=1, source_target_pairs={{0,4},{4,0},{8,12},{12,8},{16,20},{20,16},{24,28},{28,24},{1,5},{5... | collective-permute-start | bytes 24584 | tf_op jit(solution)/shard_map/ppermute | solution.py:190
  19.5 1.2 collective-permute-start.4
  19.5 9.6 %collective-permute-start.10 = (f32[4,128,512]{2,1,0:T(8,128)}, f32[4,128,512]{2,1,0:T(8,128)S(1)}, u32[]{:S(2)}, u32[]{:S(2)}) collective-permute-start(f32[4,128,512]{2,1,0:T(8,128)} %refs_0_.4), channel_id=1, source_target_pairs={{0,1},{1,0},{2,3},{3,2},{4,5},{5,4},{6,7},{7,6},{8,9},{9,8},{10,11... | collective-permute-start | bytes 3145736 | tf_op jit(solution)/shard_map/ppermute | solution.py:140
  27.1 2.9 %collective-permute-start.11 = (f32[4,128,512]{2,1,0:T(8,128)}, f32[4,128,512]{2,1,0:T(8,128)S(1)}, u32[]{:S(2)}, u32[]{:S(2)}) collective-permute-start(f32[4,128,512]{2,1,0:T(8,128)} %collective-permute-done.5.refs_2_), channel_id=1, source_target_pairs={{0,1},{1,0},{2,3},{3,2},{4,5},{5,4},{6,7},{7,6},{8,9},{9,8},{10,11... | collective-permute-start | bytes 3145736 | tf_op jit(solution)/shard_map/ppermute | solution.py:140
  27.1 9.1 %collective-permute-start.6 = (f32[1,128,512]{2,1,0:T(8,128)S(1)}, f32[1,128,512]{2,1,0:T(8,128)S(1)}, u32[]{:S(2)}, u32[]{:S(2)}) collective-permute-start(f32[1,128,512]{2,1,0:T(8,128)S(1)} %get-tuple-element.93), channel_id=1, source_target_pairs={{0,2},{1,3},{2,0},{3,1},{4,6},{5,7},{6,4},{7,5},{8,10},{9,11},{10,... | collective-permute-start | bytes 786440 | tf_op jit(solution)/shard_map/ppermute | solution.py:140
  28.8 12.6 %collective-permute-start.8 = (f32[1,128,512]{2,1,0:T(8,128)S(1)}, f32[1,128,512]{2,1,0:T(8,128)S(1)}, u32[]{:S(2)}, u32[]{:S(2)}) collective-permute-start(f32[1,128,512]{2,1,0:T(8,128)S(1)} %get-tuple-element.168), channel_id=1, source_target_pairs={{0,2},{1,3},{2,0},{3,1},{4,6},{5,7},{6,4},{7,5},{8,10},{9,11},{10,... | collective-permute-start | bytes 786440 | tf_op jit(solution)/shard_map/ppermute | solution.py:140
  30.0 1.2 %copy-start.2 = (f32[4,128,512]{2,1,0:T(8,128)S(1)}, f32[4,128,512]{2,1,0:T(8,128)}, u32[]{:S(2)}) copy-start(f32[4,128,512]{2,1,0:T(8,128)} %refs_0_.4) | copy-start | bytes 3145732
  41.4 2.3 %collective-permute-start.12 = (f32[1,128,512]{2,1,0:T(8,128)S(1)}, f32[1,128,512]{2,1,0:T(8,128)S(1)}, u32[]{:S(2)}, u32[]{:S(2)}) collective-permute-start(f32[1,128,512]{2,1,0:T(8,128)S(1)} %collective-permute-done.8.refs_2_), channel_id=1, source_target_pairs={{0,1},{1,0},{2,3},{3,2},{4,5},{5,4},{6,7},{7,6},{8,9},{9,8},{10,11... | collective-permute-start | bytes 786440 | tf_op jit(solution)/shard_map/ppermute | solution.py:140
  41.4 2.3 %collective-permute-start.13 = (f32[1,128,512]{2,1,0:T(8,128)S(1)}, f32[1,128,512]{2,1,0:T(8,128)S(1)}, u32[]{:S(2)}, u32[]{:S(2)}) collective-permute-start(f32[1,128,512]{2,1,0:T(8,128)S(1)} %collective-permute-done.6.refs_4_), channel_id=1, source_target_pairs={{0,1},{1,0},{2,3},{3,2},{4,5},{5,4},{6,7},{7,6},{8,9},{9,8},{10,11... | collective-permute-start | bytes 786440 | tf_op jit(solution)/shard_map/ppermute | solution.py:140
  41.9 8.9 %collective-permute-start.9 = (f32[1,128,512]{2,1,0:T(8,128)S(1)}, f32[1,128,512]{2,1,0:T(8,128)S(1)}, u32[]{:S(2)}, u32[]{:S(2)}) collective-permute-start(f32[1,128,512]{2,1,0:T(8,128)S(1)} %get-tuple-element.95), channel_id=1, source_target_pairs={{0,2},{1,3},{2,0},{3,1},{4,6},{5,7},{6,4},{7,5},{8,10},{9,11},{10,... | collective-permute-start | bytes 786440 | tf_op jit(solution)/shard_map/ppermute | solution.py:140
  50.8 2.2 %collective-permute-start.14 = (f32[1,128,512]{2,1,0:T(8,128)S(1)}, f32[1,128,512]{2,1,0:T(8,128)S(1)}, u32[]{:S(2)}, u32[]{:S(2)}) collective-permute-start(f32[1,128,512]{2,1,0:T(8,128)S(1)} %collective-permute-done.9.refs_2_), channel_id=1, source_target_pairs={{0,1},{1,0},{2,3},{3,2},{4,5},{5,4},{6,7},{7,6},{8,9},{9,8},{10,11... | collective-permute-start | bytes 786440 | tf_op jit(solution)/shard_map/ppermute | solution.py:140
  50.9 7.6 %collective-permute-start.16 = (f32[72,512]{1,0:T(8,128)S(1)}, f32[72,512]{1,0:T(8,128)S(1)}, u32[]{:S(2)}, u32[]{:S(2)}) collective-permute-start(f32[72,512]{1,0:T(8,128)S(1)} %get-tuple-element.111), channel_id=1, source_target_pairs={{0,2},{1,3},{2,0},{3,1},{4,6},{5,7},{6,4},{7,5},{8,10},{9,11},{10,... | collective-permute-start | bytes 442376 | tf_op jit(solution)/shard_map/ppermute | solution.py:140
  52.4 7.5 %collective-permute-start.7 = (f32[64,512]{1,0:T(8,128)S(1)}, f32[64,512]{1,0:T(8,128)S(1)}, u32[]{:S(2)}, u32[]{:S(2)}) collective-permute-start(f32[64,512]{1,0:T(8,128)S(1)} %get-tuple-element.94), channel_id=1, source_target_pairs={{0,2},{1,3},{2,0},{3,1},{4,6},{5,7},{6,4},{7,5},{8,10},{9,11},{10,... | collective-permute-start | bytes 393224 | tf_op jit(solution)/shard_map/ppermute | solution.py:140
  56.9 8.2 %collective-permute-start.18 = (f32[128,512]{1,0:T(8,128)S(1)}, f32[128,512]{1,0:T(8,128)S(1)}, u32[]{:S(2)}, u32[]{:S(2)}) collective-permute-start(f32[128,512]{1,0:T(8,128)S(1)} %get-tuple-element.109), channel_id=1, source_target_pairs={{0,4},{4,0},{8,12},{12,8},{16,20},{20,16},{24,28},{28,24},{1,5},{5... | collective-permute-start | bytes 786440 | tf_op jit(solution)/shard_map/ppermute | solution.py:143
  58.5 2.9 %collective-permute-start.17 = (f32[72,512]{1,0:T(8,128)S(1)}, f32[72,512]{1,0:T(8,128)S(1)}, u32[]{:S(2)}, u32[]{:S(2)}) collective-permute-start(f32[72,512]{1,0:T(8,128)S(1)} %collective-permute-done.16.refs_4_.refs_0_), channel_id=1, source_target_pairs={{0,1},{1,0},{2,3},{3,2},{4,5},{5,4},{6,7},{7,6},{8,9},{9,8},{10,11... | collective-permute-start | bytes 442376 | tf_op jit(solution)/shard_map/ppermute | solution.py:140
  60.0 1.3 %collective-permute-start.15 = (f32[64,512]{1,0:T(8,128)S(1)}, f32[64,512]{1,0:T(8,128)S(1)}, u32[]{:S(2)}, u32[]{:S(2)}) collective-permute-start(f32[64,512]{1,0:T(8,128)S(1)} %collective-permute-done.7.refs_2_), channel_id=1, source_target_pairs={{0,1},{1,0},{2,3},{3,2},{4,5},{5,4},{6,7},{7,6},{8,9},{9,8},{10,11... | collective-permute-start | bytes 393224 | tf_op jit(solution)/shard_map/ppermute | solution.py:140
  65.0 13.2 %collective-permute-start.19 = (f32[256,512]{1,0:T(8,128)S(1)}, f32[256,512]{1,0:T(8,128)S(1)}, u32[]{:S(2)}, u32[]{:S(2)}) collective-permute-start(f32[256,512]{1,0:T(8,128)S(1)} %get-tuple-element.116), channel_id=1, source_target_pairs={{0,4},{4,0},{8,12},{12,8},{16,20},{20,16},{24,28},{28,24},{1,5},{5... | collective-permute-start | bytes 1572872 | tf_op jit(solution)/shard_map/ppermute | solution.py:143
  71.1 7.2 %collective-permute-start.20 = (f32[8,512]{1,0:T(8,128)S(1)}, f32[8,512]{1,0:T(8,128)S(1)}, u32[]{:S(2)}, u32[]{:S(2)}) collective-permute-start(f32[8,512]{1,0:T(8,128)S(1)} %get-tuple-element.122.flux_ref), channel_id=1, source_target_pairs={{0,4},{4,0},{8,12},{12,8},{16,20},{20,16},{24,28},{28,24},{1,5},{5... | collective-permute-start | bytes 49160 | tf_op jit(solution)/shard_map/ppermute | solution.py:143
  78.2 1.9 %collective-permute-start.21 = (f32[256,512]{1,0:T(8,128)S(1)}, f32[256,512]{1,0:T(8,128)S(1)}, u32[]{:S(2)}, u32[]{:S(2)}) collective-permute-start(f32[256,512]{1,0:T(8,128)S(1)} %collective-permute-done.19.half_ref), channel_id=1, source_target_pairs={{0,1},{1,0},{2,3},{3,2},{4,5},{5,4},{6,7},{7,6},{8,9},{9,8},{10,11... | collective-permute-start | bytes 1572872 | tf_op jit(solution)/shard_map/ppermute | solution.py:140
  81.2 8.0 %collective-permute-start.22 = (f32[128,512]{1,0:T(8,128)S(1)}, f32[128,512]{1,0:T(8,128)S(1)}, u32[]{:S(2)}, u32[]{:S(2)}) collective-permute-start(f32[128,512]{1,0:T(8,128)S(1)} %get-tuple-element.135.local_ref), channel_id=1, source_target_pairs={{24,16},{28,20},{25,17},{29,21},{26,18},{30,22},{27,19},{31,23}} | collective-permute-start | bytes 786440 | tf_op jit(solution)/shard_map/ppermute | solution.py:146
  81.9 4.9 %collective-permute-start.23 = (f32[8,512]{1,0:T(8,128)S(1)}, f32[8,512]{1,0:T(8,128)S(1)}, u32[]{:S(2)}, u32[]{:S(2)}) collective-permute-start(f32[8,512]{1,0:T(8,128)S(1)} %get-tuple-element.134.local_ref), channel_id=1, source_target_pairs={{0,8},{4,12},{1,9},{5,13},{2,10},{6,14},{3,11},{7,15}} | collective-permute-start | bytes 49160 | tf_op jit(solution)/shard_map/ppermute | solution.py:146
  87.3 0.7 collective-permute-start.24
  88.5 1.8 %collective-permute-start.26 = (f32[8,512]{1,0:T(8,128)S(1)}, f32[8,512]{1,0:T(8,128)S(1)}, u32[]{:S(2)}, u32[]{:S(2)}) collective-permute-start(f32[8,512]{1,0:T(8,128)S(1)} %forward_link.3), channel_id=1, source_target_pairs={{16,24},{20,28},{17,25},{21,29},{18,26},{22,30},{19,27},{23,31}} | collective-permute-start | bytes 49160 | tf_op jit(solution)/shard_map/ppermute | solution.py:146
  89.6 5.7 %collective-permute-start.25 = (f32[128,512]{1,0:T(8,128)S(1)}, f32[128,512]{1,0:T(8,128)S(1)}, u32[]{:S(2)}, u32[]{:S(2)}) collective-permute-start(f32[128,512]{1,0:T(8,128)S(1)} %noise_link.2), channel_id=1, source_target_pairs={{16,8},{20,12},{17,9},{21,13},{18,10},{22,14},{19,11},{23,15}} | collective-permute-start | bytes 786440 | tf_op jit(solution)/shard_map/ppermute | solution.py:146
  91.4 3.9 %collective-permute-start.27 = (f32[16,512]{1,0:T(8,128)S(1)}, f32[16,512]{1,0:T(8,128)S(1)}, u32[]{:S(2)}, u32[]{:S(2)}) collective-permute-start(f32[16,512]{1,0:T(8,128)S(1)} %pad_maximum_fusion), channel_id=1, source_target_pairs={{0,4},{4,0},{8,12},{12,8},{16,20},{20,16},{24,28},{28,24},{1,5},{5... | collective-permute-start | bytes 98312 | tf_op jit(solution)/shard_map/ppermute | solution.py:143
  92.9 2.8 %collective-permute-start.29 = (f32[8,512]{1,0:T(8,128)S(1)}, f32[8,512]{1,0:T(8,128)S(1)}, u32[]{:S(2)}, u32[]{:S(2)}) collective-permute-start(f32[8,512]{1,0:T(8,128)S(1)} %get-tuple-element.143.part_ref), channel_id=1, source_target_pairs={{24,20},{28,16},{25,21},{29,17},{26,22},{30,18},{27,23},{31,19}} | collective-permute-start | bytes 49160 | tf_op jit(solution)/shard_map/ppermute | solution.py:504
  93.6 2.2 %collective-permute-start.28 = (f32[8,512]{1,0:T(8,128)S(1)}, f32[8,512]{1,0:T(8,128)S(1)}, u32[]{:S(2)}, u32[]{:S(2)}) collective-permute-start(f32[8,512]{1,0:T(8,128)S(1)} %get-tuple-element.143.part_ref), channel_id=1, source_target_pairs={{24,16},{28,20},{25,17},{29,21},{26,18},{30,22},{27,19},{31,23}} | collective-permute-start | bytes 49160 | tf_op jit(solution)/shard_map/ppermute | solution.py:504
  96.0 13.3 %collective-permute-start.30 = (f32[128,512]{1,0:T(8,128)S(1)}, f32[128,512]{1,0:T(8,128)S(1)}, u32[]{:S(2)}, u32[]{:S(2)}) collective-permute-start(f32[128,512]{1,0:T(8,128)S(1)} %noise_link.3), channel_id=1, source_target_pairs={{8,0},{12,4},{9,1},{13,5},{10,2},{14,6},{11,3},{15,7}} | collective-permute-start | bytes 786440 | tf_op jit(solution)/shard_map/ppermute | solution.py:146
  97.3 0.7 collective-permute-start.31
  109.8 7.2 %collective-permute-start.32 = (f32[128,512]{1,0:T(8,128)S(1)}, f32[128,512]{1,0:T(8,128)S(1)}, u32[]{:S(2)}, u32[]{:S(2)}) collective-permute-start(f32[128,512]{1,0:T(8,128)S(1)} %get-tuple-element.153), channel_id=1, source_target_pairs={{0,4},{4,0},{8,12},{12,8},{16,20},{20,16},{24,28},{28,24},{1,5},{5... | collective-permute-start | bytes 786440 | tf_op jit(solution)/shard_map/ppermute | solution.py:143
  111.4 5.6 %collective-permute-start.33 = (f32[8,512]{1,0:T(8,128)S(1)}, f32[8,512]{1,0:T(8,128)S(1)}, u32[]{:S(2)}, u32[]{:S(2)}) collective-permute-start(f32[8,512]{1,0:T(8,128)S(1)} %backward_link.1), channel_id=1, source_target_pairs={{8,0},{12,4},{9,1},{13,5},{10,2},{14,6},{11,3},{15,7}} | collective-permute-start | bytes 49160 | tf_op jit(solution)/shard_map/ppermute | solution.py:146

commit v9 on v8

--- a/solution.py
+++ b/solution.py
@@ -134,7 +134,7 @@
     groups = part_count // PAIR
     chips = row_count // CORES
     early = day_count // 2
-    late = day_count - early
+    rest = day_count - 1
 
     def to_row(value, distance):
         return lax.ppermute(value, "row", [(i, i ^ distance) for i in range(row_count)])
@@ -183,7 +183,7 @@
         send_rows(rows)
     own_inverse = [inv_diag, to_row(inv_diag, 1)]
     own_link = [coupling, to_row(coupling, 1)]
-    where = after(where, keep, own_link[1], *link_rows)
+    where = after(where, keep, *link_rows)
 
     distance = part_count // 2
     while distance:
@@ -254,8 +254,6 @@
             path = split(-dot_parts(link, moved, NN))
             if day == 0:
                 store(map_outs[0], path)
-            else:
-                store(map_outs[day], split(-dot_parts(link, parts(inverse_refs[day]), NN)))
             moved = split(dot_parts(parts(inverse_refs[day + 1]), path, NN))
             store(moved_outs[day], moved)
             total = total + dot_parts(split(noise_ref[day + 1]), moved, TN)
@@ -263,7 +261,7 @@
 
     summed, *results = call(
         early_body,
-        [samples_full, *[map_parts] * (3 * early)],
+        [samples_full, *[map_parts] * (2 * early + 1)],
         "early_days",
         (where,),
         [
@@ -390,19 +388,19 @@
     gram = call(grams_body, map_parts, "grams", (), [after(gram, flux), *moveds[1:]], work=3)
 
     def late_maps_body(*refs):
-        for index in range(late):
+        for index in range(rest):
             store(
-                refs[2 * late + index],
-                split(-dot_parts(parts(refs[late + index]), parts(refs[index]), NN)),
+                refs[2 * rest + index],
+                split(-dot_parts(parts(refs[rest + index]), parts(refs[index]), NN)),
             )
 
     step_maps += call(
         late_maps_body,
-        [map_parts] * late,
+        [map_parts] * rest,
         "late_maps",
         (),
-        [after(inverses[early], gram), *inverses[early + 1 :], *links[early:]],
-        work=late,
+        [after(inverses[1], gram), *inverses[2:], *links[1:]],
+        work=rest,
     )
 
     other_rest = to_row(after(other_half, other_flux, *step_maps), 1)

time: 121 us -> 119 us (0.983)
  Pallas kernels: 41.2 us -> 37.6 us
    pallas_call x24, Pallas kernels: 41.2 us -> 37.6 us  [call(): pl.pallas_call(body, out_shape=out_shape, in_specs=[vmem] * (len(scalars)...]
    ppermute x16, waiting for transfers between devices: 17.9 us -> 19.5 us  [to_row(): lax.ppermute(value, 'row', [(i, i ^ distance) for i in range(row_count)])]
  transfers between devices with their start and end apart: 34 -> 34, of which waited for: 17 -> 18; matrix products, arithmetic and copies ran while one was open for 2% -> 2% of each run, Pallas kernels for 30% -> 27%
where the time goes in v9:
time: 119 us; the launch traced here: 118 us
  waiting for transfers between devices  42.2 us (35%)
  Pallas kernels  37.6 us (32%)
  starting transfers between devices  34.2 us (29%)
  local copies, waits for them, and re-layouts  3.55 us (3%)
    pallas_call x24, Pallas kernels, call(): pl.pallas_call(body, out_shape=out_shape, in_specs=[vmem] * (len(scalars)...  37.6 us
    ppermute x16, waiting for transfers between devices, to_row(): lax.ppermute(value, 'row', [(i, i ^ distance) for i in range(row_count)])  19.5 us
    ppermute x8, waiting for transfers between devices, to_group(): lax.ppermute(value, 'tm', [(PAIR * source + i, PAIR * target + i) for i i...  12.5 us
    ppermute x16, starting transfers between devices, to_row(): lax.ppermute(value, 'row', [(i, i ^ distance) for i in range(row_count)])  10.3 us
    ppermute x8, starting transfers between devices, to_group(): lax.ppermute(value, 'tm', [(PAIR * source + i, PAIR * target + i) for i i...  9.82 us
    ppermute x5, starting transfers between devices, to_pair(): return lax.ppermute(value, 'tm', [(i, i ^ 1) for i in range(part_count)])  6.98 us
    ppermute x3, waiting for transfers between devices, local(): lax.ppermute(sent, 'tm', [(i, i ^ distance) for i in range(part_count)])  6.42 us
    ppermute x3, starting transfers between devices, local(): lax.ppermute(sent, 'tm', [(i, i ^ distance) for i in range(part_count)])  5.86 us
  transfers between devices with their start and end apart: 34, of which 18 were waited for; matrix products, arithmetic and copies ran while one was open for 2% of the time, Pallas kernels for 27%

profile of v9, /device:TPU:0, one launch (start us, length us, event | category | flops | bytes accessed | tf_op | source)
XLA Modules:
  0.0 118.2 jit_solution(13350994037748197917)
XLA Ops:
  0.0 2.9 %collective-permute-start.5 = (f32[4,128,512]{2,1,0:T(8,128)}, f32[4,128,512]{2,1,0:T(8,128)}, u32[]{:S(2)}, u32[]{:S(2)}) collective-permute-start(f32[4,128,512]{2,1,0:T(8,128)} %refs_0_.4), channel_id=1, source_target_pairs={{0,2},{1,3},{2,0},{3,1},{4,6},{5,7},{6,4},{7,5},{8,10},{9,11},{10,... | collective-permute-start | bytes 3145736 | tf_op jit(solution)/shard_map/ppermute | solution.py:140
  2.9 0.7 reshape.10.day_ref
  3.7 0.7 reshape.11.node_ref
  4.4 0.7 reshape.12.value_ref
  5.3 1.4 %bin_observations.1 = (f32[16,512]{1,0:T(8,128)S(1)}, f32[16,512]{1,0:T(8,128)S(1)}) custom-call(s32[2,128]{1,0:T(2,128)S(1)} %broadcast_in_dim.2.where_ref, s32[8,512]{1,0:T(8,128)S(1)} %reshape.10.day_ref, s32[8,512]{1,0:T(8,128)S(1)} %reshape.11.node_ref, f32[8,512]{1,0:T(8,128)S(1)} %reshape.12.value_ref), custom_call_target="tpu_custom_call" | custom-call | flops 400000000 | bytes 1024 | tf_op jit(solution)/shard_map/bin_observations/pallas_call | solution.py:48
  6.6 2.6 %collective-permute-start.1 = (f32[16,512]{1,0:T(8,128)S(1)}, f32[16,512]{1,0:T(8,128)S(1)}, u32[]{:S(2)}, u32[]{:S(2)}) collective-permute-start(f32[16,512]{1,0:T(8,128)S(1)} %get-tuple-element.87), channel_id=1, source_target_pairs={{0,16},{4,20},{8,24},{12,28},{16,0},{20,4},{24,8},{28,12},{1,17},{... | collective-permute-start | bytes 98312 | tf_op jit(solution)/shard_map/ppermute | solution.py:190
  9.4 2.1 %collective-permute-done.1.got_ref = f32[16,512]{1,0:T(8,128)S(1)} collective-permute-done((f32[16,512]{1,0:T(8,128)S(1)}, f32[16,512]{1,0:T(8,128)S(1)}, u32[]{:S(2)}, u32[]{:S(2)}) %collective-permute-start.1) | collective-permute-done | bytes 32800 | tf_op jit(solution)/shard_map/ppermute | solution.py:190
  11.5 1.6 %collective-permute-start.2 = (f32[8,512]{1,0:T(8,128)S(1)}, f32[8,512]{1,0:T(8,128)S(1)}, u32[]{:S(2)}, u32[]{:S(2)}) collective-permute-start(f32[8,512]{1,0:T(8,128)S(1)} %get-tuple-element.89), channel_id=1, source_target_pairs={{0,8},{4,12},{8,0},{12,4},{16,24},{20,28},{24,16},{28,20},{1,9},{5... | collective-permute-start | bytes 49160 | tf_op jit(solution)/shard_map/ppermute | solution.py:190
  13.2 2.2 %collective-permute-done.2.got_ref = f32[8,512]{1,0:T(8,128)S(1)} collective-permute-done((f32[8,512]{1,0:T(8,128)S(1)}, f32[8,512]{1,0:T(8,128)S(1)}, u32[]{:S(2)}, u32[]{:S(2)}) %collective-permute-start.2) | collective-permute-done | bytes 16416 | tf_op jit(solution)/shard_map/ppermute | solution.py:190
  15.4 1.6 %collective-permute-start.3 = (f32[4,512]{1,0:T(4,128)S(1)}, f32[4,512]{1,0:T(4,128)S(1)}, u32[]{:S(2)}, u32[]{:S(2)}) collective-permute-start(f32[4,512]{1,0:T(4,128)S(1)} %get-tuple-element.91), channel_id=1, source_target_pairs={{0,4},{4,0},{8,12},{12,8},{16,20},{20,16},{24,28},{28,24},{1,5},{5... | collective-permute-start | bytes 24584 | tf_op jit(solution)/shard_map/ppermute | solution.py:190
  17.0 2.1 %collective-permute-done.3.got_ref = f32[4,512]{1,0:T(4,128)S(1)} collective-permute-done((f32[4,512]{1,0:T(4,128)S(1)}, f32[4,512]{1,0:T(4,128)S(1)}, u32[]{:S(2)}, u32[]{:S(2)}) %collective-permute-start.3) | collective-permute-done | bytes 8224 | tf_op jit(solution)/shard_map/ppermute | solution.py:190
  19.1 0.5 collective-permute-start.10
  19.6 0.7 collective-permute-done.4
  20.3 6.1 %collective-permute-done.5.refs_2_ = f32[4,128,512]{2,1,0:T(8,128)} collective-permute-done((f32[4,128,512]{2,1,0:T(8,128)}, f32[4,128,512]{2,1,0:T(8,128)}, u32[]{:S(2)}, u32[]{:S(2)}) %collective-permute-start.5) | collective-permute-done | bytes 1048608 | tf_op jit(solution)/shard_map/ppermute | solution.py:140
  26.4 0.5 collective-permute-start
  26.9 1.7 %collective-permute-start.6 = (f32[1,128,512]{2,1,0:T(8,128)S(1)}, f32[1,128,512]{2,1,0:T(8,128)S(1)}, u32[]{:S(2)}, u32[]{:S(2)}) collective-permute-start(f32[1,128,512]{2,1,0:T(8,128)S(1)} %get-tuple-element.93), channel_id=1, source_target_pairs={{0,2},{1,3},{2,0},{3,1},{4,6},{5,7},{6,4},{7,5},{8,10},{9,11},{10,... | collective-permute-start | bytes 786440 | tf_op jit(solution)/shard_map/ppermute | solution.py:140
  29.0 1.8 %collective-permute-done.11.refs_3_ = f32[4,128,512]{2,1,0:T(8,128)S(1)} collective-permute-done((f32[4,128,512]{2,1,0:T(8,128)}, f32[4,128,512]{2,1,0:T(8,128)S(1)}, u32[]{:S(2)}, u32[]{:S(2)}) %collective-permute-start.11) | collective-permute-done | bytes 1048608 | tf_op jit(solution)/shard_map/ppermute | solution.py:140
  30.8 1.2 %copy-done.2 = f32[4,128,512]{2,1,0:T(8,128)S(1)} copy-done((f32[4,128,512]{2,1,0:T(8,128)S(1)}, f32[4,128,512]{2,1,0:T(8,128)}, u32[]{:S(2)}) %copy-start.2) | copy-done | bytes 1048600
  32.0 4.9 %inverses.1 = (f32[512,512]{1,0:T(8,128)S(1)}, bf16[2,512,512]{2,1,0:T(8,128)(2,1)S(1)}, bf16[2,512,512]{2,1,0:T(8,128)(2,1)S(1)}, bf16[2,512,512]{2,1,0:T(8,128...) custom-call(s32[2,128]{1,0:T(2,128)S(1)} %broadcast_in_dim.2.where_r, ...), custom_call_target="tpu_custom_call" | custom-call | flops 800000000 | bytes 1024 | tf_op jit(solution)/shard_map/inverses/pallas_call | solution.py:48
  36.9 3.8 %collective-permute-done.8.refs_2_ = f32[1,128,512]{2,1,0:T(8,128)S(1)} collective-permute-done((f32[1,128,512]{2,1,0:T(8,128)S(1)}, f32[1,128,512]{2,1,0:T(8,128)S(1)}, u32[]{:S(2)}, u32[]{:S(2)}) %collective-permute-start.8) | collective-permute-done | bytes 262176 | tf_op jit(solution)/shard_map/ppermute | solution.py:140
  40.8 0.5 collective-permute-start.13
  41.3 1.7 %collective-permute-start.9 = (f32[1,128,512]{2,1,0:T(8,128)S(1)}, f32[1,128,512]{2,1,0:T(8,128)S(1)}, u32[]{:S(2)}, u32[]{:S(2)}) collective-permute-start(f32[1,128,512]{2,1,0:T(8,128)S(1)} %get-tuple-element.95), channel_id=1, source_target_pairs={{0,2},{1,3},{2,0},{3,1},{4,6},{5,7},{6,4},{7,5},{8,10},{9,11},{10,... | collective-permute-start | bytes 786440 | tf_op jit(solution)/shard_map/ppermute | solution.py:140
  43.0 5.1 %early_days.1 = (f32[256,512]{1,0:T(8,128)S(1)}, bf16[2,512,512]{2,1,0:T(8,128)(2,1)S(1)}, bf16[2,512,512]{2,1,0:T(8,128)(2,1)S(1)}, bf16[2,512,512]{2,1,0:T(8,1...) custom-call(s32[2,128]{1,0:T(2,128)S(1)} %broadcast_in_dim.2.where_ref, ...), custom_call_target="tpu_custom_call" | custom-call | flops 1200000000 | bytes 1024 | tf_op jit(solution)/shard_map/early_days/pallas_call | solution.py:48
  48.2 1.3 %collective-permute-done.9.refs_2_ = f32[1,128,512]{2,1,0:T(8,128)S(1)} collective-permute-done((f32[1,128,512]{2,1,0:T(8,128)S(1)}, f32[1,128,512]{2,1,0:T(8,128)S(1)}, u32[]{:S(2)}, u32[]{:S(2)}) %collective-permute-start.9) | collective-permute-done | bytes 262176 | tf_op jit(solution)/shard_map/ppermute | solution.py:140
  49.5 1.7 %collective-permute-start.16 = (f32[72,512]{1,0:T(8,128)S(1)}, f32[72,512]{1,0:T(8,128)S(1)}, u32[]{:S(2)}, u32[]{:S(2)}) collective-permute-start(f32[72,512]{1,0:T(8,128)S(1)} %get-tuple-element.111), channel_id=1, source_target_pairs={{0,2},{1,3},{2,0},{3,1},{4,6},{5,7},{6,4},{7,5},{8,10},{9,11},{10,... | collective-permute-start | bytes 442376 | tf_op jit(solution)/shard_map/ppermute | solution.py:140
  51.5 2.7 %day_2.1 = (bf16[2,512,512]{2,1,0:T(8,128)(2,1)S(1)}, bf16[2,512,512]{2,1,0:T(8,128)(2,1)S(1)}, f32[128,512]{1,0:T(8,128)S(1)}, f32[128,512]{1,0:T(8,128)S(1)}) custom-call(s32[2,128]{1,0:T(2,128)S(1)} %broadcast_in_dim.2.where_ref, f32[4,128,512]{2,1,0:T(8,128)S(1)} %copy-done.1, f32[4,128,512]{2,1,0:T(8,128)S(1)} %collective-permute-done.refs_1_, ...), custom_call_target="tpu_custom_call" | custom-call | flops 600000000 | bytes 1024 | tf_op jit(solution)/shard_map/day_2/pallas_call | solution.py:48
  54.2 1.8 %collective-permute-start.18 = (f32[128,512]{1,0:T(8,128)S(1)}, f32[128,512]{1,0:T(8,128)S(1)}, u32[]{:S(2)}, u32[]{:S(2)}) collective-permute-start(f32[128,512]{1,0:T(8,128)S(1)} %get-tuple-element.109), channel_id=1, source_target_pairs={{0,4},{4,0},{8,12},{12,8},{16,20},{20,16},{24,28},{28,24},{1,5},{5... | collective-permute-start | bytes 786440 | tf_op jit(solution)/shard_map/ppermute | solution.py:143
  56.1 2.4 %collective-permute-done.7.refs_2_ = f32[64,512]{1,0:T(8,128)S(1)} collective-permute-done((f32[64,512]{1,0:T(8,128)S(1)}, f32[64,512]{1,0:T(8,128)S(1)}, u32[]{:S(2)}, u32[]{:S(2)}) %collective-permute-start.7) | collective-permute-done | bytes 131104 | tf_op jit(solution)/shard_map/ppermute | solution.py:140
  58.6 1.3 %collective-permute-done.15.refs_3_ = f32[64,512]{1,0:T(8,128)S(1)} collective-permute-done((f32[64,512]{1,0:T(8,128)S(1)}, f32[64,512]{1,0:T(8,128)S(1)}, u32[]{:S(2)}, u32[]{:S(2)}) %collective-permute-start.15) | collective-permute-done | bytes 131104 | tf_op jit(solution)/shard_map/ppermute | solution.py:140
  59.9 1.2 %last_link.1 = (f32[512,512]{1,0:T(8,128)S(1)}, f32[256,512]{1,0:T(8,128)S(1)}, bf16[2,512,512]{2,1,0:T(8,128)(2,1)S(1)}) custom-call(s32[2,128]{1,0:T(2,128)S(1)} %broadcast_in_dim.2.where_ref, f32[4,128,512]{2,1,0:T(8,128)S(1)} %copy-done.1, f32[4,128,512]{2,1,0:T(8,128)S(1)} %collective-permute-done.refs_1_, ...), custom_call_target="tpu_custom_call" | custom-call | flops 300000000 | bytes 1024 | tf_op jit(solution)/shard_map/last_link/pallas_call | solution.py:48
  61.1 1.3 %collective-permute-done.18.other_ref = f32[128,512]{1,0:T(8,128)S(1)} collective-permute-done((f32[128,512]{1,0:T(8,128)S(1)}, f32[128,512]{1,0:T(8,128)S(1)}, u32[]{:S(2)}, u32[]{:S(2)}) %collective-permute-start.18) | collective-permute-done | bytes 262176 | tf_op jit(solution)/shard_map/ppermute | solution.py:143
  62.4 1.7 %collective-permute-start.19 = (f32[256,512]{1,0:T(8,128)S(1)}, f32[256,512]{1,0:T(8,128)S(1)}, u32[]{:S(2)}, u32[]{:S(2)}) collective-permute-start(f32[256,512]{1,0:T(8,128)S(1)} %get-tuple-element.116), channel_id=1, source_target_pairs={{0,4},{4,0},{8,12},{12,8},{16,20},{20,16},{24,28},{28,24},{1,5},{5... | collective-permute-start | bytes 1572872 | tf_op jit(solution)/shard_map/ppermute | solution.py:143
  64.2 4.5 %lines.1 = (f32[8,512]{1,0:T(8,128)S(1)}, f32[8,512]{1,0:T(8,128)S(1)}, f32[4,8,512]{2,1,0:T(8,128)S(1)}) custom-call(f32[4,512]{1,0:T(4,128)S(1)} %add.3.source_ref, f32[72,512]{1,0:T(8,128)S(1)} %collective-permute-done.16.refs_4_.refs_0_, bf16[2,512,512]{2,1,0:T(8,128)(2,1)S(1)} %get-tuple-element.102.refs_8_.refs_1_.refs_3_.refs_2_, ...), custom_call_target="tpu_custom_call" | custom-call | flops 1000000000 | bytes 1024 | tf_op jit(solution)/shard_map/lines/pallas_call | solution.py:48
  69.0 2.7 %grams.1.gram_ref = bf16[2,512,512]{2,1,0:T(8,128)(2,1)S(1)} custom-call(f32[512,512]{1,0:T(8,128)S(1)} %get-tuple-element.124.gram_ref, bf16[2,512,512]{2,1,0:T(8,128)(2,1)S(1)} %get-tuple-element.119.refs_6_.refs_0_.refs_5_, bf16[2,512,512]{2,1,0:T(8,128)(2,1)S(1)} %get-tuple-element.108.refs_7_.refs_9_.refs_1_.refs_8_, ...), custom_call_target="tpu_custom_call" | custom-call | flops 600000000 | bytes 1024 | tf_op jit(solution)/shard_map/grams/pallas_call | solution.py:48
  71.7 2.6 %late_maps.1 = (bf16[2,512,512]{2,1,0:T(8,128)(2,1)S(1)}, bf16[2,512,512]{2,1,0:T(8,128)(2,1)S(1)}, bf16[2,512,512]{2,1,0:T(8,128)(2,1)S(1)}) custom-call(bf16[2,512,512]{2,1,0:T(8,128)(2,1)S(1)} %get-tuple-element.125.refs_9_.refs_4_.refs_0_, bf16[2,512,512]{2,1,0:T(8,128)(2,1)S(1)} %get-tuple-element.104.refs_10_.refs_7_.refs_1_, ...), custom_call_target="tpu_custom_call" | custom-call | flops 600000000 | bytes 1024 | tf_op jit(solution)/shard_map/late_maps/pallas_call | solution.py:48
  74.3 1.4 %collective-permute-done.20.other_flux_ref = f32[8,512]{1,0:T(8,128)S(1)} collective-permute-done((f32[8,512]{1,0:T(8,128)S(1)}, f32[8,512]{1,0:T(8,128)S(1)}, u32[]{:S(2)}, u32[]{:S(2)}) %collective-permute-start.20) | collective-permute-done | bytes 16416 | tf_op jit(solution)/shard_map/ppermute | solution.py:143
  75.7 1.9 %collective-permute-done.21.rest_ref = f32[256,512]{1,0:T(8,128)S(1)} collective-permute-done((f32[256,512]{1,0:T(8,128)S(1)}, f32[256,512]{1,0:T(8,128)S(1)}, u32[]{:S(2)}, u32[]{:S(2)}) %collective-permute-start.21) | collective-permute-done | bytes 524320 | tf_op jit(solution)/shard_map/ppermute | solution.py:140
  77.7 1.0 pair_maps.1
  78.7 0.7 collective-permute-start.22
  79.4 3.7 %collective-permute-start.23 = (f32[8,512]{1,0:T(8,128)S(1)}, f32[8,512]{1,0:T(8,128)S(1)}, u32[]{:S(2)}, u32[]{:S(2)}) collective-permute-start(f32[8,512]{1,0:T(8,128)S(1)} %get-tuple-element.134.local_ref), channel_id=1, source_target_pairs={{0,8},{4,12},{1,9},{5,13},{2,10},{6,14},{3,11},{7,15}} | collective-permute-start | bytes 49160 | tf_op jit(solution)/shard_map/ppermute | solution.py:146
  83.1 1.0 group_map.1.map_ref
  84.1 0.4 collective-permute-done.23.refs_0_
  84.5 0.5 forward_link.2
  85.0 0.7 collective-permute-start.24
  85.7 0.5 forward_link.3
  86.2 0.7 collective-permute-start.26
  86.9 0.4 noise_link.2
  87.3 0.7 collective-permute-start.25
  88.0 1.1 mean_turn.1
  89.0 1.5 %collective-permute-start.27 = (f32[16,512]{1,0:T(8,128)S(1)}, f32[16,512]{1,0:T(8,128)S(1)}, u32[]{:S(2)}, u32[]{:S(2)}) collective-permute-start(f32[16,512]{1,0:T(8,128)S(1)} %pad_maximum_fusion), channel_id=1, source_target_pairs={{0,4},{4,0},{8,12},{12,8},{16,20},{20,16},{24,28},{28,24},{1,5},{5... | collective-permute-start | bytes 98312 | tf_op jit(solution)/shard_map/ppermute | solution.py:143
  90.6 0.7 collective-permute-start.29
  91.2 0.7 collective-permute-start.28
  91.9 1.1 collective-permute-done.27
  93.0 0.4 noise_link.3
  93.4 0.3 first_back.1
  93.7 1.3 %collective-permute-start.30 = (f32[128,512]{1,0:T(8,128)S(1)}, f32[128,512]{1,0:T(8,128)S(1)}, u32[]{:S(2)}, u32[]{:S(2)}) collective-permute-start(f32[128,512]{1,0:T(8,128)S(1)} %noise_link.3), channel_id=1, source_target_pairs={{8,0},{12,4},{9,1},{13,5},{10,2},{14,6},{11,3},{15,7}} | collective-permute-start | bytes 786440 | tf_op jit(solution)/shard_map/ppermute | solution.py:146
  95.0 0.7 collective-permute-start.31
  96.0 11.0 %collective-permute-done.30.refs_2_ = f32[128,512]{1,0:T(8,128)S(1)} collective-permute-done((f32[128,512]{1,0:T(8,128)S(1)}, f32[128,512]{1,0:T(8,128)S(1)}, u32[]{:S(2)}, u32[]{:S(2)}) %collective-permute-start.30) | collective-permute-done | bytes 262176 | tf_op jit(solution)/shard_map/ppermute | solution.py:146
  107.0 0.4 divide.1
  107.4 1.6 %collective-permute-start.32 = (f32[128,512]{1,0:T(8,128)S(1)}, f32[128,512]{1,0:T(8,128)S(1)}, u32[]{:S(2)}, u32[]{:S(2)}) collective-permute-start(f32[128,512]{1,0:T(8,128)S(1)} %get-tuple-element.153), channel_id=1, source_target_pairs={{0,4},{4,0},{8,12},{12,8},{16,20},{20,16},{24,28},{28,24},{1,5},{5... | collective-permute-start | bytes 786440 | tf_op jit(solution)/shard_map/ppermute | solution.py:143
  109.0 1.5 %collective-permute-start.33 = (f32[8,512]{1,0:T(8,128)S(1)}, f32[8,512]{1,0:T(8,128)S(1)}, u32[]{:S(2)}, u32[]{:S(2)}) collective-permute-start(f32[8,512]{1,0:T(8,128)S(1)} %backward_link.1), channel_id=1, source_target_pairs={{8,0},{12,4},{9,1},{13,5},{10,2},{14,6},{11,3},{15,7}} | collective-permute-start | bytes 49160 | tf_op jit(solution)/shard_map/ppermute | solution.py:146
  110.5 3.1 %mean_terms.1 = (f32[256,512]{1,0:T(8,128)S(1)}, f32[256,512]{1,0:T(8,128)S(1)}, f32[256,512]{1,0:T(8,128)S(1)}, f32[256,512]{1,0:T(8,128)S(1)}) custom-call(f32[8,512]{1,0:T(8,128)S(1)} %get-tuple-element.156.entering_ref, f32[4,8,512]{2,1,0:T(8,128)S(1)} %get-tuple-element.157.current_ref, f32[256,512]{1,0:T(8,128)S(1)} %get-tuple-element.101.refs_7_.refs_0_, ...), custom_call_target="tpu_custom_call" | custom-call | flops 800000000 | bytes 1024 | tf_op jit(solution)/shard_map/mean_terms/pallas_call | solution.py:48
  113.6 1.0 collective-permute-done.33.refs_3_
  114.7 3.4 %last_days.1 = f32[4,512,256]{2,1,0:T(8,128)} custom-call(s32[2,128]{1,0:T(2,128)S(1)} %broadcast_in_dim.2.where_ref, f32[128,512]{1,0:T(8,128)S(1)} %get-tuple-element.152.keep_ref, f32[128,512]{1,0:T(8,128)S(1)} %collective-permute-done.32.got_ref, f32[8,512]{1,0:T(8,128)S(1)} %get-tuple-element.154.back_ref, ...), custom_call_target="tpu_custom_call" | custom-call | flops 800000000 | bytes 1024 | tf_op jit(solution)/shard_map/last_days/pallas_call | solution.py:48
  (43 shorter events, 1.7 us)
Async XLA Ops:
  0.0 9.3 %copy-start.1 = (f32[4,128,512]{2,1,0:T(8,128)S(1)}, f32[4,128,512]{2,1,0:T(8,128)}, u32[]{:S(2)}) copy-start(f32[4,128,512]{2,1,0:T(8,128)} %refs_0_.7) | copy-start | bytes 3145732
  0.0 30.7 %copy-start = (f32[4,512,256]{2,1,0:T(8,128)S(1)}, f32[4,512,256]{2,1,0:T(8,128)}, u32[]{:S(2)}) copy-start(f32[4,512,256]{2,1,0:T(8,128)} %refs_4_.3) | copy-start | bytes 6291460
  0.0 26.4 %collective-permute-start.5 = (f32[4,128,512]{2,1,0:T(8,128)}, f32[4,128,512]{2,1,0:T(8,128)}, u32[]{:S(2)}, u32[]{:S(2)}) collective-permute-start(f32[4,128,512]{2,1,0:T(8,128)} %refs_0_.4), channel_id=1, source_target_pairs={{0,2},{1,3},{2,0},{3,1},{4,6},{5,7},{6,4},{7,5},{8,10},{9,11},{10,... | collective-permute-start | bytes 3145736 | tf_op jit(solution)/shard_map/ppermute | solution.py:140
  6.6 4.9 %collective-permute-start.1 = (f32[16,512]{1,0:T(8,128)S(1)}, f32[16,512]{1,0:T(8,128)S(1)}, u32[]{:S(2)}, u32[]{:S(2)}) collective-permute-start(f32[16,512]{1,0:T(8,128)S(1)} %get-tuple-element.87), channel_id=1, source_target_pairs={{0,16},{4,20},{8,24},{12,28},{16,0},{20,4},{24,8},{28,12},{1,17},{... | collective-permute-start | bytes 98312 | tf_op jit(solution)/shard_map/ppermute | solution.py:190
  11.5 3.8 %collective-permute-start.2 = (f32[8,512]{1,0:T(8,128)S(1)}, f32[8,512]{1,0:T(8,128)S(1)}, u32[]{:S(2)}, u32[]{:S(2)}) collective-permute-start(f32[8,512]{1,0:T(8,128)S(1)} %get-tuple-element.89), channel_id=1, source_target_pairs={{0,8},{4,12},{8,0},{12,4},{16,24},{20,28},{24,16},{28,20},{1,9},{5... | collective-permute-start | bytes 49160 | tf_op jit(solution)/shard_map/ppermute | solution.py:190
  15.4 3.7 %collective-permute-start.3 = (f32[4,512]{1,0:T(4,128)S(1)}, f32[4,512]{1,0:T(4,128)S(1)}, u32[]{:S(2)}, u32[]{:S(2)}) collective-permute-start(f32[4,512]{1,0:T(4,128)S(1)} %get-tuple-element.91), channel_id=1, source_target_pairs={{0,4},{4,0},{8,12},{12,8},{16,20},{20,16},{24,28},{28,24},{1,5},{5... | collective-permute-start | bytes 24584 | tf_op jit(solution)/shard_map/ppermute | solution.py:190
  19.1 1.2 collective-permute-start.4
  19.1 9.8 %collective-permute-start.10 = (f32[4,128,512]{2,1,0:T(8,128)}, f32[4,128,512]{2,1,0:T(8,128)S(1)}, u32[]{:S(2)}, u32[]{:S(2)}) collective-permute-start(f32[4,128,512]{2,1,0:T(8,128)} %refs_0_.4), channel_id=1, source_target_pairs={{0,1},{1,0},{2,3},{3,2},{4,5},{5,4},{6,7},{7,6},{8,9},{9,8},{10,11... | collective-permute-start | bytes 3145736 | tf_op jit(solution)/shard_map/ppermute | solution.py:140
  26.4 4.3 %collective-permute-start.11 = (f32[4,128,512]{2,1,0:T(8,128)}, f32[4,128,512]{2,1,0:T(8,128)S(1)}, u32[]{:S(2)}, u32[]{:S(2)}) collective-permute-start(f32[4,128,512]{2,1,0:T(8,128)} %collective-permute-done.5.refs_2_), channel_id=1, source_target_pairs={{0,1},{1,0},{2,3},{3,2},{4,5},{5,4},{6,7},{7,6},{8,9},{9,8},{10,11... | collective-permute-start | bytes 3145736 | tf_op jit(solution)/shard_map/ppermute | solution.py:140
  26.4 16.6 %collective-permute-start = (f32[4,128,512]{2,1,0:T(8,128)S(1)}, f32[4,128,512]{2,1,0:T(8,128)S(1)}, u32[]{:S(2)}, u32[]{:S(2)}) collective-permute-start(f32[4,128,512]{2,1,0:T(8,128)S(1)} %copy-done.1), channel_id=1, source_target_pairs={{0,1},{1,0},{2,3},{3,2},{4,5},{5,4},{6,7},{7,6},{8,9},{9,8},{10,11... | collective-permute-start | bytes 3145736 | tf_op jit(solution)/shard_map/ppermute | solution.py:140
  26.9 10.0 %collective-permute-start.6 = (f32[1,128,512]{2,1,0:T(8,128)S(1)}, f32[1,128,512]{2,1,0:T(8,128)S(1)}, u32[]{:S(2)}, u32[]{:S(2)}) collective-permute-start(f32[1,128,512]{2,1,0:T(8,128)S(1)} %get-tuple-element.93), channel_id=1, source_target_pairs={{0,2},{1,3},{2,0},{3,1},{4,6},{5,7},{6,4},{7,5},{8,10},{9,11},{10,... | collective-permute-start | bytes 786440 | tf_op jit(solution)/shard_map/ppermute | solution.py:140
  28.7 12.1 %collective-permute-start.8 = (f32[1,128,512]{2,1,0:T(8,128)S(1)}, f32[1,128,512]{2,1,0:T(8,128)S(1)}, u32[]{:S(2)}, u32[]{:S(2)}) collective-permute-start(f32[1,128,512]{2,1,0:T(8,128)S(1)} %get-tuple-element.168), channel_id=1, source_target_pairs={{0,2},{1,3},{2,0},{3,1},{4,6},{5,7},{6,4},{7,5},{8,10},{9,11},{10,... | collective-permute-start | bytes 786440 | tf_op jit(solution)/shard_map/ppermute | solution.py:140
  30.8 1.2 %copy-start.2 = (f32[4,128,512]{2,1,0:T(8,128)S(1)}, f32[4,128,512]{2,1,0:T(8,128)}, u32[]{:S(2)}) copy-start(f32[4,128,512]{2,1,0:T(8,128)} %refs_0_.4) | copy-start | bytes 3145732
  40.8 2.3 %collective-permute-start.12 = (f32[1,128,512]{2,1,0:T(8,128)S(1)}, f32[1,128,512]{2,1,0:T(8,128)S(1)}, u32[]{:S(2)}, u32[]{:S(2)}) collective-permute-start(f32[1,128,512]{2,1,0:T(8,128)S(1)} %collective-permute-done.8.refs_2_), channel_id=1, source_target_pairs={{0,1},{1,0},{2,3},{3,2},{4,5},{5,4},{6,7},{7,6},{8,9},{9,8},{10,11... | collective-permute-start | bytes 786440 | tf_op jit(solution)/shard_map/ppermute | solution.py:140
  40.8 2.3 %collective-permute-start.13 = (f32[1,128,512]{2,1,0:T(8,128)S(1)}, f32[1,128,512]{2,1,0:T(8,128)S(1)}, u32[]{:S(2)}, u32[]{:S(2)}) collective-permute-start(f32[1,128,512]{2,1,0:T(8,128)S(1)} %collective-permute-done.6.refs_4_), channel_id=1, source_target_pairs={{0,1},{1,0},{2,3},{3,2},{4,5},{5,4},{6,7},{7,6},{8,9},{9,8},{10,11... | collective-permute-start | bytes 786440 | tf_op jit(solution)/shard_map/ppermute | solution.py:140
  41.3 8.2 %collective-permute-start.9 = (f32[1,128,512]{2,1,0:T(8,128)S(1)}, f32[1,128,512]{2,1,0:T(8,128)S(1)}, u32[]{:S(2)}, u32[]{:S(2)}) collective-permute-start(f32[1,128,512]{2,1,0:T(8,128)S(1)} %get-tuple-element.95), channel_id=1, source_target_pairs={{0,2},{1,3},{2,0},{3,1},{4,6},{5,7},{6,4},{7,5},{8,10},{9,11},{10,... | collective-permute-start | bytes 786440 | tf_op jit(solution)/shard_map/ppermute | solution.py:140
  49.5 2.0 %collective-permute-start.14 = (f32[1,128,512]{2,1,0:T(8,128)S(1)}, f32[1,128,512]{2,1,0:T(8,128)S(1)}, u32[]{:S(2)}, u32[]{:S(2)}) collective-permute-start(f32[1,128,512]{2,1,0:T(8,128)S(1)} %collective-permute-done.9.refs_2_), channel_id=1, source_target_pairs={{0,1},{1,0},{2,3},{3,2},{4,5},{5,4},{6,7},{7,6},{8,9},{9,8},{10,11... | collective-permute-start | bytes 786440 | tf_op jit(solution)/shard_map/ppermute | solution.py:140
  49.5 6.6 %collective-permute-start.16 = (f32[72,512]{1,0:T(8,128)S(1)}, f32[72,512]{1,0:T(8,128)S(1)}, u32[]{:S(2)}, u32[]{:S(2)}) collective-permute-start(f32[72,512]{1,0:T(8,128)S(1)} %get-tuple-element.111), channel_id=1, source_target_pairs={{0,2},{1,3},{2,0},{3,1},{4,6},{5,7},{6,4},{7,5},{8,10},{9,11},{10,... | collective-permute-start | bytes 442376 | tf_op jit(solution)/shard_map/ppermute | solution.py:140
  51.2 7.3 %collective-permute-start.7 = (f32[64,512]{1,0:T(8,128)S(1)}, f32[64,512]{1,0:T(8,128)S(1)}, u32[]{:S(2)}, u32[]{:S(2)}) collective-permute-start(f32[64,512]{1,0:T(8,128)S(1)} %get-tuple-element.94), channel_id=1, source_target_pairs={{0,2},{1,3},{2,0},{3,1},{4,6},{5,7},{6,4},{7,5},{8,10},{9,11},{10,... | collective-permute-start | bytes 393224 | tf_op jit(solution)/shard_map/ppermute | solution.py:140
  54.2 8.3 %collective-permute-start.18 = (f32[128,512]{1,0:T(8,128)S(1)}, f32[128,512]{1,0:T(8,128)S(1)}, u32[]{:S(2)}, u32[]{:S(2)}) collective-permute-start(f32[128,512]{1,0:T(8,128)S(1)} %get-tuple-element.109), channel_id=1, source_target_pairs={{0,4},{4,0},{8,12},{12,8},{16,20},{20,16},{24,28},{28,24},{1,5},{5... | collective-permute-start | bytes 786440 | tf_op jit(solution)/shard_map/ppermute | solution.py:143
  56.1 3.8 %collective-permute-start.17 = (f32[72,512]{1,0:T(8,128)S(1)}, f32[72,512]{1,0:T(8,128)S(1)}, u32[]{:S(2)}, u32[]{:S(2)}) collective-permute-start(f32[72,512]{1,0:T(8,128)S(1)} %collective-permute-done.16.refs_4_.refs_0_), channel_id=1, source_target_pairs={{0,1},{1,0},{2,3},{3,2},{4,5},{5,4},{6,7},{7,6},{8,9},{9,8},{10,11... | collective-permute-start | bytes 442376 | tf_op jit(solution)/shard_map/ppermute | solution.py:140
  58.6 1.3 %collective-permute-start.15 = (f32[64,512]{1,0:T(8,128)S(1)}, f32[64,512]{1,0:T(8,128)S(1)}, u32[]{:S(2)}, u32[]{:S(2)}) collective-permute-start(f32[64,512]{1,0:T(8,128)S(1)} %collective-permute-done.7.refs_2_), channel_id=1, source_target_pairs={{0,1},{1,0},{2,3},{3,2},{4,5},{5,4},{6,7},{7,6},{8,9},{9,8},{10,11... | collective-permute-start | bytes 393224 | tf_op jit(solution)/shard_map/ppermute | solution.py:140
  62.4 13.3 %collective-permute-start.19 = (f32[256,512]{1,0:T(8,128)S(1)}, f32[256,512]{1,0:T(8,128)S(1)}, u32[]{:S(2)}, u32[]{:S(2)}) collective-permute-start(f32[256,512]{1,0:T(8,128)S(1)} %get-tuple-element.116), channel_id=1, source_target_pairs={{0,4},{4,0},{8,12},{12,8},{16,20},{20,16},{24,28},{28,24},{1,5},{5... | collective-permute-start | bytes 1572872 | tf_op jit(solution)/shard_map/ppermute | solution.py:143
  68.7 7.0 %collective-permute-start.20 = (f32[8,512]{1,0:T(8,128)S(1)}, f32[8,512]{1,0:T(8,128)S(1)}, u32[]{:S(2)}, u32[]{:S(2)}) collective-permute-start(f32[8,512]{1,0:T(8,128)S(1)} %get-tuple-element.122.flux_ref), channel_id=1, source_target_pairs={{0,4},{4,0},{8,12},{12,8},{16,20},{20,16},{24,28},{28,24},{1,5},{5... | collective-permute-start | bytes 49160 | tf_op jit(solution)/shard_map/ppermute | solution.py:143
  75.7 1.9 %collective-permute-start.21 = (f32[256,512]{1,0:T(8,128)S(1)}, f32[256,512]{1,0:T(8,128)S(1)}, u32[]{:S(2)}, u32[]{:S(2)}) collective-permute-start(f32[256,512]{1,0:T(8,128)S(1)} %collective-permute-done.19.half_ref), channel_id=1, source_target_pairs={{0,1},{1,0},{2,3},{3,2},{4,5},{5,4},{6,7},{7,6},{8,9},{9,8},{10,11... | collective-permute-start | bytes 1572872 | tf_op jit(solution)/shard_map/ppermute | solution.py:140
  78.7 8.2 %collective-permute-start.22 = (f32[128,512]{1,0:T(8,128)S(1)}, f32[128,512]{1,0:T(8,128)S(1)}, u32[]{:S(2)}, u32[]{:S(2)}) collective-permute-start(f32[128,512]{1,0:T(8,128)S(1)} %get-tuple-element.135.local_ref), channel_id=1, source_target_pairs={{24,16},{28,20},{25,17},{29,21},{26,18},{30,22},{27,19},{31,23}} | collective-permute-start | bytes 786440 | tf_op jit(solution)/shard_map/ppermute | solution.py:146
  79.4 5.1 %collective-permute-start.23 = (f32[8,512]{1,0:T(8,128)S(1)}, f32[8,512]{1,0:T(8,128)S(1)}, u32[]{:S(2)}, u32[]{:S(2)}) collective-permute-start(f32[8,512]{1,0:T(8,128)S(1)} %get-tuple-element.134.local_ref), channel_id=1, source_target_pairs={{0,8},{4,12},{1,9},{5,13},{2,10},{6,14},{3,11},{7,15}} | collective-permute-start | bytes 49160 | tf_op jit(solution)/shard_map/ppermute | solution.py:146
  85.0 0.7 collective-permute-start.24
  86.2 1.8 %collective-permute-start.26 = (f32[8,512]{1,0:T(8,128)S(1)}, f32[8,512]{1,0:T(8,128)S(1)}, u32[]{:S(2)}, u32[]{:S(2)}) collective-permute-start(f32[8,512]{1,0:T(8,128)S(1)} %forward_link.3), channel_id=1, source_target_pairs={{16,24},{20,28},{17,25},{21,29},{18,26},{22,30},{19,27},{23,31}} | collective-permute-start | bytes 49160 | tf_op jit(solution)/shard_map/ppermute | solution.py:146
  87.3 5.7 %collective-permute-start.25 = (f32[128,512]{1,0:T(8,128)S(1)}, f32[128,512]{1,0:T(8,128)S(1)}, u32[]{:S(2)}, u32[]{:S(2)}) collective-permute-start(f32[128,512]{1,0:T(8,128)S(1)} %noise_link.2), channel_id=1, source_target_pairs={{16,8},{20,12},{17,9},{21,13},{18,10},{22,14},{19,11},{23,15}} | collective-permute-start | bytes 786440 | tf_op jit(solution)/shard_map/ppermute | solution.py:146
  89.0 3.9 %collective-permute-start.27 = (f32[16,512]{1,0:T(8,128)S(1)}, f32[16,512]{1,0:T(8,128)S(1)}, u32[]{:S(2)}, u32[]{:S(2)}) collective-permute-start(f32[16,512]{1,0:T(8,128)S(1)} %pad_maximum_fusion), channel_id=1, source_target_pairs={{0,4},{4,0},{8,12},{12,8},{16,20},{20,16},{24,28},{28,24},{1,5},{5... | collective-permute-start | bytes 98312 | tf_op jit(solution)/shard_map/ppermute | solution.py:143
  90.6 2.8 %collective-permute-start.29 = (f32[8,512]{1,0:T(8,128)S(1)}, f32[8,512]{1,0:T(8,128)S(1)}, u32[]{:S(2)}, u32[]{:S(2)}) collective-permute-start(f32[8,512]{1,0:T(8,128)S(1)} %get-tuple-element.143.part_ref), channel_id=1, source_target_pairs={{24,20},{28,16},{25,21},{29,17},{26,22},{30,18},{27,23},{31,19}} | collective-permute-start | bytes 49160 | tf_op jit(solution)/shard_map/ppermute | solution.py:502
  91.2 2.1 %collective-permute-start.28 = (f32[8,512]{1,0:T(8,128)S(1)}, f32[8,512]{1,0:T(8,128)S(1)}, u32[]{:S(2)}, u32[]{:S(2)}) collective-permute-start(f32[8,512]{1,0:T(8,128)S(1)} %get-tuple-element.143.part_ref), channel_id=1, source_target_pairs={{24,16},{28,20},{25,17},{29,21},{26,18},{30,22},{27,19},{31,23}} | collective-permute-start | bytes 49160 | tf_op jit(solution)/shard_map/ppermute | solution.py:502
  93.7 13.3 %collective-permute-start.30 = (f32[128,512]{1,0:T(8,128)S(1)}, f32[128,512]{1,0:T(8,128)S(1)}, u32[]{:S(2)}, u32[]{:S(2)}) collective-permute-start(f32[128,512]{1,0:T(8,128)S(1)} %noise_link.3), channel_id=1, source_target_pairs={{8,0},{12,4},{9,1},{13,5},{10,2},{14,6},{11,3},{15,7}} | collective-permute-start | bytes 786440 | tf_op jit(solution)/shard_map/ppermute | solution.py:146
  95.0 0.7 collective-permute-start.31
  107.4 7.2 %collective-permute-start.32 = (f32[128,512]{1,0:T(8,128)S(1)}, f32[128,512]{1,0:T(8,128)S(1)}, u32[]{:S(2)}, u32[]{:S(2)}) collective-permute-start(f32[128,512]{1,0:T(8,128)S(1)} %get-tuple-element.153), channel_id=1, source_target_pairs={{0,4},{4,0},{8,12},{12,8},{16,20},{20,16},{24,28},{28,24},{1,5},{5... | collective-permute-start | bytes 786440 | tf_op jit(solution)/shard_map/ppermute | solution.py:143
  109.0 5.6 %collective-permute-start.33 = (f32[8,512]{1,0:T(8,128)S(1)}, f32[8,512]{1,0:T(8,128)S(1)}, u32[]{:S(2)}, u32[]{:S(2)}) collective-permute-start(f32[8,512]{1,0:T(8,128)S(1)} %backward_link.1), channel_id=1, source_target_pairs={{8,0},{12,4},{9,1},{13,5},{10,2},{14,6},{11,3},{15,7}} | collective-permute-start | bytes 49160 | tf_op jit(solution)/shard_map/ppermute | solution.py:146

commit v10 on v9

--- a/solution.py
+++ b/solution.py
@@ -122,6 +122,18 @@
         out_ref[0, at, :], out_ref[1, at, :] = split(ref[...])
 
 
+def gather_halves(where_ref, own_refs, day, first_refs, rest_refs, out_ref):
+    share = own_refs[0].shape[-2]
+    count = share // 2
+    halves = [(ref.at[day, pl.ds(0, count)], ref.at[day, pl.ds(count, count)]) for ref in own_refs]
+    halves += zip(first_refs, rest_refs, strict=True)
+    for offset, pair in enumerate(halves):
+        for index, ref in enumerate(pair):
+            start = (where_ref[0, 0] ^ offset) * share + index * count
+            at = pl.ds(pl.multiple_of(start, count), count)
+            out_ref[0, at, :], out_ref[1, at, :] = split(ref[...])
+
+
 def local(inv_diag, coupling, noise, obs_day, obs_node, obs_value):
     part_count = lax.axis_size("tm")
     row_count = lax.axis_size("row")
@@ -179,8 +191,12 @@
 
     pieces = []
     link_rows = [coupling[day : day + 1] for day in range(day_count)]
+    first_rows = share // 2
     for rows in (inv_diag, *link_rows[:-1]):
-        send_rows(rows)
+        if rows is link_rows[early - 1]:
+            send_rows(rows[0, :first_rows], rows[0, first_rows:])
+        else:
+            send_rows(rows)
     own_inverse = [inv_diag, to_row(inv_diag, 1)]
     own_link = [coupling, to_row(coupling, 1)]
     where = after(where, keep, *link_rows)
@@ -191,8 +207,6 @@
         distance //= 2
         keep, sent = halved(where, distance, keep, got)
     right_side = keep + to_row(keep, 1)
-
-    first_rows = share // 2
 
     def pack_body(rows_ref, source_ref, first_out, rest_out):
         first_out[...] = rows_ref[0, :first_rows, :]
@@ -209,7 +223,8 @@
         work=0.1,
     )
     send_rows(*packed)
-    got_inverses, got_links = pieces[0], pieces[1:]
+    got_inverses, *got_links = pieces
+    halved_day = got_links.pop(early)
 
     def store(out_ref, pair):
         out_ref[0], out_ref[1] = pair
@@ -237,16 +252,22 @@
     def early_body(where_ref, *refs):
         own_refs, refs = refs[:CORES], refs[CORES:]
         count = row_count - CORES
-        got_refs, refs = refs[: count * early], refs[count * early :]
+        got_refs, refs = refs[: count * (early + 1)], refs[count * (early + 1) :]
         noise_ref, term_ref, refs = refs[0], refs[1], refs[2:]
         inverse_refs, refs = refs[: early + 1], refs[early + 1 :]
         sum_out, *outs = refs
         link_outs, moved_outs, map_outs = outs[:early], outs[early : 2 * early], outs[2 * early :]
         for day in range(early):
-            row_refs = (*own_refs, *got_refs[count * day : count * (day + 1)])
-            gather_rows(
-                where_ref, row_refs, lambda offset: day if offset < CORES else 0, link_outs[day]
-            )
+            got = got_refs[count * day : count * (day + 1)]
+            if day < early - 1:
+                gather_rows(
+                    where_ref,
+                    (*own_refs, *got),
+                    lambda offset: day if offset < CORES else 0,
+                    link_outs[day],
+                )
+            else:
+                gather_halves(where_ref, own_refs, day, got, got_refs[count * early :], link_outs[day])
         total = term_ref[...]
         moved = parts(inverse_refs[0])
         for day in range(early):
@@ -266,7 +287,7 @@
         (where,),
         [
             *own_link,
-            *(piece for got in got_links[:early] for piece in shared(got, gram)),
+            *(piece for got in (*got_links[:early], halved_day) for piece in shared(got, gram)),
             noise, local_terms[0], *inverses[: early + 1],
         ],
         work=6,
@@ -316,17 +337,7 @@
         first_refs, rest_refs, refs = refs[:count], refs[count : 2 * count], refs[2 * count :]
         moved_ref, whole_out, half_out, link_out = refs
         rest_refs = [ref.at[pl.ds(0, share - first_rows)] for ref in rest_refs]
-        pairs = [
-            (ref.at[day_count - 1, pl.ds(0, first_rows)], ref.at[day_count - 1, pl.ds(first_rows, share - first_rows)])
-            for ref in own_refs
-        ] + list(zip(first_refs, rest_refs, strict=True))
-        for offset, pair in enumerate(pairs):
-            for ref, start, size in zip(
-                pair, (0, first_rows), (first_rows, share - first_rows), strict=True
-            ):
-                start = (where_ref[0, 0] ^ offset) * share + start
-                at = pl.ds(pl.multiple_of(start, first_rows), size)
-                link_out[0, at, :], link_out[1, at, :] = split(ref[...])
+        gather_halves(where_ref, own_refs, day_count - 1, first_refs, rest_refs, link_out)
         whole_out[...] = -dot_parts(parts(link_out), parts(moved_ref), NN)
         half_out[...] = whole_out[
             pl.ds(pl.multiple_of((where_ref[0, 0] & (CORES - 1)) * half_nodes, half_nodes), half_nodes), :

time: 119 us -> 117 us (0.983)
  waiting for transfers between devices: 42.2 us -> 38.3 us
  starting transfers between devices: 34.2 us -> 36.7 us
    ppermute x16 -> x18, waiting for transfers between devices: 19.5 us -> 15.7 us  [to_row(): lax.ppermute(value, 'row', [(i, i ^ distance) for i in range(row_count)])]
    ppermute x16 -> x18, starting transfers between devices: 10.3 us -> 12.6 us  [to_row(): lax.ppermute(value, 'row', [(i, i ^ distance) for i in range(row_count)])]
  transfers between devices with their start and end apart: 34 -> 36, of which waited for: 18 -> 18; matrix products, arithmetic and copies ran while one was open for 2% -> 2% of each run, Pallas kernels for 27% -> 28%
where the time goes in v10:
time: 117 us
  waiting for transfers between devices  38.3 us (33%)
  Pallas kernels  37.5 us (32%)
  starting transfers between devices  36.7 us (31%)
  local copies, waits for them, and re-layouts  3.54 us (3%)
    pallas_call x24, Pallas kernels, call(): pl.pallas_call(body, out_shape=out_shape, in_specs=[vmem] * (len(scalars)...  37.5 us
    ppermute x18, waiting for transfers between devices, to_row(): lax.ppermute(value, 'row', [(i, i ^ distance) for i in range(row_count)])  15.7 us
    ppermute x18, starting transfers between devices, to_row(): lax.ppermute(value, 'row', [(i, i ^ distance) for i in range(row_count)])  12.6 us
    ppermute x8, waiting for transfers between devices, to_group(): lax.ppermute(value, 'tm', [(PAIR * source + i, PAIR * target + i) for i i...  12.5 us
    ppermute x8, starting transfers between devices, to_group(): lax.ppermute(value, 'tm', [(PAIR * source + i, PAIR * target + i) for i i...  9.83 us
    ppermute x5, starting transfers between devices, to_pair(): return lax.ppermute(value, 'tm', [(i, i ^ 1) for i in range(part_count)])  7.07 us
    ppermute x3, waiting for transfers between devices, local(): lax.ppermute(sent, 'tm', [(i, i ^ distance) for i in range(part_count)])  6.45 us
    ppermute x3, starting transfers between devices, local(): lax.ppermute(sent, 'tm', [(i, i ^ distance) for i in range(part_count)])  5.86 us
  transfers between devices with their start and end apart: 36, of which 18 were waited for; matrix products, arithmetic and copies ran while one was open for 2% of the time, Pallas kernels for 28%

profile of v10, /device:TPU:0, one launch (start us, length us, event | category | flops | bytes accessed | tf_op | source)
XLA Modules:
  0.0 116.6 jit_solution(1525641460015076667)
XLA Ops:
  0.0 2.9 %collective-permute-start.5 = (f32[4,128,512]{2,1,0:T(8,128)}, f32[4,128,512]{2,1,0:T(8,128)}, u32[]{:S(2)}, u32[]{:S(2)}) collective-permute-start(f32[4,128,512]{2,1,0:T(8,128)} %refs_0_.4), channel_id=1, source_target_pairs={{0,2},{1,3},{2,0},{3,1},{4,6},{5,7},{6,4},{7,5},{8,10},{9,11},{10,... | collective-permute-start | bytes 3145736 | tf_op jit(solution)/shard_map/ppermute | solution.py:152
  2.9 0.7 reshape.10.day_ref
  3.7 0.7 reshape.11.node_ref
  4.4 0.7 reshape.12.value_ref
  5.3 1.4 %bin_observations.1 = (f32[16,512]{1,0:T(8,128)S(1)}, f32[16,512]{1,0:T(8,128)S(1)}) custom-call(s32[2,128]{1,0:T(2,128)S(1)} %broadcast_in_dim.2.where_ref, s32[8,512]{1,0:T(8,128)S(1)} %reshape.10.day_ref, s32[8,512]{1,0:T(8,128)S(1)} %reshape.11.node_ref, f32[8,512]{1,0:T(8,128)S(1)} %reshape.12.value_ref), custom_call_target="tpu_custom_call" | custom-call | flops 400000000 | bytes 1024 | tf_op jit(solution)/shard_map/bin_observations/pallas_call | solution.py:48
  6.6 2.6 %collective-permute-start.1 = (f32[16,512]{1,0:T(8,128)S(1)}, f32[16,512]{1,0:T(8,128)S(1)}, u32[]{:S(2)}, u32[]{:S(2)}) collective-permute-start(f32[16,512]{1,0:T(8,128)S(1)} %get-tuple-element.89), channel_id=1, source_target_pairs={{0,16},{4,20},{8,24},{12,28},{16,0},{20,4},{24,8},{28,12},{1,17},{... | collective-permute-start | bytes 98312 | tf_op jit(solution)/shard_map/ppermute | solution.py:206
  9.3 2.2 %collective-permute-done.1.got_ref = f32[16,512]{1,0:T(8,128)S(1)} collective-permute-done((f32[16,512]{1,0:T(8,128)S(1)}, f32[16,512]{1,0:T(8,128)S(1)}, u32[]{:S(2)}, u32[]{:S(2)}) %collective-permute-start.1) | collective-permute-done | bytes 32800 | tf_op jit(solution)/shard_map/ppermute | solution.py:206
  11.5 1.6 %collective-permute-start.2 = (f32[8,512]{1,0:T(8,128)S(1)}, f32[8,512]{1,0:T(8,128)S(1)}, u32[]{:S(2)}, u32[]{:S(2)}) collective-permute-start(f32[8,512]{1,0:T(8,128)S(1)} %get-tuple-element.91), channel_id=1, source_target_pairs={{0,8},{4,12},{8,0},{12,4},{16,24},{20,28},{24,16},{28,20},{1,9},{5... | collective-permute-start | bytes 49160 | tf_op jit(solution)/shard_map/ppermute | solution.py:206
  13.2 2.2 %collective-permute-done.2.got_ref = f32[8,512]{1,0:T(8,128)S(1)} collective-permute-done((f32[8,512]{1,0:T(8,128)S(1)}, f32[8,512]{1,0:T(8,128)S(1)}, u32[]{:S(2)}, u32[]{:S(2)}) %collective-permute-start.2) | collective-permute-done | bytes 16416 | tf_op jit(solution)/shard_map/ppermute | solution.py:206
  15.4 1.6 %collective-permute-start.3 = (f32[4,512]{1,0:T(4,128)S(1)}, f32[4,512]{1,0:T(4,128)S(1)}, u32[]{:S(2)}, u32[]{:S(2)}) collective-permute-start(f32[4,512]{1,0:T(4,128)S(1)} %get-tuple-element.93), channel_id=1, source_target_pairs={{0,4},{4,0},{8,12},{12,8},{16,20},{20,16},{24,28},{28,24},{1,5},{5... | collective-permute-start | bytes 24584 | tf_op jit(solution)/shard_map/ppermute | solution.py:206
  17.0 2.1 %collective-permute-done.3.got_ref = f32[4,512]{1,0:T(4,128)S(1)} collective-permute-done((f32[4,512]{1,0:T(4,128)S(1)}, f32[4,512]{1,0:T(4,128)S(1)}, u32[]{:S(2)}, u32[]{:S(2)}) %collective-permute-start.3) | collective-permute-done | bytes 8224 | tf_op jit(solution)/shard_map/ppermute | solution.py:206
  19.1 0.5 collective-permute-start.10
  19.6 0.7 collective-permute-done.4
  20.3 6.1 %collective-permute-done.5.refs_2_ = f32[4,128,512]{2,1,0:T(8,128)} collective-permute-done((f32[4,128,512]{2,1,0:T(8,128)}, f32[4,128,512]{2,1,0:T(8,128)}, u32[]{:S(2)}, u32[]{:S(2)}) %collective-permute-start.5) | collective-permute-done | bytes 1048608 | tf_op jit(solution)/shard_map/ppermute | solution.py:152
  26.4 0.5 collective-permute-start
  26.9 1.7 %collective-permute-start.8 = (f32[1,128,512]{2,1,0:T(8,128)S(1)}, f32[1,128,512]{2,1,0:T(8,128)S(1)}, u32[]{:S(2)}, u32[]{:S(2)}) collective-permute-start(f32[1,128,512]{2,1,0:T(8,128)S(1)} %get-tuple-element.173), channel_id=1, source_target_pairs={{0,2},{1,3},{2,0},{3,1},{4,6},{5,7},{6,4},{7,5},{8,10},{9,11},{10,... | collective-permute-start | bytes 786440 | tf_op jit(solution)/shard_map/ppermute | solution.py:152
  29.0 1.7 %collective-permute-start.13 = (f32[64,512]{1,0:T(8,128)S(1)}, f32[64,512]{1,0:T(8,128)S(1)}, u32[]{:S(2)}, u32[]{:S(2)}) collective-permute-start(f32[64,512]{1,0:T(8,128)S(1)} %get-tuple-element.102), channel_id=1, source_target_pairs={{0,2},{1,3},{2,0},{3,1},{4,6},{5,7},{6,4},{7,5},{8,10},{9,11},{10,... | collective-permute-start | bytes 393224 | tf_op jit(solution)/shard_map/ppermute | solution.py:152
  30.8 1.2 %copy-done.2 = f32[4,128,512]{2,1,0:T(8,128)S(1)} copy-done((f32[4,128,512]{2,1,0:T(8,128)S(1)}, f32[4,128,512]{2,1,0:T(8,128)}, u32[]{:S(2)}) %copy-start.2) | copy-done | bytes 1048600
  32.0 4.9 %inverses.1 = (f32[512,512]{1,0:T(8,128)S(1)}, bf16[2,512,512]{2,1,0:T(8,128)(2,1)S(1)}, bf16[2,512,512]{2,1,0:T(8,128)(2,1)S(1)}, bf16[2,512,512]{2,1,0:T(8,128...) custom-call(s32[2,128]{1,0:T(2,128)S(1)} %broadcast_in_dim.2.where_r, ...), custom_call_target="tpu_custom_call" | custom-call | flops 800000000 | bytes 1024 | tf_op jit(solution)/shard_map/inverses/pallas_call | solution.py:48
  37.1 1.8 %collective-permute-start.9 = (f32[1,128,512]{2,1,0:T(8,128)S(1)}, f32[1,128,512]{2,1,0:T(8,128)S(1)}, u32[]{:S(2)}, u32[]{:S(2)}) collective-permute-start(f32[1,128,512]{2,1,0:T(8,128)S(1)} %get-tuple-element.97), channel_id=1, source_target_pairs={{0,2},{1,3},{2,0},{3,1},{4,6},{5,7},{6,4},{7,5},{8,10},{9,11},{10,... | collective-permute-start | bytes 786440 | tf_op jit(solution)/shard_map/ppermute | solution.py:152
  38.9 2.4 %collective-permute-done.13.refs_4_ = f32[64,512]{1,0:T(8,128)S(1)} collective-permute-done((f32[64,512]{1,0:T(8,128)S(1)}, f32[64,512]{1,0:T(8,128)S(1)}, u32[]{:S(2)}, u32[]{:S(2)}) %collective-permute-start.13) | collective-permute-done | bytes 131104 | tf_op jit(solution)/shard_map/ppermute | solution.py:152
  41.3 0.5 collective-permute-start.15
  41.8 0.8 collective-permute-done.14.refs_5_
  42.8 5.1 %early_days.1 = (f32[256,512]{1,0:T(8,128)S(1)}, bf16[2,512,512]{2,1,0:T(8,128)(2,1)S(1)}, bf16[2,512,512]{2,1,0:T(8,128)(2,1)S(1)}, bf16[2,512,512]{2,1,0:T(8,1...) custom-call(s32[2,128]{1,0:T(2,128)S(1)} %broadcast_in_dim.2.where_ref, ...), custom_call_target="tpu_custom_call" | custom-call | flops 1200000000 | bytes 1024 | tf_op jit(solution)/shard_map/early_days/pallas_call | solution.py:48
  47.9 0.4 collective-permute-start.16
  48.3 1.8 %collective-permute-start.18 = (f32[72,512]{1,0:T(8,128)S(1)}, f32[72,512]{1,0:T(8,128)S(1)}, u32[]{:S(2)}, u32[]{:S(2)}) collective-permute-start(f32[72,512]{1,0:T(8,128)S(1)} %get-tuple-element.115), channel_id=1, source_target_pairs={{0,2},{1,3},{2,0},{3,1},{4,6},{5,7},{6,4},{7,5},{8,10},{9,11},{10,... | collective-permute-start | bytes 442376 | tf_op jit(solution)/shard_map/ppermute | solution.py:152
  50.3 2.7 %day_2.1 = (bf16[2,512,512]{2,1,0:T(8,128)(2,1)S(1)}, bf16[2,512,512]{2,1,0:T(8,128)(2,1)S(1)}, f32[128,512]{1,0:T(8,128)S(1)}, f32[128,512]{1,0:T(8,128)S(1)}) custom-call(s32[2,128]{1,0:T(2,128)S(1)} %broadcast_in_dim.2.where_ref, f32[4,128,512]{2,1,0:T(8,128)S(1)} %copy-done.1, f32[4,128,512]{2,1,0:T(8,128)S(1)} %collective-permute-done.refs_1_, ...), custom_call_target="tpu_custom_call" | custom-call | flops 600000000 | bytes 1024 | tf_op jit(solution)/shard_map/day_2/pallas_call | solution.py:48
  53.0 1.9 %collective-permute-start.20 = (f32[128,512]{1,0:T(8,128)S(1)}, f32[128,512]{1,0:T(8,128)S(1)}, u32[]{:S(2)}, u32[]{:S(2)}) collective-permute-start(f32[128,512]{1,0:T(8,128)S(1)} %get-tuple-element.113), channel_id=1, source_target_pairs={{0,4},{4,0},{8,12},{12,8},{16,20},{20,16},{24,28},{28,24},{1,5},{5... | collective-permute-start | bytes 786440 | tf_op jit(solution)/shard_map/ppermute | solution.py:155
  55.0 2.1 %collective-permute-done.7.refs_2_ = f32[64,512]{1,0:T(8,128)S(1)} collective-permute-done((f32[64,512]{1,0:T(8,128)S(1)}, f32[64,512]{1,0:T(8,128)S(1)}, u32[]{:S(2)}, u32[]{:S(2)}) %collective-permute-start.7) | collective-permute-done | bytes 131104 | tf_op jit(solution)/shard_map/ppermute | solution.py:152
  57.1 1.3 %collective-permute-done.17.refs_3_ = f32[64,512]{1,0:T(8,128)S(1)} collective-permute-done((f32[64,512]{1,0:T(8,128)S(1)}, f32[64,512]{1,0:T(8,128)S(1)}, u32[]{:S(2)}, u32[]{:S(2)}) %collective-permute-start.17) | collective-permute-done | bytes 131104 | tf_op jit(solution)/shard_map/ppermute | solution.py:152
  58.4 1.2 %last_link.1 = (f32[512,512]{1,0:T(8,128)S(1)}, f32[256,512]{1,0:T(8,128)S(1)}, bf16[2,512,512]{2,1,0:T(8,128)(2,1)S(1)}) custom-call(s32[2,128]{1,0:T(2,128)S(1)} %broadcast_in_dim.2.where_ref, f32[4,128,512]{2,1,0:T(8,128)S(1)} %copy-done.1, f32[4,128,512]{2,1,0:T(8,128)S(1)} %collective-permute-done.refs_1_, ...), custom_call_target="tpu_custom_call" | custom-call | flops 300000000 | bytes 1024 | tf_op jit(solution)/shard_map/last_link/pallas_call | solution.py:48
  59.6 1.3 %collective-permute-done.20.other_ref = f32[128,512]{1,0:T(8,128)S(1)} collective-permute-done((f32[128,512]{1,0:T(8,128)S(1)}, f32[128,512]{1,0:T(8,128)S(1)}, u32[]{:S(2)}, u32[]{:S(2)}) %collective-permute-start.20) | collective-permute-done | bytes 262176 | tf_op jit(solution)/shard_map/ppermute | solution.py:155
  61.0 1.7 %collective-permute-start.21 = (f32[256,512]{1,0:T(8,128)S(1)}, f32[256,512]{1,0:T(8,128)S(1)}, u32[]{:S(2)}, u32[]{:S(2)}) collective-permute-start(f32[256,512]{1,0:T(8,128)S(1)} %get-tuple-element.120), channel_id=1, source_target_pairs={{0,4},{4,0},{8,12},{12,8},{16,20},{20,16},{24,28},{28,24},{1,5},{5... | collective-permute-start | bytes 1572872 | tf_op jit(solution)/shard_map/ppermute | solution.py:155
  62.7 4.5 %lines.1 = (f32[8,512]{1,0:T(8,128)S(1)}, f32[8,512]{1,0:T(8,128)S(1)}, f32[4,8,512]{2,1,0:T(8,128)S(1)}) custom-call(f32[4,512]{1,0:T(4,128)S(1)} %add.3.source_ref, f32[72,512]{1,0:T(8,128)S(1)} %collective-permute-done.18.refs_4_.refs_0_, bf16[2,512,512]{2,1,0:T(8,128)(2,1)S(1)} %get-tuple-element.106.refs_10_.refs_1_.refs_3_.refs_2_, ...), custom_call_target="tpu_custom_call" | custom-call | flops 1000000000 | bytes 1024 | tf_op jit(solution)/shard_map/lines/pallas_call | solution.py:48
  67.5 2.7 %grams.1.gram_ref = bf16[2,512,512]{2,1,0:T(8,128)(2,1)S(1)} custom-call(f32[512,512]{1,0:T(8,128)S(1)} %get-tuple-element.128.gram_ref, bf16[2,512,512]{2,1,0:T(8,128)(2,1)S(1)} %get-tuple-element.123.refs_6_.refs_0_.refs_5_, bf16[2,512,512]{2,1,0:T(8,128)(2,1)S(1)} %get-tuple-element.112.refs_7_.refs_9_.refs_1_.refs_8_, ...), custom_call_target="tpu_custom_call" | custom-call | flops 600000000 | bytes 1024 | tf_op jit(solution)/shard_map/grams/pallas_call | solution.py:48
  70.2 2.6 %late_maps.1 = (bf16[2,512,512]{2,1,0:T(8,128)(2,1)S(1)}, bf16[2,512,512]{2,1,0:T(8,128)(2,1)S(1)}, bf16[2,512,512]{2,1,0:T(8,128)(2,1)S(1)}) custom-call(bf16[2,512,512]{2,1,0:T(8,128)(2,1)S(1)} %get-tuple-element.129.refs_11_.refs_4_.refs_0_, bf16[2,512,512]{2,1,0:T(8,128)(2,1)S(1)} %get-tuple-element.108.refs_12_.refs_7_.refs_1_, ...), custom_call_target="tpu_custom_call" | custom-call | flops 600000000 | bytes 1024 | tf_op jit(solution)/shard_map/late_maps/pallas_call | solution.py:48
  72.9 1.2 %collective-permute-done.22.other_flux_ref = f32[8,512]{1,0:T(8,128)S(1)} collective-permute-done((f32[8,512]{1,0:T(8,128)S(1)}, f32[8,512]{1,0:T(8,128)S(1)}, u32[]{:S(2)}, u32[]{:S(2)}) %collective-permute-start.22) | collective-permute-done | bytes 16416 | tf_op jit(solution)/shard_map/ppermute | solution.py:155
  74.1 1.9 %collective-permute-done.23.rest_ref = f32[256,512]{1,0:T(8,128)S(1)} collective-permute-done((f32[256,512]{1,0:T(8,128)S(1)}, f32[256,512]{1,0:T(8,128)S(1)}, u32[]{:S(2)}, u32[]{:S(2)}) %collective-permute-start.23) | collective-permute-done | bytes 524320 | tf_op jit(solution)/shard_map/ppermute | solution.py:152
  76.0 1.0 pair_maps.1
  77.1 0.7 collective-permute-start.24
  77.8 3.7 %collective-permute-start.25 = (f32[8,512]{1,0:T(8,128)S(1)}, f32[8,512]{1,0:T(8,128)S(1)}, u32[]{:S(2)}, u32[]{:S(2)}) collective-permute-start(f32[8,512]{1,0:T(8,128)S(1)} %get-tuple-element.138.local_ref), channel_id=1, source_target_pairs={{0,8},{4,12},{1,9},{5,13},{2,10},{6,14},{3,11},{7,15}} | collective-permute-start | bytes 49160 | tf_op jit(solution)/shard_map/ppermute | solution.py:158
  81.5 1.0 group_map.1.map_ref
  82.4 0.4 collective-permute-done.25.refs_0_
  82.9 0.5 forward_link.2
  83.4 0.7 collective-permute-start.26
  84.1 0.5 forward_link.3
  84.6 0.7 collective-permute-start.28
  85.3 0.4 noise_link.2
  85.7 0.7 collective-permute-start.27
  86.4 1.1 mean_turn.1
  87.4 1.5 %collective-permute-start.29 = (f32[16,512]{1,0:T(8,128)S(1)}, f32[16,512]{1,0:T(8,128)S(1)}, u32[]{:S(2)}, u32[]{:S(2)}) collective-permute-start(f32[16,512]{1,0:T(8,128)S(1)} %pad_maximum_fusion), channel_id=1, source_target_pairs={{0,4},{4,0},{8,12},{12,8},{16,20},{20,16},{24,28},{28,24},{1,5},{5... | collective-permute-start | bytes 98312 | tf_op jit(solution)/shard_map/ppermute | solution.py:155
  89.0 0.7 collective-permute-start.31
  89.6 0.7 collective-permute-start.30
  90.3 1.1 collective-permute-done.29
  91.4 0.4 noise_link.3
  92.1 1.3 %collective-permute-start.32 = (f32[128,512]{1,0:T(8,128)S(1)}, f32[128,512]{1,0:T(8,128)S(1)}, u32[]{:S(2)}, u32[]{:S(2)}) collective-permute-start(f32[128,512]{1,0:T(8,128)S(1)} %noise_link.3), channel_id=1, source_target_pairs={{8,0},{12,4},{9,1},{13,5},{10,2},{14,6},{11,3},{15,7}} | collective-permute-start | bytes 786440 | tf_op jit(solution)/shard_map/ppermute | solution.py:158
  93.4 0.7 collective-permute-start.33
  94.4 11.0 %collective-permute-done.32.refs_2_ = f32[128,512]{1,0:T(8,128)S(1)} collective-permute-done((f32[128,512]{1,0:T(8,128)S(1)}, f32[128,512]{1,0:T(8,128)S(1)}, u32[]{:S(2)}, u32[]{:S(2)}) %collective-permute-start.32) | collective-permute-done | bytes 262176 | tf_op jit(solution)/shard_map/ppermute | solution.py:158
  105.4 0.4 divide.1
  105.8 1.6 %collective-permute-start.34 = (f32[128,512]{1,0:T(8,128)S(1)}, f32[128,512]{1,0:T(8,128)S(1)}, u32[]{:S(2)}, u32[]{:S(2)}) collective-permute-start(f32[128,512]{1,0:T(8,128)S(1)} %get-tuple-element.157), channel_id=1, source_target_pairs={{0,4},{4,0},{8,12},{12,8},{16,20},{20,16},{24,28},{28,24},{1,5},{5... | collective-permute-start | bytes 786440 | tf_op jit(solution)/shard_map/ppermute | solution.py:155
  107.4 1.5 %collective-permute-start.35 = (f32[8,512]{1,0:T(8,128)S(1)}, f32[8,512]{1,0:T(8,128)S(1)}, u32[]{:S(2)}, u32[]{:S(2)}) collective-permute-start(f32[8,512]{1,0:T(8,128)S(1)} %backward_link.1), channel_id=1, source_target_pairs={{8,0},{12,4},{9,1},{13,5},{10,2},{14,6},{11,3},{15,7}} | collective-permute-start | bytes 49160 | tf_op jit(solution)/shard_map/ppermute | solution.py:158
  108.9 3.1 %mean_terms.1 = (f32[256,512]{1,0:T(8,128)S(1)}, f32[256,512]{1,0:T(8,128)S(1)}, f32[256,512]{1,0:T(8,128)S(1)}, f32[256,512]{1,0:T(8,128)S(1)}) custom-call(f32[8,512]{1,0:T(8,128)S(1)} %get-tuple-element.160.entering_ref, f32[4,8,512]{2,1,0:T(8,128)S(1)} %get-tuple-element.161.current_ref, f32[256,512]{1,0:T(8,128)S(1)} %get-tuple-element.105.refs_9_.refs_0_, ...), custom_call_target="tpu_custom_call" | custom-call | flops 800000000 | bytes 1024 | tf_op jit(solution)/shard_map/mean_terms/pallas_call | solution.py:48
  112.0 1.0 collective-permute-done.35.refs_3_
  113.1 3.4 %last_days.1 = f32[4,512,256]{2,1,0:T(8,128)} custom-call(s32[2,128]{1,0:T(2,128)S(1)} %broadcast_in_dim.2.where_ref, f32[128,512]{1,0:T(8,128)S(1)} %get-tuple-element.156.keep_ref, f32[128,512]{1,0:T(8,128)S(1)} %collective-permute-done.34.got_ref, f32[8,512]{1,0:T(8,128)S(1)} %get-tuple-element.158.back_ref, ...), custom_call_target="tpu_custom_call" | custom-call | flops 800000000 | bytes 1024 | tf_op jit(solution)/shard_map/last_days/pallas_call | solution.py:48
  (48 shorter events, 2.4 us)
Async XLA Ops:
  0.0 9.3 %copy-start.1 = (f32[4,128,512]{2,1,0:T(8,128)S(1)}, f32[4,128,512]{2,1,0:T(8,128)}, u32[]{:S(2)}) copy-start(f32[4,128,512]{2,1,0:T(8,128)} %refs_0_.7) | copy-start | bytes 3145732
  0.0 30.8 %copy-start = (f32[4,512,256]{2,1,0:T(8,128)S(1)}, f32[4,512,256]{2,1,0:T(8,128)}, u32[]{:S(2)}) copy-start(f32[4,512,256]{2,1,0:T(8,128)} %refs_4_.3) | copy-start | bytes 6291460
  0.0 26.4 %collective-permute-start.5 = (f32[4,128,512]{2,1,0:T(8,128)}, f32[4,128,512]{2,1,0:T(8,128)}, u32[]{:S(2)}, u32[]{:S(2)}) collective-permute-start(f32[4,128,512]{2,1,0:T(8,128)} %refs_0_.4), channel_id=1, source_target_pairs={{0,2},{1,3},{2,0},{3,1},{4,6},{5,7},{6,4},{7,5},{8,10},{9,11},{10,... | collective-permute-start | bytes 3145736 | tf_op jit(solution)/shard_map/ppermute | solution.py:152
  6.6 4.9 %collective-permute-start.1 = (f32[16,512]{1,0:T(8,128)S(1)}, f32[16,512]{1,0:T(8,128)S(1)}, u32[]{:S(2)}, u32[]{:S(2)}) collective-permute-start(f32[16,512]{1,0:T(8,128)S(1)} %get-tuple-element.89), channel_id=1, source_target_pairs={{0,16},{4,20},{8,24},{12,28},{16,0},{20,4},{24,8},{28,12},{1,17},{... | collective-permute-start | bytes 98312 | tf_op jit(solution)/shard_map/ppermute | solution.py:206
  11.5 3.8 %collective-permute-start.2 = (f32[8,512]{1,0:T(8,128)S(1)}, f32[8,512]{1,0:T(8,128)S(1)}, u32[]{:S(2)}, u32[]{:S(2)}) collective-permute-start(f32[8,512]{1,0:T(8,128)S(1)} %get-tuple-element.91), channel_id=1, source_target_pairs={{0,8},{4,12},{8,0},{12,4},{16,24},{20,28},{24,16},{28,20},{1,9},{5... | collective-permute-start | bytes 49160 | tf_op jit(solution)/shard_map/ppermute | solution.py:206
  15.4 3.7 %collective-permute-start.3 = (f32[4,512]{1,0:T(4,128)S(1)}, f32[4,512]{1,0:T(4,128)S(1)}, u32[]{:S(2)}, u32[]{:S(2)}) collective-permute-start(f32[4,512]{1,0:T(4,128)S(1)} %get-tuple-element.93), channel_id=1, source_target_pairs={{0,4},{4,0},{8,12},{12,8},{16,20},{20,16},{24,28},{28,24},{1,5},{5... | collective-permute-start | bytes 24584 | tf_op jit(solution)/shard_map/ppermute | solution.py:206
  19.1 1.2 %collective-permute-start.4 = (f32[4,512]{1,0:T(4,128)S(1)}, f32[4,512]{1,0:T(4,128)S(1)}, u32[]{:S(2)}, u32[]{:S(2)}) collective-permute-start(f32[4,512]{1,0:T(4,128)S(1)} %halved.5), channel_id=1, source_target_pairs={{0,1},{1,0},{2,3},{3,2},{4,5},{5,4},{6,7},{7,6},{8,9},{9,8},{10,11... | collective-permute-start | bytes 24584 | tf_op jit(solution)/shard_map/ppermute | solution.py:152
  19.1 9.9 %collective-permute-start.10 = (f32[4,128,512]{2,1,0:T(8,128)}, f32[4,128,512]{2,1,0:T(8,128)S(1)}, u32[]{:S(2)}, u32[]{:S(2)}) collective-permute-start(f32[4,128,512]{2,1,0:T(8,128)} %refs_0_.4), channel_id=1, source_target_pairs={{0,1},{1,0},{2,3},{3,2},{4,5},{5,4},{6,7},{7,6},{8,9},{9,8},{10,11... | collective-permute-start | bytes 3145736 | tf_op jit(solution)/shard_map/ppermute | solution.py:152
  26.4 4.4 %collective-permute-start.11 = (f32[4,128,512]{2,1,0:T(8,128)}, f32[4,128,512]{2,1,0:T(8,128)S(1)}, u32[]{:S(2)}, u32[]{:S(2)}) collective-permute-start(f32[4,128,512]{2,1,0:T(8,128)} %collective-permute-done.5.refs_2_), channel_id=1, source_target_pairs={{0,1},{1,0},{2,3},{3,2},{4,5},{5,4},{6,7},{7,6},{8,9},{9,8},{10,11... | collective-permute-start | bytes 3145736 | tf_op jit(solution)/shard_map/ppermute | solution.py:152
  26.4 15.4 %collective-permute-start = (f32[4,128,512]{2,1,0:T(8,128)S(1)}, f32[4,128,512]{2,1,0:T(8,128)S(1)}, u32[]{:S(2)}, u32[]{:S(2)}) collective-permute-start(f32[4,128,512]{2,1,0:T(8,128)S(1)} %copy-done.1), channel_id=1, source_target_pairs={{0,1},{1,0},{2,3},{3,2},{4,5},{5,4},{6,7},{7,6},{8,9},{9,8},{10,11... | collective-permute-start | bytes 3145736 | tf_op jit(solution)/shard_map/ppermute | solution.py:152
  26.9 10.0 %collective-permute-start.8 = (f32[1,128,512]{2,1,0:T(8,128)S(1)}, f32[1,128,512]{2,1,0:T(8,128)S(1)}, u32[]{:S(2)}, u32[]{:S(2)}) collective-permute-start(f32[1,128,512]{2,1,0:T(8,128)S(1)} %get-tuple-element.173), channel_id=1, source_target_pairs={{0,2},{1,3},{2,0},{3,1},{4,6},{5,7},{6,4},{7,5},{8,10},{9,11},{10,... | collective-permute-start | bytes 786440 | tf_op jit(solution)/shard_map/ppermute | solution.py:152
  28.7 10.2 %collective-permute-start.6 = (f32[64,512]{1,0:T(8,128)S(1)}, f32[64,512]{1,0:T(8,128)S(1)}, u32[]{:S(2)}, u32[]{:S(2)}) collective-permute-start(f32[64,512]{1,0:T(8,128)S(1)} %get-tuple-element.95), channel_id=1, source_target_pairs={{0,2},{1,3},{2,0},{3,1},{4,6},{5,7},{6,4},{7,5},{8,10},{9,11},{10,... | collective-permute-start | bytes 393224 | tf_op jit(solution)/shard_map/ppermute | solution.py:152
  29.0 12.2 %collective-permute-start.13 = (f32[64,512]{1,0:T(8,128)S(1)}, f32[64,512]{1,0:T(8,128)S(1)}, u32[]{:S(2)}, u32[]{:S(2)}) collective-permute-start(f32[64,512]{1,0:T(8,128)S(1)} %get-tuple-element.102), channel_id=1, source_target_pairs={{0,2},{1,3},{2,0},{3,1},{4,6},{5,7},{6,4},{7,5},{8,10},{9,11},{10,... | collective-permute-start | bytes 393224 | tf_op jit(solution)/shard_map/ppermute | solution.py:152
  30.8 1.2 %copy-start.2 = (f32[4,128,512]{2,1,0:T(8,128)S(1)}, f32[4,128,512]{2,1,0:T(8,128)}, u32[]{:S(2)}) copy-start(f32[4,128,512]{2,1,0:T(8,128)} %refs_0_.4) | copy-start | bytes 3145732
  37.0 5.8 %collective-permute-start.12 = (f32[1,128,512]{2,1,0:T(8,128)S(1)}, f32[1,128,512]{2,1,0:T(8,128)S(1)}, u32[]{:S(2)}, u32[]{:S(2)}) collective-permute-start(f32[1,128,512]{2,1,0:T(8,128)S(1)} %collective-permute-done.8.refs_2_), channel_id=1, source_target_pairs={{0,1},{1,0},{2,3},{3,2},{4,5},{5,4},{6,7},{7,6},{8,9},{9,8},{10,11... | collective-permute-start | bytes 786440 | tf_op jit(solution)/shard_map/ppermute | solution.py:152
  37.1 10.8 %collective-permute-start.9 = (f32[1,128,512]{2,1,0:T(8,128)S(1)}, f32[1,128,512]{2,1,0:T(8,128)S(1)}, u32[]{:S(2)}, u32[]{:S(2)}) collective-permute-start(f32[1,128,512]{2,1,0:T(8,128)S(1)} %get-tuple-element.97), channel_id=1, source_target_pairs={{0,2},{1,3},{2,0},{3,1},{4,6},{5,7},{6,4},{7,5},{8,10},{9,11},{10,... | collective-permute-start | bytes 786440 | tf_op jit(solution)/shard_map/ppermute | solution.py:152
  41.3 1.3 %collective-permute-start.14 = (f32[64,512]{1,0:T(8,128)S(1)}, f32[64,512]{1,0:T(8,128)S(1)}, u32[]{:S(2)}, u32[]{:S(2)}) collective-permute-start(f32[64,512]{1,0:T(8,128)S(1)} %collective-permute-done.13.refs_4_), channel_id=1, source_target_pairs={{0,1},{1,0},{2,3},{3,2},{4,5},{5,4},{6,7},{7,6},{8,9},{9,8},{10,11... | collective-permute-start | bytes 393224 | tf_op jit(solution)/shard_map/ppermute | solution.py:152
  41.3 1.5 %collective-permute-start.15 = (f32[64,512]{1,0:T(8,128)S(1)}, f32[64,512]{1,0:T(8,128)S(1)}, u32[]{:S(2)}, u32[]{:S(2)}) collective-permute-start(f32[64,512]{1,0:T(8,128)S(1)} %collective-permute-done.6.refs_6_), channel_id=1, source_target_pairs={{0,1},{1,0},{2,3},{3,2},{4,5},{5,4},{6,7},{7,6},{8,9},{9,8},{10,11... | collective-permute-start | bytes 393224 | tf_op jit(solution)/shard_map/ppermute | solution.py:152
  47.9 2.4 %collective-permute-start.16 = (f32[1,128,512]{2,1,0:T(8,128)S(1)}, f32[1,128,512]{2,1,0:T(8,128)S(1)}, u32[]{:S(2)}, u32[]{:S(2)}) collective-permute-start(f32[1,128,512]{2,1,0:T(8,128)S(1)} %collective-permute-done.9.refs_2_), channel_id=1, source_target_pairs={{0,1},{1,0},{2,3},{3,2},{4,5},{5,4},{6,7},{7,6},{8,9},{9,8},{10,11... | collective-permute-start | bytes 786440 | tf_op jit(solution)/shard_map/ppermute | solution.py:152
  48.3 6.7 %collective-permute-start.18 = (f32[72,512]{1,0:T(8,128)S(1)}, f32[72,512]{1,0:T(8,128)S(1)}, u32[]{:S(2)}, u32[]{:S(2)}) collective-permute-start(f32[72,512]{1,0:T(8,128)S(1)} %get-tuple-element.115), channel_id=1, source_target_pairs={{0,2},{1,3},{2,0},{3,1},{4,6},{5,7},{6,4},{7,5},{8,10},{9,11},{10,... | collective-permute-start | bytes 442376 | tf_op jit(solution)/shard_map/ppermute | solution.py:152
  50.1 7.0 %collective-permute-start.7 = (f32[64,512]{1,0:T(8,128)S(1)}, f32[64,512]{1,0:T(8,128)S(1)}, u32[]{:S(2)}, u32[]{:S(2)}) collective-permute-start(f32[64,512]{1,0:T(8,128)S(1)} %get-tuple-element.96), channel_id=1, source_target_pairs={{0,2},{1,3},{2,0},{3,1},{4,6},{5,7},{6,4},{7,5},{8,10},{9,11},{10,... | collective-permute-start | bytes 393224 | tf_op jit(solution)/shard_map/ppermute | solution.py:152
  53.0 8.0 %collective-permute-start.20 = (f32[128,512]{1,0:T(8,128)S(1)}, f32[128,512]{1,0:T(8,128)S(1)}, u32[]{:S(2)}, u32[]{:S(2)}) collective-permute-start(f32[128,512]{1,0:T(8,128)S(1)} %get-tuple-element.113), channel_id=1, source_target_pairs={{0,4},{4,0},{8,12},{12,8},{16,20},{20,16},{24,28},{28,24},{1,5},{5... | collective-permute-start | bytes 786440 | tf_op jit(solution)/shard_map/ppermute | solution.py:155
  55.0 3.5 %collective-permute-start.19 = (f32[72,512]{1,0:T(8,128)S(1)}, f32[72,512]{1,0:T(8,128)S(1)}, u32[]{:S(2)}, u32[]{:S(2)}) collective-permute-start(f32[72,512]{1,0:T(8,128)S(1)} %collective-permute-done.18.refs_4_.refs_0_), channel_id=1, source_target_pairs={{0,1},{1,0},{2,3},{3,2},{4,5},{5,4},{6,7},{7,6},{8,9},{9,8},{10,11... | collective-permute-start | bytes 442376 | tf_op jit(solution)/shard_map/ppermute | solution.py:152
  57.1 1.3 %collective-permute-start.17 = (f32[64,512]{1,0:T(8,128)S(1)}, f32[64,512]{1,0:T(8,128)S(1)}, u32[]{:S(2)}, u32[]{:S(2)}) collective-permute-start(f32[64,512]{1,0:T(8,128)S(1)} %collective-permute-done.7.refs_2_), channel_id=1, source_target_pairs={{0,1},{1,0},{2,3},{3,2},{4,5},{5,4},{6,7},{7,6},{8,9},{9,8},{10,11... | collective-permute-start | bytes 393224 | tf_op jit(solution)/shard_map/ppermute | solution.py:152
  61.0 13.1 %collective-permute-start.21 = (f32[256,512]{1,0:T(8,128)S(1)}, f32[256,512]{1,0:T(8,128)S(1)}, u32[]{:S(2)}, u32[]{:S(2)}) collective-permute-start(f32[256,512]{1,0:T(8,128)S(1)} %get-tuple-element.120), channel_id=1, source_target_pairs={{0,4},{4,0},{8,12},{12,8},{16,20},{20,16},{24,28},{28,24},{1,5},{5... | collective-permute-start | bytes 1572872 | tf_op jit(solution)/shard_map/ppermute | solution.py:155
  67.3 6.9 %collective-permute-start.22 = (f32[8,512]{1,0:T(8,128)S(1)}, f32[8,512]{1,0:T(8,128)S(1)}, u32[]{:S(2)}, u32[]{:S(2)}) collective-permute-start(f32[8,512]{1,0:T(8,128)S(1)} %get-tuple-element.126.flux_ref), channel_id=1, source_target_pairs={{0,4},{4,0},{8,12},{12,8},{16,20},{20,16},{24,28},{28,24},{1,5},{5... | collective-permute-start | bytes 49160 | tf_op jit(solution)/shard_map/ppermute | solution.py:155
  74.1 1.9 %collective-permute-start.23 = (f32[256,512]{1,0:T(8,128)S(1)}, f32[256,512]{1,0:T(8,128)S(1)}, u32[]{:S(2)}, u32[]{:S(2)}) collective-permute-start(f32[256,512]{1,0:T(8,128)S(1)} %collective-permute-done.21.half_ref), channel_id=1, source_target_pairs={{0,1},{1,0},{2,3},{3,2},{4,5},{5,4},{6,7},{7,6},{8,9},{9,8},{10,11... | collective-permute-start | bytes 1572872 | tf_op jit(solution)/shard_map/ppermute | solution.py:152
  77.1 8.2 %collective-permute-start.24 = (f32[128,512]{1,0:T(8,128)S(1)}, f32[128,512]{1,0:T(8,128)S(1)}, u32[]{:S(2)}, u32[]{:S(2)}) collective-permute-start(f32[128,512]{1,0:T(8,128)S(1)} %get-tuple-element.139.local_ref), channel_id=1, source_target_pairs={{24,16},{28,20},{25,17},{29,21},{26,18},{30,22},{27,19},{31,23}} | collective-permute-start | bytes 786440 | tf_op jit(solution)/shard_map/ppermute | solution.py:158
  77.8 5.1 %collective-permute-start.25 = (f32[8,512]{1,0:T(8,128)S(1)}, f32[8,512]{1,0:T(8,128)S(1)}, u32[]{:S(2)}, u32[]{:S(2)}) collective-permute-start(f32[8,512]{1,0:T(8,128)S(1)} %get-tuple-element.138.local_ref), channel_id=1, source_target_pairs={{0,8},{4,12},{1,9},{5,13},{2,10},{6,14},{3,11},{7,15}} | collective-permute-start | bytes 49160 | tf_op jit(solution)/shard_map/ppermute | solution.py:158
  83.4 0.7 collective-permute-start.26
  84.6 1.8 %collective-permute-start.28 = (f32[8,512]{1,0:T(8,128)S(1)}, f32[8,512]{1,0:T(8,128)S(1)}, u32[]{:S(2)}, u32[]{:S(2)}) collective-permute-start(f32[8,512]{1,0:T(8,128)S(1)} %forward_link.3), channel_id=1, source_target_pairs={{16,24},{20,28},{17,25},{21,29},{18,26},{22,30},{19,27},{23,31}} | collective-permute-start | bytes 49160 | tf_op jit(solution)/shard_map/ppermute | solution.py:158
  85.7 5.7 %collective-permute-start.27 = (f32[128,512]{1,0:T(8,128)S(1)}, f32[128,512]{1,0:T(8,128)S(1)}, u32[]{:S(2)}, u32[]{:S(2)}) collective-permute-start(f32[128,512]{1,0:T(8,128)S(1)} %noise_link.2), channel_id=1, source_target_pairs={{16,8},{20,12},{17,9},{21,13},{18,10},{22,14},{19,11},{23,15}} | collective-permute-start | bytes 786440 | tf_op jit(solution)/shard_map/ppermute | solution.py:158
  87.4 3.9 %collective-permute-start.29 = (f32[16,512]{1,0:T(8,128)S(1)}, f32[16,512]{1,0:T(8,128)S(1)}, u32[]{:S(2)}, u32[]{:S(2)}) collective-permute-start(f32[16,512]{1,0:T(8,128)S(1)} %pad_maximum_fusion), channel_id=1, source_target_pairs={{0,4},{4,0},{8,12},{12,8},{16,20},{20,16},{24,28},{28,24},{1,5},{5... | collective-permute-start | bytes 98312 | tf_op jit(solution)/shard_map/ppermute | solution.py:155
  89.0 2.8 %collective-permute-start.31 = (f32[8,512]{1,0:T(8,128)S(1)}, f32[8,512]{1,0:T(8,128)S(1)}, u32[]{:S(2)}, u32[]{:S(2)}) collective-permute-start(f32[8,512]{1,0:T(8,128)S(1)} %get-tuple-element.147.part_ref), channel_id=1, source_target_pairs={{24,20},{28,16},{25,21},{29,17},{26,22},{30,18},{27,23},{31,19}} | collective-permute-start | bytes 49160 | tf_op jit(solution)/shard_map/ppermute | solution.py:513
  89.6 2.1 %collective-permute-start.30 = (f32[8,512]{1,0:T(8,128)S(1)}, f32[8,512]{1,0:T(8,128)S(1)}, u32[]{:S(2)}, u32[]{:S(2)}) collective-permute-start(f32[8,512]{1,0:T(8,128)S(1)} %get-tuple-element.147.part_ref), channel_id=1, source_target_pairs={{24,16},{28,20},{25,17},{29,21},{26,18},{30,22},{27,19},{31,23}} | collective-permute-start | bytes 49160 | tf_op jit(solution)/shard_map/ppermute | solution.py:513
  92.1 13.3 %collective-permute-start.32 = (f32[128,512]{1,0:T(8,128)S(1)}, f32[128,512]{1,0:T(8,128)S(1)}, u32[]{:S(2)}, u32[]{:S(2)}) collective-permute-start(f32[128,512]{1,0:T(8,128)S(1)} %noise_link.3), channel_id=1, source_target_pairs={{8,0},{12,4},{9,1},{13,5},{10,2},{14,6},{11,3},{15,7}} | collective-permute-start | bytes 786440 | tf_op jit(solution)/shard_map/ppermute | solution.py:158
  93.4 0.7 collective-permute-start.33
  105.8 7.2 %collective-permute-start.34 = (f32[128,512]{1,0:T(8,128)S(1)}, f32[128,512]{1,0:T(8,128)S(1)}, u32[]{:S(2)}, u32[]{:S(2)}) collective-permute-start(f32[128,512]{1,0:T(8,128)S(1)} %get-tuple-element.157), channel_id=1, source_target_pairs={{0,4},{4,0},{8,12},{12,8},{16,20},{20,16},{24,28},{28,24},{1,5},{5... | collective-permute-start | bytes 786440 | tf_op jit(solution)/shard_map/ppermute | solution.py:155
  107.4 5.6 %collective-permute-start.35 = (f32[8,512]{1,0:T(8,128)S(1)}, f32[8,512]{1,0:T(8,128)S(1)}, u32[]{:S(2)}, u32[]{:S(2)}) collective-permute-start(f32[8,512]{1,0:T(8,128)S(1)} %backward_link.1), channel_id=1, source_target_pairs={{8,0},{12,4},{9,1},{13,5},{10,2},{14,6},{11,3},{15,7}} | collective-permute-start | bytes 49160 | tf_op jit(solution)/shard_map/ppermute | solution.py:158

commit v11 on v10

--- a/solution.py
+++ b/solution.py
@@ -537,7 +537,8 @@
     value = pair_sum
     for group in range(groups - 1, 0, -1):
         got = to_group(after(value, ahead), group, group - 1)
-        ahead = next(hops)
+        if group > 1:
+            ahead = next(hops)
         if group == groups - 1:
             ahead = next(hops, ahead)
         leaving.append(after(got, ahead))
@@ -546,9 +547,6 @@
             noise_step[:] = [value]
             if group < groups - 1:
                 ahead = next(hops, ahead)
-    for _ in hops:
-        pass
-
     def divide_body(where_ref, map_ref, sum_ref, *refs):
         keep_out, send_out = refs[-2:]
         given = refs[0][...]
@@ -564,6 +562,9 @@
         [high_map, high_sum, *leaving],
     )
     got_half = to_pair(sent_half)
+    noise_step[:] = [sent_half]
+    for _ in hops:
+        pass
 
     def terms_body(entering_ref, current_ref, *refs):
         outs = refs[-day_count:]

time: 117 us -> 120 us (1.026)
  waiting for transfers between devices: 38.3 us -> 41.1 us
    ppermute x8, waiting for transfers between devices: 12.5 us -> 15.4 us  [to_group(): lax.ppermute(value, 'tm', [(PAIR * source + i, PAIR * target + i) for i i...]
  transfers between devices with their start and end apart: 36 -> 36, of which waited for: 18 -> 18; matrix products, arithmetic and copies ran while one was open for 2% -> 2% of each run, Pallas kernels for 28% -> 27%
where the time goes in v11:
time: 120 us; the launch traced here: 119 us
  waiting for transfers between devices  41.1 us (34%)
  Pallas kernels  37.5 us (31%)
  starting transfers between devices  36.7 us (31%)
  local copies, waits for them, and re-layouts  3.54 us (3%)
    pallas_call x24, Pallas kernels, call(): pl.pallas_call(body, out_shape=out_shape, in_specs=[vmem] * (len(scalars)...  37.5 us
    ppermute x18, waiting for transfers between devices, to_row(): lax.ppermute(value, 'row', [(i, i ^ distance) for i in range(row_count)])  15.7 us
    ppermute x8, waiting for transfers between devices, to_group(): lax.ppermute(value, 'tm', [(PAIR * source + i, PAIR * target + i) for i i...  15.4 us
    ppermute x18, starting transfers between devices, to_row(): lax.ppermute(value, 'row', [(i, i ^ distance) for i in range(row_count)])  12.6 us
    ppermute x8, starting transfers between devices, to_group(): lax.ppermute(value, 'tm', [(PAIR * source + i, PAIR * target + i) for i i...  9.83 us
    ppermute x5, starting transfers between devices, to_pair(): return lax.ppermute(value, 'tm', [(i, i ^ 1) for i in range(part_count)])  7.07 us
    ppermute x3, waiting for transfers between devices, local(): lax.ppermute(sent, 'tm', [(i, i ^ distance) for i in range(part_count)])  6.45 us
    ppermute x3, starting transfers between devices, local(): lax.ppermute(sent, 'tm', [(i, i ^ distance) for i in range(part_count)])  5.86 us
  transfers between devices with their start and end apart: 36, of which 18 were waited for; matrix products, arithmetic and copies ran while one was open for 2% of the time, Pallas kernels for 27%

profile of v11, /device:TPU:0, one launch (start us, length us, event | category | flops | bytes accessed | tf_op | source)
XLA Modules:
  0.0 119.4 jit_solution(4284240139193548626)
XLA Ops:
  0.0 2.9 %collective-permute-start.5 = (f32[4,128,512]{2,1,0:T(8,128)}, f32[4,128,512]{2,1,0:T(8,128)}, u32[]{:S(2)}, u32[]{:S(2)}) collective-permute-start(f32[4,128,512]{2,1,0:T(8,128)} %refs_0_.4), channel_id=1, source_target_pairs={{0,2},{1,3},{2,0},{3,1},{4,6},{5,7},{6,4},{7,5},{8,10},{9,11},{10,... | collective-permute-start | bytes 3145736 | tf_op jit(solution)/shard_map/ppermute | solution.py:152
  2.9 0.7 reshape.10.day_ref
  3.7 0.7 reshape.11.node_ref
  4.4 0.7 reshape.12.value_ref
  5.3 1.4 %bin_observations.1 = (f32[16,512]{1,0:T(8,128)S(1)}, f32[16,512]{1,0:T(8,128)S(1)}) custom-call(s32[2,128]{1,0:T(2,128)S(1)} %broadcast_in_dim.2.where_ref, s32[8,512]{1,0:T(8,128)S(1)} %reshape.10.day_ref, s32[8,512]{1,0:T(8,128)S(1)} %reshape.11.node_ref, f32[8,512]{1,0:T(8,128)S(1)} %reshape.12.value_ref), custom_call_target="tpu_custom_call" | custom-call | flops 400000000 | bytes 1024 | tf_op jit(solution)/shard_map/bin_observations/pallas_call | solution.py:48
  6.6 2.6 %collective-permute-start.1 = (f32[16,512]{1,0:T(8,128)S(1)}, f32[16,512]{1,0:T(8,128)S(1)}, u32[]{:S(2)}, u32[]{:S(2)}) collective-permute-start(f32[16,512]{1,0:T(8,128)S(1)} %get-tuple-element.89), channel_id=1, source_target_pairs={{0,16},{4,20},{8,24},{12,28},{16,0},{20,4},{24,8},{28,12},{1,17},{... | collective-permute-start | bytes 98312 | tf_op jit(solution)/shard_map/ppermute | solution.py:206
  9.3 2.2 %collective-permute-done.1.got_ref = f32[16,512]{1,0:T(8,128)S(1)} collective-permute-done((f32[16,512]{1,0:T(8,128)S(1)}, f32[16,512]{1,0:T(8,128)S(1)}, u32[]{:S(2)}, u32[]{:S(2)}) %collective-permute-start.1) | collective-permute-done | bytes 32800 | tf_op jit(solution)/shard_map/ppermute | solution.py:206
  11.5 1.6 %collective-permute-start.2 = (f32[8,512]{1,0:T(8,128)S(1)}, f32[8,512]{1,0:T(8,128)S(1)}, u32[]{:S(2)}, u32[]{:S(2)}) collective-permute-start(f32[8,512]{1,0:T(8,128)S(1)} %get-tuple-element.91), channel_id=1, source_target_pairs={{0,8},{4,12},{8,0},{12,4},{16,24},{20,28},{24,16},{28,20},{1,9},{5... | collective-permute-start | bytes 49160 | tf_op jit(solution)/shard_map/ppermute | solution.py:206
  13.2 2.2 %collective-permute-done.2.got_ref = f32[8,512]{1,0:T(8,128)S(1)} collective-permute-done((f32[8,512]{1,0:T(8,128)S(1)}, f32[8,512]{1,0:T(8,128)S(1)}, u32[]{:S(2)}, u32[]{:S(2)}) %collective-permute-start.2) | collective-permute-done | bytes 16416 | tf_op jit(solution)/shard_map/ppermute | solution.py:206
  15.4 1.6 %collective-permute-start.3 = (f32[4,512]{1,0:T(4,128)S(1)}, f32[4,512]{1,0:T(4,128)S(1)}, u32[]{:S(2)}, u32[]{:S(2)}) collective-permute-start(f32[4,512]{1,0:T(4,128)S(1)} %get-tuple-element.93), channel_id=1, source_target_pairs={{0,4},{4,0},{8,12},{12,8},{16,20},{20,16},{24,28},{28,24},{1,5},{5... | collective-permute-start | bytes 24584 | tf_op jit(solution)/shard_map/ppermute | solution.py:206
  17.0 2.1 %collective-permute-done.3.got_ref = f32[4,512]{1,0:T(4,128)S(1)} collective-permute-done((f32[4,512]{1,0:T(4,128)S(1)}, f32[4,512]{1,0:T(4,128)S(1)}, u32[]{:S(2)}, u32[]{:S(2)}) %collective-permute-start.3) | collective-permute-done | bytes 8224 | tf_op jit(solution)/shard_map/ppermute | solution.py:206
  19.1 0.5 collective-permute-start.10
  19.6 0.7 collective-permute-done.4
  20.3 6.1 %collective-permute-done.5.refs_2_ = f32[4,128,512]{2,1,0:T(8,128)} collective-permute-done((f32[4,128,512]{2,1,0:T(8,128)}, f32[4,128,512]{2,1,0:T(8,128)}, u32[]{:S(2)}, u32[]{:S(2)}) %collective-permute-start.5) | collective-permute-done | bytes 1048608 | tf_op jit(solution)/shard_map/ppermute | solution.py:152
  26.4 0.5 collective-permute-start
  26.9 1.7 %collective-permute-start.8 = (f32[1,128,512]{2,1,0:T(8,128)S(1)}, f32[1,128,512]{2,1,0:T(8,128)S(1)}, u32[]{:S(2)}, u32[]{:S(2)}) collective-permute-start(f32[1,128,512]{2,1,0:T(8,128)S(1)} %get-tuple-element.173), channel_id=1, source_target_pairs={{0,2},{1,3},{2,0},{3,1},{4,6},{5,7},{6,4},{7,5},{8,10},{9,11},{10,... | collective-permute-start | bytes 786440 | tf_op jit(solution)/shard_map/ppermute | solution.py:152
  29.0 1.7 %collective-permute-start.13 = (f32[64,512]{1,0:T(8,128)S(1)}, f32[64,512]{1,0:T(8,128)S(1)}, u32[]{:S(2)}, u32[]{:S(2)}) collective-permute-start(f32[64,512]{1,0:T(8,128)S(1)} %get-tuple-element.102), channel_id=1, source_target_pairs={{0,2},{1,3},{2,0},{3,1},{4,6},{5,7},{6,4},{7,5},{8,10},{9,11},{10,... | collective-permute-start | bytes 393224 | tf_op jit(solution)/shard_map/ppermute | solution.py:152
  30.8 1.2 %copy-done.2 = f32[4,128,512]{2,1,0:T(8,128)S(1)} copy-done((f32[4,128,512]{2,1,0:T(8,128)S(1)}, f32[4,128,512]{2,1,0:T(8,128)}, u32[]{:S(2)}) %copy-start.2) | copy-done | bytes 1048600
  32.0 4.9 %inverses.1 = (f32[512,512]{1,0:T(8,128)S(1)}, bf16[2,512,512]{2,1,0:T(8,128)(2,1)S(1)}, bf16[2,512,512]{2,1,0:T(8,128)(2,1)S(1)}, bf16[2,512,512]{2,1,0:T(8,128...) custom-call(s32[2,128]{1,0:T(2,128)S(1)} %broadcast_in_dim.2.where_r, ...), custom_call_target="tpu_custom_call" | custom-call | flops 800000000 | bytes 1024 | tf_op jit(solution)/shard_map/inverses/pallas_call | solution.py:48
  37.1 1.8 %collective-permute-start.9 = (f32[1,128,512]{2,1,0:T(8,128)S(1)}, f32[1,128,512]{2,1,0:T(8,128)S(1)}, u32[]{:S(2)}, u32[]{:S(2)}) collective-permute-start(f32[1,128,512]{2,1,0:T(8,128)S(1)} %get-tuple-element.97), channel_id=1, source_target_pairs={{0,2},{1,3},{2,0},{3,1},{4,6},{5,7},{6,4},{7,5},{8,10},{9,11},{10,... | collective-permute-start | bytes 786440 | tf_op jit(solution)/shard_map/ppermute | solution.py:152
  38.9 2.4 %collective-permute-done.13.refs_4_ = f32[64,512]{1,0:T(8,128)S(1)} collective-permute-done((f32[64,512]{1,0:T(8,128)S(1)}, f32[64,512]{1,0:T(8,128)S(1)}, u32[]{:S(2)}, u32[]{:S(2)}) %collective-permute-start.13) | collective-permute-done | bytes 131104 | tf_op jit(solution)/shard_map/ppermute | solution.py:152
  41.3 0.5 collective-permute-start.15
  41.8 0.8 collective-permute-done.14.refs_5_
  42.8 5.1 %early_days.1 = (f32[256,512]{1,0:T(8,128)S(1)}, bf16[2,512,512]{2,1,0:T(8,128)(2,1)S(1)}, bf16[2,512,512]{2,1,0:T(8,128)(2,1)S(1)}, bf16[2,512,512]{2,1,0:T(8,1...) custom-call(s32[2,128]{1,0:T(2,128)S(1)} %broadcast_in_dim.2.where_ref, ...), custom_call_target="tpu_custom_call" | custom-call | flops 1200000000 | bytes 1024 | tf_op jit(solution)/shard_map/early_days/pallas_call | solution.py:48
  47.9 0.4 collective-permute-start.16
  48.3 1.8 %collective-permute-start.18 = (f32[72,512]{1,0:T(8,128)S(1)}, f32[72,512]{1,0:T(8,128)S(1)}, u32[]{:S(2)}, u32[]{:S(2)}) collective-permute-start(f32[72,512]{1,0:T(8,128)S(1)} %get-tuple-element.115), channel_id=1, source_target_pairs={{0,2},{1,3},{2,0},{3,1},{4,6},{5,7},{6,4},{7,5},{8,10},{9,11},{10,... | collective-permute-start | bytes 442376 | tf_op jit(solution)/shard_map/ppermute | solution.py:152
  50.3 2.7 %day_2.1 = (bf16[2,512,512]{2,1,0:T(8,128)(2,1)S(1)}, bf16[2,512,512]{2,1,0:T(8,128)(2,1)S(1)}, f32[128,512]{1,0:T(8,128)S(1)}, f32[128,512]{1,0:T(8,128)S(1)}) custom-call(s32[2,128]{1,0:T(2,128)S(1)} %broadcast_in_dim.2.where_ref, f32[4,128,512]{2,1,0:T(8,128)S(1)} %copy-done.1, f32[4,128,512]{2,1,0:T(8,128)S(1)} %collective-permute-done.refs_1_, ...), custom_call_target="tpu_custom_call" | custom-call | flops 600000000 | bytes 1024 | tf_op jit(solution)/shard_map/day_2/pallas_call | solution.py:48
  53.0 1.9 %collective-permute-start.20 = (f32[128,512]{1,0:T(8,128)S(1)}, f32[128,512]{1,0:T(8,128)S(1)}, u32[]{:S(2)}, u32[]{:S(2)}) collective-permute-start(f32[128,512]{1,0:T(8,128)S(1)} %get-tuple-element.113), channel_id=1, source_target_pairs={{0,4},{4,0},{8,12},{12,8},{16,20},{20,16},{24,28},{28,24},{1,5},{5... | collective-permute-start | bytes 786440 | tf_op jit(solution)/shard_map/ppermute | solution.py:155
  55.0 2.1 %collective-permute-done.7.refs_2_ = f32[64,512]{1,0:T(8,128)S(1)} collective-permute-done((f32[64,512]{1,0:T(8,128)S(1)}, f32[64,512]{1,0:T(8,128)S(1)}, u32[]{:S(2)}, u32[]{:S(2)}) %collective-permute-start.7) | collective-permute-done | bytes 131104 | tf_op jit(solution)/shard_map/ppermute | solution.py:152
  57.1 1.3 %collective-permute-done.17.refs_3_ = f32[64,512]{1,0:T(8,128)S(1)} collective-permute-done((f32[64,512]{1,0:T(8,128)S(1)}, f32[64,512]{1,0:T(8,128)S(1)}, u32[]{:S(2)}, u32[]{:S(2)}) %collective-permute-start.17) | collective-permute-done | bytes 131104 | tf_op jit(solution)/shard_map/ppermute | solution.py:152
  58.4 1.2 last_link.1
  59.6 1.3 %collective-permute-done.20.other_ref = f32[128,512]{1,0:T(8,128)S(1)} collective-permute-done((f32[128,512]{1,0:T(8,128)S(1)}, f32[128,512]{1,0:T(8,128)S(1)}, u32[]{:S(2)}, u32[]{:S(2)}) %collective-permute-start.20) | collective-permute-done | bytes 262176 | tf_op jit(solution)/shard_map/ppermute | solution.py:155
  61.0 1.7 %collective-permute-start.21 = (f32[256,512]{1,0:T(8,128)S(1)}, f32[256,512]{1,0:T(8,128)S(1)}, u32[]{:S(2)}, u32[]{:S(2)}) collective-permute-start(f32[256,512]{1,0:T(8,128)S(1)} %get-tuple-element.120), channel_id=1, source_target_pairs={{0,4},{4,0},{8,12},{12,8},{16,20},{20,16},{24,28},{28,24},{1,5},{5... | collective-permute-start | bytes 1572872 | tf_op jit(solution)/shard_map/ppermute | solution.py:155
  62.7 4.5 %lines.1 = (f32[8,512]{1,0:T(8,128)S(1)}, f32[8,512]{1,0:T(8,128)S(1)}, f32[4,8,512]{2,1,0:T(8,128)S(1)}) custom-call(f32[4,512]{1,0:T(4,128)S(1)} %add.3.source_ref, f32[72,512]{1,0:T(8,128)S(1)} %collective-permute-done.18.refs_4_.refs_0_, bf16[2,512,512]{2,1,0:T(8,128)(2,1)S(1)} %get-tuple-element.106.refs_10_.refs_1_.refs_3_.refs_2_, ...), custom_call_target="tpu_custom_call" | custom-call | flops 1000000000 | bytes 1024 | tf_op jit(solution)/shard_map/lines/pallas_call | solution.py:48
  67.5 2.7 %grams.1.gram_ref = bf16[2,512,512]{2,1,0:T(8,128)(2,1)S(1)} custom-call(f32[512,512]{1,0:T(8,128)S(1)} %get-tuple-element.128.gram_ref, bf16[2,512,512]{2,1,0:T(8,128)(2,1)S(1)} %get-tuple-element.123.refs_6_.refs_0_.refs_5_, bf16[2,512,512]{2,1,0:T(8,128)(2,1)S(1)} %get-tuple-element.112.refs_7_.refs_9_.refs_1_.refs_8_, ...), custom_call_target="tpu_custom_call" | custom-call | flops 600000000 | bytes 1024 | tf_op jit(solution)/shard_map/grams/pallas_call | solution.py:48
  70.2 2.6 %late_maps.1 = (bf16[2,512,512]{2,1,0:T(8,128)(2,1)S(1)}, bf16[2,512,512]{2,1,0:T(8,128)(2,1)S(1)}, bf16[2,512,512]{2,1,0:T(8,128)(2,1)S(1)}) custom-call(bf16[2,512,512]{2,1,0:T(8,128)(2,1)S(1)} %get-tuple-element.129.refs_11_.refs_4_.refs_0_, bf16[2,512,512]{2,1,0:T(8,128)(2,1)S(1)} %get-tuple-element.108.refs_12_.refs_7_.refs_1_, ...), custom_call_target="tpu_custom_call" | custom-call | flops 600000000 | bytes 1024 | tf_op jit(solution)/shard_map/late_maps/pallas_call | solution.py:48
  72.9 1.2 %collective-permute-done.22.other_flux_ref = f32[8,512]{1,0:T(8,128)S(1)} collective-permute-done((f32[8,512]{1,0:T(8,128)S(1)}, f32[8,512]{1,0:T(8,128)S(1)}, u32[]{:S(2)}, u32[]{:S(2)}) %collective-permute-start.22) | collective-permute-done | bytes 16416 | tf_op jit(solution)/shard_map/ppermute | solution.py:155
  74.1 1.9 %collective-permute-done.23.rest_ref = f32[256,512]{1,0:T(8,128)S(1)} collective-permute-done((f32[256,512]{1,0:T(8,128)S(1)}, f32[256,512]{1,0:T(8,128)S(1)}, u32[]{:S(2)}, u32[]{:S(2)}) %collective-permute-start.23) | collective-permute-done | bytes 524320 | tf_op jit(solution)/shard_map/ppermute | solution.py:152
  76.0 1.0 pair_maps.1
  77.1 0.7 collective-permute-start.24
  77.8 3.7 %collective-permute-start.25 = (f32[8,512]{1,0:T(8,128)S(1)}, f32[8,512]{1,0:T(8,128)S(1)}, u32[]{:S(2)}, u32[]{:S(2)}) collective-permute-start(f32[8,512]{1,0:T(8,128)S(1)} %get-tuple-element.138.local_ref), channel_id=1, source_target_pairs={{0,8},{4,12},{1,9},{5,13},{2,10},{6,14},{3,11},{7,15}} | collective-permute-start | bytes 49160 | tf_op jit(solution)/shard_map/ppermute | solution.py:158
  81.5 1.0 group_map.1.map_ref
  82.4 0.4 collective-permute-done.25.refs_0_
  82.9 0.5 forward_link.2
  83.4 0.7 collective-permute-start.26
  84.1 0.5 forward_link.3
  84.6 0.7 collective-permute-start.28
  85.3 0.4 noise_link.2
  85.7 0.7 collective-permute-start.27
  86.4 1.1 mean_turn.1
  87.4 1.5 %collective-permute-start.29 = (f32[16,512]{1,0:T(8,128)S(1)}, f32[16,512]{1,0:T(8,128)S(1)}, u32[]{:S(2)}, u32[]{:S(2)}) collective-permute-start(f32[16,512]{1,0:T(8,128)S(1)} %pad_maximum_fusion), channel_id=1, source_target_pairs={{0,4},{4,0},{8,12},{12,8},{16,20},{20,16},{24,28},{28,24},{1,5},{5... | collective-permute-start | bytes 98312 | tf_op jit(solution)/shard_map/ppermute | solution.py:155
  89.0 0.7 collective-permute-start.31
  89.6 0.7 collective-permute-start.30
  90.3 1.1 collective-permute-done.29
  91.4 0.4 noise_link.3
  92.1 1.3 %collective-permute-start.32 = (f32[128,512]{1,0:T(8,128)S(1)}, f32[128,512]{1,0:T(8,128)S(1)}, u32[]{:S(2)}, u32[]{:S(2)}) collective-permute-start(f32[128,512]{1,0:T(8,128)S(1)} %noise_link.3), channel_id=1, source_target_pairs={{8,0},{12,4},{9,1},{13,5},{10,2},{14,6},{11,3},{15,7}} | collective-permute-start | bytes 786440 | tf_op jit(solution)/shard_map/ppermute | solution.py:158
  93.4 12.0 %collective-permute-done.32.refs_2_ = f32[128,512]{1,0:T(8,128)S(1)} collective-permute-done((f32[128,512]{1,0:T(8,128)S(1)}, f32[128,512]{1,0:T(8,128)S(1)}, u32[]{:S(2)}, u32[]{:S(2)}) %collective-permute-start.32) | collective-permute-done | bytes 262176 | tf_op jit(solution)/shard_map/ppermute | solution.py:158
  105.4 0.4 divide.1
  105.8 1.6 %collective-permute-start.33 = (f32[128,512]{1,0:T(8,128)S(1)}, f32[128,512]{1,0:T(8,128)S(1)}, u32[]{:S(2)}, u32[]{:S(2)}) collective-permute-start(f32[128,512]{1,0:T(8,128)S(1)} %get-tuple-element.155), channel_id=1, source_target_pairs={{0,4},{4,0},{8,12},{12,8},{16,20},{20,16},{24,28},{28,24},{1,5},{5... | collective-permute-start | bytes 786440 | tf_op jit(solution)/shard_map/ppermute | solution.py:155
  107.4 0.7 collective-permute-start.34
  108.4 1.5 %collective-permute-start.35 = (f32[8,512]{1,0:T(8,128)S(1)}, f32[8,512]{1,0:T(8,128)S(1)}, u32[]{:S(2)}, u32[]{:S(2)}) collective-permute-start(f32[8,512]{1,0:T(8,128)S(1)} %backward_link.1), channel_id=1, source_target_pairs={{8,0},{12,4},{9,1},{13,5},{10,2},{14,6},{11,3},{15,7}} | collective-permute-start | bytes 49160 | tf_op jit(solution)/shard_map/ppermute | solution.py:158
  109.9 3.1 %mean_terms.1 = (f32[256,512]{1,0:T(8,128)S(1)}, f32[256,512]{1,0:T(8,128)S(1)}, f32[256,512]{1,0:T(8,128)S(1)}, f32[256,512]{1,0:T(8,128)S(1)}) custom-call(f32[8,512]{1,0:T(8,128)S(1)} %get-tuple-element.160.entering_ref, f32[4,8,512]{2,1,0:T(8,128)S(1)} %get-tuple-element.161.current_ref, f32[256,512]{1,0:T(8,128)S(1)} %get-tuple-element.105.refs_9_.refs_0_, ...), custom_call_target="tpu_custom_call" | custom-call | flops 800000000 | bytes 1024 | tf_op jit(solution)/shard_map/mean_terms/pallas_call | solution.py:48
  113.0 2.9 %collective-permute-done.35.refs_3_ = f32[8,512]{1,0:T(8,128)S(1)} collective-permute-done((f32[8,512]{1,0:T(8,128)S(1)}, f32[8,512]{1,0:T(8,128)S(1)}, u32[]{:S(2)}, u32[]{:S(2)}) %collective-permute-start.35) | collective-permute-done | bytes 16416 | tf_op jit(solution)/shard_map/ppermute | solution.py:158
  115.9 3.4 %last_days.1 = f32[4,512,256]{2,1,0:T(8,128)} custom-call(s32[2,128]{1,0:T(2,128)S(1)} %broadcast_in_dim.2.where_ref, f32[128,512]{1,0:T(8,128)S(1)} %get-tuple-element.154.keep_ref, f32[128,512]{1,0:T(8,128)S(1)} %collective-permute-done.33.got_ref, f32[8,512]{1,0:T(8,128)S(1)} %get-tuple-element.156.back_ref, ...), custom_call_target="tpu_custom_call" | custom-call | flops 800000000 | bytes 1024 | tf_op jit(solution)/shard_map/last_days/pallas_call | solution.py:48
  (48 shorter events, 2.4 us)
Async XLA Ops:
  0.0 9.3 %copy-start.1 = (f32[4,128,512]{2,1,0:T(8,128)S(1)}, f32[4,128,512]{2,1,0:T(8,128)}, u32[]{:S(2)}) copy-start(f32[4,128,512]{2,1,0:T(8,128)} %refs_0_.7) | copy-start | bytes 3145732
  0.0 30.8 %copy-start = (f32[4,512,256]{2,1,0:T(8,128)S(1)}, f32[4,512,256]{2,1,0:T(8,128)}, u32[]{:S(2)}) copy-start(f32[4,512,256]{2,1,0:T(8,128)} %refs_4_.3) | copy-start | bytes 6291460
  0.0 26.4 %collective-permute-start.5 = (f32[4,128,512]{2,1,0:T(8,128)}, f32[4,128,512]{2,1,0:T(8,128)}, u32[]{:S(2)}, u32[]{:S(2)}) collective-permute-start(f32[4,128,512]{2,1,0:T(8,128)} %refs_0_.4), channel_id=1, source_target_pairs={{0,2},{1,3},{2,0},{3,1},{4,6},{5,7},{6,4},{7,5},{8,10},{9,11},{10,... | collective-permute-start | bytes 3145736 | tf_op jit(solution)/shard_map/ppermute | solution.py:152
  6.6 4.9 %collective-permute-start.1 = (f32[16,512]{1,0:T(8,128)S(1)}, f32[16,512]{1,0:T(8,128)S(1)}, u32[]{:S(2)}, u32[]{:S(2)}) collective-permute-start(f32[16,512]{1,0:T(8,128)S(1)} %get-tuple-element.89), channel_id=1, source_target_pairs={{0,16},{4,20},{8,24},{12,28},{16,0},{20,4},{24,8},{28,12},{1,17},{... | collective-permute-start | bytes 98312 | tf_op jit(solution)/shard_map/ppermute | solution.py:206
  11.5 3.8 %collective-permute-start.2 = (f32[8,512]{1,0:T(8,128)S(1)}, f32[8,512]{1,0:T(8,128)S(1)}, u32[]{:S(2)}, u32[]{:S(2)}) collective-permute-start(f32[8,512]{1,0:T(8,128)S(1)} %get-tuple-element.91), channel_id=1, source_target_pairs={{0,8},{4,12},{8,0},{12,4},{16,24},{20,28},{24,16},{28,20},{1,9},{5... | collective-permute-start | bytes 49160 | tf_op jit(solution)/shard_map/ppermute | solution.py:206
  15.4 3.7 %collective-permute-start.3 = (f32[4,512]{1,0:T(4,128)S(1)}, f32[4,512]{1,0:T(4,128)S(1)}, u32[]{:S(2)}, u32[]{:S(2)}) collective-permute-start(f32[4,512]{1,0:T(4,128)S(1)} %get-tuple-element.93), channel_id=1, source_target_pairs={{0,4},{4,0},{8,12},{12,8},{16,20},{20,16},{24,28},{28,24},{1,5},{5... | collective-permute-start | bytes 24584 | tf_op jit(solution)/shard_map/ppermute | solution.py:206
  19.1 1.2 collective-permute-start.4
  19.1 9.9 %collective-permute-start.10 = (f32[4,128,512]{2,1,0:T(8,128)}, f32[4,128,512]{2,1,0:T(8,128)S(1)}, u32[]{:S(2)}, u32[]{:S(2)}) collective-permute-start(f32[4,128,512]{2,1,0:T(8,128)} %refs_0_.4), channel_id=1, source_target_pairs={{0,1},{1,0},{2,3},{3,2},{4,5},{5,4},{6,7},{7,6},{8,9},{9,8},{10,11... | collective-permute-start | bytes 3145736 | tf_op jit(solution)/shard_map/ppermute | solution.py:152
  26.4 4.4 %collective-permute-start.11 = (f32[4,128,512]{2,1,0:T(8,128)}, f32[4,128,512]{2,1,0:T(8,128)S(1)}, u32[]{:S(2)}, u32[]{:S(2)}) collective-permute-start(f32[4,128,512]{2,1,0:T(8,128)} %collective-permute-done.5.refs_2_), channel_id=1, source_target_pairs={{0,1},{1,0},{2,3},{3,2},{4,5},{5,4},{6,7},{7,6},{8,9},{9,8},{10,11... | collective-permute-start | bytes 3145736 | tf_op jit(solution)/shard_map/ppermute | solution.py:152
  26.4 15.4 %collective-permute-start = (f32[4,128,512]{2,1,0:T(8,128)S(1)}, f32[4,128,512]{2,1,0:T(8,128)S(1)}, u32[]{:S(2)}, u32[]{:S(2)}) collective-permute-start(f32[4,128,512]{2,1,0:T(8,128)S(1)} %copy-done.1), channel_id=1, source_target_pairs={{0,1},{1,0},{2,3},{3,2},{4,5},{5,4},{6,7},{7,6},{8,9},{9,8},{10,11... | collective-permute-start | bytes 3145736 | tf_op jit(solution)/shard_map/ppermute | solution.py:152
  26.9 10.0 %collective-permute-start.8 = (f32[1,128,512]{2,1,0:T(8,128)S(1)}, f32[1,128,512]{2,1,0:T(8,128)S(1)}, u32[]{:S(2)}, u32[]{:S(2)}) collective-permute-start(f32[1,128,512]{2,1,0:T(8,128)S(1)} %get-tuple-element.173), channel_id=1, source_target_pairs={{0,2},{1,3},{2,0},{3,1},{4,6},{5,7},{6,4},{7,5},{8,10},{9,11},{10,... | collective-permute-start | bytes 786440 | tf_op jit(solution)/shard_map/ppermute | solution.py:152
  28.7 10.2 %collective-permute-start.6 = (f32[64,512]{1,0:T(8,128)S(1)}, f32[64,512]{1,0:T(8,128)S(1)}, u32[]{:S(2)}, u32[]{:S(2)}) collective-permute-start(f32[64,512]{1,0:T(8,128)S(1)} %get-tuple-element.95), channel_id=1, source_target_pairs={{0,2},{1,3},{2,0},{3,1},{4,6},{5,7},{6,4},{7,5},{8,10},{9,11},{10,... | collective-permute-start | bytes 393224 | tf_op jit(solution)/shard_map/ppermute | solution.py:152
  29.0 12.2 %collective-permute-start.13 = (f32[64,512]{1,0:T(8,128)S(1)}, f32[64,512]{1,0:T(8,128)S(1)}, u32[]{:S(2)}, u32[]{:S(2)}) collective-permute-start(f32[64,512]{1,0:T(8,128)S(1)} %get-tuple-element.102), channel_id=1, source_target_pairs={{0,2},{1,3},{2,0},{3,1},{4,6},{5,7},{6,4},{7,5},{8,10},{9,11},{10,... | collective-permute-start | bytes 393224 | tf_op jit(solution)/shard_map/ppermute | solution.py:152
  30.8 1.2 %copy-start.2 = (f32[4,128,512]{2,1,0:T(8,128)S(1)}, f32[4,128,512]{2,1,0:T(8,128)}, u32[]{:S(2)}) copy-start(f32[4,128,512]{2,1,0:T(8,128)} %refs_0_.4) | copy-start | bytes 3145732
  37.0 5.8 %collective-permute-start.12 = (f32[1,128,512]{2,1,0:T(8,128)S(1)}, f32[1,128,512]{2,1,0:T(8,128)S(1)}, u32[]{:S(2)}, u32[]{:S(2)}) collective-permute-start(f32[1,128,512]{2,1,0:T(8,128)S(1)} %collective-permute-done.8.refs_2_), channel_id=1, source_target_pairs={{0,1},{1,0},{2,3},{3,2},{4,5},{5,4},{6,7},{7,6},{8,9},{9,8},{10,11... | collective-permute-start | bytes 786440 | tf_op jit(solution)/shard_map/ppermute | solution.py:152
  37.1 10.8 %collective-permute-start.9 = (f32[1,128,512]{2,1,0:T(8,128)S(1)}, f32[1,128,512]{2,1,0:T(8,128)S(1)}, u32[]{:S(2)}, u32[]{:S(2)}) collective-permute-start(f32[1,128,512]{2,1,0:T(8,128)S(1)} %get-tuple-element.97), channel_id=1, source_target_pairs={{0,2},{1,3},{2,0},{3,1},{4,6},{5,7},{6,4},{7,5},{8,10},{9,11},{10,... | collective-permute-start | bytes 786440 | tf_op jit(solution)/shard_map/ppermute | solution.py:152
  41.3 1.3 %collective-permute-start.14 = (f32[64,512]{1,0:T(8,128)S(1)}, f32[64,512]{1,0:T(8,128)S(1)}, u32[]{:S(2)}, u32[]{:S(2)}) collective-permute-start(f32[64,512]{1,0:T(8,128)S(1)} %collective-permute-done.13.refs_4_), channel_id=1, source_target_pairs={{0,1},{1,0},{2,3},{3,2},{4,5},{5,4},{6,7},{7,6},{8,9},{9,8},{10,11... | collective-permute-start | bytes 393224 | tf_op jit(solution)/shard_map/ppermute | solution.py:152
  41.3 1.5 %collective-permute-start.15 = (f32[64,512]{1,0:T(8,128)S(1)}, f32[64,512]{1,0:T(8,128)S(1)}, u32[]{:S(2)}, u32[]{:S(2)}) collective-permute-start(f32[64,512]{1,0:T(8,128)S(1)} %collective-permute-done.6.refs_6_), channel_id=1, source_target_pairs={{0,1},{1,0},{2,3},{3,2},{4,5},{5,4},{6,7},{7,6},{8,9},{9,8},{10,11... | collective-permute-start | bytes 393224 | tf_op jit(solution)/shard_map/ppermute | solution.py:152
  47.9 2.4 %collective-permute-start.16 = (f32[1,128,512]{2,1,0:T(8,128)S(1)}, f32[1,128,512]{2,1,0:T(8,128)S(1)}, u32[]{:S(2)}, u32[]{:S(2)}) collective-permute-start(f32[1,128,512]{2,1,0:T(8,128)S(1)} %collective-permute-done.9.refs_2_), channel_id=1, source_target_pairs={{0,1},{1,0},{2,3},{3,2},{4,5},{5,4},{6,7},{7,6},{8,9},{9,8},{10,11... | collective-permute-start | bytes 786440 | tf_op jit(solution)/shard_map/ppermute | solution.py:152
  48.3 6.7 %collective-permute-start.18 = (f32[72,512]{1,0:T(8,128)S(1)}, f32[72,512]{1,0:T(8,128)S(1)}, u32[]{:S(2)}, u32[]{:S(2)}) collective-permute-start(f32[72,512]{1,0:T(8,128)S(1)} %get-tuple-element.115), channel_id=1, source_target_pairs={{0,2},{1,3},{2,0},{3,1},{4,6},{5,7},{6,4},{7,5},{8,10},{9,11},{10,... | collective-permute-start | bytes 442376 | tf_op jit(solution)/shard_map/ppermute | solution.py:152
  50.1 7.0 %collective-permute-start.7 = (f32[64,512]{1,0:T(8,128)S(1)}, f32[64,512]{1,0:T(8,128)S(1)}, u32[]{:S(2)}, u32[]{:S(2)}) collective-permute-start(f32[64,512]{1,0:T(8,128)S(1)} %get-tuple-element.96), channel_id=1, source_target_pairs={{0,2},{1,3},{2,0},{3,1},{4,6},{5,7},{6,4},{7,5},{8,10},{9,11},{10,... | collective-permute-start | bytes 393224 | tf_op jit(solution)/shard_map/ppermute | solution.py:152
  53.0 8.0 %collective-permute-start.20 = (f32[128,512]{1,0:T(8,128)S(1)}, f32[128,512]{1,0:T(8,128)S(1)}, u32[]{:S(2)}, u32[]{:S(2)}) collective-permute-start(f32[128,512]{1,0:T(8,128)S(1)} %get-tuple-element.113), channel_id=1, source_target_pairs={{0,4},{4,0},{8,12},{12,8},{16,20},{20,16},{24,28},{28,24},{1,5},{5... | collective-permute-start | bytes 786440 | tf_op jit(solution)/shard_map/ppermute | solution.py:155
  55.0 3.5 %collective-permute-start.19 = (f32[72,512]{1,0:T(8,128)S(1)}, f32[72,512]{1,0:T(8,128)S(1)}, u32[]{:S(2)}, u32[]{:S(2)}) collective-permute-start(f32[72,512]{1,0:T(8,128)S(1)} %collective-permute-done.18.refs_4_.refs_0_), channel_id=1, source_target_pairs={{0,1},{1,0},{2,3},{3,2},{4,5},{5,4},{6,7},{7,6},{8,9},{9,8},{10,11... | collective-permute-start | bytes 442376 | tf_op jit(solution)/shard_map/ppermute | solution.py:152
  57.1 1.3 %collective-permute-start.17 = (f32[64,512]{1,0:T(8,128)S(1)}, f32[64,512]{1,0:T(8,128)S(1)}, u32[]{:S(2)}, u32[]{:S(2)}) collective-permute-start(f32[64,512]{1,0:T(8,128)S(1)} %collective-permute-done.7.refs_2_), channel_id=1, source_target_pairs={{0,1},{1,0},{2,3},{3,2},{4,5},{5,4},{6,7},{7,6},{8,9},{9,8},{10,11... | collective-permute-start | bytes 393224 | tf_op jit(solution)/shard_map/ppermute | solution.py:152
  61.0 13.1 %collective-permute-start.21 = (f32[256,512]{1,0:T(8,128)S(1)}, f32[256,512]{1,0:T(8,128)S(1)}, u32[]{:S(2)}, u32[]{:S(2)}) collective-permute-start(f32[256,512]{1,0:T(8,128)S(1)} %get-tuple-element.120), channel_id=1, source_target_pairs={{0,4},{4,0},{8,12},{12,8},{16,20},{20,16},{24,28},{28,24},{1,5},{5... | collective-permute-start | bytes 1572872 | tf_op jit(solution)/shard_map/ppermute | solution.py:155
  67.3 6.9 %collective-permute-start.22 = (f32[8,512]{1,0:T(8,128)S(1)}, f32[8,512]{1,0:T(8,128)S(1)}, u32[]{:S(2)}, u32[]{:S(2)}) collective-permute-start(f32[8,512]{1,0:T(8,128)S(1)} %get-tuple-element.126.flux_ref), channel_id=1, source_target_pairs={{0,4},{4,0},{8,12},{12,8},{16,20},{20,16},{24,28},{28,24},{1,5},{5... | collective-permute-start | bytes 49160 | tf_op jit(solution)/shard_map/ppermute | solution.py:155
  74.1 1.9 %collective-permute-start.23 = (f32[256,512]{1,0:T(8,128)S(1)}, f32[256,512]{1,0:T(8,128)S(1)}, u32[]{:S(2)}, u32[]{:S(2)}) collective-permute-start(f32[256,512]{1,0:T(8,128)S(1)} %collective-permute-done.21.half_ref), channel_id=1, source_target_pairs={{0,1},{1,0},{2,3},{3,2},{4,5},{5,4},{6,7},{7,6},{8,9},{9,8},{10,11... | collective-permute-start | bytes 1572872 | tf_op jit(solution)/shard_map/ppermute | solution.py:152
  77.1 8.2 %collective-permute-start.24 = (f32[128,512]{1,0:T(8,128)S(1)}, f32[128,512]{1,0:T(8,128)S(1)}, u32[]{:S(2)}, u32[]{:S(2)}) collective-permute-start(f32[128,512]{1,0:T(8,128)S(1)} %get-tuple-element.139.local_ref), channel_id=1, source_target_pairs={{24,16},{28,20},{25,17},{29,21},{26,18},{30,22},{27,19},{31,23}} | collective-permute-start | bytes 786440 | tf_op jit(solution)/shard_map/ppermute | solution.py:158
  77.8 5.1 %collective-permute-start.25 = (f32[8,512]{1,0:T(8,128)S(1)}, f32[8,512]{1,0:T(8,128)S(1)}, u32[]{:S(2)}, u32[]{:S(2)}) collective-permute-start(f32[8,512]{1,0:T(8,128)S(1)} %get-tuple-element.138.local_ref), channel_id=1, source_target_pairs={{0,8},{4,12},{1,9},{5,13},{2,10},{6,14},{3,11},{7,15}} | collective-permute-start | bytes 49160 | tf_op jit(solution)/shard_map/ppermute | solution.py:158
  83.4 0.7 collective-permute-start.26
  84.6 1.8 %collective-permute-start.28 = (f32[8,512]{1,0:T(8,128)S(1)}, f32[8,512]{1,0:T(8,128)S(1)}, u32[]{:S(2)}, u32[]{:S(2)}) collective-permute-start(f32[8,512]{1,0:T(8,128)S(1)} %forward_link.3), channel_id=1, source_target_pairs={{16,24},{20,28},{17,25},{21,29},{18,26},{22,30},{19,27},{23,31}} | collective-permute-start | bytes 49160 | tf_op jit(solution)/shard_map/ppermute | solution.py:158
  85.7 5.7 %collective-permute-start.27 = (f32[128,512]{1,0:T(8,128)S(1)}, f32[128,512]{1,0:T(8,128)S(1)}, u32[]{:S(2)}, u32[]{:S(2)}) collective-permute-start(f32[128,512]{1,0:T(8,128)S(1)} %noise_link.2), channel_id=1, source_target_pairs={{16,8},{20,12},{17,9},{21,13},{18,10},{22,14},{19,11},{23,15}} | collective-permute-start | bytes 786440 | tf_op jit(solution)/shard_map/ppermute | solution.py:158
  87.4 3.9 %collective-permute-start.29 = (f32[16,512]{1,0:T(8,128)S(1)}, f32[16,512]{1,0:T(8,128)S(1)}, u32[]{:S(2)}, u32[]{:S(2)}) collective-permute-start(f32[16,512]{1,0:T(8,128)S(1)} %pad_maximum_fusion), channel_id=1, source_target_pairs={{0,4},{4,0},{8,12},{12,8},{16,20},{20,16},{24,28},{28,24},{1,5},{5... | collective-permute-start | bytes 98312 | tf_op jit(solution)/shard_map/ppermute | solution.py:155
  89.0 2.8 %collective-permute-start.31 = (f32[8,512]{1,0:T(8,128)S(1)}, f32[8,512]{1,0:T(8,128)S(1)}, u32[]{:S(2)}, u32[]{:S(2)}) collective-permute-start(f32[8,512]{1,0:T(8,128)S(1)} %get-tuple-element.147.part_ref), channel_id=1, source_target_pairs={{24,20},{28,16},{25,21},{29,17},{26,22},{30,18},{27,23},{31,19}} | collective-permute-start | bytes 49160 | tf_op jit(solution)/shard_map/ppermute | solution.py:513
  89.6 2.1 %collective-permute-start.30 = (f32[8,512]{1,0:T(8,128)S(1)}, f32[8,512]{1,0:T(8,128)S(1)}, u32[]{:S(2)}, u32[]{:S(2)}) collective-permute-start(f32[8,512]{1,0:T(8,128)S(1)} %get-tuple-element.147.part_ref), channel_id=1, source_target_pairs={{24,16},{28,20},{25,17},{29,21},{26,18},{30,22},{27,19},{31,23}} | collective-permute-start | bytes 49160 | tf_op jit(solution)/shard_map/ppermute | solution.py:513
  92.1 13.3 %collective-permute-start.32 = (f32[128,512]{1,0:T(8,128)S(1)}, f32[128,512]{1,0:T(8,128)S(1)}, u32[]{:S(2)}, u32[]{:S(2)}) collective-permute-start(f32[128,512]{1,0:T(8,128)S(1)} %noise_link.3), channel_id=1, source_target_pairs={{8,0},{12,4},{9,1},{13,5},{10,2},{14,6},{11,3},{15,7}} | collective-permute-start | bytes 786440 | tf_op jit(solution)/shard_map/ppermute | solution.py:158
  105.8 10.1 %collective-permute-start.33 = (f32[128,512]{1,0:T(8,128)S(1)}, f32[128,512]{1,0:T(8,128)S(1)}, u32[]{:S(2)}, u32[]{:S(2)}) collective-permute-start(f32[128,512]{1,0:T(8,128)S(1)} %get-tuple-element.155), channel_id=1, source_target_pairs={{0,4},{4,0},{8,12},{12,8},{16,20},{20,16},{24,28},{28,24},{1,5},{5... | collective-permute-start | bytes 786440 | tf_op jit(solution)/shard_map/ppermute | solution.py:155
  107.4 0.7 collective-permute-start.34
  108.4 7.5 %collective-permute-start.35 = (f32[8,512]{1,0:T(8,128)S(1)}, f32[8,512]{1,0:T(8,128)S(1)}, u32[]{:S(2)}, u32[]{:S(2)}) collective-permute-start(f32[8,512]{1,0:T(8,128)S(1)} %backward_link.1), channel_id=1, source_target_pairs={{8,0},{12,4},{9,1},{13,5},{10,2},{14,6},{11,3},{15,7}} | collective-permute-start | bytes 49160 | tf_op jit(solution)/shard_map/ppermute | solution.py:158
